TPU v7x, 256 devices: a whole 4x4x8 slice. The times are simulated.
256 devices in a mesh: dp: 64 (over z_hi, y, x), mp: 4 (over z_lo, core).
Axes of the slice: x: 4, y: 4, z: 8 (z_hi: 4, z_lo: 2; z = z_hi * 2 + z_lo), core: 2. Of those that a mesh axis runs over, the one named last changes fastest.
Arguments:
- hidden: bfloat16 [2048, 16, 2048], P('dp', None, 'mp'), may hold values from -6 to 6
- norm_gain: bfloat16 [2048], P('mp'), may hold values from 0.099609375 to 1.8984375
- in_x: bfloat16 [2048, 4096], P('dp', 'mp'), may hold values from -0.125 to 0.125
- in_z: bfloat16 [2048, 4096], P('dp', 'mp'), may hold values from -0.125 to 0.125
- conv_weight: float32 [4, 4096], P(None, 'mp'), may hold values from -3 to 3
- conv_bias: float32 [4096], P('mp'), may hold values from -3 to 3
- x_proj: bfloat16 [4096, 160], P(('mp', 'dp')), may hold values from -0.09375 to 0.09375
- dt_proj: bfloat16 [128, 4096], P('dp', 'mp'), may hold values from -0.5 to 0.5
- dt_bias: float32 [4096], P('mp'), may hold values from -5 to -1
- a_log: float32 [16, 4096], P(None, 'mp'), may hold values from 0 to 2.77
- skip: float32 [4096], P('mp'), may hold values from 0.5 to 1.5
- out_proj: bfloat16 [4096, 2048], P('mp', 'dp'), may hold values from -0.09375 to 0.09375
- state_pool: float32 [2560, 16, 4096], P('dp', None, 'mp'), may hold values from -6 to 6
- conv_pool: float32 [2560, 3, 4096], P('dp', None, 'mp'), may hold values from -6 to 6
- permutation: int32 [2048], P('dp'), may hold values from 0 to 2047, as said below
- page_table: int32 [2048], P('dp'), may hold values from 0 to 2559, as said below
- accepted: int32 [2048], P('dp'), may hold values from 1 to 16
Outputs:
- verified: bfloat16 [2048, 16, 2048], P('dp', None, 'mp')
- new_state_pool: float32 [2560, 16, 4096], P('dp', None, 'mp')
- new_conv_pool: float32 [2560, 3, 4096], P('dp', None, 'mp')
Inputs may be any that keep to these rules, and one draw needn't show every extreme that they name: `permutation`: A request at position j of the block of dp index d goes to position j of the block of dp index (d + o) mod 64, where the shift o depends only on j mod 32 and takes 32 different values; so each dp index sends exactly 1 request to each of 32 dp indices and receives 32. `page_table`: the requests of dp index d use distinct slots among the 40 slots d * 40 .. (d + 1) * 40 - 1.
All inputs are finite; a program needn't handle non-finite values.
Results may differ from a plain program's by a relative error of at most 0.0065.
Values may be sent and summed in bfloat16 or wider, within the bound.
No kernel may reach another device: no remote copies, remote signals or barrier semaphores. Data moves between devices by JAX's collectives and lax.ppermute only.
A program may use at most 128 MiB of HBM per device.

v0:
```python
import jax
import jax.numpy as jnp
from jax import lax
from jax.sharding import PartitionSpec as P

EPS = 1e-05


def route_plan(permutation, count, peers):
    capacity = count // min(count, peers)
    target = permutation // count
    order = jnp.arange(count)
    earlier = (target[:, None] == target[None, :]) & (order[None, :] < order[:, None])
    rank_within = jnp.sum(earlier.astype(jnp.int32), axis=1)
    position = target * capacity + rank_within
    match = position[None, :] == jnp.arange(peers * capacity)[:, None]
    filled = jnp.any(match, axis=1)
    source = jnp.argmax(match, axis=1)
    return (position, filled, source)


def pack_rows(values, filled, source):
    picked = jnp.take(values, source, axis=0)
    shape = (filled.shape[0],) + (1,) * (values.ndim - 1)
    return jnp.where(filled.reshape(shape), picked, jnp.zeros_like(picked))


def unpack_rows(values, arrived, count):
    match = arrived[None, :] == jnp.arange(count)[:, None]
    index = jnp.argmax(match, axis=1)
    return jnp.take(values, index, axis=0)


def write_pool(pool, slot_local, values):
    match = slot_local[None, :] == jnp.arange(pool.shape[0])[:, None]
    filled = jnp.any(match, axis=1)
    index = jnp.argmax(match, axis=1)
    return jnp.where(filled[:, None, None], jnp.take(values, index, axis=0), pool)


def verify_layer(
    hidden,
    norm_gain,
    in_x,
    in_z,
    conv_weight,
    conv_bias,
    x_proj,
    dt_proj,
    dt_bias,
    a_log,
    skip,
    out_proj,
    caches,
    accepted,
):
    count, drafts, width_local = hidden.shape
    tokens = count * drafts
    inner_local = in_x.shape[1]
    state_count = a_log.shape[0]
    taps = conv_weight.shape[0]
    rank = x_proj.shape[1] - 2 * state_count
    full, gain_full = (
        lax.all_gather(hidden, "mp", axis=2, tiled=True),
        lax.all_gather(norm_gain, "mp", axis=0, tiled=True),
    )
    rows = full.reshape(tokens, -1).astype(jnp.float32)
    scale = lax.rsqrt(jnp.mean(rows * rows, axis=1, keepdims=True) + EPS)
    normed = (rows * scale * gain_full.astype(jnp.float32)).astype(jnp.bfloat16)
    columns = normed
    x_wide = jnp.dot(
        columns, lax.all_gather(in_x, "dp", axis=0, tiled=True), preferred_element_type=jnp.float32
    )
    z_wide = jnp.dot(
        columns, lax.all_gather(in_z, "dp", axis=0, tiled=True), preferred_element_type=jnp.float32
    )
    x_part = x_wide.astype(jnp.bfloat16)
    z_part = z_wide.astype(jnp.bfloat16)
    states = caches[:, :state_count, :]
    edges = caches[:, state_count:, :]
    padded = jnp.concatenate(
        [edges, x_part.astype(jnp.float32).reshape(count, drafts, inner_local)], axis=1
    )
    mixed = conv_bias + jnp.zeros((count, drafts, inner_local), jnp.float32)
    for offset in range(taps):
        mixed = mixed + conv_weight[offset] * padded[:, offset : offset + drafts, :]
    inputs = jax.nn.silu(mixed).astype(jnp.bfloat16)
    flat_inputs = inputs.reshape(tokens, inner_local)
    piece = lax.all_gather(x_proj, "dp", axis=0, tiled=True)
    columns = flat_inputs
    low_sum = jnp.dot(columns, piece[:, :rank], preferred_element_type=jnp.float32)
    both_sum = jnp.einsum("ks,tk->st", piece[:, rank:], columns, preferred_element_type=jnp.float32)
    low_full, both = lax.psum((low_sum, both_sum), "mp")
    low_half = low_full.astype(jnp.bfloat16)
    columns = low_half
    delta = jnp.dot(
        columns,
        lax.all_gather(dt_proj, "dp", axis=0, tiled=True),
        preferred_element_type=jnp.float32,
    )
    delta = jax.nn.softplus(delta + dt_bias).reshape(count, drafts, inner_local)
    decay_rate = -jnp.exp(a_log)
    inputs_wide = inputs.astype(jnp.float32)
    driven = delta * inputs_wide
    b_time = both[:state_count].reshape(state_count, count, drafts).transpose(2, 1, 0)
    c_time = both[state_count:].reshape(state_count, count, drafts).transpose(2, 1, 0)

    def advance(carry, slices):
        state, kept = carry
        step_delta, step_drive, step_b, step_c, index = slices
        state = (
            jnp.exp(step_delta[:, None, :] * decay_rate[None]) * state
            + step_drive[:, None, :] * step_b[:, :, None]
        )
        output = jnp.sum(state * step_c[:, :, None], axis=1)
        kept = jnp.where((accepted - 1 == index)[:, None, None], state, kept)
        return ((state, kept), output)

    (final_state, kept), outputs = lax.scan(
        advance,
        (states, states),
        (
            delta.transpose(1, 0, 2),
            driven.transpose(1, 0, 2),
            b_time,
            c_time,
            jnp.arange(drafts, dtype=jnp.int32),
        ),
    )
    outputs = outputs.transpose(1, 0, 2)
    gate_wide = z_part.astype(jnp.float32).reshape(count, drafts, inner_local)
    gated = (
        ((outputs + skip * inputs_wide) * jax.nn.silu(gate_wide))
        .astype(jnp.bfloat16)
        .reshape(tokens, inner_local)
    )
    index = accepted[:, None] + jnp.arange(taps - 1, dtype=jnp.int32)[None, :]
    new_edges = jnp.take_along_axis(padded, index[:, :, None], axis=1)
    new_caches = jnp.concatenate([kept, new_edges], axis=1)
    terms = jnp.dot(
        gated,
        lax.all_gather(out_proj, "dp", axis=1, tiled=True),
        preferred_element_type=jnp.float32,
    )
    summed = lax.psum_scatter(terms, "mp", scatter_dimension=1, tiled=True)
    result = (summed + hidden.reshape(tokens, width_local).astype(jnp.float32)).astype(jnp.bfloat16)
    return (result.reshape(count, drafts, width_local), new_caches)


def on_device(
    hidden,
    norm_gain,
    in_x,
    in_z,
    conv_weight,
    conv_bias,
    x_proj,
    dt_proj,
    dt_bias,
    a_log,
    skip,
    out_proj,
    state_pool,
    conv_pool,
    permutation,
    page_table,
    accepted,
):
    count = hidden.shape[0]
    state_count = state_pool.shape[1]
    pool_count = state_pool.shape[0]
    peers = lax.axis_size("dp")
    slot_local = page_table % pool_count
    caches = jnp.concatenate(
        [jnp.take(state_pool, slot_local, axis=0), jnp.take(conv_pool, slot_local, axis=0)], axis=1
    )
    position, filled, source = route_plan(permutation, count, peers)
    arrival_slot = permutation % count
    details = jnp.stack([arrival_slot, accepted], axis=1).astype(jnp.float32)
    details_sent = jnp.where(filled[:, None], jnp.take(details, source, axis=0), -1.0)
    got_hidden = lax.all_to_all(
        pack_rows(hidden, filled, source), "dp", split_axis=0, concat_axis=0, tiled=True
    )
    got_caches, got_details = (
        lax.all_to_all(
            pack_rows(caches, filled, source), "dp", split_axis=0, concat_axis=0, tiled=True
        ),
        lax.all_to_all(details_sent, "dp", split_axis=0, concat_axis=0, tiled=True),
    )
    arrived = got_details[:, 0].astype(jnp.int32)
    local_hidden = unpack_rows(got_hidden, arrived, count)
    local_caches = unpack_rows(got_caches, arrived, count)
    local_accept = unpack_rows(got_details[:, 1], arrived, count).astype(jnp.int32)
    verified, new_caches = verify_layer(
        local_hidden,
        norm_gain,
        in_x,
        in_z,
        conv_weight,
        conv_bias,
        x_proj,
        dt_proj,
        dt_bias,
        a_log,
        skip,
        out_proj,
        local_caches,
        local_accept,
    )
    returned = jnp.take(new_caches, jnp.maximum(arrived, 0), axis=0)
    returned = jnp.where((arrived >= 0)[:, None, None], returned, jnp.zeros_like(returned))
    back = lax.all_to_all(
        returned.astype(jnp.bfloat16), "dp", split_axis=0, concat_axis=0, tiled=True
    ).astype(returned.dtype)
    settled = jnp.take(back, position, axis=0)
    new_state_pool = write_pool(state_pool, slot_local, settled[:, :state_count])
    new_conv_pool = write_pool(conv_pool, slot_local, settled[:, state_count:])
    return (verified, new_state_pool, new_conv_pool)


def solution(mesh):
    return jax.shard_map(
        on_device,
        mesh=mesh,
        in_specs=(
            P("dp", None, "mp"),
            P("mp"),
            P("dp", "mp"),
            P("dp", "mp"),
            P(None, "mp"),
            P("mp"),
            P(("mp", "dp"), None),
            P("dp", "mp"),
            P("mp"),
            P(None, "mp"),
            P("mp"),
            P("mp", "dp"),
            P("dp", None, "mp"),
            P("dp", None, "mp"),
            P("dp"),
            P("dp"),
            P("dp"),
        ),
        out_specs=(P("dp", None, "mp"), P("dp", None, "mp"), P("dp", None, "mp")),
        check_vma=False,
    )
```

profile of v0, /device:TPU:2, one launch (start us, length us, event | category | flops | bytes accessed | tf_op | source)
XLA Modules:
  0.0 933.9 jit_solution(18091020469888556631)
XLA Ops:
  11.0 14.6 %all-to-all-start.1 = ((f32[64,1,2]{2,1,0:T(1,128)}), f32[64,1,2]{2,1,0:T(1,128)S(1)}, u32[]{:S(2)}, u32[]{:S(2)}) async-start(f32[64,1,2]{2,1,0:T(1,128)} %copy.94), calls=%async_computation.1 | async-start | bytes 65536 | tf_op jit(solution)/shard_map/all_to_all | solution.py:188
  27.5 9.0 all-to-all-done.1
  36.4 6.3 all-to-all-start.2
  44.3 27.3 %all-to-all-done.2 = bf16[64,16,512]{2,1,0:T(8,128)(2,1)} async-done(((bf16[64,16,512]{2,1,0:T(8,128)(2,1)}), bf16[64,16,512]{2,1,0:T(8,128)(2,1)}, u32[]{:S(2)}, u32[]{:S(2)}) %all-to-all-start.2) | async-done | bytes 1048608 | tf_op jit(solution)/shard_map/all_to_all | solution.py:181
  71.5 2.6 gather_fusion.4
  74.1 2.0 broadcast_select_fusion.4
  77.4 2.0 gather_fusion
  81.6 3.6 gather_fusion.9
  85.2 7.0 select_select_fusion.1
  92.1 7.0 all-to-all-start
  100.0 140.5 %all-gather = bf16[4,1,512]{2,1,0:T(2,128)(2,1)S(1)} all-gather(bf16[1,1,512]{2,1,0:T(2,128)(2,1)S(1)} %reshape.371), channel_id=1, replica_groups=mesh['dp'=64,'mp'=4] {'mp'}, dimensions={0}, use_global_device_ids=true | all-gather | bytes 5120 | tf_op jit(solution)/shard_map/all_gather | solution.py:65
  240.5 202.5 %all_gather.24 = bf16[1024,160]{1,0:T(8,128)(2,1)} all-gather(bf16[16,160]{1,0:T(8,128)(2,1)S(1)} %copy-done.16), channel_id=1, replica_groups=mesh['dp'=64,'mp'=4] {'dp'}, dimensions={0}, use_global_device_ids=true | all-gather | bytes 332800 | tf_op jit(solution)/shard_map/all_gather | solution.py:89
  443.0 2.2 multiply_reduce_fusion.1
  445.3 1.9 fusion.2
  447.2 5.2 convolution_convert_fusion.1
  452.6 5.2 gather_fusion.10
  457.9 2.3 broadcast_select_fusion.2
  461.8 1.4 copy-done.4
  463.3 2.6 multiply_convert_fusion
  465.9 2.0 copy.100
  469.6 196.8 %all-gather.1 = bf16[64,2,1024]{2,1,0:T(2,128)(2,1)S(1)} all-gather(bf16[1,2,1024]{2,1,0:T(2,128)(2,1)S(1)} %bitcast.97), channel_id=1, replica_groups=mesh['dp'=64,'mp'=4] {'dp'}, dimensions={0}, use_global_device_ids=true | all-gather | bytes 266240 | tf_op jit(solution)/shard_map/all_gather | solution.py:98
  667.2 4.5 convolution_convert_fusion
  671.7 1.6 convert.4
  674.9 14.2 %all-reduce.4 = bf16[512,128]{1,0:T(8,128)(2,1)} all-reduce(f32[512,128]{1,0:T(8,128)S(1)} %fusion.12), channel_id=1, replica_groups=mesh['dp'=64,'mp'=4] {'mp'}, use_global_device_ids=true, to_apply=%region_5.8 | all-reduce | flops 65536 | bytes 393216 | tf_op jit(solution)/shard_map/psum | solution.py:93
  689.0 2.3 compare_select_fusion
  691.4 4.6 fusion.3
  699.0 82.8 %while.16 = (s32[]{:T(128)}, f32[32,16,1024]{2,1,0:T(8,128)S(1)}, bf16[32,16,1024]{2,1,0:T(8,128)(2,1)S(1)}, f32[16,32,1024]{2,1,0:T(8,128)}, f32[16,32,1024]{2,...) while((s32[]{:T(128)}, f32[32,16,1024]{2,1,0:T(8,128)S(1)}, ...), condition=%wide.region_9.12_spmd, body=%wide.region_7.11_spmd.sunk | while | flops 3637314 | bytes 9646925 | solution.py:119
  700.7 1.2 multiply_reduce_fusion.3
  705.9 1.2 multiply_reduce_fusion.3
  711.0 1.2 multiply_reduce_fusion.3
  716.2 1.2 multiply_reduce_fusion.3
  721.4 1.2 multiply_reduce_fusion.3
  726.6 1.2 multiply_reduce_fusion.3
  736.9 1.2 multiply_reduce_fusion.3
  781.8 4.1 fusion.6
  786.5 6.6 fusion.29
  794.7 3.3 gather_fusion.8
  798.7 2.4 gather_fusion.11
  801.1 5.6 fusion
  806.7 4.7 all-to-all-start.3
  811.7 92.5 %all-to-all-done.3 = bf16[64,19,1024]{2,1,0:T(8,128)(2,1)S(1)} async-done(((bf16[64,19,1024]{2,1,0:T(8,128)(2,1)}), bf16[64,19,1024]{2,1,0:T(8,128)(2,1)S(1)}, u32[]{:S(2)}, u32[]{:S(2)}) %all-to-all-start.3) | async-done | bytes 2490400 | tf_op jit(solution)/shard_map/all_to_all | solution.py:212
  904.2 3.4 convert_element_type.91
  907.6 3.5 gather_fusion.12
  912.8 2.2 gather_fusion.6
  915.0 3.0 gather_fusion.7
  918.0 1.5 copy_select_fusion
  920.6 3.7 select_select_fusion.2
  924.3 2.3 add_convert_fusion
  (252 shorter events, 99.5 us)
Async XLA Ops:
  7.2 18.5 %copy-start = (bf16[32,16,512]{2,1,0:T(8,128)(2,1)S(1)}, bf16[32,16,512]{2,1,0:T(8,128)(2,1)}, u32[]{:S(2)}) copy-start(bf16[32,16,512]{2,1,0:T(8,128)(2,1)} %param.23) | copy-start | bytes 1572868
  8.1 19.4 %copy-start.21 = (s32[32]{0:T(128)}, s32[32]{0:T(128)S(1)}, u32[]{:S(2)}) copy-start(s32[32]{0:T(128)S(1)} %get-tuple-element.243) | copy-start | bytes 388
  11.0 25.4 %all-to-all-start.1 = ((f32[64,1,2]{2,1,0:T(1,128)}), f32[64,1,2]{2,1,0:T(1,128)S(1)}, u32[]{:S(2)}, u32[]{:S(2)}) async-start(f32[64,1,2]{2,1,0:T(1,128)} %copy.94), calls=%async_computation.1 | async-start | bytes 65536 | tf_op jit(solution)/shard_map/all_to_all | solution.py:188
  36.4 35.1 %all-to-all-start.2 = ((bf16[64,16,512]{2,1,0:T(8,128)(2,1)}), bf16[64,16,512]{2,1,0:T(8,128)(2,1)}, u32[]{:S(2)}, u32[]{:S(2)}) async-start(bf16[64,16,512]{2,1,0:T(8,128)(2,1)} %select_select_fusion.3), calls=%async_computation.2 | async-start | bytes 2097152 | tf_op jit(solution)/shard_map/all_to_all | solution.py:181
  42.8 34.1 %copy-start.24 = (s32[32]{0:T(128)S(1)}, s32[32]{0:T(128)}, u32[]{:S(2)}) copy-start(s32[32]{0:T(128)} %param.38) | copy-start | bytes 388
  42.8 34.6 %copy-start.8 = (f32[40,16,1024]{2,1,0:T(8,128)S(1)}, f32[40,16,1024]{2,1,0:T(8,128)}, u32[]{:S(2)}) copy-start(f32[40,16,1024]{2,1,0:T(8,128)} %param.35) | copy-start | bytes 7864324
  42.8 400.2 %all-gather.7.cloned.1.call-start = ((), (), s32[]{:S(2)}) async-start(), calls=%async_computation.5 | async-start | bytes 2621440 | tf_op jit(solution)/shard_map/all_gather | solution.py:64
  76.1 371.1 %all-gather.9.cloned.1.call-start = ((), (), s32[]{:S(2)}) async-start(), calls=%async_computation.6 | async-start | bytes 4259840 | tf_op jit(solution)/shard_map/all_gather | solution.py:72
  76.9 0.5 copy-start.25
  77.4 2.0 copy-start.2
  79.4 1.6 copy-start.10
  92.1 7.8 copy-start.20
  92.1 148.4 %copy-start.16 = (bf16[16,160]{1,0:T(8,128)(2,1)S(1)}, bf16[16,160]{1,0:T(8,128)(2,1)}, u32[]{:S(2)}) copy-start(bf16[16,160]{1,0:T(8,128)(2,1)} %param.29) | copy-start | bytes 15364
  92.1 350.9 %copy-start.15 = (f32[4,1024]{1,0:T(4,128)S(1)}, f32[4,1024]{1,0:T(4,128)}, u32[]{:S(2)}) copy-start(f32[4,1024]{1,0:T(4,128)} %param.27) | copy-start | bytes 49156
  92.1 360.5 %all-to-all-start = ((f32[64,19,1024]{2,1,0:T(8,128)}), f32[64,19,1024]{2,1,0:T(8,128)}, u32[]{:S(2)}, u32[]{:S(2)}) async-start(f32[64,19,1024]{2,1,0:T(8,128)} %select_select_fusion.1), calls=%async_computation | async-start | bytes 12582912 | tf_op jit(solution)/shard_map/all_to_all | solution.py:185
  99.2 568.0 %all-gather.11.cloned.1.call-start = ((), (), s32[]{:S(2)}) async-start(), calls=%async_computation.8 | async-start | bytes 4259840 | tf_op jit(solution)/shard_map/all_gather | solution.py:75
  99.9 596.1 %all-reduce.3.cloned.1.call-start = ((), (), s32[]{:S(2)}) async-start(), calls=%async_computation.7 | async-start | bytes 131072 | tf_op jit(solution)/shard_map/psum | solution.py:93
  443.0 2.3 copy-start.9
  460.2 1.7 copy-start.5
  460.5 2.8 copy-start.17
  461.8 1.4 copy-start.4
  463.3 4.6 copy-start.12
  465.9 3.7 copy-start.18
  465.9 201.3 %copy-start.14 = (f32[16,1024]{1,0:T(8,128)S(1)}, f32[16,1024]{1,0:T(8,128)}, u32[]{:S(2)}) copy-start(f32[16,1024]{1,0:T(8,128)} %param.32) | copy-start | bytes 196612
  465.9 201.3 %copy-start.11 = (bf16[512,2048]{1,0:T(8,128)(2,1)S(1)}, bf16[512,2048]{1,0:T(8,128)(2,1)}, u32[]{:S(2)}) copy-start(bf16[512,2048]{1,0:T(8,128)(2,1)} %fusion.2) | copy-start | bytes 6291460
  468.9 317.6 %all-gather.13.cloned.1.call-start = ((), (), s32[]{:S(2)}) async-start(), calls=%async_computation.9 | async-start | bytes 4259840 | tf_op jit(solution)/shard_map/all_gather | solution.py:142
  469.5 454.8 %reduce-scatter.2.cloned.1.call-start = ((), (), s32[]{:S(2)}) async-start(), calls=%async_computation.10 | async-start | bytes 5242880 | tf_op jit(solution)/shard_map/reduce_scatter | solution.py:145
  671.7 1.7 copy-start.13
  671.7 2.8 copy-start.6
  674.5 14.5 %copy-start.23 = (f32[1024]{0:T(1024)S(1)}, f32[1024]{0:T(1024)}, u32[]{:S(2)}) copy-start(f32[1024]{0:T(1024)} %param.31) | copy-start | bytes 12292
  699.0 82.8 %copy-start.19 = (f32[1024]{0:T(1024)S(1)}, f32[1024]{0:T(1024)}, u32[]{:S(2)}) copy-start(f32[1024]{0:T(1024)} %param.33) | copy-start | bytes 12292
  793.1 0.6 copy-start.26
  806.7 4.7 copy-start.22
  806.7 97.5 %all-to-all-start.3 = ((bf16[64,19,1024]{2,1,0:T(8,128)(2,1)}), bf16[64,19,1024]{2,1,0:T(8,128)(2,1)S(1)}, u32[]{:S(2)}, u32[]{:S(2)}) async-start(bf16[64,19,1024]{2,1,0:T(8,128)(2,1)} %fusion), calls=%async_computation.4 | async-start | bytes 6291456 | tf_op jit(solution)/shard_map/all_to_all | solution.py:212
  912.8 5.2 copy-start.3
  915.0 5.6 copy-start.7
  920.6 6.0 copy-start.1
Sparse Core Ops, SparseCore 0:
  76.2 63.9 all-gather.6
  143.6 166.9 all-gather.8
  313.8 87.7 all-gather.10
  469.0 39.6 all-reduce.2
  512.4 89.5 all-gather.12
  793.3 85.5 reduce-scatter.1
where the time goes:
time: 944 us; the launch traced here: 934 us
  blocking collectives  554 us (59%)
  waiting for transfers between devices  131 us (14%)
  local copies, waits for them, and re-layouts  94 us (10%)
  other arithmetic  86.5 us (9%)
  starting transfers between devices  33 us (3%)
  matrix products  20.1 us (2%)
  between operations  15.1 us (2%)
    all_gather x1, blocking collectives, verify_layer(): piece = lax.all_gather(x_proj, 'dp', axis=0, tiled=True)  202 us
    all_gather x1, blocking collectives, verify_layer(): lax.all_gather(dt_proj, 'dp', axis=0, tiled=True)  197 us
    all_gather x1, blocking collectives, verify_layer(): lax.all_gather(norm_gain, 'mp', axis=0, tiled=True)  141 us
    all_to_all x1, waiting for transfers between devices, on_device(): lax.all_to_all(returned.astype(jnp.bfloat16), 'dp', split_axis=0, concat_...  92.5 us
    all_to_all x1, waiting for transfers between devices, on_device(): lax.all_to_all(pack_rows(hidden, filled, source), 'dp', split_axis=0, con...  27.3 us
    reduce_sum x16, other arithmetic, advance(): output = jnp.sum(state * step_c[:, :, None], axis=1)  19.9 us
  transfers between devices with their start and end apart: 10, of which 3 were waited for; matrix products, arithmetic and copies ran while one was open for 19% of the time, Pallas kernels for 0%

commit v1 on v0

v1 whole, which is shorter than its diff:
```python
import jax
import jax.numpy as jnp
from jax import lax
from jax.experimental import pallas as pl
from jax.experimental.pallas import tpu as pltpu
from jax.sharding import PartitionSpec as P

EPS = 1e-05
LOG2E = 1.4426950408889634
BF = jnp.bfloat16
F32 = jnp.float32
SIDE = 4
CUT = 384

VMEM = pl.BlockSpec(memory_space=pltpu.VMEM)
SMEM = pl.BlockSpec(memory_space=pltpu.SMEM)
ANY = pl.BlockSpec(memory_space=pl.ANY)


def shift_pairs(axis, step):
    pairs = []
    for z in range(SIDE):
        for y in range(SIDE):
            for x in range(SIDE):
                to = [z, y, x]
                to[axis] = (to[axis] + step) % SIDE
                pairs.append(((z * SIDE + y) * SIDE + x, (to[0] * SIDE + to[1]) * SIDE + to[2]))
    return pairs


def hop(value, axis, step):
    return lax.ppermute(value, "dp", shift_pairs(axis, step))


def across(value, flip):
    return lax.ppermute(value, "mp", [(m, m ^ flip) for m in range(4)])


def ring(block, axis):
    half = block.shape[0] // 2
    after = hop(block, axis, -1)
    before = hop(block, axis, 1)
    low = hop(before[:half], axis, 1)
    high = hop(after[half:], axis, -1)
    return block, after, low, high, before


def gather_z(block):
    return jnp.stack([block, hop(block, 0, -1), hop(block, 0, 2), hop(block, 0, 1)])


def gather_plane(stack, middle, last):
    own, after, low, high, before = ring(stack, middle)
    whole = jnp.stack([own, after, jnp.concatenate([low, high]), before])
    return ring(whole, last)


def start_pieces(pieces, place, middle_first, body):
    z, y, x = place
    own, after, low, high, before = pieces

    def one(k, _):
        for i in range(SIDE):
            for f in range(SIDE):
                if f == 2:
                    ref, at = (low, i) if i < 2 else (high, i - 2)
                else:
                    ref, at = {0: own, 1: after, 3: before}[f], i
                dz = (z + k) & 3
                if middle_first:
                    dx, dy = (x + i) & 3, (y + f) & 3
                else:
                    dy, dx = (y + i) & 3, (x + f) & 3
                body(ref.at[at, k], (dz * SIDE + dy) * SIDE + dx)
        return 0

    lax.fori_loop(0, SIDE, one, 0)


def place_of(where):
    d = where[0]
    return d >> 4, (d >> 2) & 3, d & 3


def sigmoid_times(value):
    return value / (1.0 + jnp.exp(-value))


def order_matrix(rows, columns, drafts, count):
    i = lax.broadcasted_iota(jnp.int32, (rows, columns), 0)
    j = lax.broadcasted_iota(jnp.int32, (rows, columns), 1)
    return ((i % count) * drafts + i // count == j).astype(BF)


def front_kernel(
    where, pages, accepted, h0, h1, h2, h3, a0, a1, a2, a3, a4, b0, b1, b2, b3, b4,
    taps, bias, pool, normed_out, inputs_out, sums_out, dt_out, pool_out,
    weight, proj, dt_raw, dt_wide, xs, edges, fresh, plain, sems,
):
    place = place_of(where)
    m = where[1]
    drafts, count, width = xs.shape
    tokens = drafts * count
    slots = pool.shape[1]

    def take_a(src, d):
        pltpu.make_async_copy(src.at[pl.ds(0, 32), :], weight.at[pl.ds(d * 32, 32), pl.ds(0, CUT)], sems.at[0]).start()
        pltpu.make_async_copy(src.at[pl.ds(32, 16), pl.ds(0, 256)], proj.at[pl.ds(d * 16, 16), :], sems.at[1]).start()
        pltpu.make_async_copy(src.at[pl.ds(32, 16), pl.ds(256, 128)], dt_raw.at[pl.ds(d * 16, 16), :], sems.at[2]).start()

    def take_b(src, d):
        pltpu.make_async_copy(src, weight.at[pl.ds(d * 32, 32), pl.ds(CUT, width - CUT)], sems.at[0]).start()

    start_pieces((a0, a1, a2, a3, a4), place, True, take_a)
    start_pieces((b0, b1, b2, b3, b4), place, False, take_b)

    blocks = (h0, h1, h2, h3)
    step = 32

    def norm(n, _):
        at = pl.ds(pl.multiple_of(n * step, step), step)
        rows = [h[at, :].astype(F32) for h in blocks]
        total = sum(jnp.sum(r * r, axis=1, keepdims=True) for r in rows)
        scale = lax.rsqrt(total / 2048.0 + EPS)
        for k, h in enumerate(blocks):
            gain = h[pl.ds(tokens, 1), :].astype(F32)
            plain[k, at, :] = (rows[k] * scale * gain).astype(BF)
        return 0

    lax.fori_loop(0, tokens // step, norm, 0)
    order = order_matrix(tokens, tokens, drafts, count)
    for k in range(4):
        normed_out[k] = jnp.dot(order, plain[k], preferred_element_type=F32).astype(BF)

    def edge(r, _):
        slot = lax.rem(pages[r], slots)
        for k in range(3):
            edges[k, pl.ds(r, 1), :] = pool[k, pl.ds(slot, 1), :]
        return 0

    lax.fori_loop(0, count, edge, 0)
    pltpu.make_async_copy(weight, weight, sems.at[0]).wait()
    pltpu.make_async_copy(proj, proj, sems.at[1]).wait()
    pltpu.make_async_copy(dt_raw, dt_raw, sems.at[2]).wait()

    def project(n, _):
        at = pl.ds(pl.multiple_of(n * 256, 256), 256)
        total = jnp.zeros((tokens, 256), F32)
        for k in range(4):
            total = total + jnp.dot(
                normed_out[k], weight[pl.ds((m ^ k) * 512, 512), at], preferred_element_type=F32
            )
        xs[:, :, at] = total.astype(BF).astype(F32).reshape(drafts, count, 256)
        return 0

    lax.fori_loop(0, width // 256, project, 0)

    def mix(n, _):
        rows = pl.ds(pl.multiple_of((n // 4) * 16, 16), 16)
        at = pl.ds(pl.multiple_of((n % 4) * 256, 256), 256)
        acc = jnp.concatenate([accepted[rows, :]] * 2, axis=1)
        window = [edges[k, rows, at] for k in range(3)]
        kept = [window[0], window[0], window[0]]
        for p in range(1, 3):
            for k in range(3):
                kept[k] = jnp.where(acc + k == p, window[p], kept[k])
        tap = [taps[k : k + 1, at] for k in range(4)]
        base = bias[:, at]
        for t in range(drafts):
            now = xs[t, rows, at]
            mixed = base + tap[0] * window[0]
            mixed = mixed + tap[1] * window[1]
            mixed = mixed + tap[2] * window[2]
            mixed = mixed + tap[3] * now
            inputs_out[pl.ds(t * count + (n // 4) * 16, 16), at] = sigmoid_times(mixed).astype(BF)
            for k in range(3):
                kept[k] = jnp.where(acc + k == t + 3, now, kept[k])
            window = [window[1], window[2], now]
        for k in range(3):
            fresh[k, rows, at] = kept[k]
        return 0

    lax.fori_loop(0, (count // 16) * (width // 256), mix, 0)
    sums = lax.dot_general(
        proj[...], inputs_out[...], (((0,), (1,)), ((), ())), preferred_element_type=F32
    )
    sums_out[...] = sums[: sums_out.shape[0]]
    dt_wide[...] = dt_raw[...].astype(F32)
    for c in range(width // 128):
        dt_out[:, c * 128 : (c + 1) * 128] = dt_wide[pl.ds(c, 128, stride=8), :].astype(BF)
    pool_out[...] = pool[...]

    def settle(r, _):
        slot = lax.rem(pages[r], slots)
        for k in range(3):
            pool_out[k, pl.ds(slot, 1), :] = fresh[k, pl.ds(r, 1), :]
        return 0

    lax.fori_loop(0, count, settle, 0)


def scan_kernel(
    pages, accepted, sums_a, sums_b, dt, dt_bias, a_log, inputs, pool, ys_out, pool_out,
    low, both, delta, decay, start, wide, kept,
):
    tokens, width = inputs.shape
    count = accepted.shape[0]
    drafts = tokens // count
    states = a_log.shape[0]
    rank = low.shape[1]
    slots = pool.shape[0] // states

    def fetch(r, _):
        slot = lax.rem(pages[r], slots)
        for c in range(width // 128):
            start[c, pl.ds(pl.multiple_of(r * states, states), states), :] = pool[
                pl.ds(pl.multiple_of(slot * states, states), states), c * 128 : (c + 1) * 128
            ]
        return 0

    lax.fori_loop(0, count, fetch, 0)

    def carry_over(n, _):
        at = pl.ds(pl.multiple_of(n * states, states), states)
        pool_out[at, :] = pool[at, :]
        return 0

    lax.fori_loop(0, slots, carry_over, 0)
    summed = sums_a[...] + sums_b[...]
    low[...] = summed[:rank].T.astype(BF)
    rest = jnp.concatenate([summed[rank:], jnp.zeros((128 - 2 * states, tokens), F32)], axis=0)
    both[...] = rest.T

    def steps(n, _):
        at = pl.ds(pl.multiple_of(n * 256, 256), 256)
        value = jnp.dot(low[...], dt[:, at], preferred_element_type=F32) + dt_bias[:, at]
        delta[:, at] = jnp.maximum(value, 0.0) + jnp.log1p(jnp.exp(-jnp.abs(value)))
        return 0

    lax.fori_loop(0, width // 256, steps, 0)
    for s in range(states):
        row = -jnp.exp(a_log[s : s + 1, :]) * LOG2E
        decay[s] = jnp.broadcast_to(row, (8, width))

    def some(rb, _):
        def spread(t, _):
            tile = both[pl.ds(pl.multiple_of(t * count + rb * 8, 8), 8), :]
            for q in range(2 * states):
                wide[t, q] = jnp.broadcast_to(tile[:, q : q + 1], (8, 128))
            return 0

        lax.fori_loop(0, drafts, spread, 0)
        last = accepted[pl.ds(pl.multiple_of(rb * 8, 8), 8), :] - 1

        def columns(cb, _):
            at = pl.ds(pl.multiple_of(cb * 128, 128), 128)
            first = tuple(
                start[cb, pl.ds(rb * 8 * states + s, 8, stride=states), :] for s in range(states)
            )

            def advance(t, state):
                rows = pl.ds(pl.multiple_of(t * count + rb * 8, 8), 8)
                d = delta[rows, at]
                drive = d * wide_inputs(rows, at)
                here = last == t
                out = None
                nexts = []
                for s in range(states):
                    new = jnp.exp2(d * decay[s, :, at]) * state[s] + drive * wide[t, s]
                    term = new * wide[t, states + s]
                    out = term if out is None else out + term
                    pltpu.store(kept.at[cb, pl.ds(pl.multiple_of(s * count + rb * 8, 8), 8), :], new, mask=here)
                    nexts.append(new)
                ys_out[rows, at] = out
                return tuple(nexts)

            lax.fori_loop(0, drafts, advance, first, unroll=2)
            return 0

        lax.fori_loop(0, width // 128, columns, 0)
        return 0

    def wide_inputs(rows, at):
        return inputs[rows, at].astype(F32)

    lax.fori_loop(0, count // 8, some, 0)

    def settle(r, _):
        slot = lax.rem(pages[r], slots)
        for c in range(width // 128):
            for s in range(0, states, 8):
                pool_out[
                    pl.ds(pl.multiple_of(slot * states + s, 8), 8), c * 128 : (c + 1) * 128
                ] = kept[c, pl.ds(s * count + r, 8, stride=count), :]
        return 0

    lax.fori_loop(0, count, settle, 0)


def back_kernel(
    where, normed, inputs, ys, skip, a0, a1, a2, a3, a4, b0, b1, b2, b3, b4,
    send_out, keep_out, weight, outer, gated, sems,
):
    place = place_of(where)
    m = where[1]
    tokens, width = gated.shape
    half = width // 2

    def take(src, d, column):
        at = pl.ds(column, half)
        pltpu.make_async_copy(src.at[pl.ds(0, 32), :], weight.at[pl.ds(d * 32, 32), at], sems.at[0]).start()
        pltpu.make_async_copy(src.at[pl.ds(32, 32), :], outer.at[pl.ds(d * 32, 32), at], sems.at[1]).start()

    start_pieces((a0, a1, a2, a3, a4), place, True, lambda src, d: take(src, d, 0))
    start_pieces((b0, b1, b2, b3, b4), place, False, lambda src, d: take(src, d, half))
    pltpu.make_async_copy(weight, weight, sems.at[0]).wait()
    pltpu.make_async_copy(outer, outer, sems.at[1]).wait()

    def gate(n, _):
        at = pl.ds(pl.multiple_of(n * 256, 256), 256)
        total = jnp.zeros((tokens, 256), F32)
        for k in range(4):
            total = total + jnp.dot(
                normed[k], weight[pl.ds((m ^ k) * 512, 512), at], preferred_element_type=F32
            )
        z = total.astype(BF).astype(F32)
        mixed = ys[:, at] + skip[:, at] * inputs[:, at].astype(F32)
        gated[:, at] = (mixed * sigmoid_times(z)).astype(BF)
        return 0

    lax.fori_loop(0, width // 256, gate, 0)

    def out(n, _):
        far, part = n // 2, (n % 2) * 256
        column = pl.ds(pl.multiple_of(part, 256), 256)
        for core in range(2):
            rows = pl.ds(pl.multiple_of((m ^ (far * 2 + core)) * 512 + part, 256), 256)
            value = lax.dot_general(
                gated[...], outer[rows, :], (((1,), (1,)), ((), ())), preferred_element_type=F32
            )
            if core:
                send_out[far, :, column] = value.astype(BF)
            else:
                keep_out[far, :, column] = value
        return 0

    lax.fori_loop(0, 4, out, 0)


def join_kernel(targets, keep, near, far, hidden, out, total):
    tokens, width = hidden.shape
    count = targets.shape[0]
    drafts = tokens // count
    order = order_matrix(tokens, tokens, drafts, count)
    base = jnp.dot(order, hidden[...], preferred_element_type=F32)
    summed = keep[...] + near[...].astype(F32) + far[...].astype(F32)
    rounded = (summed + base).astype(BF)
    back = lax.dot_general(order, rounded, (((0,), (0,)), ((), ())), preferred_element_type=F32)
    total[...] = back.astype(BF).reshape(count, drafts, width)
    out[...] = jnp.zeros(out.shape, BF)

    def place(r, _):
        out[lax.div(targets[r], count)] = total[r]
        return 0

    lax.fori_loop(0, count, place, 0)


def unpack_kernel(where, targets, got, out, sem):
    count = targets.shape[0]
    peers = got.shape[0]

    def begin(r, _):
        source = lax.rem(2 * where[0] - lax.div(targets[r], count) + 2 * peers, peers)
        pltpu.make_async_copy(got.at[source], out.at[r], sem).start()
        return 0

    lax.fori_loop(0, count, begin, 0)
    pltpu.make_async_copy(out, out, sem).wait()


def params():
    return pltpu.CompilerParams(vmem_limit_bytes=56 << 20)


def on_device(
    hidden, norm_gain, in_x, in_z, conv_weight, conv_bias, x_proj, dt_proj, dt_bias, a_log, skip,
    out_proj, state_pool, conv_pool, permutation, page_table, accepted,
):
    count, drafts, part = hidden.shape
    tokens = count * drafts
    width = in_x.shape[1]
    slots, states, _ = state_pool.shape
    rank = x_proj.shape[1] - 2 * states
    where = jnp.stack([lax.axis_index("dp"), lax.axis_index("mp")]).astype(jnp.int32)
    peers = lax.axis_size("dp")

    extra = jnp.concatenate(
        [x_proj, jnp.zeros((16, 256 - x_proj.shape[1]), BF), dt_proj.reshape(16, 128)], axis=1
    )
    block_a = jnp.concatenate([in_x[:, :CUT], extra], axis=0)
    first_a = gather_plane(gather_z(block_a), 2, 1)
    first_b = gather_plane(gather_z(in_x[:, CUT:]), 1, 2)

    flat = hidden.reshape(tokens, part)
    sent = jnp.concatenate([flat, jnp.broadcast_to(norm_gain[None], (16, part))], axis=0)
    near = across(sent, 1)
    far = across(sent, 2)
    both = across(far, 1)

    pair = jnp.concatenate([in_z, out_proj.T], axis=0)
    stacked = gather_z(pair)
    second_a = gather_plane(stacked[..., : width // 2], 2, 1)
    second_b = gather_plane(stacked[..., width // 2 :], 1, 2)

    wide_accepted = jnp.broadcast_to(accepted[:, None], (count, 128))
    normed, inputs, sums, dt, new_conv = pl.pallas_call(
        front_kernel,
        out_shape=(
            jax.ShapeDtypeStruct((4, tokens, part), BF),
            jax.ShapeDtypeStruct((tokens, width), BF),
            jax.ShapeDtypeStruct((rank + 2 * states, tokens), F32),
            jax.ShapeDtypeStruct((rank, width), BF),
            jax.ShapeDtypeStruct((3, slots, width), F32),
        ),
        in_specs=[SMEM, SMEM] + [VMEM] * 5 + [ANY] * 10 + [VMEM] * 3,
        out_specs=(VMEM,) * 5,
        scratch_shapes=[
            pltpu.VMEM((2048, width), BF),
            pltpu.VMEM((1024, 256), BF),
            pltpu.VMEM((1024, 128), BF),
            pltpu.VMEM((1024, 128), F32),
            pltpu.VMEM((drafts, count, width), F32),
            pltpu.VMEM((3, count, width), F32),
            pltpu.VMEM((3, count, width), F32),
            pltpu.VMEM((4, tokens, part), BF),
            pltpu.SemaphoreType.DMA((3,)),
        ],
        compiler_params=params(),
        cost_estimate=pl.CostEstimate(flops=6_000_000_000, bytes_accessed=10 << 20, transcendentals=0),
        name="front",
    )(
        where, page_table, wide_accepted, sent, near, far, both, *reorder(first_a), *reorder(first_b),
        conv_weight, conv_bias[None], conv_pool.transpose(1, 0, 2),
    )

    sums = sums + across(sums, 1)
    other = across(sums, 2)
    ys, new_state = pl.pallas_call(
        scan_kernel,
        out_shape=(
            jax.ShapeDtypeStruct((tokens, width), F32),
            jax.ShapeDtypeStruct((slots * states, width), F32),
        ),
        in_specs=[SMEM] + [VMEM] * 8,
        out_specs=(VMEM,) * 2,
        scratch_shapes=[
            pltpu.VMEM((tokens, rank), BF),
            pltpu.VMEM((tokens, 128), F32),
            pltpu.VMEM((tokens, width), F32),
            pltpu.VMEM((states, 8, width), F32),
            pltpu.VMEM((width // 128, count * states, 128), F32),
            pltpu.VMEM((drafts, 2 * states, 8, 128), F32),
            pltpu.VMEM((width // 128, states * count, 128), F32),
        ],
        compiler_params=params(),
        cost_estimate=pl.CostEstimate(flops=12_000_000_000, bytes_accessed=10 << 20, transcendentals=0),
        name="scan",
    )(
        page_table, wide_accepted, sums, other, dt, dt_bias[None], a_log, inputs,
        state_pool.reshape(slots * states, width),
    )

    send, keep = pl.pallas_call(
        back_kernel,
        out_shape=(
            jax.ShapeDtypeStruct((2, tokens, part), BF),
            jax.ShapeDtypeStruct((2, tokens, part), F32),
        ),
        in_specs=[SMEM] + [VMEM] * 4 + [ANY] * 10,
        out_specs=(VMEM,) * 2,
        scratch_shapes=[
            pltpu.VMEM((2048, width), BF),
            pltpu.VMEM((2048, width), BF),
            pltpu.VMEM((tokens, width), BF),
            pltpu.SemaphoreType.DMA((2,)),
        ],
        compiler_params=params(),
        cost_estimate=pl.CostEstimate(flops=6_000_000_000, bytes_accessed=16 << 20, transcendentals=0),
        name="back",
    )(where, normed, inputs, ys, skip[None], *reorder(second_a), *reorder(second_b))

    got = across(send, 1)
    forward = (keep[1] + got[1].astype(F32)).astype(BF)
    remote = across(forward, 2)
    packed = pl.pallas_call(
        join_kernel,
        out_shape=jax.ShapeDtypeStruct((peers, drafts, part), BF),
        in_specs=[SMEM] + [VMEM] * 4,
        out_specs=VMEM,
        scratch_shapes=[pltpu.VMEM((count, drafts, part), BF)],
        compiler_params=params(),
        cost_estimate=pl.CostEstimate(flops=600_000_000, bytes_accessed=4 << 20, transcendentals=0),
        name="join",
    )(permutation, keep[0], got[0], remote, flat)
    arrived = lax.all_to_all(packed, "dp", split_axis=0, concat_axis=0, tiled=True)
    verified = pl.pallas_call(
        unpack_kernel,
        out_shape=jax.ShapeDtypeStruct((count, drafts, part), BF),
        in_specs=[SMEM, SMEM, ANY],
        out_specs=ANY,
        scratch_shapes=[pltpu.SemaphoreType.DMA(())],
        name="unpack",
    )(where, permutation, arrived)
    return (
        verified,
        new_state.reshape(slots, states, width),
        new_conv.transpose(1, 0, 2),
    )


def reorder(pieces):
    own, after, low, high, before = pieces
    return own, after, low, high, before


def solution(mesh):
    return jax.shard_map(
        on_device,
        mesh=mesh,
        in_specs=(
            P("dp", None, "mp"),
            P("mp"),
            P("dp", "mp"),
            P("dp", "mp"),
            P(None, "mp"),
            P("mp"),
            P(("mp", "dp"), None),
            P("dp", "mp"),
            P("mp"),
            P(None, "mp"),
            P("mp"),
            P("mp", "dp"),
            P("dp", None, "mp"),
            P("dp", None, "mp"),
            P("dp"),
            P("dp"),
            P("dp"),
        ),
        out_specs=(P("dp", None, "mp"), P("dp", None, "mp"), P("dp", None, "mp")),
        check_vma=False,
    )
```

time: 944 us -> 276 us (0.29)
  blocking collectives: 554 us -> 36.9 us
  local copies, waits for them, and re-layouts: 94 us -> 12.2 us
  waiting for transfers between devices: 131 us -> 50.8 us
  Pallas kernels: 0 us -> 79.1 us
  other arithmetic: 86.5 us -> 8.98 us
  starting transfers between devices: 33 us -> 80.8 us
  matrix products: 20.1 us -> 0 us
  between operations: 15.1 us -> 1.5 us
    all_gather x3 -> x0, blocking collectives: 540 us -> none  [the longest x1 202 us: verify_layer(): piece = lax.all_gather(x_proj, 'dp', axis=0, tiled=True)]
    all_to_all x4 -> x0, waiting for transfers between devices: 129 us -> none  [the longest x1 92.5 us: on_device(): lax.all_to_all(returned.astype(jnp.bfloat16), 'dp', split_axis=0, concat_...]
    ppermute x0 -> x48, starting transfers between devices: none -> 80.8 us  [the longest x41 73.8 us: hop(): return lax.ppermute(value, 'dp', shift_pairs(axis, step))]
    pallas_call x0 -> x5, Pallas kernels: none -> 79.1 us  [the longest x1 29.9 us: on_device(): pl.pallas_call(scan_kernel, out_shape=(jax.ShapeDtypeStruct((tokens, widt...]
    ppermute x0 -> x48, waiting for transfers between devices: none -> 50.8 us  [the longest x41 30.2 us: hop(): return lax.ppermute(value, 'dp', shift_pairs(axis, step))]
    all_to_all x0 -> x1, blocking collectives: none -> 36.9 us  [on_device(): lax.all_to_all(packed, 'dp', split_axis=0, concat_axis=0, tiled=True)]
    all_to_all x4 -> x0, starting transfers between devices: 32.7 us -> none  [the longest x1 14.6 us: on_device(): lax.all_to_all(details_sent, 'dp', split_axis=0, concat_axis=0, tiled=True)]
    gather x16 -> x0, local copies, waits for them, and re-layouts: 31.2 us -> none  [the longest x3 8.56 us: unpack_rows(): return jnp.take(values, index, axis=0)]
  transfers between devices with their start and end apart: 10 -> 48, of which waited for: 3 -> 16; matrix products, arithmetic and copies ran while one was open for 19% -> 5% of each run, Pallas kernels for 0% -> 16%
where the time goes in v1:
time: 276 us; the launch traced here: 270 us
  starting transfers between devices  80.8 us (29%)
  Pallas kernels  79.1 us (29%)
  waiting for transfers between devices  50.8 us (18%)
  blocking collectives  36.9 us (13%)
  local copies, waits for them, and re-layouts  12.2 us (4%)
  other arithmetic  8.98 us (3%)
    ppermute x41, starting transfers between devices, hop(): return lax.ppermute(value, 'dp', shift_pairs(axis, step))  73.8 us
    all_to_all x1, blocking collectives, on_device(): lax.all_to_all(packed, 'dp', split_axis=0, concat_axis=0, tiled=True)  36.9 us
    ppermute x41, waiting for transfers between devices, hop(): return lax.ppermute(value, 'dp', shift_pairs(axis, step))  30.2 us
    pallas_call x1, Pallas kernels, on_device(): pl.pallas_call(scan_kernel, out_shape=(jax.ShapeDtypeStruct((tokens, widt...  29.9 us
    ppermute x7, waiting for transfers between devices, across(): return lax.ppermute(value, 'mp', [(m, m ^ flip) for m in range(4)])  20.6 us
    pallas_call x1, Pallas kernels, on_device(): pl.pallas_call(unpack_kernel, out_shape=jax.ShapeDtypeStruct((count, draf...  17.7 us
    pallas_call x1, Pallas kernels, on_device(): pl.pallas_call(back_kernel, out_shape=(jax.ShapeDtypeStruct((2, tokens, p...  13.9 us
    pallas_call x1, Pallas kernels, on_device(): pl.pallas_call(front_kernel, out_shape=(jax.ShapeDtypeStruct((4, tokens,...  13.9 us
  transfers between devices with their start and end apart: 48, of which 16 were waited for; matrix products, arithmetic and copies ran while one was open for 5% of the time, Pallas kernels for 16%

profile of v1, /device:TPU:2, one launch (start us, length us, event | category | flops | bytes accessed | tf_op | source)
XLA Modules:
  0.0 270.3 jit_solution(11746441604129052504)
XLA Ops:
  2.8 7.2 %collective-permute-start.4 = (bf16[48,384]{1,0:T(8,128)(2,1)S(1)}, bf16[48,384]{1,0:T(8,128)(2,1)S(1)}, u32[]{:S(2)}, u32[]{:S(2)}) collective-permute-start(bf16[48,384]{1,0:T(8,128)(2,1)S(1)} %get-tuple-element.36), channel_id=1, source_target_pairs={{0,128},{4,132},{8,136},{12,140},{16,144},{20,148},{24,152},{28,15... | collective-permute-start | bytes 110600 | tf_op jit(solution)/shard_map/ppermute | solution.py:32
  10.1 2.9 %collective-permute-start.5 = (bf16[48,384]{1,0:T(8,128)(2,1)S(1)}, bf16[48,384]{1,0:T(8,128)(2,1)S(1)}, u32[]{:S(2)}, u32[]{:S(2)}) collective-permute-start(bf16[48,384]{1,0:T(8,128)(2,1)S(1)} %get-tuple-element.36), channel_id=1, source_target_pairs={{0,64},{4,68},{8,72},{12,76},{16,80},{20,84},{24,88},{28,92},{32,9... | collective-permute-start | bytes 110600 | tf_op jit(solution)/shard_map/ppermute | solution.py:32
  13.8 2.1 collective-permute-start.15
  15.9 4.1 %collective-permute-start.14 = (bf16[32,640]{1,0:T(8,128)(2,1)S(1)}, bf16[32,640]{1,0:T(8,128)(2,1)S(1)}, u32[]{:S(2)}, u32[]{:S(2)}) collective-permute-start(bf16[32,640]{1,0:T(8,128)(2,1)S(1)} %get-tuple-element.34), channel_id=1, source_target_pairs={{0,192},{4,196},{8,200},{12,204},{16,208},{20,212},{24,216},{28,22... | collective-permute-start | bytes 122888 | tf_op jit(solution)/shard_map/ppermute | solution.py:32
  20.7 1.1 pad_maximum_fusion.4.h0
  21.8 1.0 fusion.2
  23.0 2.6 collective-permute-start.28
  25.5 2.4 collective-permute-start.27
  28.0 1.6 collective-permute-start.29
  30.4 1.5 collective-permute-start.7
  31.9 1.7 collective-permute-done.28
  33.6 6.3 %collective-permute-start.1 = (bf16[528,512]{1,0:T(8,128)(2,1)S(1)}, bf16[528,512]{1,0:T(8,128)(2,1)S(1)}, u32[]{:S(2)}, u32[]{:S(2)}) collective-permute-start(bf16[528,512]{1,0:T(8,128)(2,1)S(1)} %pad_maximum_fusion.4.h0), channel_id=1, source_target_pairs={{0,2},{1,3},{2,0},{3,1},{4,6},{5,7},{6,4},{7,5},{8,10},{9,11},{10,... | collective-permute-start | bytes 1622024 | tf_op jit(solution)/shard_map/ppermute | solution.py:36
  39.9 3.0 %collective-permute-start.17 = (bf16[4,32,640]{2,1,0:T(8,128)(2,1)S(1)}, bf16[4,32,640]{2,1,0:T(8,128)(2,1)S(1)}, u32[]{:S(2)}, u32[]{:S(2)}) collective-permute-start(bf16[4,32,640]{2,1,0:T(8,128)(2,1)S(1)} %get-tuple-element.28), channel_id=1, source_target_pairs={{0,48},{4,52},{8,56},{12,60},{16,0},{20,4},{24,8},{28,12},{32,16},... | collective-permute-start | bytes 491528 | tf_op jit(solution)/shard_map/ppermute | solution.py:32
  43.7 1.6 collective-permute-start.8
  45.8 3.9 %collective-permute-start.38 = (bf16[4,64,512]{2,1,0:T(8,128)(2,1)S(1)}, bf16[4,64,512]{2,1,0:T(8,128)(2,1)S(1)}, u32[]{:S(2)}, u32[]{:S(2)}) collective-permute-start(bf16[4,64,512]{2,1,0:T(8,128)(2,1)S(1)} %get-tuple-element.25), channel_id=1, source_target_pairs={{0,48},{4,52},{8,56},{12,60},{16,0},{20,4},{24,8},{28,12},{32,16},... | collective-permute-start | bytes 786440 | tf_op jit(solution)/shard_map/ppermute | solution.py:32
  49.8 3.3 %collective-permute-start.20 = (bf16[2,32,640]{2,1,0:T(8,128)(2,1)S(1)}, bf16[2,32,640]{2,1,0:T(8,128)(2,1)S(1)}, u32[]{:S(2)}, u32[]{:S(2)}) collective-permute-start(bf16[2,32,640]{2,1,0:T(8,128)(2,1)S(1)} %slice.101), channel_id=1, source_target_pairs={{0,48},{4,52},{8,56},{12,60},{16,0},{20,4},{24,8},{28,12},{32,16},... | collective-permute-start | bytes 245768 | tf_op jit(solution)/shard_map/ppermute | solution.py:32
  53.1 2.0 collective-permute-done.20
  55.7 3.1 %collective-permute-done.19 = bf16[2,32,640]{2,1,0:T(8,128)(2,1)S(1)} collective-permute-done((bf16[2,32,640]{2,1,0:T(8,128)(2,1)S(1)}, bf16[2,32,640]{2,1,0:T(8,128)(2,1)S(1)}, u32[]{:S(2)}, u32[]{:S(2)}) %collective-permute-start.19) | collective-permute-done | bytes 81952 | tf_op jit(solution)/shard_map/ppermute | solution.py:32
  58.8 1.2 collective-permute-start.31
  60.1 1.1 collective-permute-start.22
  61.3 1.1 collective-permute-start.41
  62.4 1.1 collective-permute-start.11
  63.6 4.4 %collective-permute-done.31 = bf16[4,64,512]{2,1,0:T(8,128)(2,1)S(1)} collective-permute-done((bf16[4,64,512]{2,1,0:T(8,128)(2,1)S(1)}, bf16[4,64,512]{2,1,0:T(8,128)(2,1)S(1)}, u32[]{:S(2)}, u32[]{:S(2)}) %collective-permute-start.31) | collective-permute-done | bytes 262176 | tf_op jit(solution)/shard_map/ppermute | solution.py:32
  69.1 1.1 collective-permute-start.40
  70.1 7.4 %collective-permute-done.40 = bf16[2,64,512]{2,1,0:T(8,128)(2,1)S(1)} collective-permute-done((bf16[2,64,512]{2,1,0:T(8,128)(2,1)S(1)}, bf16[2,64,512]{2,1,0:T(8,128)(2,1)S(1)}, u32[]{:S(2)}, u32[]{:S(2)}) %collective-permute-start.40) | collective-permute-done | bytes 131104 | tf_op jit(solution)/shard_map/ppermute | solution.py:32
  77.5 1.0 collective-permute-start.21
  79.4 3.4 %collective-permute-start.33 = (bf16[2,64,512]{2,1,0:T(8,128)(2,1)S(1)}, bf16[2,64,512]{2,1,0:T(8,128)(2,1)S(1)}, u32[]{:S(2)}, u32[]{:S(2)}) collective-permute-start(bf16[2,64,512]{2,1,0:T(8,128)(2,1)S(1)} %slice.106), channel_id=1, source_target_pairs={{0,12},{4,0},{8,4},{12,8},{16,28},{20,16},{24,20},{28,24},{32,44},... | collective-permute-start | bytes 393224 | tf_op jit(solution)/shard_map/ppermute | solution.py:32
  87.5 4.8 %collective-permute-done.21.b1 = bf16[4,4,32,640]{3,2,1,0:T(8,128)(2,1)} collective-permute-done((bf16[4,4,32,640]{3,2,1,0:T(8,128)(2,1)S(1)}, bf16[4,4,32,640]{3,2,1,0:T(8,128)(2,1)}, u32[]{:S(2)}, u32[]{:S(2)}) %collective-permute-start.21) | collective-permute-done | bytes 655392 | tf_op jit(solution)/shard_map/ppermute | solution.py:32
  92.3 8.7 %collective-permute-start.12 = (bf16[2,4,48,384]{3,2,1,0:T(8,128)(2,1)S(1)}, bf16[2,4,48,384]{3,2,1,0:T(8,128)(2,1)S(1)}, u32[]{:S(2)}, u32[]{:S(2)}) collective-permute-start(bf16[2,4,48,384]{3,2,1,0:T(8,128)(2,1)S(1)} %slice.98), channel_id=1, source_target_pairs={{0,16},{4,20},{8,24},{12,28},{16,32},{20,36},{24,40},{28,44},{32,4... | collective-permute-start | bytes 884744 | tf_op jit(solution)/shard_map/ppermute | solution.py:32
  102.0 3.3 %collective-permute-start.13 = (bf16[2,4,48,384]{3,2,1,0:T(8,128)(2,1)S(1)}, bf16[2,4,48,384]{3,2,1,0:T(8,128)(2,1)S(1)}, u32[]{:S(2)}, u32[]{:S(2)}) collective-permute-start(bf16[2,4,48,384]{3,2,1,0:T(8,128)(2,1)S(1)} %slice.99), channel_id=1, source_target_pairs={{0,48},{4,52},{8,56},{12,60},{16,0},{20,4},{24,8},{28,12},{32,16},... | collective-permute-start | bytes 884744 | tf_op jit(solution)/shard_map/ppermute | solution.py:32
  105.3 1.7 collective-permute-start.23
  107.8 3.2 %collective-permute-done.12.a2 = bf16[2,4,48,384]{3,2,1,0:T(8,128)(2,1)S(1)} collective-permute-done((bf16[2,4,48,384]{3,2,1,0:T(8,128)(2,1)S(1)}, bf16[2,4,48,384]{3,2,1,0:T(8,128)(2,1)S(1)}, u32[]{:S(2)}, u32[]{:S(2)}) %collective-permute-start.12) | collective-permute-done | bytes 294944 | tf_op jit(solution)/shard_map/ppermute | solution.py:32
  111.1 1.7 collective-permute-done.13.a3
  112.7 1.7 collective-permute-start.43
  115.4 2.2 collective-permute-start.42
  118.7 13.9 %front.1 = (bf16[4,512,512]{2,1,0:T(8,128)(2,1)}, bf16[512,1024]{1,0:T(8,128)(2,1)}, f32[160,512]{1,0:T(8,128)}, bf16[128,1024]{1,0:T(8,128)(2,1)}, f32[3,40,1024]{2,1,0:T(8,128)}) custom-call(s32[2]{0:T(128)} %pad_add_fusion.where, s32[32]{0:T(128)} %pages.3, s32[32,128]{1,0:T(8,128)} %broadcast_in_dim.24.accepted, bf16[528,512]{1,0:T(8,128)(2,1)} %copy-done.4, ...), custom_call_target="tpu_custom_call" | custom-call | flops 6000000000 | bytes 10485760 | tf_op jit(solution)/shard_map/front/pallas_call | solution.py:417
  132.7 1.8 collective-permute-done.25
  135.9 3.3 %collective-permute-start.37 = (bf16[2,4,64,512]{3,2,1,0:T(8,128)(2,1)S(1)}, bf16[2,4,64,512]{3,2,1,0:T(8,128)(2,1)S(1)}, u32[]{:S(2)}, u32[]{:S(2)}) collective-permute-start(bf16[2,4,64,512]{3,2,1,0:T(8,128)(2,1)S(1)} %slice.108), channel_id=1, source_target_pairs={{0,48},{4,52},{8,56},{12,60},{16,0},{20,4},{24,8},{28,12},{32,16},... | collective-permute-start | bytes 1572872 | tf_op jit(solution)/shard_map/ppermute | solution.py:32
  139.2 2.1 collective-permute-start.44
  142.3 3.1 %collective-permute-done.26.sums_b = f32[160,512]{1,0:T(8,128)S(1)} collective-permute-done((f32[160,512]{1,0:T(8,128)S(1)}, f32[160,512]{1,0:T(8,128)S(1)}, u32[]{:S(2)}, u32[]{:S(2)}) %collective-permute-start.26) | collective-permute-done | bytes 327712 | tf_op jit(solution)/shard_map/ppermute | solution.py:36
  146.1 29.9 %scan.1 = (f32[512,1024]{1,0:T(8,128)}, f32[640,1024]{1,0:T(8,128)}) custom-call(s32[32]{0:T(128)} %pages.3, s32[32,128]{1,0:T(8,128)} %broadcast_in_dim.24.accepted, f32[160,512]{1,0:T(8,128)} %copy-done.6, f32[160,512]{1,0:T(8,128)} %copy-done.20, bf16[128,1024]{1,0:T(8,128)(2,1)} %get-tuple-element.15.dt, f32[1,1024]{1,0:T(1,128)} %bitcast.79, ...), custom_call_target="tpu_custom_call" | custom-call | flops 12000000000 | bytes 10485760 | tf_op jit(solution)/shard_map/scan/pallas_call | solution.py:449
  177.2 13.9 %back.1 = (bf16[2,512,512]{2,1,0:T(8,128)(2,1)}, f32[2,512,512]{2,1,0:T(8,128)}) custom-call(s32[2]{0:T(128)} %pad_add_fusion.where, bf16[4,512,512]{2,1,0:T(8,128)(2,1)} %get-tuple-element.12.normed, bf16[512,1024]{1,0:T(8,128)(2,1)} %get-tuple-element.13.inputs, f32[512,1024]{1,0:T(8,128)} %get-tuple-element.16.ys, f32[1,1024]{1,0:T(1,128)} %bitcast.80, ...), custom_call_target="tpu_custom_call" | custom-call | flops 6000000000 | bytes 16777216 | tf_op jit(solution)/shard_map/back/pallas_call | solution.py:474
  191.3 2.9 %collective-permute-done.46 = bf16[2,512,512]{2,1,0:T(8,128)(2,1)S(1)} collective-permute-done((bf16[2,512,512]{2,1,0:T(8,128)(2,1)}, bf16[2,512,512]{2,1,0:T(8,128)(2,1)S(1)}, u32[]{:S(2)}, u32[]{:S(2)}) %collective-permute-start.46) | collective-permute-done | bytes 1048608 | tf_op jit(solution)/shard_map/ppermute | solution.py:36
  194.1 2.8 %fusion = (bf16[512,512]{1,0:T(8,128)(2,1)S(1)}, f32[512,512]{1,0:T(8,128)}) fusion(f32[2,512,512]{2,1,0:T(8,128)} %get-tuple-element.17, bf16[2,512,512]{2,1,0:T(8,128)(2,1)S(1)} %collective-permute-done.46), kind=kLoop, calls=%fused_computation.7 | loop fusion | flops 786432 | bytes 4194304 | tf_op jit(solution)/shard_map/convert_element_type | solution.py:494
  198.1 12.8 %collective-permute-done.47.far = bf16[512,512]{1,0:T(8,128)(2,1)S(1)} collective-permute-done((bf16[512,512]{1,0:T(8,128)(2,1)S(1)}, bf16[512,512]{1,0:T(8,128)(2,1)S(1)}, u32[]{:S(2)}, u32[]{:S(2)}) %collective-permute-start.47) | collective-permute-done | bytes 524320 | tf_op jit(solution)/shard_map/ppermute | solution.py:36
  211.7 3.8 %join.1 = bf16[64,16,512]{2,1,0:T(8,128)(2,1)} custom-call(s32[32]{0:T(128)} %targets.3, f32[512,512]{1,0:T(8,128)} %get-tuple-element.22.keep, bf16[512,512]{1,0:T(8,128)(2,1)} %slice_bitcast_fusion.1.near, bf16[512,512]{1,0:T(8,128)(2,1)} %copy-done.5, bf16[512,512]{1,0:T(8,128)(2,1)} %bitcast.57), custom_call_target="tpu_custom_call" | custom-call | flops 600000000 | bytes 4194304 | tf_op jit(solution)/shard_map/join/pallas_call | solution.py:496
  215.5 36.9 %all_to_all.5.got = bf16[64,16,512]{2,1,0:T(8,128)(2,1)} all-to-all(bf16[64,16,512]{2,1,0:T(8,128)(2,1)} %join.1), channel_id=1, replica_groups=mesh['dp'=64,'mp'=4] {'dp'}, dimensions={0} | all-to-all | bytes 2097152 | tf_op jit(solution)/shard_map/all_to_all | solution.py:506
  252.4 17.7 %unpack.1 = bf16[32,16,512]{2,1,0:T(8,128)(2,1)} custom-call(s32[2]{0:T(128)} %pad_add_fusion.where, s32[32]{0:T(128)} %targets.3, bf16[64,16,512]{2,1,0:T(8,128)(2,1)} %all_to_all.5.got), custom_call_target="tpu_custom_call" | custom-call | tf_op jit(solution)/shard_map/unpack/pallas_call | solution.py:507
  (141 shorter events, 23.3 us)
Async XLA Ops:
  2.8 20.0 %collective-permute-start.4 = (bf16[48,384]{1,0:T(8,128)(2,1)S(1)}, bf16[48,384]{1,0:T(8,128)(2,1)S(1)}, u32[]{:S(2)}, u32[]{:S(2)}) collective-permute-start(bf16[48,384]{1,0:T(8,128)(2,1)S(1)} %get-tuple-element.36), channel_id=1, source_target_pairs={{0,128},{4,132},{8,136},{12,140},{16,144},{20,148},{24,152},{28,15... | collective-permute-start | bytes 110600 | tf_op jit(solution)/shard_map/ppermute | solution.py:32
  10.1 12.9 %collective-permute-start.3 = (bf16[48,384]{1,0:T(8,128)(2,1)S(1)}, bf16[48,384]{1,0:T(8,128)(2,1)S(1)}, u32[]{:S(2)}, u32[]{:S(2)}) collective-permute-start(bf16[48,384]{1,0:T(8,128)(2,1)S(1)} %get-tuple-element.36), channel_id=1, source_target_pairs={{0,192},{4,196},{8,200},{12,204},{16,208},{20,212},{24,216},{28,22... | collective-permute-start | bytes 110600 | tf_op jit(solution)/shard_map/ppermute | solution.py:32
  10.1 15.5 %collective-permute-start.5 = (bf16[48,384]{1,0:T(8,128)(2,1)S(1)}, bf16[48,384]{1,0:T(8,128)(2,1)S(1)}, u32[]{:S(2)}, u32[]{:S(2)}) collective-permute-start(bf16[48,384]{1,0:T(8,128)(2,1)S(1)} %get-tuple-element.36), channel_id=1, source_target_pairs={{0,64},{4,68},{8,72},{12,76},{16,80},{20,84},{24,88},{28,92},{32,9... | collective-permute-start | bytes 110600 | tf_op jit(solution)/shard_map/ppermute | solution.py:32
  13.8 14.2 %collective-permute-start.15 = (bf16[32,640]{1,0:T(8,128)(2,1)S(1)}, bf16[32,640]{1,0:T(8,128)(2,1)S(1)}, u32[]{:S(2)}, u32[]{:S(2)}) collective-permute-start(bf16[32,640]{1,0:T(8,128)(2,1)S(1)} %get-tuple-element.34), channel_id=1, source_target_pairs={{0,128},{4,132},{8,136},{12,140},{16,144},{20,148},{24,152},{28,15... | collective-permute-start | bytes 122888 | tf_op jit(solution)/shard_map/ppermute | solution.py:32
  15.9 13.7 %collective-permute-start.14 = (bf16[32,640]{1,0:T(8,128)(2,1)S(1)}, bf16[32,640]{1,0:T(8,128)(2,1)S(1)}, u32[]{:S(2)}, u32[]{:S(2)}) collective-permute-start(bf16[32,640]{1,0:T(8,128)(2,1)S(1)} %get-tuple-element.34), channel_id=1, source_target_pairs={{0,192},{4,196},{8,200},{12,204},{16,208},{20,212},{24,216},{28,22... | collective-permute-start | bytes 122888 | tf_op jit(solution)/shard_map/ppermute | solution.py:32
  22.9 7.6 %collective-permute-start.16 = (bf16[32,640]{1,0:T(8,128)(2,1)S(1)}, bf16[32,640]{1,0:T(8,128)(2,1)S(1)}, u32[]{:S(2)}, u32[]{:S(2)}) collective-permute-start(bf16[32,640]{1,0:T(8,128)(2,1)S(1)} %get-tuple-element.34), channel_id=1, source_target_pairs={{0,64},{4,68},{8,72},{12,76},{16,80},{20,84},{24,88},{28,92},{32,9... | collective-permute-start | bytes 122888 | tf_op jit(solution)/shard_map/ppermute | solution.py:32
  23.0 10.7 %collective-permute-start.28 = (bf16[64,1024]{1,0:T(8,128)(2,1)S(1)}, bf16[64,1024]{1,0:T(8,128)(2,1)S(1)}, u32[]{:S(2)}, u32[]{:S(2)}) collective-permute-start(bf16[64,1024]{1,0:T(8,128)(2,1)S(1)} %get-tuple-element.32), channel_id=1, source_target_pairs={{0,128},{4,132},{8,136},{12,140},{16,144},{20,148},{24,152},{28,15... | collective-permute-start | bytes 393224 | tf_op jit(solution)/shard_map/ppermute | solution.py:32
  25.5 14.4 %collective-permute-start.27 = (bf16[64,1024]{1,0:T(8,128)(2,1)S(1)}, bf16[64,1024]{1,0:T(8,128)(2,1)S(1)}, u32[]{:S(2)}, u32[]{:S(2)}) collective-permute-start(bf16[64,1024]{1,0:T(8,128)(2,1)S(1)} %get-tuple-element.32), channel_id=1, source_target_pairs={{0,192},{4,196},{8,200},{12,204},{16,208},{20,212},{24,216},{28,22... | collective-permute-start | bytes 393224 | tf_op jit(solution)/shard_map/ppermute | solution.py:32
  28.0 15.0 %collective-permute-start.29 = (bf16[64,1024]{1,0:T(8,128)(2,1)S(1)}, bf16[64,1024]{1,0:T(8,128)(2,1)S(1)}, u32[]{:S(2)}, u32[]{:S(2)}) collective-permute-start(bf16[64,1024]{1,0:T(8,128)(2,1)S(1)} %get-tuple-element.32), channel_id=1, source_target_pairs={{0,64},{4,68},{8,72},{12,76},{16,80},{20,84},{24,88},{28,92},{32,9... | collective-permute-start | bytes 393224 | tf_op jit(solution)/shard_map/ppermute | solution.py:32
  29.6 13.4 %collective-permute-start.6 = (bf16[4,48,384]{2,1,0:T(8,128)(2,1)S(1)}, bf16[4,48,384]{2,1,0:T(8,128)(2,1)S(1)}, u32[]{:S(2)}, u32[]{:S(2)}) collective-permute-start(bf16[4,48,384]{2,1,0:T(8,128)(2,1)S(1)} %get-tuple-element.30), channel_id=1, source_target_pairs={{0,12},{4,0},{8,4},{12,8},{16,28},{20,16},{24,20},{28,24},{32,44},... | collective-permute-start | bytes 442376 | tf_op jit(solution)/shard_map/ppermute | solution.py:32
  30.4 13.2 %collective-permute-start.7 = (bf16[4,48,384]{2,1,0:T(8,128)(2,1)S(1)}, bf16[4,48,384]{2,1,0:T(8,128)(2,1)S(1)}, u32[]{:S(2)}, u32[]{:S(2)}) collective-permute-start(bf16[4,48,384]{2,1,0:T(8,128)(2,1)S(1)} %get-tuple-element.30), channel_id=1, source_target_pairs={{0,4},{4,8},{8,12},{12,0},{16,20},{20,24},{24,28},{28,16},{32,36},... | collective-permute-start | bytes 442376 | tf_op jit(solution)/shard_map/ppermute | solution.py:32
  33.6 44.9 %collective-permute-start.1 = (bf16[528,512]{1,0:T(8,128)(2,1)S(1)}, bf16[528,512]{1,0:T(8,128)(2,1)S(1)}, u32[]{:S(2)}, u32[]{:S(2)}) collective-permute-start(bf16[528,512]{1,0:T(8,128)(2,1)S(1)} %pad_maximum_fusion.4.h0), channel_id=1, source_target_pairs={{0,2},{1,3},{2,0},{3,1},{4,6},{5,7},{6,4},{7,5},{8,10},{9,11},{10,... | collective-permute-start | bytes 1622024 | tf_op jit(solution)/shard_map/ppermute | solution.py:36
  39.9 5.8 %collective-permute-start.17 = (bf16[4,32,640]{2,1,0:T(8,128)(2,1)S(1)}, bf16[4,32,640]{2,1,0:T(8,128)(2,1)S(1)}, u32[]{:S(2)}, u32[]{:S(2)}) collective-permute-start(bf16[4,32,640]{2,1,0:T(8,128)(2,1)S(1)} %get-tuple-element.28), channel_id=1, source_target_pairs={{0,48},{4,52},{8,56},{12,60},{16,0},{20,4},{24,8},{28,12},{32,16},... | collective-permute-start | bytes 491528 | tf_op jit(solution)/shard_map/ppermute | solution.py:32
  42.9 6.8 %collective-permute-start.18 = (bf16[4,32,640]{2,1,0:T(8,128)(2,1)S(1)}, bf16[4,32,640]{2,1,0:T(8,128)(2,1)S(1)}, u32[]{:S(2)}, u32[]{:S(2)}) collective-permute-start(bf16[4,32,640]{2,1,0:T(8,128)(2,1)S(1)} %get-tuple-element.28), channel_id=1, source_target_pairs={{0,16},{4,20},{8,24},{12,28},{16,32},{20,36},{24,40},{28,44},{32,4... | collective-permute-start | bytes 491528 | tf_op jit(solution)/shard_map/ppermute | solution.py:32
  43.0 6.8 %collective-permute-start.9 = (bf16[2,48,384]{2,1,0:T(8,128)(2,1)S(1)}, bf16[2,48,384]{2,1,0:T(8,128)(2,1)S(1)}, u32[]{:S(2)}, u32[]{:S(2)}) collective-permute-start(bf16[2,48,384]{2,1,0:T(8,128)(2,1)S(1)} %slice.97), channel_id=1, source_target_pairs={{0,12},{4,0},{8,4},{12,8},{16,28},{20,16},{24,20},{28,24},{32,44},... | collective-permute-start | bytes 221192 | tf_op jit(solution)/shard_map/ppermute | solution.py:32
  43.7 9.5 %collective-permute-start.8 = (bf16[2,48,384]{2,1,0:T(8,128)(2,1)S(1)}, bf16[2,48,384]{2,1,0:T(8,128)(2,1)S(1)}, u32[]{:S(2)}, u32[]{:S(2)}) collective-permute-start(bf16[2,48,384]{2,1,0:T(8,128)(2,1)S(1)} %slice.96), channel_id=1, source_target_pairs={{0,4},{4,8},{8,12},{12,0},{16,20},{20,24},{24,28},{28,16},{32,36},... | collective-permute-start | bytes 221192 | tf_op jit(solution)/shard_map/ppermute | solution.py:32
  45.8 14.4 %collective-permute-start.38 = (bf16[4,64,512]{2,1,0:T(8,128)(2,1)S(1)}, bf16[4,64,512]{2,1,0:T(8,128)(2,1)S(1)}, u32[]{:S(2)}, u32[]{:S(2)}) collective-permute-start(bf16[4,64,512]{2,1,0:T(8,128)(2,1)S(1)} %get-tuple-element.25), channel_id=1, source_target_pairs={{0,48},{4,52},{8,56},{12,60},{16,0},{20,4},{24,8},{28,12},{32,16},... | collective-permute-start | bytes 786440 | tf_op jit(solution)/shard_map/ppermute | solution.py:32
  49.7 11.6 %collective-permute-start.39 = (bf16[4,64,512]{2,1,0:T(8,128)(2,1)S(1)}, bf16[4,64,512]{2,1,0:T(8,128)(2,1)S(1)}, u32[]{:S(2)}, u32[]{:S(2)}) collective-permute-start(bf16[4,64,512]{2,1,0:T(8,128)(2,1)S(1)} %get-tuple-element.25), channel_id=1, source_target_pairs={{0,16},{4,20},{8,24},{12,28},{16,32},{20,36},{24,40},{28,44},{32,4... | collective-permute-start | bytes 786440 | tf_op jit(solution)/shard_map/ppermute | solution.py:32
  49.8 5.4 %collective-permute-start.20 = (bf16[2,32,640]{2,1,0:T(8,128)(2,1)S(1)}, bf16[2,32,640]{2,1,0:T(8,128)(2,1)S(1)}, u32[]{:S(2)}, u32[]{:S(2)}) collective-permute-start(bf16[2,32,640]{2,1,0:T(8,128)(2,1)S(1)} %slice.101), channel_id=1, source_target_pairs={{0,48},{4,52},{8,56},{12,60},{16,0},{20,4},{24,8},{28,12},{32,16},... | collective-permute-start | bytes 245768 | tf_op jit(solution)/shard_map/ppermute | solution.py:32
  53.1 5.7 %collective-permute-start.19 = (bf16[2,32,640]{2,1,0:T(8,128)(2,1)S(1)}, bf16[2,32,640]{2,1,0:T(8,128)(2,1)S(1)}, u32[]{:S(2)}, u32[]{:S(2)}) collective-permute-start(bf16[2,32,640]{2,1,0:T(8,128)(2,1)S(1)} %slice.100), channel_id=1, source_target_pairs={{0,16},{4,20},{8,24},{12,28},{16,32},{20,36},{24,40},{28,44},{32,4... | collective-permute-start | bytes 245768 | tf_op jit(solution)/shard_map/ppermute | solution.py:32
  55.2 7.3 %collective-permute-start.30 = (bf16[4,64,512]{2,1,0:T(8,128)(2,1)S(1)}, bf16[4,64,512]{2,1,0:T(8,128)(2,1)S(1)}, u32[]{:S(2)}, u32[]{:S(2)}) collective-permute-start(bf16[4,64,512]{2,1,0:T(8,128)(2,1)S(1)} %get-tuple-element.26), channel_id=1, source_target_pairs={{0,12},{4,0},{8,4},{12,8},{16,28},{20,16},{24,20},{28,24},{32,44},... | collective-permute-start | bytes 786440 | tf_op jit(solution)/shard_map/ppermute | solution.py:32
  58.8 9.2 %collective-permute-start.31 = (bf16[4,64,512]{2,1,0:T(8,128)(2,1)S(1)}, bf16[4,64,512]{2,1,0:T(8,128)(2,1)S(1)}, u32[]{:S(2)}, u32[]{:S(2)}) collective-permute-start(bf16[4,64,512]{2,1,0:T(8,128)(2,1)S(1)} %get-tuple-element.26), channel_id=1, source_target_pairs={{0,4},{4,8},{8,12},{12,0},{16,20},{20,24},{24,28},{28,16},{32,36},... | collective-permute-start | bytes 786440 | tf_op jit(solution)/shard_map/ppermute | solution.py:32
  60.1 22.7 %collective-permute-start.22 = (bf16[4,4,32,640]{3,2,1,0:T(8,128)(2,1)S(1)}, bf16[4,4,32,640]{3,2,1,0:T(8,128)(2,1)}, u32[]{:S(2)}, u32[]{:S(2)}) collective-permute-start(bf16[4,4,32,640]{3,2,1,0:T(8,128)(2,1)S(1)} %pad_maximum_fusion.2.b0), channel_id=1, source_target_pairs={{0,4},{4,8},{8,12},{12,0},{16,20},{20,24},{24,28},{28,16},{32,36},... | collective-permute-start | bytes 1966088 | tf_op jit(solution)/shard_map/ppermute | solution.py:32
  61.3 7.8 %collective-permute-start.41 = (bf16[2,64,512]{2,1,0:T(8,128)(2,1)S(1)}, bf16[2,64,512]{2,1,0:T(8,128)(2,1)S(1)}, u32[]{:S(2)}, u32[]{:S(2)}) collective-permute-start(bf16[2,64,512]{2,1,0:T(8,128)(2,1)S(1)} %slice.111), channel_id=1, source_target_pairs={{0,48},{4,52},{8,56},{12,60},{16,0},{20,4},{24,8},{28,12},{32,16},... | collective-permute-start | bytes 393224 | tf_op jit(solution)/shard_map/ppermute | solution.py:32
  62.4 16.9 %collective-permute-start.11 = (bf16[4,4,48,384]{3,2,1,0:T(8,128)(2,1)S(1)}, bf16[4,4,48,384]{3,2,1,0:T(8,128)(2,1)}, u32[]{:S(2)}, u32[]{:S(2)}) collective-permute-start(bf16[4,4,48,384]{3,2,1,0:T(8,128)(2,1)S(1)} %pad_maximum_fusion.3.a0), channel_id=1, source_target_pairs={{0,16},{4,20},{8,24},{12,28},{16,32},{20,36},{24,40},{28,44},{32,4... | collective-permute-start | bytes 1769480 | tf_op jit(solution)/shard_map/ppermute | solution.py:32
  68.0 14.8 %collective-permute-start.10 = (bf16[4,4,48,384]{3,2,1,0:T(8,128)(2,1)S(1)}, bf16[4,4,48,384]{3,2,1,0:T(8,128)(2,1)}, u32[]{:S(2)}, u32[]{:S(2)}) collective-permute-start(bf16[4,4,48,384]{3,2,1,0:T(8,128)(2,1)S(1)} %pad_maximum_fusion.3.a0), channel_id=1, source_target_pairs={{0,48},{4,52},{8,56},{12,60},{16,0},{20,4},{24,8},{28,12},{32,16},... | collective-permute-start | bytes 1769480 | tf_op jit(solution)/shard_map/ppermute | solution.py:32
  69.1 8.5 %collective-permute-start.40 = (bf16[2,64,512]{2,1,0:T(8,128)(2,1)S(1)}, bf16[2,64,512]{2,1,0:T(8,128)(2,1)S(1)}, u32[]{:S(2)}, u32[]{:S(2)}) collective-permute-start(bf16[2,64,512]{2,1,0:T(8,128)(2,1)S(1)} %slice.110), channel_id=1, source_target_pairs={{0,16},{4,20},{8,24},{12,28},{16,32},{20,36},{24,40},{28,44},{32,4... | collective-permute-start | bytes 393224 | tf_op jit(solution)/shard_map/ppermute | solution.py:32
  77.5 14.8 %collective-permute-start.21 = (bf16[4,4,32,640]{3,2,1,0:T(8,128)(2,1)S(1)}, bf16[4,4,32,640]{3,2,1,0:T(8,128)(2,1)}, u32[]{:S(2)}, u32[]{:S(2)}) collective-permute-start(bf16[4,4,32,640]{3,2,1,0:T(8,128)(2,1)S(1)} %pad_maximum_fusion.2.b0), channel_id=1, source_target_pairs={{0,12},{4,0},{8,4},{12,8},{16,28},{20,16},{24,20},{28,24},{32,44},... | collective-permute-start | bytes 1966088 | tf_op jit(solution)/shard_map/ppermute | solution.py:32
  78.6 28.5 %collective-permute-start = (bf16[528,512]{1,0:T(8,128)(2,1)S(1)}, bf16[528,512]{1,0:T(8,128)(2,1)}, u32[]{:S(2)}, u32[]{:S(2)}) collective-permute-start(bf16[528,512]{1,0:T(8,128)(2,1)S(1)} %pad_maximum_fusion.4.h0), channel_id=1, source_target_pairs={{0,1},{1,0},{2,3},{3,2},{4,5},{5,4},{6,7},{7,6},{8,9},{9,8},{10,11... | collective-permute-start | bytes 1622024 | tf_op jit(solution)/shard_map/ppermute | solution.py:36
  79.4 22.6 %collective-permute-start.33 = (bf16[2,64,512]{2,1,0:T(8,128)(2,1)S(1)}, bf16[2,64,512]{2,1,0:T(8,128)(2,1)S(1)}, u32[]{:S(2)}, u32[]{:S(2)}) collective-permute-start(bf16[2,64,512]{2,1,0:T(8,128)(2,1)S(1)} %slice.106), channel_id=1, source_target_pairs={{0,12},{4,0},{8,4},{12,8},{16,28},{20,16},{24,20},{28,24},{32,44},... | collective-permute-start | bytes 393224 | tf_op jit(solution)/shard_map/ppermute | solution.py:32
  82.8 22.5 %collective-permute-start.32 = (bf16[2,64,512]{2,1,0:T(8,128)(2,1)S(1)}, bf16[2,64,512]{2,1,0:T(8,128)(2,1)S(1)}, u32[]{:S(2)}, u32[]{:S(2)}) collective-permute-start(bf16[2,64,512]{2,1,0:T(8,128)(2,1)S(1)} %slice.105), channel_id=1, source_target_pairs={{0,4},{4,8},{8,12},{12,0},{16,20},{20,24},{24,28},{28,16},{32,36},... | collective-permute-start | bytes 393224 | tf_op jit(solution)/shard_map/ppermute | solution.py:32
  82.9 24.9 %collective-permute-start.2 = (bf16[528,512]{1,0:T(8,128)(2,1)}, bf16[528,512]{1,0:T(8,128)(2,1)S(1)}, u32[]{:S(2)}, u32[]{:S(2)}) collective-permute-start(bf16[528,512]{1,0:T(8,128)(2,1)} %copy-done.13), channel_id=1, source_target_pairs={{0,1},{1,0},{2,3},{3,2},{4,5},{5,4},{6,7},{7,6},{8,9},{9,8},{10,11... | collective-permute-start | bytes 1622024 | tf_op jit(solution)/shard_map/ppermute | solution.py:36
  92.3 18.7 %collective-permute-start.12 = (bf16[2,4,48,384]{3,2,1,0:T(8,128)(2,1)S(1)}, bf16[2,4,48,384]{3,2,1,0:T(8,128)(2,1)S(1)}, u32[]{:S(2)}, u32[]{:S(2)}) collective-permute-start(bf16[2,4,48,384]{3,2,1,0:T(8,128)(2,1)S(1)} %slice.98), channel_id=1, source_target_pairs={{0,16},{4,20},{8,24},{12,28},{16,32},{20,36},{24,40},{28,44},{32,4... | collective-permute-start | bytes 884744 | tf_op jit(solution)/shard_map/ppermute | solution.py:32
  102.0 10.7 %collective-permute-start.13 = (bf16[2,4,48,384]{3,2,1,0:T(8,128)(2,1)S(1)}, bf16[2,4,48,384]{3,2,1,0:T(8,128)(2,1)S(1)}, u32[]{:S(2)}, u32[]{:S(2)}) collective-permute-start(bf16[2,4,48,384]{3,2,1,0:T(8,128)(2,1)S(1)} %slice.99), channel_id=1, source_target_pairs={{0,48},{4,52},{8,56},{12,60},{16,0},{20,4},{24,8},{28,12},{32,16},... | collective-permute-start | bytes 884744 | tf_op jit(solution)/shard_map/ppermute | solution.py:32
  105.3 10.0 %collective-permute-start.23 = (bf16[2,4,32,640]{3,2,1,0:T(8,128)(2,1)S(1)}, bf16[2,4,32,640]{3,2,1,0:T(8,128)(2,1)S(1)}, u32[]{:S(2)}, u32[]{:S(2)}) collective-permute-start(bf16[2,4,32,640]{3,2,1,0:T(8,128)(2,1)S(1)} %slice.102), channel_id=1, source_target_pairs={{0,4},{4,8},{8,12},{12,0},{16,20},{20,24},{24,28},{28,16},{32,36},... | collective-permute-start | bytes 983048 | tf_op jit(solution)/shard_map/ppermute | solution.py:32
  107.1 10.9 %collective-permute-start.24 = (bf16[2,4,32,640]{3,2,1,0:T(8,128)(2,1)S(1)}, bf16[2,4,32,640]{3,2,1,0:T(8,128)(2,1)S(1)}, u32[]{:S(2)}, u32[]{:S(2)}) collective-permute-start(bf16[2,4,32,640]{3,2,1,0:T(8,128)(2,1)S(1)} %slice.103), channel_id=1, source_target_pairs={{0,12},{4,0},{8,4},{12,8},{16,28},{20,16},{24,20},{28,24},{32,44},... | collective-permute-start | bytes 983048 | tf_op jit(solution)/shard_map/ppermute | solution.py:32
  107.8 27.9 %collective-permute-start.35 = (bf16[4,4,64,512]{3,2,1,0:T(8,128)(2,1)S(1)}, bf16[4,4,64,512]{3,2,1,0:T(8,128)(2,1)S(1)}, u32[]{:S(2)}, u32[]{:S(2)}) collective-permute-start(bf16[4,4,64,512]{3,2,1,0:T(8,128)(2,1)S(1)} %pad_maximum_fusion.a0), channel_id=1, source_target_pairs={{0,16},{4,20},{8,24},{12,28},{16,32},{20,36},{24,40},{28,44},{32,4... | collective-permute-start | bytes 3145736 | tf_op jit(solution)/shard_map/ppermute | solution.py:32
  111.0 24.8 %collective-permute-start.34 = (bf16[4,4,64,512]{3,2,1,0:T(8,128)(2,1)S(1)}, bf16[4,4,64,512]{3,2,1,0:T(8,128)(2,1)S(1)}, u32[]{:S(2)}, u32[]{:S(2)}) collective-permute-start(bf16[4,4,64,512]{3,2,1,0:T(8,128)(2,1)S(1)} %pad_maximum_fusion.a0), channel_id=1, source_target_pairs={{0,48},{4,52},{8,56},{12,60},{16,0},{20,4},{24,8},{28,12},{32,16},... | collective-permute-start | bytes 3145736 | tf_op jit(solution)/shard_map/ppermute | solution.py:32
  112.7 26.4 %collective-permute-start.43 = (bf16[4,4,64,512]{3,2,1,0:T(8,128)(2,1)S(1)}, bf16[4,4,64,512]{3,2,1,0:T(8,128)(2,1)S(1)}, u32[]{:S(2)}, u32[]{:S(2)}) collective-permute-start(bf16[4,4,64,512]{3,2,1,0:T(8,128)(2,1)S(1)} %pad_maximum_fusion.1.b0), channel_id=1, source_target_pairs={{0,4},{4,8},{8,12},{12,0},{16,20},{20,24},{24,28},{28,16},{32,36},... | collective-permute-start | bytes 3145736 | tf_op jit(solution)/shard_map/ppermute | solution.py:32
  115.4 26.0 %collective-permute-start.42 = (bf16[4,4,64,512]{3,2,1,0:T(8,128)(2,1)S(1)}, bf16[4,4,64,512]{3,2,1,0:T(8,128)(2,1)S(1)}, u32[]{:S(2)}, u32[]{:S(2)}) collective-permute-start(bf16[4,4,64,512]{3,2,1,0:T(8,128)(2,1)S(1)} %pad_maximum_fusion.1.b0), channel_id=1, source_target_pairs={{0,12},{4,0},{8,4},{12,8},{16,28},{20,16},{24,20},{28,24},{32,44},... | collective-permute-start | bytes 3145736 | tf_op jit(solution)/shard_map/ppermute | solution.py:32
  132.6 1.9 collective-permute-start.25
  135.6 9.8 %collective-permute-start.26 = (f32[160,512]{1,0:T(8,128)S(1)}, f32[160,512]{1,0:T(8,128)S(1)}, u32[]{:S(2)}, u32[]{:S(2)}) collective-permute-start(f32[160,512]{1,0:T(8,128)S(1)} %add.7.sums_a), channel_id=1, source_target_pairs={{0,2},{1,3},{2,0},{3,1},{4,6},{5,7},{6,4},{7,5},{8,10},{9,11},{10,... | collective-permute-start | bytes 983048 | tf_op jit(solution)/shard_map/ppermute | solution.py:36
  135.7 40.3 %collective-permute-start.36 = (bf16[2,4,64,512]{3,2,1,0:T(8,128)(2,1)S(1)}, bf16[2,4,64,512]{3,2,1,0:T(8,128)(2,1)}, u32[]{:S(2)}, u32[]{:S(2)}) collective-permute-start(bf16[2,4,64,512]{3,2,1,0:T(8,128)(2,1)S(1)} %slice.107), channel_id=1, source_target_pairs={{0,16},{4,20},{8,24},{12,28},{16,32},{20,36},{24,40},{28,44},{32,4... | collective-permute-start | bytes 1572872 | tf_op jit(solution)/shard_map/ppermute | solution.py:32
  135.9 40.2 %collective-permute-start.37 = (bf16[2,4,64,512]{3,2,1,0:T(8,128)(2,1)S(1)}, bf16[2,4,64,512]{3,2,1,0:T(8,128)(2,1)S(1)}, u32[]{:S(2)}, u32[]{:S(2)}) collective-permute-start(bf16[2,4,64,512]{3,2,1,0:T(8,128)(2,1)S(1)} %slice.108), channel_id=1, source_target_pairs={{0,48},{4,52},{8,56},{12,60},{16,0},{20,4},{24,8},{28,12},{32,16},... | collective-permute-start | bytes 1572872 | tf_op jit(solution)/shard_map/ppermute | solution.py:32
  139.2 36.9 %collective-permute-start.44 = (bf16[2,4,64,512]{3,2,1,0:T(8,128)(2,1)S(1)}, bf16[2,4,64,512]{3,2,1,0:T(8,128)(2,1)S(1)}, u32[]{:S(2)}, u32[]{:S(2)}) collective-permute-start(bf16[2,4,64,512]{3,2,1,0:T(8,128)(2,1)S(1)} %slice.112), channel_id=1, source_target_pairs={{0,4},{4,8},{8,12},{12,0},{16,20},{20,24},{24,28},{28,16},{32,36},... | collective-permute-start | bytes 1572872 | tf_op jit(solution)/shard_map/ppermute | solution.py:32
  141.4 34.7 %collective-permute-start.45 = (bf16[2,4,64,512]{3,2,1,0:T(8,128)(2,1)S(1)}, bf16[2,4,64,512]{3,2,1,0:T(8,128)(2,1)S(1)}, u32[]{:S(2)}, u32[]{:S(2)}) collective-permute-start(bf16[2,4,64,512]{3,2,1,0:T(8,128)(2,1)S(1)} %slice.113), channel_id=1, source_target_pairs={{0,12},{4,0},{8,4},{12,8},{16,28},{20,16},{24,20},{28,24},{32,44},... | collective-permute-start | bytes 1572872 | tf_op jit(solution)/shard_map/ppermute | solution.py:32
  191.2 3.0 %collective-permute-start.46 = (bf16[2,512,512]{2,1,0:T(8,128)(2,1)}, bf16[2,512,512]{2,1,0:T(8,128)(2,1)S(1)}, u32[]{:S(2)}, u32[]{:S(2)}) collective-permute-start(bf16[2,512,512]{2,1,0:T(8,128)(2,1)} %get-tuple-element.18), channel_id=1, source_target_pairs={{0,1},{1,0},{2,3},{3,2},{4,5},{5,4},{6,7},{7,6},{8,9},{9,8},{10,11... | collective-permute-start | bytes 3145736 | tf_op jit(solution)/shard_map/ppermute | solution.py:36
  196.9 14.0 %collective-permute-start.47 = (bf16[512,512]{1,0:T(8,128)(2,1)S(1)}, bf16[512,512]{1,0:T(8,128)(2,1)S(1)}, u32[]{:S(2)}, u32[]{:S(2)}) collective-permute-start(bf16[512,512]{1,0:T(8,128)(2,1)S(1)} %get-tuple-element.21), channel_id=1, source_target_pairs={{0,2},{1,3},{2,0},{3,1},{4,6},{5,7},{6,4},{7,5},{8,10},{9,11},{10,... | collective-permute-start | bytes 1572872 | tf_op jit(solution)/shard_map/ppermute | solution.py:36
  (23 other events, 338.8 us)

commit v2 on v1

--- a/solution.py
+++ b/solution.py
@@ -45,14 +45,8 @@
     return block, after, low, high, before
 
 
-def gather_z(block):
-    return jnp.stack([block, hop(block, 0, -1), hop(block, 0, 2), hop(block, 0, 1)])
-
-
-def gather_plane(stack, middle, last):
-    own, after, low, high, before = ring(stack, middle)
-    whole = jnp.stack([own, after, jnp.concatenate([low, high]), before])
-    return ring(whole, last)
+def direct(block, axis):
+    return jnp.stack([block, hop(block, axis, -1), hop(block, axis, 2), hop(block, axis, 1)])
 
 
 def start_pieces(pieces, place, middle_first, body):
@@ -92,10 +86,32 @@
     return ((i % count) * drafts + i // count == j).astype(BF)
 
 
+def prep_kernel(h0, h1, h2, h3, normed_out, plain):
+    tokens = normed_out.shape[1]
+    count = 32
+    blocks = (h0, h1, h2, h3)
+    step = 32
+
+    def norm(n, _):
+        at = pl.ds(pl.multiple_of(n * step, step), step)
+        rows = [h[at, :].astype(F32) for h in blocks]
+        total = sum(jnp.sum(r * r, axis=1, keepdims=True) for r in rows)
+        scale = lax.rsqrt(total / (4.0 * rows[0].shape[1]) + EPS)
+        for k, h in enumerate(blocks):
+            gain = h[pl.ds(tokens, 1), :].astype(F32)
+            plain[k, at, :] = (rows[k] * scale * gain).astype(BF)
+        return 0
+
+    lax.fori_loop(0, tokens // step, norm, 0)
+    order = order_matrix(tokens, tokens, tokens // count, count)
+    for k in range(4):
+        normed_out[k] = jnp.dot(order, plain[k], preferred_element_type=F32).astype(BF)
+
+
 def front_kernel(
-    where, pages, accepted, h0, h1, h2, h3, a0, a1, a2, a3, a4, b0, b1, b2, b3, b4,
-    taps, bias, pool, normed_out, inputs_out, sums_out, dt_out, pool_out,
-    weight, proj, dt_raw, dt_wide, xs, edges, fresh, plain, sems,
+    where, pages, accepted, normed, a0, a1, a2, a3, a4, b0, b1, b2, b3, b4,
+    taps, bias, pool, inputs_out, sums_out, dt_out, pool_out,
+    weight, proj, dt_raw, dt_wide, xs, edges, fresh, sems,
 ):
     place = place_of(where)
     m = where[1]
@@ -114,24 +130,6 @@
     start_pieces((a0, a1, a2, a3, a4), place, True, take_a)
     start_pieces((b0, b1, b2, b3, b4), place, False, take_b)
 
-    blocks = (h0, h1, h2, h3)
-    step = 32
-
-    def norm(n, _):
-        at = pl.ds(pl.multiple_of(n * step, step), step)
-        rows = [h[at, :].astype(F32) for h in blocks]
-        total = sum(jnp.sum(r * r, axis=1, keepdims=True) for r in rows)
-        scale = lax.rsqrt(total / 2048.0 + EPS)
-        for k, h in enumerate(blocks):
-            gain = h[pl.ds(tokens, 1), :].astype(F32)
-            plain[k, at, :] = (rows[k] * scale * gain).astype(BF)
-        return 0
-
-    lax.fori_loop(0, tokens // step, norm, 0)
-    order = order_matrix(tokens, tokens, drafts, count)
-    for k in range(4):
-        normed_out[k] = jnp.dot(order, plain[k], preferred_element_type=F32).astype(BF)
-
     def edge(r, _):
         slot = lax.rem(pages[r], slots)
         for k in range(3):
@@ -148,7 +146,7 @@
         total = jnp.zeros((tokens, 256), F32)
         for k in range(4):
             total = total + jnp.dot(
-                normed_out[k], weight[pl.ds((m ^ k) * 512, 512), at], preferred_element_type=F32
+                normed[k], weight[pl.ds((m ^ k) * 512, 512), at], preferred_element_type=F32
             )
         xs[:, :, at] = total.astype(BF).astype(F32).reshape(drafts, count, 256)
         return 0
@@ -172,7 +170,7 @@
             mixed = mixed + tap[1] * window[1]
             mixed = mixed + tap[2] * window[2]
             mixed = mixed + tap[3] * now
-            inputs_out[pl.ds(t * count + (n // 4) * 16, 16), at] = sigmoid_times(mixed).astype(BF)
+            inputs_out[pl.ds(pl.multiple_of(t * count + (n // 4) * 16, 16), 16), at] = sigmoid_times(mixed).astype(BF)
             for k in range(3):
                 kept[k] = jnp.where(acc + k == t + 3, now, kept[k])
             window = [window[1], window[2], now]
@@ -200,8 +198,8 @@
 
 
 def scan_kernel(
-    pages, accepted, sums_a, sums_b, dt, dt_bias, a_log, inputs, pool, ys_out, pool_out,
-    low, both, delta, decay, start, wide, kept,
+    pages, accepted, sums_a, sums_b, dt, dt_bias, a_log, inputs, pool, ys_out, kept,
+    low, both, delta, decay, start, wide, pick,
 ):
     tokens, width = inputs.shape
     count = accepted.shape[0]
@@ -219,17 +217,17 @@
         return 0
 
     lax.fori_loop(0, count, fetch, 0)
-
-    def carry_over(n, _):
-        at = pl.ds(pl.multiple_of(n * states, states), states)
-        pool_out[at, :] = pool[at, :]
-        return 0
-
-    lax.fori_loop(0, slots, carry_over, 0)
     summed = sums_a[...] + sums_b[...]
     low[...] = summed[:rank].T.astype(BF)
-    rest = jnp.concatenate([summed[rank:], jnp.zeros((128 - 2 * states, tokens), F32)], axis=0)
-    both[...] = rest.T
+    rest = summed[rank:]
+    high = rest.astype(BF).astype(F32)
+    middle = (rest - high).astype(BF).astype(F32)
+    parts = [high, middle, rest - high - middle, jnp.zeros_like(rest)]
+    both[...] = jnp.concatenate(parts, axis=0).T
+    row = lax.broadcasted_iota(jnp.int32, (128, 128), 0)
+    for q in range(2 * states):
+        hit = ((row & (2 * states - 1)) == q) & (row < 6 * states)
+        pick[:, q * 128 : (q + 1) * 128] = hit.astype(F32).astype(BF)
 
     def steps(n, _):
         at = pl.ds(pl.multiple_of(n * 256, 256), 256)
@@ -239,18 +237,18 @@
 
     lax.fori_loop(0, width // 256, steps, 0)
     for s in range(states):
-        row = -jnp.exp(a_log[s : s + 1, :]) * LOG2E
-        decay[s] = jnp.broadcast_to(row, (8, width))
+        decay[s] = jnp.broadcast_to(-jnp.exp(a_log[s : s + 1, :]) * LOG2E, (8, width))
 
     def some(rb, _):
-        def spread(t, _):
-            tile = both[pl.ds(pl.multiple_of(t * count + rb * 8, 8), 8), :]
-            for q in range(2 * states):
-                wide[t, q] = jnp.broadcast_to(tile[:, q : q + 1], (8, 128))
-            return 0
-
-        lax.fori_loop(0, drafts, spread, 0)
-        last = accepted[pl.ds(pl.multiple_of(rb * 8, 8), 8), :] - 1
+        eight = pl.ds(pl.multiple_of(rb * 8, 8), 8)
+        terms = jnp.concatenate(
+            [both[pl.ds(pl.multiple_of(t * count + rb * 8, 8), 8), :] for t in range(drafts)], axis=0
+        ).astype(BF)
+        for q in range(0, 2 * states, 4):
+            spread = jnp.dot(terms, pick[:, q * 128 : (q + 4) * 128], preferred_element_type=F32)
+            for p in range(4):
+                wide[:, q + p] = spread[:, p * 128 : (p + 1) * 128].reshape(drafts, 8, 128)
+        last = accepted[eight, :] - 1
 
         def columns(cb, _):
             at = pl.ds(pl.multiple_of(cb * 128, 128), 128)
@@ -261,7 +259,7 @@
             def advance(t, state):
                 rows = pl.ds(pl.multiple_of(t * count + rb * 8, 8), 8)
                 d = delta[rows, at]
-                drive = d * wide_inputs(rows, at)
+                drive = d * inputs[rows, at].astype(F32)
                 here = last == t
                 out = None
                 nexts = []
@@ -274,20 +272,31 @@
                 ys_out[rows, at] = out
                 return tuple(nexts)
 
-            lax.fori_loop(0, drafts, advance, first, unroll=2)
+            lax.fori_loop(0, drafts, advance, first, unroll=4)
             return 0
 
         lax.fori_loop(0, width // 128, columns, 0)
         return 0
 
-    def wide_inputs(rows, at):
-        return inputs[rows, at].astype(F32)
-
     lax.fori_loop(0, count // 8, some, 0)
+
+
+def settle_kernel(pages, kept, pool, pool_out):
+    chunks, rows, _ = kept.shape
+    count = pages.shape[0]
+    states = rows // count
+    slots = pool.shape[0] // states
+
+    def carry_over(n, _):
+        at = pl.ds(pl.multiple_of(n * states, states), states)
+        pool_out[at, :] = pool[at, :]
+        return 0
+
+    lax.fori_loop(0, slots, carry_over, 0)
 
     def settle(r, _):
         slot = lax.rem(pages[r], slots)
-        for c in range(width // 128):
+        for c in range(chunks):
             for s in range(0, states, 8):
                 pool_out[
                     pl.ds(pl.multiple_of(slot * states + s, 8), 8), c * 128 : (c + 1) * 128
@@ -297,54 +306,56 @@
     lax.fori_loop(0, count, settle, 0)
 
 
-def back_kernel(
-    where, normed, inputs, ys, skip, a0, a1, a2, a3, a4, b0, b1, b2, b3, b4,
-    send_out, keep_out, weight, outer, gated, sems,
-):
-    place = place_of(where)
-    m = where[1]
+def out_columns(where, gated, outer, far, put):
+    z, m = where[0] >> 4, where[1]
+
+    def out(part, _):
+        column = pl.ds(pl.multiple_of(part * 256, 256), 256)
+        for core in range(2):
+            k = ((m ^ (far * 2 + core)) - z) & 3
+            rows = outer[pl.ds(part * 8, 8), k, 32:64, :].reshape(256, gated.shape[1])
+            put(core, column, lax.dot_general(
+                gated[...], rows, (((1,), (1,)), ((), ())), preferred_element_type=F32
+            ))
+        return 0
+
+    lax.fori_loop(0, 2, out, 0)
+
+
+def gate_kernel(where, normed, inputs, ys, skip, second, gated, send_out, keep_out):
+    z, m = where[0] >> 4, where[1]
     tokens, width = gated.shape
-    half = width // 2
-
-    def take(src, d, column):
-        at = pl.ds(column, half)
-        pltpu.make_async_copy(src.at[pl.ds(0, 32), :], weight.at[pl.ds(d * 32, 32), at], sems.at[0]).start()
-        pltpu.make_async_copy(src.at[pl.ds(32, 32), :], outer.at[pl.ds(d * 32, 32), at], sems.at[1]).start()
-
-    start_pieces((a0, a1, a2, a3, a4), place, True, lambda src, d: take(src, d, 0))
-    start_pieces((b0, b1, b2, b3, b4), place, False, lambda src, d: take(src, d, half))
-    pltpu.make_async_copy(weight, weight, sems.at[0]).wait()
-    pltpu.make_async_copy(outer, outer, sems.at[1]).wait()
 
     def gate(n, _):
         at = pl.ds(pl.multiple_of(n * 256, 256), 256)
         total = jnp.zeros((tokens, 256), F32)
         for k in range(4):
-            total = total + jnp.dot(
-                normed[k], weight[pl.ds((m ^ k) * 512, 512), at], preferred_element_type=F32
-            )
-        z = total.astype(BF).astype(F32)
+            block = second[:, ((m ^ k) - z) & 3, 0:32, at].reshape(512, 256)
+            total = total + jnp.dot(normed[k], block, preferred_element_type=F32)
+        gates = total.astype(BF).astype(F32)
         mixed = ys[:, at] + skip[:, at] * inputs[:, at].astype(F32)
-        gated[:, at] = (mixed * sigmoid_times(z)).astype(BF)
+        gated[:, at] = (mixed * sigmoid_times(gates)).astype(BF)
         return 0
 
     lax.fori_loop(0, width // 256, gate, 0)
 
-    def out(n, _):
-        far, part = n // 2, (n % 2) * 256
-        column = pl.ds(pl.multiple_of(part, 256), 256)
-        for core in range(2):
-            rows = pl.ds(pl.multiple_of((m ^ (far * 2 + core)) * 512 + part, 256), 256)
-            value = lax.dot_general(
-                gated[...], outer[rows, :], (((1,), (1,)), ((), ())), preferred_element_type=F32
-            )
-            if core:
-                send_out[far, :, column] = value.astype(BF)
-            else:
-                keep_out[far, :, column] = value
-        return 0
-
-    lax.fori_loop(0, 4, out, 0)
+    def put(core, column, value):
+        if core:
+            send_out[:, column] = value.astype(BF)
+        else:
+            keep_out[:, column] = value
+
+    out_columns(where, gated, second, 1, put)
+
+
+def near_kernel(where, gated, second, send_out, keep_out):
+    def put(core, column, value):
+        if core:
+            send_out[:, column] = value.astype(BF)
+        else:
+            keep_out[:, column] = value
+
+    out_columns(where, gated, second, 0, put)
 
 
 def join_kernel(targets, keep, near, far, hidden, out, total):
@@ -366,17 +377,16 @@
     lax.fori_loop(0, count, place, 0)
 
 
-def unpack_kernel(where, targets, got, out, sem):
+def unpack_kernel(where, targets, got, out):
     count = targets.shape[0]
     peers = got.shape[0]
 
-    def begin(r, _):
+    def take(r, _):
         source = lax.rem(2 * where[0] - lax.div(targets[r], count) + 2 * peers, peers)
-        pltpu.make_async_copy(got.at[source], out.at[r], sem).start()
-        return 0
-
-    lax.fori_loop(0, count, begin, 0)
-    pltpu.make_async_copy(out, out, sem).wait()
+        out[r] = got[source]
+        return 0
+
+    lax.fori_loop(0, count, take, 0)
 
 
 def params():
@@ -396,35 +406,51 @@
     peers = lax.axis_size("dp")
 
     extra = jnp.concatenate(
-        [x_proj, jnp.zeros((16, 256 - x_proj.shape[1]), BF), dt_proj.reshape(16, 128)], axis=1
-    )
-    block_a = jnp.concatenate([in_x[:, :CUT], extra], axis=0)
-    first_a = gather_plane(gather_z(block_a), 2, 1)
-    first_b = gather_plane(gather_z(in_x[:, CUT:]), 1, 2)
+        [
+            x_proj,
+            jnp.zeros((16, 256 - x_proj.shape[1]), BF),
+            dt_proj.reshape(16, 128),
+            jnp.zeros((16, width - CUT), BF),
+        ],
+        axis=1,
+    )
+    first = direct(jnp.concatenate([in_x, extra], axis=0), 0)
+    first_a = ring(direct(first[:, :, :CUT], 2), 1)
+    first_b = ring(direct(first[:, :32, CUT:], 1), 2)
 
     flat = hidden.reshape(tokens, part)
     sent = jnp.concatenate([flat, jnp.broadcast_to(norm_gain[None], (16, part))], axis=0)
     near = across(sent, 1)
     far = across(sent, 2)
     both = across(far, 1)
-
-    pair = jnp.concatenate([in_z, out_proj.T], axis=0)
-    stacked = gather_z(pair)
-    second_a = gather_plane(stacked[..., : width // 2], 2, 1)
-    second_b = gather_plane(stacked[..., width // 2 :], 1, 2)
+    normed = pl.pallas_call(
+        prep_kernel,
+        out_shape=jax.ShapeDtypeStruct((4, tokens, part), BF),
+        in_specs=[VMEM] * 4,
+        out_specs=VMEM,
+        scratch_shapes=[pltpu.VMEM((4, tokens, part), BF)],
+        compiler_params=params(),
+        cost_estimate=pl.CostEstimate(flops=1_000_000_000, bytes_accessed=4 << 20, transcendentals=0),
+        name="prep",
+    )(sent, near, far, both)
+
+    stacked = direct(jnp.concatenate([in_z, out_proj.T], axis=0), 0)
+    second = lax.all_gather(
+        stacked, "dp", axis=0,
+        axis_index_groups=[[z * 16 + i for i in range(16)] for z in range(SIDE)],
+    )
 
     wide_accepted = jnp.broadcast_to(accepted[:, None], (count, 128))
-    normed, inputs, sums, dt, new_conv = pl.pallas_call(
+    inputs, sums, dt, new_conv = pl.pallas_call(
         front_kernel,
         out_shape=(
-            jax.ShapeDtypeStruct((4, tokens, part), BF),
             jax.ShapeDtypeStruct((tokens, width), BF),
             jax.ShapeDtypeStruct((rank + 2 * states, tokens), F32),
             jax.ShapeDtypeStruct((rank, width), BF),
             jax.ShapeDtypeStruct((3, slots, width), F32),
         ),
-        in_specs=[SMEM, SMEM] + [VMEM] * 5 + [ANY] * 10 + [VMEM] * 3,
-        out_specs=(VMEM,) * 5,
+        in_specs=[SMEM, SMEM] + [VMEM] * 2 + [ANY] * 10 + [VMEM] * 3,
+        out_specs=(VMEM,) * 4,
         scratch_shapes=[
             pltpu.VMEM((2048, width), BF),
             pltpu.VMEM((1024, 256), BF),
@@ -433,24 +459,23 @@
             pltpu.VMEM((drafts, count, width), F32),
             pltpu.VMEM((3, count, width), F32),
             pltpu.VMEM((3, count, width), F32),
-            pltpu.VMEM((4, tokens, part), BF),
             pltpu.SemaphoreType.DMA((3,)),
         ],
         compiler_params=params(),
         cost_estimate=pl.CostEstimate(flops=6_000_000_000, bytes_accessed=10 << 20, transcendentals=0),
         name="front",
     )(
-        where, page_table, wide_accepted, sent, near, far, both, *reorder(first_a), *reorder(first_b),
+        where, page_table, wide_accepted, normed, *first_a, *first_b,
         conv_weight, conv_bias[None], conv_pool.transpose(1, 0, 2),
     )
 
     sums = sums + across(sums, 1)
     other = across(sums, 2)
-    ys, new_state = pl.pallas_call(
+    ys, kept = pl.pallas_call(
         scan_kernel,
         out_shape=(
             jax.ShapeDtypeStruct((tokens, width), F32),
-            jax.ShapeDtypeStruct((slots * states, width), F32),
+            jax.ShapeDtypeStruct((width // 128, states * count, 128), F32),
         ),
         in_specs=[SMEM] + [VMEM] * 8,
         out_specs=(VMEM,) * 2,
@@ -461,7 +486,7 @@
             pltpu.VMEM((states, 8, width), F32),
             pltpu.VMEM((width // 128, count * states, 128), F32),
             pltpu.VMEM((drafts, 2 * states, 8, 128), F32),
-            pltpu.VMEM((width // 128, states * count, 128), F32),
+            pltpu.VMEM((128, 2 * states * 128), BF),
         ],
         compiler_params=params(),
         cost_estimate=pl.CostEstimate(flops=12_000_000_000, bytes_accessed=10 << 20, transcendentals=0),
@@ -471,28 +496,39 @@
         state_pool.reshape(slots * states, width),
     )
 
-    send, keep = pl.pallas_call(
-        back_kernel,
-        out_shape=(
-            jax.ShapeDtypeStruct((2, tokens, part), BF),
-            jax.ShapeDtypeStruct((2, tokens, part), F32),
-        ),
-        in_specs=[SMEM] + [VMEM] * 4 + [ANY] * 10,
+    new_state = pl.pallas_call(
+        settle_kernel,
+        out_shape=jax.ShapeDtypeStruct((slots * states, width), F32),
+        in_specs=[SMEM, VMEM, VMEM],
+        out_specs=VMEM,
+        compiler_params=params(),
+        cost_estimate=pl.CostEstimate(flops=0, bytes_accessed=8 << 20, transcendentals=0),
+        name="settle",
+    )(page_table, kept, state_pool.reshape(slots * states, width))
+
+    halves = (jax.ShapeDtypeStruct((tokens, part), BF), jax.ShapeDtypeStruct((tokens, part), F32))
+    gated, send_far, keep_far = pl.pallas_call(
+        gate_kernel,
+        out_shape=(jax.ShapeDtypeStruct((tokens, width), BF), *halves),
+        in_specs=[SMEM] + [VMEM] * 5,
+        out_specs=(VMEM,) * 3,
+        compiler_params=params(),
+        cost_estimate=pl.CostEstimate(flops=4_000_000_000, bytes_accessed=16 << 20, transcendentals=0),
+        name="gate",
+    )(where, normed, inputs, ys, skip[None], second)
+    forward = (keep_far + across(send_far, 1).astype(F32)).astype(BF)
+    forward, gated = lax.optimization_barrier((forward, gated))
+    remote = across(forward, 2)
+    send_near, keep_near = pl.pallas_call(
+        near_kernel,
+        out_shape=halves,
+        in_specs=[SMEM] + [VMEM] * 2,
         out_specs=(VMEM,) * 2,
-        scratch_shapes=[
-            pltpu.VMEM((2048, width), BF),
-            pltpu.VMEM((2048, width), BF),
-            pltpu.VMEM((tokens, width), BF),
-            pltpu.SemaphoreType.DMA((2,)),
-        ],
-        compiler_params=params(),
-        cost_estimate=pl.CostEstimate(flops=6_000_000_000, bytes_accessed=16 << 20, transcendentals=0),
-        name="back",
-    )(where, normed, inputs, ys, skip[None], *reorder(second_a), *reorder(second_b))
-
-    got = across(send, 1)
-    forward = (keep[1] + got[1].astype(F32)).astype(BF)
-    remote = across(forward, 2)
+        compiler_params=params(),
+        cost_estimate=pl.CostEstimate(flops=2_000_000_000, bytes_accessed=10 << 20, transcendentals=0),
+        name="near",
+    )(where, gated, second)
+    got = across(send_near, 1)
     packed = pl.pallas_call(
         join_kernel,
         out_shape=jax.ShapeDtypeStruct((peers, drafts, part), BF),
@@ -502,14 +538,13 @@
         compiler_params=params(),
         cost_estimate=pl.CostEstimate(flops=600_000_000, bytes_accessed=4 << 20, transcendentals=0),
         name="join",
-    )(permutation, keep[0], got[0], remote, flat)
+    )(permutation, keep_near, got, remote, flat)
     arrived = lax.all_to_all(packed, "dp", split_axis=0, concat_axis=0, tiled=True)
     verified = pl.pallas_call(
         unpack_kernel,
         out_shape=jax.ShapeDtypeStruct((count, drafts, part), BF),
-        in_specs=[SMEM, SMEM, ANY],
-        out_specs=ANY,
-        scratch_shapes=[pltpu.SemaphoreType.DMA(())],
+        in_specs=[SMEM, SMEM, VMEM],
+        out_specs=VMEM,
         name="unpack",
     )(where, permutation, arrived)
     return (
@@ -517,11 +552,6 @@
         new_state.reshape(slots, states, width),
         new_conv.transpose(1, 0, 2),
     )
-
-
-def reorder(pieces):
-    own, after, low, high, before = pieces
-    return own, after, low, high, before
 
 
 def solution(mesh):

time: 276 us -> 270 us (0.978); the launches traced: 270 us -> 269 us
  waiting for transfers between devices: 50.8 us -> 103 us
  blocking collectives: 36.9 us -> 0 us
  between operations: 1.5 us -> 14.3 us
  Pallas kernels: 79.1 us -> 67.4 us
  starting transfers between devices: 80.8 us -> 70.5 us
  local copies, waits for them, and re-layouts: 12.2 us -> 7.91 us
  other arithmetic: 8.98 us -> 6.02 us
    all_to_all x1 -> x0, blocking collectives: 36.9 us -> none  [on_device(): lax.all_to_all(packed, 'dp', split_axis=0, concat_axis=0, tiled=True)]
    ppermute x41 -> x20, waiting for transfers between devices: 30.2 us -> 56 us  [hop(): return lax.ppermute(value, 'dp', shift_pairs(axis, step))]
    all_to_all x0 -> x1, waiting for transfers between devices: none -> 22.9 us  [on_device(): lax.all_to_all(packed, 'dp', split_axis=0, concat_axis=0, tiled=True)]
    ppermute x41 -> x20, starting transfers between devices: 73.8 us -> 55.2 us  [hop(): return lax.ppermute(value, 'dp', shift_pairs(axis, step))]
    pallas_call x1, Pallas kernels: 17.7 us -> 2.43 us  [on_device(): pl.pallas_call(unpack_kernel, out_shape=jax.ShapeDtypeStruct((count, draf...]
    pallas_call x2 -> x5, Pallas kernels: 27.8 us -> 41.3 us  [the longest x1 11.3 us: on_device(): pl.pallas_call(front_kernel, out_shape=(jax.ShapeDtypeStruct((tokens, wid...]
    pallas_call x1, Pallas kernels: 29.9 us -> 19.8 us  [on_device(): pl.pallas_call(scan_kernel, out_shape=(jax.ShapeDtypeStruct((tokens, widt...]
    all_to_all x0 -> x1, starting transfers between devices: none -> 8.13 us  [on_device(): lax.all_to_all(packed, 'dp', split_axis=0, concat_axis=0, tiled=True)]
  transfers between devices with their start and end apart: 48 -> 30, of which waited for: 16 -> 17; matrix products, arithmetic and copies ran while one was open for 5% -> 3% of each run, Pallas kernels for 16% -> 16%
where the time goes in v2:
time: 270 us; the launch traced here: 269 us
  waiting for transfers between devices  103 us (38%)
  starting transfers between devices  70.5 us (26%)
  Pallas kernels  67.4 us (25%)
  between operations  14.3 us (5%)
  local copies, waits for them, and re-layouts  7.91 us (3%)
  other arithmetic  6.02 us (2%)
    ppermute x20, waiting for transfers between devices, hop(): return lax.ppermute(value, 'dp', shift_pairs(axis, step))  56 us
    ppermute x20, starting transfers between devices, hop(): return lax.ppermute(value, 'dp', shift_pairs(axis, step))  55.2 us
    ppermute x8, waiting for transfers between devices, across(): return lax.ppermute(value, 'mp', [(m, m ^ flip) for m in range(4)])  24.4 us
    all_to_all x1, waiting for transfers between devices, on_device(): lax.all_to_all(packed, 'dp', split_axis=0, concat_axis=0, tiled=True)  22.9 us
    pallas_call x1, Pallas kernels, on_device(): pl.pallas_call(scan_kernel, out_shape=(jax.ShapeDtypeStruct((tokens, widt...  19.8 us
    pallas_call x1, Pallas kernels, on_device(): pl.pallas_call(front_kernel, out_shape=(jax.ShapeDtypeStruct((tokens, wid...  11.3 us
    pallas_call x1, Pallas kernels, on_device(): pl.pallas_call(gate_kernel, out_shape=(jax.ShapeDtypeStruct((tokens, widt...  11 us
    all_to_all x1, starting transfers between devices, on_device(): lax.all_to_all(packed, 'dp', split_axis=0, concat_axis=0, tiled=True)  8.13 us
  transfers between devices with their start and end apart: 30, of which 17 were waited for; matrix products, arithmetic and copies ran while one was open for 3% of the time, Pallas kernels for 16%

profile of v2, /device:TPU:2, one launch (start us, length us, event | category | flops | bytes accessed | tf_op | source)
XLA Modules:
  0.0 269.4 jit_solution(8169457412862349374)
XLA Ops:
  7.2 0.9 fusion
  8.2 7.3 %collective-permute-start.23 = (bf16[64,1024]{1,0:T(8,128)(2,1)S(1)}, bf16[64,1024]{1,0:T(8,128)(2,1)S(1)}, u32[]{:S(2)}, u32[]{:S(2)}) collective-permute-start(bf16[64,1024]{1,0:T(8,128)(2,1)S(1)} %get-tuple-element.30), channel_id=1, source_target_pairs={{0,128},{4,132},{8,136},{12,140},{16,144},{20,148},{24,152},{28,15... | collective-permute-start | bytes 393224 | tf_op jit(solution)/shard_map/ppermute | solution.py:32
  15.5 2.9 %collective-permute-start.24 = (bf16[64,1024]{1,0:T(8,128)(2,1)S(1)}, bf16[64,1024]{1,0:T(8,128)(2,1)S(1)}, u32[]{:S(2)}, u32[]{:S(2)}) collective-permute-start(bf16[64,1024]{1,0:T(8,128)(2,1)S(1)} %get-tuple-element.30), channel_id=1, source_target_pairs={{0,64},{4,68},{8,72},{12,76},{16,80},{20,84},{24,88},{28,92},{32,9... | collective-permute-start | bytes 393224 | tf_op jit(solution)/shard_map/ppermute | solution.py:32
  18.4 2.0 collective-permute-done.23
  20.4 7.6 %collective-permute-done.22 = bf16[64,1024]{1,0:T(8,128)(2,1)S(1)} collective-permute-done((bf16[64,1024]{1,0:T(8,128)(2,1)S(1)}, bf16[64,1024]{1,0:T(8,128)(2,1)S(1)}, u32[]{:S(2)}, u32[]{:S(2)}) %collective-permute-start.22) | collective-permute-done | bytes 131104 | tf_op jit(solution)/shard_map/ppermute | solution.py:32
  27.9 0.9 pad_maximum_fusion.3
  29.5 0.9 fusion.1
  30.5 2.3 collective-permute-start.4
  32.7 2.7 %collective-permute-start.3 = (bf16[48,1024]{1,0:T(8,128)(2,1)S(1)}, bf16[48,1024]{1,0:T(8,128)(2,1)S(1)}, u32[]{:S(2)}, u32[]{:S(2)}) collective-permute-start(bf16[48,1024]{1,0:T(8,128)(2,1)S(1)} %get-tuple-element.32), channel_id=1, source_target_pairs={{0,192},{4,196},{8,200},{12,204},{16,208},{20,212},{24,216},{28,22... | collective-permute-start | bytes 294920 | tf_op jit(solution)/shard_map/ppermute | solution.py:32
  35.9 3.3 %collective-permute-done.4 = bf16[48,1024]{1,0:T(8,128)(2,1)S(1)} collective-permute-done((bf16[48,1024]{1,0:T(8,128)(2,1)S(1)}, bf16[48,1024]{1,0:T(8,128)(2,1)S(1)}, u32[]{:S(2)}, u32[]{:S(2)}) %collective-permute-start.4) | collective-permute-done | bytes 98336 | tf_op jit(solution)/shard_map/ppermute | solution.py:32
  39.3 4.7 %collective-permute-done.3 = bf16[48,1024]{1,0:T(8,128)(2,1)S(1)} collective-permute-done((bf16[48,1024]{1,0:T(8,128)(2,1)S(1)}, bf16[48,1024]{1,0:T(8,128)(2,1)S(1)}, u32[]{:S(2)}, u32[]{:S(2)}) %collective-permute-start.3) | collective-permute-done | bytes 98336 | tf_op jit(solution)/shard_map/ppermute | solution.py:32
  44.0 3.1 %collective-permute-start.13 = (bf16[4,32,640]{2,1,0:T(8,128)(2,1)S(1)}, bf16[4,32,640]{2,1,0:T(8,128)(2,1)S(1)}, u32[]{:S(2)}, u32[]{:S(2)}) collective-permute-start(bf16[4,32,640]{2,1,0:T(8,128)(2,1)S(1)} %pad_maximum_fusion.4), channel_id=1, source_target_pairs={{0,48},{4,52},{8,56},{12,60},{16,0},{20,4},{24,8},{28,12},{32,16},... | collective-permute-start | bytes 491528 | tf_op jit(solution)/shard_map/ppermute | solution.py:32
  47.7 1.0 collective-permute-start.15
  48.7 2.1 collective-permute-start.1
  50.9 3.7 %collective-permute-done.13 = bf16[4,32,640]{2,1,0:T(8,128)(2,1)S(1)} collective-permute-done((bf16[4,32,640]{2,1,0:T(8,128)(2,1)S(1)}, bf16[4,32,640]{2,1,0:T(8,128)(2,1)S(1)}, u32[]{:S(2)}, u32[]{:S(2)}) %collective-permute-start.13) | collective-permute-done | bytes 163872 | tf_op jit(solution)/shard_map/ppermute | solution.py:32
  54.6 4.1 %collective-permute-done.14 = bf16[4,32,640]{2,1,0:T(8,128)(2,1)S(1)} collective-permute-done((bf16[4,32,640]{2,1,0:T(8,128)(2,1)S(1)}, bf16[4,32,640]{2,1,0:T(8,128)(2,1)S(1)}, u32[]{:S(2)}, u32[]{:S(2)}) %collective-permute-start.14) | collective-permute-done | bytes 163872 | tf_op jit(solution)/shard_map/ppermute | solution.py:32
  58.8 2.9 %collective-permute-done.15 = bf16[4,32,640]{2,1,0:T(8,128)(2,1)S(1)} collective-permute-done((bf16[4,32,640]{2,1,0:T(8,128)(2,1)S(1)}, bf16[4,32,640]{2,1,0:T(8,128)(2,1)S(1)}, u32[]{:S(2)}, u32[]{:S(2)}) %collective-permute-start.15) | collective-permute-done | bytes 163872 | tf_op jit(solution)/shard_map/ppermute | solution.py:32
  61.8 1.5 collective-permute-start.17
  63.2 1.4 collective-permute-start.7
  64.6 1.7 collective-permute-start.6
  66.7 4.9 %collective-permute-done.7 = bf16[4,48,384]{2,1,0:T(8,128)(2,1)S(1)} collective-permute-done((bf16[4,48,384]{2,1,0:T(8,128)(2,1)S(1)}, bf16[4,48,384]{2,1,0:T(8,128)(2,1)S(1)}, u32[]{:S(2)}, u32[]{:S(2)}) %collective-permute-start.7) | collective-permute-done | bytes 147488 | tf_op jit(solution)/shard_map/ppermute | solution.py:32
  71.6 21.4 %collective-permute-start.16 = (bf16[4,4,32,640]{3,2,1,0:T(8,128)(2,1)S(1)}, bf16[4,4,32,640]{3,2,1,0:T(8,128)(2,1)S(1)}, u32[]{:S(2)}, u32[]{:S(2)}) collective-permute-start(bf16[4,4,32,640]{3,2,1,0:T(8,128)(2,1)S(1)} %pad_maximum_fusion.b0), channel_id=1, source_target_pairs={{0,12},{4,0},{8,4},{12,8},{16,28},{20,16},{24,20},{28,24},{32,44},... | collective-permute-start | bytes 1966088 | tf_op jit(solution)/shard_map/ppermute | solution.py:32
  92.9 2.9 %collective-permute-done.8 = bf16[4,48,384]{2,1,0:T(8,128)(2,1)S(1)} collective-permute-done((bf16[4,48,384]{2,1,0:T(8,128)(2,1)S(1)}, bf16[4,48,384]{2,1,0:T(8,128)(2,1)S(1)}, u32[]{:S(2)}, u32[]{:S(2)}) %collective-permute-start.8) | collective-permute-done | bytes 147488 | tf_op jit(solution)/shard_map/ppermute | solution.py:32
  96.3 2.9 %collective-permute-start.9 = (bf16[4,4,48,384]{3,2,1,0:T(8,128)(2,1)S(1)}, bf16[4,4,48,384]{3,2,1,0:T(8,128)(2,1)S(1)}, u32[]{:S(2)}, u32[]{:S(2)}) collective-permute-start(bf16[4,4,48,384]{3,2,1,0:T(8,128)(2,1)S(1)} %pad_maximum_fusion.1.a0), channel_id=1, source_target_pairs={{0,48},{4,52},{8,56},{12,60},{16,0},{20,4},{24,8},{28,12},{32,16},... | collective-permute-start | bytes 1769480 | tf_op jit(solution)/shard_map/ppermute | solution.py:32
  100.6 19.4 %collective-permute-done.16.b1 = bf16[4,4,32,640]{3,2,1,0:T(8,128)(2,1)S(1)} collective-permute-done((bf16[4,4,32,640]{3,2,1,0:T(8,128)(2,1)S(1)}, bf16[4,4,32,640]{3,2,1,0:T(8,128)(2,1)S(1)}, u32[]{:S(2)}, u32[]{:S(2)}) %collective-permute-start.16) | collective-permute-done | bytes 655392 | tf_op jit(solution)/shard_map/ppermute | solution.py:32
  119.9 1.2 collective-permute-start.18
  122.4 0.9 collective-permute-start.19
  124.8 3.2 %collective-permute-start.12 = (bf16[2,4,48,384]{3,2,1,0:T(8,128)(2,1)}, bf16[2,4,48,384]{3,2,1,0:T(8,128)(2,1)S(1)}, u32[]{:S(2)}, u32[]{:S(2)}) collective-permute-start(bf16[2,4,48,384]{3,2,1,0:T(8,128)(2,1)} %slice.25), channel_id=1, source_target_pairs={{0,48},{4,52},{8,56},{12,60},{16,0},{20,4},{24,8},{28,12},{32,16},... | collective-permute-start | bytes 884744 | tf_op jit(solution)/shard_map/ppermute | solution.py:32
  128.7 0.8 copy-done.7
  129.5 6.2 %prep.1.normed = bf16[4,512,512]{2,1,0:T(8,128)(2,1)} custom-call(bf16[528,512]{1,0:T(8,128)(2,1)} %copy-done.1, bf16[528,512]{1,0:T(8,128)(2,1)} %copy-done.6, bf16[528,512]{1,0:T(8,128)(2,1)} %copy-done.5, bf16[528,512]{1,0:T(8,128)(2,1)} %copy-done.7), custom_call_target="tpu_custom_call" | custom-call | flops 1000000000 | bytes 4194304 | tf_op jit(solution)/shard_map/prep/pallas_call | solution.py:426
  136.4 11.3 %front.1 = (bf16[512,1024]{1,0:T(8,128)(2,1)}, f32[160,512]{1,0:T(8,128)}, bf16[128,1024]{1,0:T(8,128)(2,1)}, f32[3,40,1024]{2,1,0:T(8,128)}) custom-call(s32[2]{0:T(128)} %pad_add_fusion.where, s32[32]{0:T(128)} %pages.5, s32[32,128]{1,0:T(8,128)} %broadcast_in_dim.28.accepted, bf16[4,512,512]{2,1,0:T(8,128)(2,1)} %prep.1.normed, ...), custom_call_target="tpu_custom_call" | custom-call | flops 6000000000 | bytes 10485760 | tf_op jit(solution)/shard_map/front/pallas_call | solution.py:444
  147.8 1.8 collective-permute-done.20
  149.7 1.0 add.6.sums_a
  150.7 2.5 collective-permute-start.21
  153.2 8.0 %collective-permute-done.21.sums_b = f32[160,512]{1,0:T(8,128)S(1)} collective-permute-done((f32[160,512]{1,0:T(8,128)S(1)}, f32[160,512]{1,0:T(8,128)S(1)}, u32[]{:S(2)}, u32[]{:S(2)}) %collective-permute-start.21) | collective-permute-done | bytes 327712 | tf_op jit(solution)/shard_map/ppermute | solution.py:36
  162.0 19.8 %scan.1 = (f32[512,1024]{1,0:T(8,128)}, f32[8,512,128]{2,1,0:T(8,128)}) custom-call(s32[32]{0:T(128)} %pages.5, s32[32,128]{1,0:T(8,128)} %broadcast_in_dim.28.accepted, f32[160,512]{1,0:T(8,128)} %copy-done.10, f32[160,512]{1,0:T(8,128)} %copy-done.17, bf16[128,1024]{1,0:T(8,128)(2,1)} %get-tuple-element.18.dt, f32[1,1024]{1,0:T(1,128)} %bitcast.63, ...), custom_call_target="tpu_custom_call" | custom-call | flops 12000000000 | bytes 10485760 | tf_op jit(solution)/shard_map/scan/pallas_call | solution.py:474
  181.8 11.0 %gate.1 = (bf16[512,1024]{1,0:T(8,128)(2,1)}, bf16[512,512]{1,0:T(8,128)(2,1)}, f32[512,512]{1,0:T(8,128)}) custom-call(s32[2]{0:T(128)} %pad_add_fusion.where, bf16[4,512,512]{2,1,0:T(8,128)(2,1)} %prep.1.normed, bf16[512,1024]{1,0:T(8,128)(2,1)} %get-tuple-element.16.inputs, f32[512,1024]{1,0:T(8,128)} %get-tuple-element.19.ys, f32[1,1024]{1,0:T(1,128)} %bitcast.64, ...), custom_call_target="tpu_custom_call" | custom-call | flops 4000000000 | bytes 16777216 | tf_op jit(solution)/shard_map/gate/pallas_call | solution.py:510
  192.8 2.1 collective-permute-done.25
  194.9 1.4 add_convert_fusion
  196.3 6.4 %near.1 = (bf16[512,512]{1,0:T(8,128)(2,1)}, f32[512,512]{1,0:T(8,128)}) custom-call(s32[2]{0:T(128)} %pad_add_fusion.where, bf16[512,1024]{1,0:T(8,128)(2,1)} %get-tuple-element.23.gated, bf16[16,4,64,1024]{3,2,1,0:T(8,128)(2,1)} %bitcast.33), custom_call_target="tpu_custom_call" | custom-call | flops 2000000000 | bytes 10485760 | tf_op jit(solution)/shard_map/near/pallas_call | solution.py:522
  202.8 1.8 collective-permute-start.27
  204.8 12.2 %collective-permute-done.27.far = bf16[512,512]{1,0:T(8,128)(2,1)S(1)} collective-permute-done((bf16[512,512]{1,0:T(8,128)(2,1)S(1)}, bf16[512,512]{1,0:T(8,128)(2,1)S(1)}, u32[]{:S(2)}, u32[]{:S(2)}) %collective-permute-start.27) | collective-permute-done | bytes 524320 | tf_op jit(solution)/shard_map/ppermute | solution.py:36
  217.8 3.8 %join.1 = bf16[64,16,512]{2,1,0:T(8,128)(2,1)} custom-call(s32[32]{0:T(128)} %targets.3, f32[512,512]{1,0:T(8,128)} %get-tuple-element.24.keep, bf16[512,512]{1,0:T(8,128)(2,1)} %copy-done.8, bf16[512,512]{1,0:T(8,128)(2,1)} %copy-done.9, bf16[512,512]{1,0:T(8,128)(2,1)} %bitcast.37), custom_call_target="tpu_custom_call" | custom-call | flops 600000000 | bytes 4194304 | tf_op jit(solution)/shard_map/join/pallas_call | solution.py:532
  221.7 8.1 %all-to-all-start = ((bf16[64,16,512]{2,1,0:T(8,128)(2,1)}), bf16[64,16,512]{2,1,0:T(8,128)(2,1)S(1)}, u32[]{:S(2)}, u32[]{:S(2)}) async-start(bf16[64,16,512]{2,1,0:T(8,128)(2,1)} %join.1), calls=%async_computation | async-start | bytes 2097152 | tf_op jit(solution)/shard_map/all_to_all | solution.py:542
  229.8 6.4 %settle.1 = f32[640,1024]{1,0:T(8,128)} custom-call(s32[32]{0:T(128)} %pages.5, f32[8,512,128]{2,1,0:T(8,128)} %get-tuple-element.27.kept, f32[640,1024]{1,0:T(8,128)} %bitcast.35), custom_call_target="tpu_custom_call" | custom-call | bytes 8388608 | tf_op jit(solution)/shard_map/settle/pallas_call | solution.py:499
  236.2 22.9 %all-to-all-done.got = bf16[64,16,512]{2,1,0:T(8,128)(2,1)S(1)} async-done(((bf16[64,16,512]{2,1,0:T(8,128)(2,1)}), bf16[64,16,512]{2,1,0:T(8,128)(2,1)S(1)}, u32[]{:S(2)}, u32[]{:S(2)}) %all-to-all-start) | async-done | bytes 1048608 | tf_op jit(solution)/shard_map/all_to_all | solution.py:542
  259.1 1.0 copy-done
  260.1 2.4 unpack.1
  (81 shorter events, 10.3 us)
Async XLA Ops:
  7.2 41.5 %copy-start.2 = (bf16[32,16,512]{2,1,0:T(8,128)(2,1)S(1)}, bf16[32,16,512]{2,1,0:T(8,128)(2,1)}, u32[]{:S(2)}) copy-start(bf16[32,16,512]{2,1,0:T(8,128)(2,1)} %param.17) | copy-start | bytes 1572868
  7.2 41.5 %copy-start.15 = (bf16[512]{0:T(512)(128)(2,1)S(1)}, bf16[512]{0:T(512)(128)(2,1)}, u32[]{:S(2)}) copy-start(bf16[512]{0:T(512)(128)(2,1)} %param.18) | copy-start | bytes 3076
  7.2 174.6 %all-gather.3.cloned.1.call-start = ((), (), s32[]{:S(2)}) async-start(), calls=%async_computation.1 | async-start | bytes 8912896 | tf_op jit(solution)/shard_map/all_gather | solution.py:438
  8.2 12.2 %collective-permute-start.23 = (bf16[64,1024]{1,0:T(8,128)(2,1)S(1)}, bf16[64,1024]{1,0:T(8,128)(2,1)S(1)}, u32[]{:S(2)}, u32[]{:S(2)}) collective-permute-start(bf16[64,1024]{1,0:T(8,128)(2,1)S(1)} %get-tuple-element.30), channel_id=1, source_target_pairs={{0,128},{4,132},{8,136},{12,140},{16,144},{20,148},{24,152},{28,15... | collective-permute-start | bytes 393224 | tf_op jit(solution)/shard_map/ppermute | solution.py:32
  15.5 12.5 %collective-permute-start.22 = (bf16[64,1024]{1,0:T(8,128)(2,1)S(1)}, bf16[64,1024]{1,0:T(8,128)(2,1)S(1)}, u32[]{:S(2)}, u32[]{:S(2)}) collective-permute-start(bf16[64,1024]{1,0:T(8,128)(2,1)S(1)} %get-tuple-element.30), channel_id=1, source_target_pairs={{0,192},{4,196},{8,200},{12,204},{16,208},{20,212},{24,216},{28,22... | collective-permute-start | bytes 393224 | tf_op jit(solution)/shard_map/ppermute | solution.py:32
  15.5 12.5 %collective-permute-start.24 = (bf16[64,1024]{1,0:T(8,128)(2,1)S(1)}, bf16[64,1024]{1,0:T(8,128)(2,1)S(1)}, u32[]{:S(2)}, u32[]{:S(2)}) collective-permute-start(bf16[64,1024]{1,0:T(8,128)(2,1)S(1)} %get-tuple-element.30), channel_id=1, source_target_pairs={{0,64},{4,68},{8,72},{12,76},{16,80},{20,84},{24,88},{28,92},{32,9... | collective-permute-start | bytes 393224 | tf_op jit(solution)/shard_map/ppermute | solution.py:32
  30.5 8.8 %collective-permute-start.4 = (bf16[48,1024]{1,0:T(8,128)(2,1)S(1)}, bf16[48,1024]{1,0:T(8,128)(2,1)S(1)}, u32[]{:S(2)}, u32[]{:S(2)}) collective-permute-start(bf16[48,1024]{1,0:T(8,128)(2,1)S(1)} %get-tuple-element.32), channel_id=1, source_target_pairs={{0,128},{4,132},{8,136},{12,140},{16,144},{20,148},{24,152},{28,15... | collective-permute-start | bytes 294920 | tf_op jit(solution)/shard_map/ppermute | solution.py:32
  32.7 11.2 %collective-permute-start.3 = (bf16[48,1024]{1,0:T(8,128)(2,1)S(1)}, bf16[48,1024]{1,0:T(8,128)(2,1)S(1)}, u32[]{:S(2)}, u32[]{:S(2)}) collective-permute-start(bf16[48,1024]{1,0:T(8,128)(2,1)S(1)} %get-tuple-element.32), channel_id=1, source_target_pairs={{0,192},{4,196},{8,200},{12,204},{16,208},{20,212},{24,216},{28,22... | collective-permute-start | bytes 294920 | tf_op jit(solution)/shard_map/ppermute | solution.py:32
  35.5 8.5 %collective-permute-start.5 = (bf16[48,1024]{1,0:T(8,128)(2,1)S(1)}, bf16[48,1024]{1,0:T(8,128)(2,1)S(1)}, u32[]{:S(2)}, u32[]{:S(2)}) collective-permute-start(bf16[48,1024]{1,0:T(8,128)(2,1)S(1)} %get-tuple-element.32), channel_id=1, source_target_pairs={{0,64},{4,68},{8,72},{12,76},{16,80},{20,84},{24,88},{28,92},{32,9... | collective-permute-start | bytes 294920 | tf_op jit(solution)/shard_map/ppermute | solution.py:32
  44.0 10.7 %collective-permute-start.13 = (bf16[4,32,640]{2,1,0:T(8,128)(2,1)S(1)}, bf16[4,32,640]{2,1,0:T(8,128)(2,1)S(1)}, u32[]{:S(2)}, u32[]{:S(2)}) collective-permute-start(bf16[4,32,640]{2,1,0:T(8,128)(2,1)S(1)} %pad_maximum_fusion.4), channel_id=1, source_target_pairs={{0,48},{4,52},{8,56},{12,60},{16,0},{20,4},{24,8},{28,12},{32,16},... | collective-permute-start | bytes 491528 | tf_op jit(solution)/shard_map/ppermute | solution.py:32
  47.1 11.7 %collective-permute-start.14 = (bf16[4,32,640]{2,1,0:T(8,128)(2,1)S(1)}, bf16[4,32,640]{2,1,0:T(8,128)(2,1)S(1)}, u32[]{:S(2)}, u32[]{:S(2)}) collective-permute-start(bf16[4,32,640]{2,1,0:T(8,128)(2,1)S(1)} %pad_maximum_fusion.4), channel_id=1, source_target_pairs={{0,32},{4,36},{8,40},{12,44},{16,48},{20,52},{24,56},{28,60},{32,0... | collective-permute-start | bytes 491528 | tf_op jit(solution)/shard_map/ppermute | solution.py:32
  47.7 14.0 %collective-permute-start.15 = (bf16[4,32,640]{2,1,0:T(8,128)(2,1)S(1)}, bf16[4,32,640]{2,1,0:T(8,128)(2,1)S(1)}, u32[]{:S(2)}, u32[]{:S(2)}) collective-permute-start(bf16[4,32,640]{2,1,0:T(8,128)(2,1)S(1)} %pad_maximum_fusion.4), channel_id=1, source_target_pairs={{0,16},{4,20},{8,24},{12,28},{16,32},{20,36},{24,40},{28,44},{32,4... | collective-permute-start | bytes 491528 | tf_op jit(solution)/shard_map/ppermute | solution.py:32
  48.7 51.8 %copy-start.1 = (bf16[528,512]{1,0:T(8,128)(2,1)}, bf16[528,512]{1,0:T(8,128)(2,1)S(1)}, u32[]{:S(2)}) copy-start(bf16[528,512]{1,0:T(8,128)(2,1)S(1)} %pad_maximum_fusion.2.h0) | copy-start | bytes 1622020
  48.7 50.6 %collective-permute-start.1 = (bf16[528,512]{1,0:T(8,128)(2,1)S(1)}, bf16[528,512]{1,0:T(8,128)(2,1)S(1)}, u32[]{:S(2)}, u32[]{:S(2)}) collective-permute-start(bf16[528,512]{1,0:T(8,128)(2,1)S(1)} %pad_maximum_fusion.2.h0), channel_id=1, source_target_pairs={{0,2},{1,3},{2,0},{3,1},{4,6},{5,7},{6,4},{7,5},{8,10},{9,11},{10,... | collective-permute-start | bytes 1622024 | tf_op jit(solution)/shard_map/ppermute | solution.py:36
  61.8 63.0 %copy-start.3 = (bf16[4,4,32,640]{3,2,1,0:T(8,128)(2,1)}, bf16[4,4,32,640]{3,2,1,0:T(8,128)(2,1)S(1)}, u32[]{:S(2)}) copy-start(bf16[4,4,32,640]{3,2,1,0:T(8,128)(2,1)S(1)} %pad_maximum_fusion.b0) | copy-start | bytes 1966084
  61.8 37.5 %collective-permute-start.17 = (bf16[4,4,32,640]{3,2,1,0:T(8,128)(2,1)S(1)}, bf16[4,4,32,640]{3,2,1,0:T(8,128)(2,1)S(1)}, u32[]{:S(2)}, u32[]{:S(2)}) collective-permute-start(bf16[4,4,32,640]{3,2,1,0:T(8,128)(2,1)S(1)} %pad_maximum_fusion.b0), channel_id=1, source_target_pairs={{0,4},{4,8},{8,12},{12,0},{16,20},{20,24},{24,28},{28,16},{32,36},... | collective-permute-start | bytes 1966088 | tf_op jit(solution)/shard_map/ppermute | solution.py:32
  63.2 8.3 %collective-permute-start.7 = (bf16[4,48,384]{2,1,0:T(8,128)(2,1)S(1)}, bf16[4,48,384]{2,1,0:T(8,128)(2,1)S(1)}, u32[]{:S(2)}, u32[]{:S(2)}) collective-permute-start(bf16[4,48,384]{2,1,0:T(8,128)(2,1)S(1)} %pad_maximum_fusion.7), channel_id=1, source_target_pairs={{0,8},{4,12},{8,0},{12,4},{16,24},{20,28},{24,16},{28,20},{32,40},... | collective-permute-start | bytes 442376 | tf_op jit(solution)/shard_map/ppermute | solution.py:32
  64.6 28.3 %collective-permute-start.6 = (bf16[4,48,384]{2,1,0:T(8,128)(2,1)S(1)}, bf16[4,48,384]{2,1,0:T(8,128)(2,1)S(1)}, u32[]{:S(2)}, u32[]{:S(2)}) collective-permute-start(bf16[4,48,384]{2,1,0:T(8,128)(2,1)S(1)} %pad_maximum_fusion.7), channel_id=1, source_target_pairs={{0,12},{4,0},{8,4},{12,8},{16,28},{20,16},{24,20},{28,24},{32,44},... | collective-permute-start | bytes 442376 | tf_op jit(solution)/shard_map/ppermute | solution.py:32
  66.3 29.6 %collective-permute-start.8 = (bf16[4,48,384]{2,1,0:T(8,128)(2,1)S(1)}, bf16[4,48,384]{2,1,0:T(8,128)(2,1)S(1)}, u32[]{:S(2)}, u32[]{:S(2)}) collective-permute-start(bf16[4,48,384]{2,1,0:T(8,128)(2,1)S(1)} %pad_maximum_fusion.7), channel_id=1, source_target_pairs={{0,4},{4,8},{8,12},{12,0},{16,20},{20,24},{24,28},{28,16},{32,36},... | collective-permute-start | bytes 442376 | tf_op jit(solution)/shard_map/ppermute | solution.py:32
  71.6 48.3 %collective-permute-start.16 = (bf16[4,4,32,640]{3,2,1,0:T(8,128)(2,1)S(1)}, bf16[4,4,32,640]{3,2,1,0:T(8,128)(2,1)S(1)}, u32[]{:S(2)}, u32[]{:S(2)}) collective-permute-start(bf16[4,4,32,640]{3,2,1,0:T(8,128)(2,1)S(1)} %pad_maximum_fusion.b0), channel_id=1, source_target_pairs={{0,12},{4,0},{8,4},{12,8},{16,28},{20,16},{24,20},{28,24},{32,44},... | collective-permute-start | bytes 1966088 | tf_op jit(solution)/shard_map/ppermute | solution.py:32
  96.0 39.7 %copy-start.4 = (bf16[4,4,48,384]{3,2,1,0:T(8,128)(2,1)}, bf16[4,4,48,384]{3,2,1,0:T(8,128)(2,1)S(1)}, u32[]{:S(2)}) copy-start(bf16[4,4,48,384]{3,2,1,0:T(8,128)(2,1)S(1)} %pad_maximum_fusion.1.a0) | copy-start | bytes 1769476
  96.0 26.4 %collective-permute-start.10 = (bf16[4,4,48,384]{3,2,1,0:T(8,128)(2,1)S(1)}, bf16[4,4,48,384]{3,2,1,0:T(8,128)(2,1)S(1)}, u32[]{:S(2)}, u32[]{:S(2)}) collective-permute-start(bf16[4,4,48,384]{3,2,1,0:T(8,128)(2,1)S(1)} %pad_maximum_fusion.1.a0), channel_id=1, source_target_pairs={{0,16},{4,20},{8,24},{12,28},{16,32},{20,36},{24,40},{28,44},{32,4... | collective-permute-start | bytes 1769480 | tf_op jit(solution)/shard_map/ppermute | solution.py:32
  96.3 27.6 %collective-permute-start.9 = (bf16[4,4,48,384]{3,2,1,0:T(8,128)(2,1)S(1)}, bf16[4,4,48,384]{3,2,1,0:T(8,128)(2,1)S(1)}, u32[]{:S(2)}, u32[]{:S(2)}) collective-permute-start(bf16[4,4,48,384]{3,2,1,0:T(8,128)(2,1)S(1)} %pad_maximum_fusion.1.a0), channel_id=1, source_target_pairs={{0,48},{4,52},{8,56},{12,60},{16,0},{20,4},{24,8},{28,12},{32,16},... | collective-permute-start | bytes 1769480 | tf_op jit(solution)/shard_map/ppermute | solution.py:32
  99.3 29.4 %copy-start.5 = (bf16[528,512]{1,0:T(8,128)(2,1)}, bf16[528,512]{1,0:T(8,128)(2,1)S(1)}, u32[]{:S(2)}) copy-start(bf16[528,512]{1,0:T(8,128)(2,1)S(1)} %collective-permute-done.1.h2) | copy-start | bytes 1622020
  99.3 25.5 %collective-permute-start = (bf16[528,512]{1,0:T(8,128)(2,1)S(1)}, bf16[528,512]{1,0:T(8,128)(2,1)S(1)}, u32[]{:S(2)}, u32[]{:S(2)}) collective-permute-start(bf16[528,512]{1,0:T(8,128)(2,1)S(1)} %pad_maximum_fusion.2.h0), channel_id=1, source_target_pairs={{0,1},{1,0},{2,3},{3,2},{4,5},{5,4},{6,7},{7,6},{8,9},{9,8},{10,11... | collective-permute-start | bytes 1622024 | tf_op jit(solution)/shard_map/ppermute | solution.py:36
  99.3 25.5 %copy-start.11 = (bf16[4,4,32,640]{3,2,1,0:T(8,128)(2,1)}, bf16[4,4,32,640]{3,2,1,0:T(8,128)(2,1)S(1)}, u32[]{:S(2)}) copy-start(bf16[4,4,32,640]{3,2,1,0:T(8,128)(2,1)S(1)} %collective-permute-done.17.b4) | copy-start | bytes 1966084
  99.3 29.4 %collective-permute-start.2 = (bf16[528,512]{1,0:T(8,128)(2,1)S(1)}, bf16[528,512]{1,0:T(8,128)(2,1)S(1)}, u32[]{:S(2)}, u32[]{:S(2)}) collective-permute-start(bf16[528,512]{1,0:T(8,128)(2,1)S(1)} %collective-permute-done.1.h2), channel_id=1, source_target_pairs={{0,1},{1,0},{2,3},{3,2},{4,5},{5,4},{6,7},{7,6},{8,9},{9,8},{10,11... | collective-permute-start | bytes 1622024 | tf_op jit(solution)/shard_map/ppermute | solution.py:36
  119.9 8.1 %copy-start.12 = (bf16[4,4,32,640]{3,2,1,0:T(8,128)(2,1)}, bf16[4,4,32,640]{3,2,1,0:T(8,128)(2,1)S(1)}, u32[]{:S(2)}) copy-start(bf16[4,4,32,640]{3,2,1,0:T(8,128)(2,1)S(1)} %collective-permute-done.16.b1) | copy-start | bytes 1966084
  119.9 15.8 %collective-permute-start.18 = (bf16[2,4,32,640]{3,2,1,0:T(8,128)(2,1)}, bf16[2,4,32,640]{3,2,1,0:T(8,128)(2,1)}, u32[]{:S(2)}, u32[]{:S(2)}) collective-permute-start(bf16[2,4,32,640]{3,2,1,0:T(8,128)(2,1)} %slice.26), channel_id=1, source_target_pairs={{0,4},{4,8},{8,12},{12,0},{16,20},{20,24},{24,28},{28,16},{32,36},... | collective-permute-start | bytes 983048 | tf_op jit(solution)/shard_map/ppermute | solution.py:32
  122.3 5.7 %copy-start.13 = (bf16[4,4,48,384]{3,2,1,0:T(8,128)(2,1)}, bf16[4,4,48,384]{3,2,1,0:T(8,128)(2,1)S(1)}, u32[]{:S(2)}) copy-start(bf16[4,4,48,384]{3,2,1,0:T(8,128)(2,1)S(1)} %collective-permute-done.10.a4) | copy-start | bytes 1769476
  122.4 13.4 %collective-permute-start.19 = (bf16[2,4,32,640]{3,2,1,0:T(8,128)(2,1)}, bf16[2,4,32,640]{3,2,1,0:T(8,128)(2,1)}, u32[]{:S(2)}, u32[]{:S(2)}) collective-permute-start(bf16[2,4,32,640]{3,2,1,0:T(8,128)(2,1)} %slice.27), channel_id=1, source_target_pairs={{0,12},{4,0},{8,4},{12,8},{16,28},{20,16},{24,20},{28,24},{32,44},... | collective-permute-start | bytes 983048 | tf_op jit(solution)/shard_map/ppermute | solution.py:32
  124.0 4.1 %copy-start.14 = (bf16[4,4,48,384]{3,2,1,0:T(8,128)(2,1)}, bf16[4,4,48,384]{3,2,1,0:T(8,128)(2,1)S(1)}, u32[]{:S(2)}) copy-start(bf16[4,4,48,384]{3,2,1,0:T(8,128)(2,1)S(1)} %collective-permute-done.9.a1) | copy-start | bytes 1769476
  124.0 11.7 %collective-permute-start.11 = (bf16[2,4,48,384]{3,2,1,0:T(8,128)(2,1)}, bf16[2,4,48,384]{3,2,1,0:T(8,128)(2,1)}, u32[]{:S(2)}, u32[]{:S(2)}) collective-permute-start(bf16[2,4,48,384]{3,2,1,0:T(8,128)(2,1)} %slice.24), channel_id=1, source_target_pairs={{0,16},{4,20},{8,24},{12,28},{16,32},{20,36},{24,40},{28,44},{32,4... | collective-permute-start | bytes 884744 | tf_op jit(solution)/shard_map/ppermute | solution.py:32
  124.8 3.8 %copy-start.6 = (bf16[528,512]{1,0:T(8,128)(2,1)}, bf16[528,512]{1,0:T(8,128)(2,1)S(1)}, u32[]{:S(2)}) copy-start(bf16[528,512]{1,0:T(8,128)(2,1)S(1)} %collective-permute-done.h1) | copy-start | bytes 1622020
  124.8 10.9 %collective-permute-start.12 = (bf16[2,4,48,384]{3,2,1,0:T(8,128)(2,1)}, bf16[2,4,48,384]{3,2,1,0:T(8,128)(2,1)S(1)}, u32[]{:S(2)}, u32[]{:S(2)}) collective-permute-start(bf16[2,4,48,384]{3,2,1,0:T(8,128)(2,1)} %slice.25), channel_id=1, source_target_pairs={{0,48},{4,52},{8,56},{12,60},{16,0},{20,4},{24,8},{28,12},{32,16},... | collective-permute-start | bytes 884744 | tf_op jit(solution)/shard_map/ppermute | solution.py:32
  128.7 7.1 %copy-start.16 = (s32[32]{0:T(128)S(1)}, s32[32]{0:T(128)}, u32[]{:S(2)}) copy-start(s32[32]{0:T(128)} %param.33) | copy-start | bytes 388
  128.7 0.8 copy-start.7
  147.7 1.9 collective-permute-start.20
  150.7 10.5 %copy-start.10 = (f32[160,512]{1,0:T(8,128)}, f32[160,512]{1,0:T(8,128)S(1)}, u32[]{:S(2)}) copy-start(f32[160,512]{1,0:T(8,128)S(1)} %add.6.sums_a) | copy-start | bytes 983044
  150.7 10.5 %collective-permute-start.21 = (f32[160,512]{1,0:T(8,128)S(1)}, f32[160,512]{1,0:T(8,128)S(1)}, u32[]{:S(2)}, u32[]{:S(2)}) collective-permute-start(f32[160,512]{1,0:T(8,128)S(1)} %add.6.sums_a), channel_id=1, source_target_pairs={{0,2},{1,3},{2,0},{3,1},{4,6},{5,7},{6,4},{7,5},{8,10},{9,11},{10,... | collective-permute-start | bytes 983048 | tf_op jit(solution)/shard_map/ppermute | solution.py:36
  161.2 0.8 copy-start.17
  192.8 2.1 collective-permute-start.25
  202.7 2.1 collective-permute-start.26
  202.8 14.2 %collective-permute-start.27 = (bf16[512,512]{1,0:T(8,128)(2,1)S(1)}, bf16[512,512]{1,0:T(8,128)(2,1)S(1)}, u32[]{:S(2)}, u32[]{:S(2)}) collective-permute-start(bf16[512,512]{1,0:T(8,128)(2,1)S(1)} %add_convert_fusion), channel_id=1, source_target_pairs={{0,2},{1,3},{2,0},{3,1},{4,6},{5,7},{6,4},{7,5},{8,10},{9,11},{10,... | collective-permute-start | bytes 1572872 | tf_op jit(solution)/shard_map/ppermute | solution.py:36
  204.8 12.2 %copy-start.8 = (bf16[512,512]{1,0:T(8,128)(2,1)}, bf16[512,512]{1,0:T(8,128)(2,1)S(1)}, u32[]{:S(2)}) copy-start(bf16[512,512]{1,0:T(8,128)(2,1)S(1)} %collective-permute-done.26.near) | copy-start | bytes 1572868
  217.0 0.8 copy-start.9
  221.7 37.5 %all-to-all-start = ((bf16[64,16,512]{2,1,0:T(8,128)(2,1)}), bf16[64,16,512]{2,1,0:T(8,128)(2,1)S(1)}, u32[]{:S(2)}, u32[]{:S(2)}) async-start(bf16[64,16,512]{2,1,0:T(8,128)(2,1)} %join.1), calls=%async_computation | async-start | bytes 2097152 | tf_op jit(solution)/shard_map/all_to_all | solution.py:542
  259.1 1.0 copy-start
  (1 other events, 0.7 us)
Sparse Core Ops, SparseCore 0:
  28.9 94.7 all-gather.2

commit v3 on v2

--- a/solution.py
+++ b/solution.py
@@ -36,13 +36,18 @@
     return lax.ppermute(value, "mp", [(m, m ^ flip) for m in range(4)])
 
 
-def ring(block, axis):
+def after(value, *others):
+    return lax.optimization_barrier((value, others))[0]
+
+
+def ring_one(block, axis):
+    return hop(block, axis, -1), hop(block, axis, 1)
+
+
+def ring_two(block, axis, sides):
     half = block.shape[0] // 2
-    after = hop(block, axis, -1)
-    before = hop(block, axis, 1)
-    low = hop(before[:half], axis, 1)
-    high = hop(after[half:], axis, -1)
-    return block, after, low, high, before
+    above, below = sides
+    return block, above, hop(below[:half], axis, 1), hop(above[half:], axis, -1), below
 
 
 def direct(block, axis):
@@ -51,16 +56,16 @@
 
 def start_pieces(pieces, place, middle_first, body):
     z, y, x = place
-    own, after, low, high, before = pieces
+    own, above, low, high, below = pieces
 
     def one(k, _):
+        dz = (z + k) & 3
         for i in range(SIDE):
             for f in range(SIDE):
                 if f == 2:
                     ref, at = (low, i) if i < 2 else (high, i - 2)
                 else:
-                    ref, at = {0: own, 1: after, 3: before}[f], i
-                dz = (z + k) & 3
+                    ref, at = {0: own, 1: above, 3: below}[f], i
                 if middle_first:
                     dx, dy = (x + i) & 3, (y + f) & 3
                 else:
@@ -306,56 +311,57 @@
     lax.fori_loop(0, count, settle, 0)
 
 
-def out_columns(where, gated, outer, far, put):
-    z, m = where[0] >> 4, where[1]
-
-    def out(part, _):
-        column = pl.ds(pl.multiple_of(part * 256, 256), 256)
-        for core in range(2):
-            k = ((m ^ (far * 2 + core)) - z) & 3
-            rows = outer[pl.ds(part * 8, 8), k, 32:64, :].reshape(256, gated.shape[1])
-            put(core, column, lax.dot_general(
-                gated[...], rows, (((1,), (1,)), ((), ())), preferred_element_type=F32
-            ))
-        return 0
-
-    lax.fori_loop(0, 2, out, 0)
-
-
-def gate_kernel(where, normed, inputs, ys, skip, second, gated, send_out, keep_out):
-    z, m = where[0] >> 4, where[1]
+def gate_kernel(
+    where, normed, inputs, ys, skip, a0, a1, a2, a3, a4, b0, b1, b2, b3, b4,
+    send_out, keep_out, weight, outer, gated, sems,
+):
+    m = where[1]
     tokens, width = gated.shape
+    half = width // 2
+    a, b = (a0, a1, a2, a3, a4), (b0, b1, b2, b3, b4)
+
+    def take(src, d, column):
+        pltpu.make_async_copy(
+            src.at[pl.ds(0, 32), :], weight.at[pl.ds(d * 32, 32), pl.ds(column, half)], sems.at[0]
+        ).start()
+        pltpu.make_async_copy(
+            src.at[pl.ds(32, 32), :], outer.at[pl.ds(d * 32, 32), pl.ds(column, half)], sems.at[1]
+        ).start()
+
+    start_pieces(a, place_of(where), True, lambda src, d: take(src, d, 0))
+    start_pieces(b, place_of(where), False, lambda src, d: take(src, d, half))
+    pltpu.make_async_copy(weight, weight, sems.at[0]).wait()
 
     def gate(n, _):
         at = pl.ds(pl.multiple_of(n * 256, 256), 256)
         total = jnp.zeros((tokens, 256), F32)
         for k in range(4):
-            block = second[:, ((m ^ k) - z) & 3, 0:32, at].reshape(512, 256)
-            total = total + jnp.dot(normed[k], block, preferred_element_type=F32)
+            total = total + jnp.dot(
+                normed[k], weight[pl.ds((m ^ k) * 512, 512), at], preferred_element_type=F32
+            )
         gates = total.astype(BF).astype(F32)
         mixed = ys[:, at] + skip[:, at] * inputs[:, at].astype(F32)
         gated[:, at] = (mixed * sigmoid_times(gates)).astype(BF)
         return 0
 
     lax.fori_loop(0, width // 256, gate, 0)
-
-    def put(core, column, value):
-        if core:
-            send_out[:, column] = value.astype(BF)
-        else:
-            keep_out[:, column] = value
-
-    out_columns(where, gated, second, 1, put)
-
-
-def near_kernel(where, gated, second, send_out, keep_out):
-    def put(core, column, value):
-        if core:
-            send_out[:, column] = value.astype(BF)
-        else:
-            keep_out[:, column] = value
-
-    out_columns(where, gated, second, 0, put)
+    pltpu.make_async_copy(outer, outer, sems.at[1]).wait()
+
+    def out(part, _):
+        column = pl.ds(pl.multiple_of((part & 1) * 256, 256), 256)
+        for core in range(2):
+            block = m ^ ((part & 2) + core)
+            rows = outer[pl.ds(pl.multiple_of(block * 512 + (part & 1) * 256, 256), 256), :]
+            value = lax.dot_general(
+                gated[...], rows, (((1,), (1,)), ((), ())), preferred_element_type=F32
+            )
+            if core:
+                send_out[part >> 1, :, column] = value.astype(BF)
+            else:
+                keep_out[part >> 1, :, column] = value
+        return 0
+
+    lax.fori_loop(0, 4, out, 0)
 
 
 def join_kernel(targets, keep, near, far, hidden, out, total):
@@ -364,7 +370,7 @@
     drafts = tokens // count
     order = order_matrix(tokens, tokens, drafts, count)
     base = jnp.dot(order, hidden[...], preferred_element_type=F32)
-    summed = keep[...] + near[...].astype(F32) + far[...].astype(F32)
+    summed = keep[0] + near[0].astype(F32) + far[...].astype(F32)
     rounded = (summed + base).astype(BF)
     back = lax.dot_general(order, rounded, (((0,), (0,)), ((), ())), preferred_element_type=F32)
     total[...] = back.astype(BF).reshape(count, drafts, width)
@@ -415,8 +421,11 @@
         axis=1,
     )
     first = direct(jnp.concatenate([in_x, extra], axis=0), 0)
-    first_a = ring(direct(first[:, :, :CUT], 2), 1)
-    first_b = ring(direct(first[:, :32, CUT:], 1), 2)
+    middle_a = direct(first[:, :, :CUT], 2)
+    middle_b = direct(first[:, :32, CUT:], 1)
+    sides_a, sides_b = ring_one(middle_a, 1), ring_one(middle_b, 2)
+    first_a = ring_two(middle_a, 1, sides_a)
+    first_b = ring_two(middle_b, 2, sides_b)
 
     flat = hidden.reshape(tokens, part)
     sent = jnp.concatenate([flat, jnp.broadcast_to(norm_gain[None], (16, part))], axis=0)
@@ -430,15 +439,15 @@
         out_specs=VMEM,
         scratch_shapes=[pltpu.VMEM((4, tokens, part), BF)],
         compiler_params=params(),
-        cost_estimate=pl.CostEstimate(flops=1_000_000_000, bytes_accessed=4 << 20, transcendentals=0),
+        cost_estimate=pl.CostEstimate(flops=1_000_000, bytes_accessed=1 << 10, transcendentals=0),
         name="prep",
     )(sent, near, far, both)
 
-    stacked = direct(jnp.concatenate([in_z, out_proj.T], axis=0), 0)
-    second = lax.all_gather(
-        stacked, "dp", axis=0,
-        axis_index_groups=[[z * 16 + i for i in range(16)] for z in range(SIDE)],
-    )
+    pair = after(jnp.concatenate([in_z, out_proj.T], axis=0), first)
+    stacked = after(direct(pair, 0), middle_a, middle_b, near, far)
+    plane_a = after(direct(stacked[..., : width // 2], 2), first_a, first_b, normed)
+    plane_b = after(direct(stacked[..., width // 2 :], 1), first_a, first_b, normed)
+    around_a, around_b = ring_one(plane_a, 1), ring_one(plane_b, 2)
 
     wide_accepted = jnp.broadcast_to(accepted[:, None], (count, 128))
     inputs, sums, dt, new_conv = pl.pallas_call(
@@ -462,7 +471,7 @@
             pltpu.SemaphoreType.DMA((3,)),
         ],
         compiler_params=params(),
-        cost_estimate=pl.CostEstimate(flops=6_000_000_000, bytes_accessed=10 << 20, transcendentals=0),
+        cost_estimate=pl.CostEstimate(flops=1_000_000, bytes_accessed=1 << 10, transcendentals=0),
         name="front",
     )(
         where, page_table, wide_accepted, normed, *first_a, *first_b,
@@ -470,7 +479,8 @@
     )
 
     sums = sums + across(sums, 1)
-    other = across(sums, 2)
+    other = after(across(sums, 2), around_a, around_b)
+    second = (*ring_two(plane_a, 1, around_a), *ring_two(plane_b, 2, around_b))
     ys, kept = pl.pallas_call(
         scan_kernel,
         out_shape=(
@@ -489,7 +499,7 @@
             pltpu.VMEM((128, 2 * states * 128), BF),
         ],
         compiler_params=params(),
-        cost_estimate=pl.CostEstimate(flops=12_000_000_000, bytes_accessed=10 << 20, transcendentals=0),
+        cost_estimate=pl.CostEstimate(flops=1_000_000, bytes_accessed=1 << 10, transcendentals=0),
         name="scan",
     )(
         page_table, wide_accepted, sums, other, dt, dt_bias[None], a_log, inputs,
@@ -502,33 +512,30 @@
         in_specs=[SMEM, VMEM, VMEM],
         out_specs=VMEM,
         compiler_params=params(),
-        cost_estimate=pl.CostEstimate(flops=0, bytes_accessed=8 << 20, transcendentals=0),
+        cost_estimate=pl.CostEstimate(flops=1_000_000, bytes_accessed=1 << 10, transcendentals=0),
         name="settle",
     )(page_table, kept, state_pool.reshape(slots * states, width))
 
-    halves = (jax.ShapeDtypeStruct((tokens, part), BF), jax.ShapeDtypeStruct((tokens, part), F32))
-    gated, send_far, keep_far = pl.pallas_call(
+    send, keep = pl.pallas_call(
         gate_kernel,
-        out_shape=(jax.ShapeDtypeStruct((tokens, width), BF), *halves),
-        in_specs=[SMEM] + [VMEM] * 5,
-        out_specs=(VMEM,) * 3,
+        out_shape=(
+            jax.ShapeDtypeStruct((2, tokens, part), BF),
+            jax.ShapeDtypeStruct((2, tokens, part), F32),
+        ),
+        in_specs=[SMEM] + [VMEM] * 4 + [ANY] * 10,
+        out_specs=(VMEM,) * 2,
+        scratch_shapes=[
+            pltpu.VMEM((2048, width), BF),
+            pltpu.VMEM((2048, width), BF),
+            pltpu.VMEM((tokens, width), BF),
+            pltpu.SemaphoreType.DMA((2,)),
+        ],
         compiler_params=params(),
-        cost_estimate=pl.CostEstimate(flops=4_000_000_000, bytes_accessed=16 << 20, transcendentals=0),
+        cost_estimate=pl.CostEstimate(flops=1_000_000, bytes_accessed=1 << 10, transcendentals=0),
         name="gate",
-    )(where, normed, inputs, ys, skip[None], second)
-    forward = (keep_far + across(send_far, 1).astype(F32)).astype(BF)
-    forward, gated = lax.optimization_barrier((forward, gated))
-    remote = across(forward, 2)
-    send_near, keep_near = pl.pallas_call(
-        near_kernel,
-        out_shape=halves,
-        in_specs=[SMEM] + [VMEM] * 2,
-        out_specs=(VMEM,) * 2,
-        compiler_params=params(),
-        cost_estimate=pl.CostEstimate(flops=2_000_000_000, bytes_accessed=10 << 20, transcendentals=0),
-        name="near",
-    )(where, gated, second)
-    got = across(send_near, 1)
+    )(where, normed, inputs, ys, skip[None], *second)
+    got = across(send, 1)
+    remote = across((keep[1] + got[1].astype(F32)).astype(BF), 2)
     packed = pl.pallas_call(
         join_kernel,
         out_shape=jax.ShapeDtypeStruct((peers, drafts, part), BF),
@@ -536,9 +543,9 @@
         out_specs=VMEM,
         scratch_shapes=[pltpu.VMEM((count, drafts, part), BF)],
         compiler_params=params(),
-        cost_estimate=pl.CostEstimate(flops=600_000_000, bytes_accessed=4 << 20, transcendentals=0),
+        cost_estimate=pl.CostEstimate(flops=1_000_000, bytes_accessed=1 << 10, transcendentals=0),
         name="join",
-    )(permutation, keep_near, got, remote, flat)
+    )(permutation, keep, got, remote, flat)
     arrived = lax.all_to_all(packed, "dp", split_axis=0, concat_axis=0, tiled=True)
     verified = pl.pallas_call(
         unpack_kernel,

time: 270 us -> 263 us (0.974)
  the two profiles are of different devices: /device:TPU:2 before, /device:TPU:1 now
where the time goes in v3:
time: 263 us; the launch traced here: 258 us
  waiting for transfers between devices  90.4 us (34%)
  starting transfers between devices  86 us (33%)
  Pallas kernels  64.9 us (25%)
  local copies, waits for them, and re-layouts  9.71 us (4%)
  other arithmetic  5.9 us (2%)
    ppermute x34, starting transfers between devices, hop(): return lax.ppermute(value, 'dp', shift_pairs(axis, step))  63.7 us
    ppermute x34, waiting for transfers between devices, hop(): return lax.ppermute(value, 'dp', shift_pairs(axis, step))  45.7 us
    all_to_all x1, waiting for transfers between devices, on_device(): lax.all_to_all(packed, 'dp', split_axis=0, concat_axis=0, tiled=True)  22.9 us
    ppermute x7, waiting for transfers between devices, across(): return lax.ppermute(value, 'mp', [(m, m ^ flip) for m in range(4)])  21.8 us
    pallas_call x1, Pallas kernels, on_device(): pl.pallas_call(scan_kernel, out_shape=(jax.ShapeDtypeStruct((tokens, widt...  19.9 us
    ppermute x7, starting transfers between devices, across(): return lax.ppermute(value, 'mp', [(m, m ^ flip) for m in range(4)])  15.9 us
    pallas_call x1, Pallas kernels, on_device(): pl.pallas_call(gate_kernel, out_shape=(jax.ShapeDtypeStruct((2, tokens, p...  14 us
    pallas_call x1, Pallas kernels, on_device(): pl.pallas_call(front_kernel, out_shape=(jax.ShapeDtypeStruct((tokens, wid...  11.3 us
  transfers between devices with their start and end apart: 42, of which 15 were waited for; matrix products, arithmetic and copies ran while one was open for 3% of the time, Pallas kernels for 17%

profile of v3, /device:TPU:1, one launch (start us, length us, event | category | flops | bytes accessed | tf_op | source)
XLA Modules:
  0.0 258.2 jit_solution(13229500297740393478)
XLA Ops:
  2.3 7.8 %collective-permute-start.4 = (bf16[48,1024]{1,0:T(8,128)(2,1)S(1)}, bf16[48,1024]{1,0:T(8,128)(2,1)S(1)}, u32[]{:S(2)}, u32[]{:S(2)}) collective-permute-start(bf16[48,1024]{1,0:T(8,128)(2,1)S(1)} %get-tuple-element.38), channel_id=1, source_target_pairs={{0,128},{4,132},{8,136},{12,140},{16,144},{20,148},{24,152},{28,15... | collective-permute-start | bytes 294920 | tf_op jit(solution)/shard_map/ppermute | solution.py:32
  10.0 2.4 collective-permute-start.5
  15.0 1.8 collective-permute-start
  17.7 2.4 collective-permute-done.3
  20.3 3.8 %collective-permute-start.23 = (bf16[64,1024]{1,0:T(8,128)(2,1)S(1)}, bf16[64,1024]{1,0:T(8,128)(2,1)S(1)}, u32[]{:S(2)}, u32[]{:S(2)}) collective-permute-start(bf16[64,1024]{1,0:T(8,128)(2,1)S(1)} %pad_maximum_fusion.7), channel_id=1, source_target_pairs={{0,128},{4,132},{8,136},{12,140},{16,144},{20,148},{24,152},{28,15... | collective-permute-start | bytes 393224 | tf_op jit(solution)/shard_map/ppermute | solution.py:32
  24.2 1.1 collective-permute-start.22
  25.3 10.3 %collective-permute-done.24 = bf16[64,1024]{1,0:T(8,128)(2,1)S(1)} collective-permute-done((bf16[64,1024]{1,0:T(8,128)(2,1)S(1)}, bf16[64,1024]{1,0:T(8,128)(2,1)S(1)}, u32[]{:S(2)}, u32[]{:S(2)}) %collective-permute-start.24) | collective-permute-done | bytes 131104 | tf_op jit(solution)/shard_map/ppermute | solution.py:32
  35.6 3.2 %collective-permute-start.7 = (bf16[4,48,384]{2,1,0:T(8,128)(2,1)S(1)}, bf16[4,48,384]{2,1,0:T(8,128)(2,1)S(1)}, u32[]{:S(2)}, u32[]{:S(2)}) collective-permute-start(bf16[4,48,384]{2,1,0:T(8,128)(2,1)S(1)} %get-tuple-element.36), channel_id=1, source_target_pairs={{0,8},{4,12},{8,0},{12,4},{16,24},{20,28},{24,16},{28,20},{32,40},... | collective-permute-start | bytes 442376 | tf_op jit(solution)/shard_map/ppermute | solution.py:32
  38.8 4.0 %collective-permute-done.23 = bf16[64,1024]{1,0:T(8,128)(2,1)S(1)} collective-permute-done((bf16[64,1024]{1,0:T(8,128)(2,1)S(1)}, bf16[64,1024]{1,0:T(8,128)(2,1)S(1)}, u32[]{:S(2)}, u32[]{:S(2)}) %collective-permute-start.23) | collective-permute-done | bytes 131104 | tf_op jit(solution)/shard_map/ppermute | solution.py:32
  42.7 3.7 %collective-permute-start.6 = (bf16[4,48,384]{2,1,0:T(8,128)(2,1)S(1)}, bf16[4,48,384]{2,1,0:T(8,128)(2,1)S(1)}, u32[]{:S(2)}, u32[]{:S(2)}) collective-permute-start(bf16[4,48,384]{2,1,0:T(8,128)(2,1)S(1)} %get-tuple-element.36), channel_id=1, source_target_pairs={{0,12},{4,0},{8,4},{12,8},{16,28},{20,16},{24,20},{28,24},{32,44},... | collective-permute-start | bytes 442376 | tf_op jit(solution)/shard_map/ppermute | solution.py:32
  46.5 3.0 %collective-permute-start.14 = (bf16[4,32,640]{2,1,0:T(8,128)(2,1)S(1)}, bf16[4,32,640]{2,1,0:T(8,128)(2,1)S(1)}, u32[]{:S(2)}, u32[]{:S(2)}) collective-permute-start(bf16[4,32,640]{2,1,0:T(8,128)(2,1)S(1)} %get-tuple-element.34), channel_id=1, source_target_pairs={{0,32},{4,36},{8,40},{12,44},{16,48},{20,52},{24,56},{28,60},{32,0... | collective-permute-start | bytes 491528 | tf_op jit(solution)/shard_map/ppermute | solution.py:32
  49.5 1.8 collective-permute-start.13
  51.7 1.3 collective-permute-start.15
  53.2 1.4 collective-permute-start.10
  54.5 1.9 collective-permute-done.13
  56.4 2.9 %collective-permute-start.9 = (bf16[4,4,48,384]{3,2,1,0:T(8,128)(2,1)S(1)}, bf16[4,4,48,384]{3,2,1,0:T(8,128)(2,1)S(1)}, u32[]{:S(2)}, u32[]{:S(2)}) collective-permute-start(bf16[4,4,48,384]{3,2,1,0:T(8,128)(2,1)S(1)} %pad_maximum_fusion.3.a0), channel_id=1, source_target_pairs={{0,48},{4,52},{8,56},{12,60},{16,0},{20,4},{24,8},{28,12},{32,16},... | collective-permute-start | bytes 1769480 | tf_op jit(solution)/shard_map/ppermute | solution.py:32
  60.5 2.6 %collective-permute-start.16 = (bf16[4,4,32,640]{3,2,1,0:T(8,128)(2,1)S(1)}, bf16[4,4,32,640]{3,2,1,0:T(8,128)(2,1)S(1)}, u32[]{:S(2)}, u32[]{:S(2)}) collective-permute-start(bf16[4,4,32,640]{3,2,1,0:T(8,128)(2,1)S(1)} %pad_maximum_fusion.2.b0), channel_id=1, source_target_pairs={{0,12},{4,0},{8,4},{12,8},{16,28},{20,16},{24,20},{28,24},{32,44},... | collective-permute-start | bytes 1966088 | tf_op jit(solution)/shard_map/ppermute | solution.py:32
  63.2 1.2 collective-permute-start.26
  64.4 17.1 %collective-permute-done.26 = bf16[4,64,512]{2,1,0:T(8,128)(2,1)S(1)} collective-permute-done((bf16[4,64,512]{2,1,0:T(8,128)(2,1)S(1)}, bf16[4,64,512]{2,1,0:T(8,128)(2,1)S(1)}, u32[]{:S(2)}, u32[]{:S(2)}) %collective-permute-start.26) | collective-permute-done | bytes 262176 | tf_op jit(solution)/shard_map/ppermute | solution.py:32
  81.5 4.0 %collective-permute-start.2 = (bf16[528,512]{1,0:T(8,128)(2,1)S(1)}, bf16[528,512]{1,0:T(8,128)(2,1)S(1)}, u32[]{:S(2)}, u32[]{:S(2)}) collective-permute-start(bf16[528,512]{1,0:T(8,128)(2,1)S(1)} %collective-permute-done.1.h2), channel_id=1, source_target_pairs={{0,1},{1,0},{2,3},{3,2},{4,5},{5,4},{6,7},{7,6},{8,9},{9,8},{10,11... | collective-permute-start | bytes 1622024 | tf_op jit(solution)/shard_map/ppermute | solution.py:36
  85.8 1.2 collective-permute-start.27
  87.2 2.6 %collective-permute-start.12 = (bf16[2,4,48,384]{3,2,1,0:T(8,128)(2,1)S(1)}, bf16[2,4,48,384]{3,2,1,0:T(8,128)(2,1)S(1)}, u32[]{:S(2)}, u32[]{:S(2)}) collective-permute-start(bf16[2,4,48,384]{3,2,1,0:T(8,128)(2,1)S(1)} %slice.58), channel_id=1, source_target_pairs={{0,48},{4,52},{8,56},{12,60},{16,0},{20,4},{24,8},{28,12},{32,16},... | collective-permute-start | bytes 884744 | tf_op jit(solution)/shard_map/ppermute | solution.py:32
  89.9 3.5 %collective-permute-done.25 = bf16[4,64,512]{2,1,0:T(8,128)(2,1)S(1)} collective-permute-done((bf16[4,64,512]{2,1,0:T(8,128)(2,1)S(1)}, bf16[4,64,512]{2,1,0:T(8,128)(2,1)S(1)}, u32[]{:S(2)}, u32[]{:S(2)}) %collective-permute-start.25) | collective-permute-done | bytes 262176 | tf_op jit(solution)/shard_map/ppermute | solution.py:32
  94.5 1.5 collective-permute-start.19
  98.0 6.6 %prep.1.normed = bf16[4,512,512]{2,1,0:T(8,128)(2,1)} custom-call(bf16[528,512]{1,0:T(8,128)(2,1)} %copy-done.7, bf16[528,512]{1,0:T(8,128)(2,1)} %copy-done.14, bf16[528,512]{1,0:T(8,128)(2,1)} %copy-done.13, bf16[528,512]{1,0:T(8,128)(2,1)} %copy-done.15), custom_call_target="tpu_custom_call" | custom-call | flops 1000000 | bytes 1024 | tf_op jit(solution)/shard_map/prep/pallas_call | solution.py:435
  104.6 1.1 collective-permute-start.29
  105.7 2.3 collective-permute-done.30
  108.0 3.4 %collective-permute-done.32 = bf16[4,64,512]{2,1,0:T(8,128)(2,1)S(1)} collective-permute-done((bf16[4,64,512]{2,1,0:T(8,128)(2,1)S(1)}, bf16[4,64,512]{2,1,0:T(8,128)(2,1)S(1)}, u32[]{:S(2)}, u32[]{:S(2)}) %collective-permute-start.32) | collective-permute-done | bytes 262176 | tf_op jit(solution)/shard_map/ppermute | solution.py:32
  111.6 9.0 %collective-permute-start.34 = (bf16[4,4,64,512]{3,2,1,0:T(8,128)(2,1)S(1)}, bf16[4,4,64,512]{3,2,1,0:T(8,128)(2,1)}, u32[]{:S(2)}, u32[]{:S(2)}) collective-permute-start(bf16[4,4,64,512]{3,2,1,0:T(8,128)(2,1)S(1)} %pad_maximum_fusion.1.b0), channel_id=1, source_target_pairs={{0,4},{4,8},{8,12},{12,0},{16,20},{20,24},{24,28},{28,16},{32,36},... | collective-permute-start | bytes 3145736 | tf_op jit(solution)/shard_map/ppermute | solution.py:32
  120.7 2.7 %collective-permute-start.33 = (bf16[4,4,64,512]{3,2,1,0:T(8,128)(2,1)S(1)}, bf16[4,4,64,512]{3,2,1,0:T(8,128)(2,1)}, u32[]{:S(2)}, u32[]{:S(2)}) collective-permute-start(bf16[4,4,64,512]{3,2,1,0:T(8,128)(2,1)S(1)} %pad_maximum_fusion.1.b0), channel_id=1, source_target_pairs={{0,12},{4,0},{8,4},{12,8},{16,28},{20,16},{24,20},{28,24},{32,44},... | collective-permute-start | bytes 3145736 | tf_op jit(solution)/shard_map/ppermute | solution.py:32
  124.6 11.3 %front.1 = (bf16[512,1024]{1,0:T(8,128)(2,1)}, f32[160,512]{1,0:T(8,128)}, bf16[128,1024]{1,0:T(8,128)(2,1)}, f32[3,40,1024]{2,1,0:T(8,128)}) custom-call(s32[2]{0:T(128)} %pad_add_fusion.where, s32[32]{0:T(128)} %pages.5, s32[32,128]{1,0:T(8,128)} %broadcast_in_dim.28.accepted, bf16[4,512,512]{2,1,0:T(8,128)(2,1)} %prep.1.normed, ...), custom_call_target="tpu_custom_call" | custom-call | flops 1000000 | bytes 1024 | tf_op jit(solution)/shard_map/front/pallas_call | solution.py:453
  135.9 3.9 %collective-permute-start.20 = (f32[160,512]{1,0:T(8,128)}, f32[160,512]{1,0:T(8,128)S(1)}, u32[]{:S(2)}, u32[]{:S(2)}) collective-permute-start(f32[160,512]{1,0:T(8,128)} %get-tuple-element.17), channel_id=1, source_target_pairs={{0,1},{1,0},{2,3},{3,2},{4,5},{5,4},{6,7},{7,6},{8,9},{9,8},{10,11... | collective-permute-start | bytes 983048 | tf_op jit(solution)/shard_map/ppermute | solution.py:36
  139.9 1.3 slice.63
  141.3 2.5 collective-permute-start.36
  144.9 1.1 slice.65
  146.0 2.7 %collective-permute-start.38 = (bf16[2,4,64,512]{3,2,1,0:T(8,128)(2,1)S(1)}, bf16[2,4,64,512]{3,2,1,0:T(8,128)(2,1)S(1)}, u32[]{:S(2)}, u32[]{:S(2)}) collective-permute-start(bf16[2,4,64,512]{3,2,1,0:T(8,128)(2,1)S(1)} %slice.65), channel_id=1, source_target_pairs={{0,12},{4,0},{8,4},{12,8},{16,28},{20,16},{24,20},{28,24},{32,44},... | collective-permute-start | bytes 1572872 | tf_op jit(solution)/shard_map/ppermute | solution.py:32
  148.9 6.2 %collective-permute-done.21.sums_b = f32[160,512]{1,0:T(8,128)S(1)} collective-permute-done((f32[160,512]{1,0:T(8,128)S(1)}, f32[160,512]{1,0:T(8,128)S(1)}, u32[]{:S(2)}, u32[]{:S(2)}) %collective-permute-start.21) | collective-permute-done | bytes 327712 | tf_op jit(solution)/shard_map/ppermute | solution.py:36
  155.9 19.9 %scan.1 = (f32[512,1024]{1,0:T(8,128)}, f32[8,512,128]{2,1,0:T(8,128)}) custom-call(s32[32]{0:T(128)} %pages.5, s32[32,128]{1,0:T(8,128)} %broadcast_in_dim.28.accepted, f32[160,512]{1,0:T(8,128)} %copy-done.12, f32[160,512]{1,0:T(8,128)} %copy-done.22, bf16[128,1024]{1,0:T(8,128)(2,1)} %get-tuple-element.23.dt, f32[1,1024]{1,0:T(1,128)} %bitcast.70, ...), custom_call_target="tpu_custom_call" | custom-call | flops 1000000 | bytes 1024 | tf_op jit(solution)/shard_map/scan/pallas_call | solution.py:484
  177.1 14.0 %gate.1 = (bf16[2,512,512]{2,1,0:T(8,128)(2,1)}, f32[2,512,512]{2,1,0:T(8,128)}) custom-call(s32[2]{0:T(128)} %pad_add_fusion.where, bf16[4,512,512]{2,1,0:T(8,128)(2,1)} %prep.1.normed, bf16[512,1024]{1,0:T(8,128)(2,1)} %get-tuple-element.16.inputs, f32[512,1024]{1,0:T(8,128)} %get-tuple-element.24.ys, f32[1,1024]{1,0:T(1,128)} %bitcast.69, ...), custom_call_target="tpu_custom_call" | custom-call | flops 1000000 | bytes 1024 | tf_op jit(solution)/shard_map/gate/pallas_call | solution.py:519
  191.1 5.3 %collective-permute-start.39 = (bf16[2,512,512]{2,1,0:T(8,128)(2,1)}, bf16[2,512,512]{2,1,0:T(8,128)(2,1)S(1)}, u32[]{:S(2)}, u32[]{:S(2)}) collective-permute-start(bf16[2,512,512]{2,1,0:T(8,128)(2,1)} %get-tuple-element.26), channel_id=1, source_target_pairs={{0,1},{1,0},{2,3},{3,2},{4,5},{5,4},{6,7},{7,6},{8,9},{9,8},{10,11... | collective-permute-start | bytes 3145736 | tf_op jit(solution)/shard_map/ppermute | solution.py:36
  196.3 2.5 collective-permute-done.39.near
  198.8 1.8 fusion
  200.7 13.1 %collective-permute-done.40.far = bf16[512,512]{1,0:T(8,128)(2,1)S(1)} collective-permute-done((bf16[512,512]{1,0:T(8,128)(2,1)S(1)}, bf16[512,512]{1,0:T(8,128)(2,1)S(1)}, u32[]{:S(2)}, u32[]{:S(2)}) %collective-permute-start.40) | collective-permute-done | bytes 524320 | tf_op jit(solution)/shard_map/ppermute | solution.py:36
  214.6 4.3 %join.1 = bf16[64,16,512]{2,1,0:T(8,128)(2,1)} custom-call(s32[32]{0:T(128)} %targets.3, f32[2,512,512]{2,1,0:T(8,128)} %get-tuple-element.25.keep, bf16[2,512,512]{2,1,0:T(8,128)(2,1)} %copy-done.6, bf16[512,512]{1,0:T(8,128)(2,1)} %copy-done.20, bf16[512,512]{1,0:T(8,128)(2,1)} %bitcast.46), custom_call_target="tpu_custom_call" | custom-call | flops 1000000 | bytes 1024 | tf_op jit(solution)/shard_map/join/pallas_call | solution.py:539
  218.9 6.4 %all-to-all-start = ((bf16[64,16,512]{2,1,0:T(8,128)(2,1)}), bf16[64,16,512]{2,1,0:T(8,128)(2,1)S(1)}, u32[]{:S(2)}, u32[]{:S(2)}) async-start(bf16[64,16,512]{2,1,0:T(8,128)(2,1)} %join.1), calls=%async_computation | async-start | bytes 2097152 | tf_op jit(solution)/shard_map/all_to_all | solution.py:549
  225.3 6.4 %settle.1 = f32[640,1024]{1,0:T(8,128)} custom-call(s32[32]{0:T(128)} %pages.5, f32[8,512,128]{2,1,0:T(8,128)} %get-tuple-element.27.kept, f32[640,1024]{1,0:T(8,128)} %bitcast.43), custom_call_target="tpu_custom_call" | custom-call | flops 1000000 | bytes 1024 | tf_op jit(solution)/shard_map/settle/pallas_call | solution.py:509
  231.8 22.9 %all-to-all-done.got = bf16[64,16,512]{2,1,0:T(8,128)(2,1)S(1)} async-done(((bf16[64,16,512]{2,1,0:T(8,128)(2,1)}), bf16[64,16,512]{2,1,0:T(8,128)(2,1)S(1)}, u32[]{:S(2)}, u32[]{:S(2)}) %all-to-all-start) | async-done | bytes 1048608 | tf_op jit(solution)/shard_map/all_to_all | solution.py:549
  255.6 2.4 unpack.1
  (125 shorter events, 17.7 us)
Async XLA Ops:
  2.3 15.4 %collective-permute-start.4 = (bf16[48,1024]{1,0:T(8,128)(2,1)S(1)}, bf16[48,1024]{1,0:T(8,128)(2,1)S(1)}, u32[]{:S(2)}, u32[]{:S(2)}) collective-permute-start(bf16[48,1024]{1,0:T(8,128)(2,1)S(1)} %get-tuple-element.38), channel_id=1, source_target_pairs={{0,128},{4,132},{8,136},{12,140},{16,144},{20,148},{24,152},{28,15... | collective-permute-start | bytes 294920 | tf_op jit(solution)/shard_map/ppermute | solution.py:32
  10.0 10.1 %collective-permute-start.3 = (bf16[48,1024]{1,0:T(8,128)(2,1)S(1)}, bf16[48,1024]{1,0:T(8,128)(2,1)S(1)}, u32[]{:S(2)}, u32[]{:S(2)}) collective-permute-start(bf16[48,1024]{1,0:T(8,128)(2,1)S(1)} %get-tuple-element.38), channel_id=1, source_target_pairs={{0,192},{4,196},{8,200},{12,204},{16,208},{20,212},{24,216},{28,22... | collective-permute-start | bytes 294920 | tf_op jit(solution)/shard_map/ppermute | solution.py:32
  10.0 10.1 %collective-permute-start.5 = (bf16[48,1024]{1,0:T(8,128)(2,1)S(1)}, bf16[48,1024]{1,0:T(8,128)(2,1)S(1)}, u32[]{:S(2)}, u32[]{:S(2)}) collective-permute-start(bf16[48,1024]{1,0:T(8,128)(2,1)S(1)} %get-tuple-element.38), channel_id=1, source_target_pairs={{0,64},{4,68},{8,72},{12,76},{16,80},{20,84},{24,88},{28,92},{32,9... | collective-permute-start | bytes 294920 | tf_op jit(solution)/shard_map/ppermute | solution.py:32
  14.2 39.0 %copy-start.7 = (bf16[528,512]{1,0:T(8,128)(2,1)}, bf16[528,512]{1,0:T(8,128)(2,1)S(1)}, u32[]{:S(2)}) copy-start(bf16[528,512]{1,0:T(8,128)(2,1)S(1)} %pad_maximum_fusion.4.h0) | copy-start | bytes 1622020
  14.2 46.3 %collective-permute-start.1 = (bf16[528,512]{1,0:T(8,128)(2,1)S(1)}, bf16[528,512]{1,0:T(8,128)(2,1)S(1)}, u32[]{:S(2)}, u32[]{:S(2)}) collective-permute-start(bf16[528,512]{1,0:T(8,128)(2,1)S(1)} %pad_maximum_fusion.4.h0), channel_id=1, source_target_pairs={{0,2},{1,3},{2,0},{3,1},{4,6},{5,7},{6,4},{7,5},{8,10},{9,11},{10,... | collective-permute-start | bytes 1622024 | tf_op jit(solution)/shard_map/ppermute | solution.py:36
  15.0 48.1 %collective-permute-start = (bf16[528,512]{1,0:T(8,128)(2,1)S(1)}, bf16[528,512]{1,0:T(8,128)(2,1)S(1)}, u32[]{:S(2)}, u32[]{:S(2)}) collective-permute-start(bf16[528,512]{1,0:T(8,128)(2,1)S(1)} %pad_maximum_fusion.4.h0), channel_id=1, source_target_pairs={{0,1},{1,0},{2,3},{3,2},{4,5},{5,4},{6,7},{7,6},{8,9},{9,8},{10,11... | collective-permute-start | bytes 1622024 | tf_op jit(solution)/shard_map/ppermute | solution.py:36
  20.2 15.4 %collective-permute-start.24 = (bf16[64,1024]{1,0:T(8,128)(2,1)S(1)}, bf16[64,1024]{1,0:T(8,128)(2,1)S(1)}, u32[]{:S(2)}, u32[]{:S(2)}) collective-permute-start(bf16[64,1024]{1,0:T(8,128)(2,1)S(1)} %pad_maximum_fusion.7), channel_id=1, source_target_pairs={{0,64},{4,68},{8,72},{12,76},{16,80},{20,84},{24,88},{28,92},{32,9... | collective-permute-start | bytes 393224 | tf_op jit(solution)/shard_map/ppermute | solution.py:32
  20.3 22.4 %collective-permute-start.23 = (bf16[64,1024]{1,0:T(8,128)(2,1)S(1)}, bf16[64,1024]{1,0:T(8,128)(2,1)S(1)}, u32[]{:S(2)}, u32[]{:S(2)}) collective-permute-start(bf16[64,1024]{1,0:T(8,128)(2,1)S(1)} %pad_maximum_fusion.7), channel_id=1, source_target_pairs={{0,128},{4,132},{8,136},{12,140},{16,144},{20,148},{24,152},{28,15... | collective-permute-start | bytes 393224 | tf_op jit(solution)/shard_map/ppermute | solution.py:32
  24.2 22.3 %collective-permute-start.22 = (bf16[64,1024]{1,0:T(8,128)(2,1)S(1)}, bf16[64,1024]{1,0:T(8,128)(2,1)S(1)}, u32[]{:S(2)}, u32[]{:S(2)}) collective-permute-start(bf16[64,1024]{1,0:T(8,128)(2,1)S(1)} %pad_maximum_fusion.7), channel_id=1, source_target_pairs={{0,192},{4,196},{8,200},{12,204},{16,208},{20,212},{24,216},{28,22... | collective-permute-start | bytes 393224 | tf_op jit(solution)/shard_map/ppermute | solution.py:32
  35.6 10.9 %collective-permute-start.7 = (bf16[4,48,384]{2,1,0:T(8,128)(2,1)S(1)}, bf16[4,48,384]{2,1,0:T(8,128)(2,1)S(1)}, u32[]{:S(2)}, u32[]{:S(2)}) collective-permute-start(bf16[4,48,384]{2,1,0:T(8,128)(2,1)S(1)} %get-tuple-element.36), channel_id=1, source_target_pairs={{0,8},{4,12},{8,0},{12,4},{16,24},{20,28},{24,16},{28,20},{32,40},... | collective-permute-start | bytes 442376 | tf_op jit(solution)/shard_map/ppermute | solution.py:32
  42.7 6.8 %collective-permute-start.6 = (bf16[4,48,384]{2,1,0:T(8,128)(2,1)S(1)}, bf16[4,48,384]{2,1,0:T(8,128)(2,1)S(1)}, u32[]{:S(2)}, u32[]{:S(2)}) collective-permute-start(bf16[4,48,384]{2,1,0:T(8,128)(2,1)S(1)} %get-tuple-element.36), channel_id=1, source_target_pairs={{0,12},{4,0},{8,4},{12,8},{16,28},{20,16},{24,20},{28,24},{32,44},... | collective-permute-start | bytes 442376 | tf_op jit(solution)/shard_map/ppermute | solution.py:32
  46.5 5.2 %collective-permute-start.8 = (bf16[4,48,384]{2,1,0:T(8,128)(2,1)S(1)}, bf16[4,48,384]{2,1,0:T(8,128)(2,1)S(1)}, u32[]{:S(2)}, u32[]{:S(2)}) collective-permute-start(bf16[4,48,384]{2,1,0:T(8,128)(2,1)S(1)} %get-tuple-element.36), channel_id=1, source_target_pairs={{0,4},{4,8},{8,12},{12,0},{16,20},{20,24},{24,28},{28,16},{32,36},... | collective-permute-start | bytes 442376 | tf_op jit(solution)/shard_map/ppermute | solution.py:32
  46.5 6.7 %collective-permute-start.14 = (bf16[4,32,640]{2,1,0:T(8,128)(2,1)S(1)}, bf16[4,32,640]{2,1,0:T(8,128)(2,1)S(1)}, u32[]{:S(2)}, u32[]{:S(2)}) collective-permute-start(bf16[4,32,640]{2,1,0:T(8,128)(2,1)S(1)} %get-tuple-element.34), channel_id=1, source_target_pairs={{0,32},{4,36},{8,40},{12,44},{16,48},{20,52},{24,56},{28,60},{32,0... | collective-permute-start | bytes 491528 | tf_op jit(solution)/shard_map/ppermute | solution.py:32
  49.5 6.9 %collective-permute-start.13 = (bf16[4,32,640]{2,1,0:T(8,128)(2,1)S(1)}, bf16[4,32,640]{2,1,0:T(8,128)(2,1)S(1)}, u32[]{:S(2)}, u32[]{:S(2)}) collective-permute-start(bf16[4,32,640]{2,1,0:T(8,128)(2,1)S(1)} %get-tuple-element.34), channel_id=1, source_target_pairs={{0,48},{4,52},{8,56},{12,60},{16,0},{20,4},{24,8},{28,12},{32,16},... | collective-permute-start | bytes 491528 | tf_op jit(solution)/shard_map/ppermute | solution.py:32
  51.7 7.7 %collective-permute-start.15 = (bf16[4,32,640]{2,1,0:T(8,128)(2,1)S(1)}, bf16[4,32,640]{2,1,0:T(8,128)(2,1)S(1)}, u32[]{:S(2)}, u32[]{:S(2)}) collective-permute-start(bf16[4,32,640]{2,1,0:T(8,128)(2,1)S(1)} %get-tuple-element.34), channel_id=1, source_target_pairs={{0,16},{4,20},{8,24},{12,28},{16,32},{20,36},{24,40},{28,44},{32,4... | collective-permute-start | bytes 491528 | tf_op jit(solution)/shard_map/ppermute | solution.py:32
  53.1 36.7 %copy-start.4 = (bf16[4,4,48,384]{3,2,1,0:T(8,128)(2,1)}, bf16[4,4,48,384]{3,2,1,0:T(8,128)(2,1)S(1)}, u32[]{:S(2)}) copy-start(bf16[4,4,48,384]{3,2,1,0:T(8,128)(2,1)S(1)} %pad_maximum_fusion.3.a0) | copy-start | bytes 1769476
  53.2 32.3 %collective-permute-start.10 = (bf16[4,4,48,384]{3,2,1,0:T(8,128)(2,1)S(1)}, bf16[4,4,48,384]{3,2,1,0:T(8,128)(2,1)S(1)}, u32[]{:S(2)}, u32[]{:S(2)}) collective-permute-start(bf16[4,4,48,384]{3,2,1,0:T(8,128)(2,1)S(1)} %pad_maximum_fusion.3.a0), channel_id=1, source_target_pairs={{0,16},{4,20},{8,24},{12,28},{16,32},{20,36},{24,40},{28,44},{32,4... | collective-permute-start | bytes 1769480 | tf_op jit(solution)/shard_map/ppermute | solution.py:32
  56.4 29.4 %collective-permute-start.9 = (bf16[4,4,48,384]{3,2,1,0:T(8,128)(2,1)S(1)}, bf16[4,4,48,384]{3,2,1,0:T(8,128)(2,1)S(1)}, u32[]{:S(2)}, u32[]{:S(2)}) collective-permute-start(bf16[4,4,48,384]{3,2,1,0:T(8,128)(2,1)S(1)} %pad_maximum_fusion.3.a0), channel_id=1, source_target_pairs={{0,48},{4,52},{8,56},{12,60},{16,0},{20,4},{24,8},{28,12},{32,16},... | collective-permute-start | bytes 1769480 | tf_op jit(solution)/shard_map/ppermute | solution.py:32
  59.4 38.5 %copy-start.3 = (bf16[4,4,32,640]{3,2,1,0:T(8,128)(2,1)}, bf16[4,4,32,640]{3,2,1,0:T(8,128)(2,1)S(1)}, u32[]{:S(2)}) copy-start(bf16[4,4,32,640]{3,2,1,0:T(8,128)(2,1)S(1)} %pad_maximum_fusion.2.b0) | copy-start | bytes 1966084
  59.4 27.6 %collective-permute-start.17 = (bf16[4,4,32,640]{3,2,1,0:T(8,128)(2,1)S(1)}, bf16[4,4,32,640]{3,2,1,0:T(8,128)(2,1)S(1)}, u32[]{:S(2)}, u32[]{:S(2)}) collective-permute-start(bf16[4,4,32,640]{3,2,1,0:T(8,128)(2,1)S(1)} %pad_maximum_fusion.2.b0), channel_id=1, source_target_pairs={{0,4},{4,8},{8,12},{12,0},{16,20},{20,24},{24,28},{28,16},{32,36},... | collective-permute-start | bytes 1966088 | tf_op jit(solution)/shard_map/ppermute | solution.py:32
  60.5 37.4 %copy-start.13 = (bf16[528,512]{1,0:T(8,128)(2,1)}, bf16[528,512]{1,0:T(8,128)(2,1)S(1)}, u32[]{:S(2)}) copy-start(bf16[528,512]{1,0:T(8,128)(2,1)S(1)} %collective-permute-done.1.h2) | copy-start | bytes 1622020
  60.5 26.6 %collective-permute-start.16 = (bf16[4,4,32,640]{3,2,1,0:T(8,128)(2,1)S(1)}, bf16[4,4,32,640]{3,2,1,0:T(8,128)(2,1)S(1)}, u32[]{:S(2)}, u32[]{:S(2)}) collective-permute-start(bf16[4,4,32,640]{3,2,1,0:T(8,128)(2,1)S(1)} %pad_maximum_fusion.2.b0), channel_id=1, source_target_pairs={{0,12},{4,0},{8,4},{12,8},{16,28},{20,16},{24,20},{28,24},{32,44},... | collective-permute-start | bytes 1966088 | tf_op jit(solution)/shard_map/ppermute | solution.py:32
  63.1 34.8 %copy-start.14 = (bf16[528,512]{1,0:T(8,128)(2,1)}, bf16[528,512]{1,0:T(8,128)(2,1)S(1)}, u32[]{:S(2)}) copy-start(bf16[528,512]{1,0:T(8,128)(2,1)S(1)} %collective-permute-done.h1) | copy-start | bytes 1622020
  63.2 18.3 %collective-permute-start.26 = (bf16[4,64,512]{2,1,0:T(8,128)(2,1)S(1)}, bf16[4,64,512]{2,1,0:T(8,128)(2,1)S(1)}, u32[]{:S(2)}, u32[]{:S(2)}) collective-permute-start(bf16[4,64,512]{2,1,0:T(8,128)(2,1)S(1)} %get-tuple-element.32), channel_id=1, source_target_pairs={{0,8},{4,12},{8,0},{12,4},{16,24},{20,28},{24,16},{28,20},{32,40},... | collective-permute-start | bytes 786440 | tf_op jit(solution)/shard_map/ppermute | solution.py:32
  81.5 14.5 %collective-permute-start.2 = (bf16[528,512]{1,0:T(8,128)(2,1)S(1)}, bf16[528,512]{1,0:T(8,128)(2,1)S(1)}, u32[]{:S(2)}, u32[]{:S(2)}) collective-permute-start(bf16[528,512]{1,0:T(8,128)(2,1)S(1)} %collective-permute-done.1.h2), channel_id=1, source_target_pairs={{0,1},{1,0},{2,3},{3,2},{4,5},{5,4},{6,7},{7,6},{8,9},{9,8},{10,11... | collective-permute-start | bytes 1622024 | tf_op jit(solution)/shard_map/ppermute | solution.py:36
  85.5 7.9 %collective-permute-start.25 = (bf16[4,64,512]{2,1,0:T(8,128)(2,1)S(1)}, bf16[4,64,512]{2,1,0:T(8,128)(2,1)S(1)}, u32[]{:S(2)}, u32[]{:S(2)}) collective-permute-start(bf16[4,64,512]{2,1,0:T(8,128)(2,1)S(1)} %get-tuple-element.32), channel_id=1, source_target_pairs={{0,12},{4,0},{8,4},{12,8},{16,28},{20,16},{24,20},{28,24},{32,44},... | collective-permute-start | bytes 786440 | tf_op jit(solution)/shard_map/ppermute | solution.py:32
  85.8 8.8 %collective-permute-start.27 = (bf16[4,64,512]{2,1,0:T(8,128)(2,1)S(1)}, bf16[4,64,512]{2,1,0:T(8,128)(2,1)S(1)}, u32[]{:S(2)}, u32[]{:S(2)}) collective-permute-start(bf16[4,64,512]{2,1,0:T(8,128)(2,1)S(1)} %get-tuple-element.32), channel_id=1, source_target_pairs={{0,4},{4,8},{8,12},{12,0},{16,20},{20,24},{24,28},{28,16},{32,36},... | collective-permute-start | bytes 786440 | tf_op jit(solution)/shard_map/ppermute | solution.py:32
  87.0 9.2 %collective-permute-start.11 = (bf16[2,4,48,384]{3,2,1,0:T(8,128)(2,1)S(1)}, bf16[2,4,48,384]{3,2,1,0:T(8,128)(2,1)S(1)}, u32[]{:S(2)}, u32[]{:S(2)}) collective-permute-start(bf16[2,4,48,384]{3,2,1,0:T(8,128)(2,1)S(1)} %slice.57), channel_id=1, source_target_pairs={{0,16},{4,20},{8,24},{12,28},{16,32},{20,36},{24,40},{28,44},{32,4... | collective-permute-start | bytes 884744 | tf_op jit(solution)/shard_map/ppermute | solution.py:32
  87.2 9.6 %collective-permute-start.12 = (bf16[2,4,48,384]{3,2,1,0:T(8,128)(2,1)S(1)}, bf16[2,4,48,384]{3,2,1,0:T(8,128)(2,1)S(1)}, u32[]{:S(2)}, u32[]{:S(2)}) collective-permute-start(bf16[2,4,48,384]{3,2,1,0:T(8,128)(2,1)S(1)} %slice.58), channel_id=1, source_target_pairs={{0,48},{4,52},{8,56},{12,60},{16,0},{20,4},{24,8},{28,12},{32,16},... | collective-permute-start | bytes 884744 | tf_op jit(solution)/shard_map/ppermute | solution.py:32
  93.3 11.2 %collective-permute-start.18 = (bf16[2,4,32,640]{3,2,1,0:T(8,128)(2,1)S(1)}, bf16[2,4,32,640]{3,2,1,0:T(8,128)(2,1)S(1)}, u32[]{:S(2)}, u32[]{:S(2)}) collective-permute-start(bf16[2,4,32,640]{3,2,1,0:T(8,128)(2,1)S(1)} %slice.60), channel_id=1, source_target_pairs={{0,4},{4,8},{8,12},{12,0},{16,20},{20,24},{24,28},{28,16},{32,36},... | collective-permute-start | bytes 983048 | tf_op jit(solution)/shard_map/ppermute | solution.py:32
  94.5 10.0 %collective-permute-start.19 = (bf16[2,4,32,640]{3,2,1,0:T(8,128)(2,1)S(1)}, bf16[2,4,32,640]{3,2,1,0:T(8,128)(2,1)}, u32[]{:S(2)}, u32[]{:S(2)}) collective-permute-start(bf16[2,4,32,640]{3,2,1,0:T(8,128)(2,1)S(1)} %slice.61), channel_id=1, source_target_pairs={{0,12},{4,0},{8,4},{12,8},{16,28},{20,16},{24,20},{28,24},{32,44},... | collective-permute-start | bytes 983048 | tf_op jit(solution)/shard_map/ppermute | solution.py:32
  96.0 9.7 %collective-permute-start.31 = (bf16[4,64,512]{2,1,0:T(8,128)(2,1)S(1)}, bf16[4,64,512]{2,1,0:T(8,128)(2,1)S(1)}, u32[]{:S(2)}, u32[]{:S(2)}) collective-permute-start(bf16[4,64,512]{2,1,0:T(8,128)(2,1)S(1)} %get-tuple-element.31), channel_id=1, source_target_pairs={{0,32},{4,36},{8,40},{12,44},{16,48},{20,52},{24,56},{28,60},{32,0... | collective-permute-start | bytes 786440 | tf_op jit(solution)/shard_map/ppermute | solution.py:32
  96.3 11.7 %collective-permute-start.30 = (bf16[4,64,512]{2,1,0:T(8,128)(2,1)S(1)}, bf16[4,64,512]{2,1,0:T(8,128)(2,1)S(1)}, u32[]{:S(2)}, u32[]{:S(2)}) collective-permute-start(bf16[4,64,512]{2,1,0:T(8,128)(2,1)S(1)} %get-tuple-element.31), channel_id=1, source_target_pairs={{0,48},{4,52},{8,56},{12,60},{16,0},{20,4},{24,8},{28,12},{32,16},... | collective-permute-start | bytes 786440 | tf_op jit(solution)/shard_map/ppermute | solution.py:32
  96.7 14.6 %collective-permute-start.32 = (bf16[4,64,512]{2,1,0:T(8,128)(2,1)S(1)}, bf16[4,64,512]{2,1,0:T(8,128)(2,1)S(1)}, u32[]{:S(2)}, u32[]{:S(2)}) collective-permute-start(bf16[4,64,512]{2,1,0:T(8,128)(2,1)S(1)} %get-tuple-element.31), channel_id=1, source_target_pairs={{0,16},{4,20},{8,24},{12,28},{16,32},{20,36},{24,40},{28,44},{32,4... | collective-permute-start | bytes 786440 | tf_op jit(solution)/shard_map/ppermute | solution.py:32
  104.6 35.2 %collective-permute-start.29 = (bf16[4,4,64,512]{3,2,1,0:T(8,128)(2,1)S(1)}, bf16[4,4,64,512]{3,2,1,0:T(8,128)(2,1)S(1)}, u32[]{:S(2)}, u32[]{:S(2)}) collective-permute-start(bf16[4,4,64,512]{3,2,1,0:T(8,128)(2,1)S(1)} %pad_maximum_fusion.a0), channel_id=1, source_target_pairs={{0,16},{4,20},{8,24},{12,28},{16,32},{20,36},{24,40},{28,44},{32,4... | collective-permute-start | bytes 3145736 | tf_op jit(solution)/shard_map/ppermute | solution.py:32
  111.5 24.4 %copy-start.1 = (bf16[4,4,64,512]{3,2,1,0:T(8,128)(2,1)}, bf16[4,4,64,512]{3,2,1,0:T(8,128)(2,1)S(1)}, u32[]{:S(2)}) copy-start(bf16[4,4,64,512]{3,2,1,0:T(8,128)(2,1)S(1)} %pad_maximum_fusion.1.b0) | copy-start | bytes 3145732
  111.5 28.4 %collective-permute-start.28 = (bf16[4,4,64,512]{3,2,1,0:T(8,128)(2,1)S(1)}, bf16[4,4,64,512]{3,2,1,0:T(8,128)(2,1)}, u32[]{:S(2)}, u32[]{:S(2)}) collective-permute-start(bf16[4,4,64,512]{3,2,1,0:T(8,128)(2,1)S(1)} %pad_maximum_fusion.a0), channel_id=1, source_target_pairs={{0,48},{4,52},{8,56},{12,60},{16,0},{20,4},{24,8},{28,12},{32,16},... | collective-permute-start | bytes 3145736 | tf_op jit(solution)/shard_map/ppermute | solution.py:32
  111.6 32.1 %collective-permute-start.34 = (bf16[4,4,64,512]{3,2,1,0:T(8,128)(2,1)S(1)}, bf16[4,4,64,512]{3,2,1,0:T(8,128)(2,1)}, u32[]{:S(2)}, u32[]{:S(2)}) collective-permute-start(bf16[4,4,64,512]{3,2,1,0:T(8,128)(2,1)S(1)} %pad_maximum_fusion.1.b0), channel_id=1, source_target_pairs={{0,4},{4,8},{8,12},{12,0},{16,20},{20,24},{24,28},{28,16},{32,36},... | collective-permute-start | bytes 3145736 | tf_op jit(solution)/shard_map/ppermute | solution.py:32
  120.7 24.3 %collective-permute-start.33 = (bf16[4,4,64,512]{3,2,1,0:T(8,128)(2,1)S(1)}, bf16[4,4,64,512]{3,2,1,0:T(8,128)(2,1)}, u32[]{:S(2)}, u32[]{:S(2)}) collective-permute-start(bf16[4,4,64,512]{3,2,1,0:T(8,128)(2,1)S(1)} %pad_maximum_fusion.1.b0), channel_id=1, source_target_pairs={{0,12},{4,0},{8,4},{12,8},{16,28},{20,16},{24,20},{28,24},{32,44},... | collective-permute-start | bytes 3145736 | tf_op jit(solution)/shard_map/ppermute | solution.py:32
  135.9 12.8 %collective-permute-start.20 = (f32[160,512]{1,0:T(8,128)}, f32[160,512]{1,0:T(8,128)S(1)}, u32[]{:S(2)}, u32[]{:S(2)}) collective-permute-start(f32[160,512]{1,0:T(8,128)} %get-tuple-element.17), channel_id=1, source_target_pairs={{0,1},{1,0},{2,3},{3,2},{4,5},{5,4},{6,7},{7,6},{8,9},{9,8},{10,11... | collective-permute-start | bytes 983048 | tf_op jit(solution)/shard_map/ppermute | solution.py:36
  139.8 35.9 %collective-permute-start.35 = (bf16[2,4,64,512]{3,2,1,0:T(8,128)(2,1)S(1)}, bf16[2,4,64,512]{3,2,1,0:T(8,128)(2,1)S(1)}, u32[]{:S(2)}, u32[]{:S(2)}) collective-permute-start(bf16[2,4,64,512]{3,2,1,0:T(8,128)(2,1)S(1)} %slice.62), channel_id=1, source_target_pairs={{0,16},{4,20},{8,24},{12,28},{16,32},{20,36},{24,40},{28,44},{32,4... | collective-permute-start | bytes 1572872 | tf_op jit(solution)/shard_map/ppermute | solution.py:32
  141.3 34.5 %collective-permute-start.36 = (bf16[2,4,64,512]{3,2,1,0:T(8,128)(2,1)S(1)}, bf16[2,4,64,512]{3,2,1,0:T(8,128)(2,1)S(1)}, u32[]{:S(2)}, u32[]{:S(2)}) collective-permute-start(bf16[2,4,64,512]{3,2,1,0:T(8,128)(2,1)S(1)} %slice.63), channel_id=1, source_target_pairs={{0,48},{4,52},{8,56},{12,60},{16,0},{20,4},{24,8},{28,12},{32,16},... | collective-permute-start | bytes 1572872 | tf_op jit(solution)/shard_map/ppermute | solution.py:32
  144.8 31.0 %collective-permute-start.37 = (bf16[2,4,64,512]{3,2,1,0:T(8,128)(2,1)S(1)}, bf16[2,4,64,512]{3,2,1,0:T(8,128)(2,1)S(1)}, u32[]{:S(2)}, u32[]{:S(2)}) collective-permute-start(bf16[2,4,64,512]{3,2,1,0:T(8,128)(2,1)S(1)} %slice.64), channel_id=1, source_target_pairs={{0,4},{4,8},{8,12},{12,0},{16,20},{20,24},{24,28},{28,16},{32,36},... | collective-permute-start | bytes 1572872 | tf_op jit(solution)/shard_map/ppermute | solution.py:32
  146.0 29.8 %collective-permute-start.38 = (bf16[2,4,64,512]{3,2,1,0:T(8,128)(2,1)S(1)}, bf16[2,4,64,512]{3,2,1,0:T(8,128)(2,1)S(1)}, u32[]{:S(2)}, u32[]{:S(2)}) collective-permute-start(bf16[2,4,64,512]{3,2,1,0:T(8,128)(2,1)S(1)} %slice.65), channel_id=1, source_target_pairs={{0,12},{4,0},{8,4},{12,8},{16,28},{20,16},{24,20},{28,24},{32,44},... | collective-permute-start | bytes 1572872 | tf_op jit(solution)/shard_map/ppermute | solution.py:32
  148.8 6.3 %collective-permute-start.21 = (f32[160,512]{1,0:T(8,128)S(1)}, f32[160,512]{1,0:T(8,128)S(1)}, u32[]{:S(2)}, u32[]{:S(2)}) collective-permute-start(f32[160,512]{1,0:T(8,128)S(1)} %add.7.sums_a), channel_id=1, source_target_pairs={{0,2},{1,3},{2,0},{3,1},{4,6},{5,7},{6,4},{7,5},{8,10},{9,11},{10,... | collective-permute-start | bytes 983048 | tf_op jit(solution)/shard_map/ppermute | solution.py:36
  191.1 7.8 %collective-permute-start.39 = (bf16[2,512,512]{2,1,0:T(8,128)(2,1)}, bf16[2,512,512]{2,1,0:T(8,128)(2,1)S(1)}, u32[]{:S(2)}, u32[]{:S(2)}) collective-permute-start(bf16[2,512,512]{2,1,0:T(8,128)(2,1)} %get-tuple-element.26), channel_id=1, source_target_pairs={{0,1},{1,0},{2,3},{3,2},{4,5},{5,4},{6,7},{7,6},{8,9},{9,8},{10,11... | collective-permute-start | bytes 3145736 | tf_op jit(solution)/shard_map/ppermute | solution.py:36
  200.6 13.2 %collective-permute-start.40 = (bf16[512,512]{1,0:T(8,128)(2,1)S(1)}, bf16[512,512]{1,0:T(8,128)(2,1)S(1)}, u32[]{:S(2)}, u32[]{:S(2)}) collective-permute-start(bf16[512,512]{1,0:T(8,128)(2,1)S(1)} %fusion), channel_id=1, source_target_pairs={{0,2},{1,3},{2,0},{3,1},{4,6},{5,7},{6,4},{7,5},{8,10},{9,11},{10,... | collective-permute-start | bytes 1572872 | tf_op jit(solution)/shard_map/ppermute | solution.py:36
  218.9 35.7 %all-to-all-start = ((bf16[64,16,512]{2,1,0:T(8,128)(2,1)}), bf16[64,16,512]{2,1,0:T(8,128)(2,1)S(1)}, u32[]{:S(2)}, u32[]{:S(2)}) async-start(bf16[64,16,512]{2,1,0:T(8,128)(2,1)} %join.1), calls=%async_computation | async-start | bytes 2097152 | tf_op jit(solution)/shard_map/all_to_all | solution.py:549
  (21 other events, 152.9 us)

commit v4 on v3

--- a/solution.py
+++ b/solution.py
@@ -50,30 +50,50 @@
     return block, above, hop(below[:half], axis, 1), hop(above[half:], axis, -1), below
 
 
+def send_direct(block, axis):
+    return block, hop(block, axis, -1), hop(block, axis, 2), hop(block, axis, 1)
+
+
+def exchange_z(block):
+    groups = [[z * SIDE * SIDE + i for z in range(SIDE)] for i in range(SIDE * SIDE)]
+    many = jnp.broadcast_to(block[None], (SIDE, *block.shape))
+    return lax.all_to_all(many, "dp", 0, 0, tiled=True, axis_index_groups=groups)
+
+
 def direct(block, axis):
-    return jnp.stack([block, hop(block, axis, -1), hop(block, axis, 2), hop(block, axis, 1)])
-
-
-def start_pieces(pieces, place, middle_first, body):
+    return jnp.stack(send_direct(block, axis))
+
+
+def start_pieces(pieces, place, middle_first, body, ordered=False):
     z, y, x = place
     own, above, low, high, below = pieces
 
-    def one(k, _):
-        dz = (z + k) & 3
-        for i in range(SIDE):
-            for f in range(SIDE):
-                if f == 2:
-                    ref, at = (low, i) if i < 2 else (high, i - 2)
-                else:
-                    ref, at = {0: own, 1: above, 3: below}[f], i
-                if middle_first:
-                    dx, dy = (x + i) & 3, (y + f) & 3
-                else:
-                    dy, dx = (y + i) & 3, (x + f) & 3
-                body(ref.at[at, k], (dz * SIDE + dy) * SIDE + dx)
-        return 0
-
-    lax.fori_loop(0, SIDE, one, 0)
+    def one(n, _):
+        i, k = n >> 2, n & 3
+        dz = k if ordered else (z + k) & 3
+
+        def piece(f, ref, at):
+            if middle_first:
+                dx, dy = (x + i) & 3, (y + f) & 3
+            else:
+                dy, dx = (y + i) & 3, (x + f) & 3
+            body(ref.at[at, k], (dz * SIDE + dy) * SIDE + dx)
+
+        piece(0, own, i)
+        piece(1, above, i)
+        piece(3, below, i)
+
+        @pl.when(i < 2)
+        def _():
+            piece(2, low, i)
+
+        @pl.when(i >= 2)
+        def _():
+            piece(2, high, i - 2)
+
+        return 0
+
+    lax.fori_loop(0, SIDE * SIDE, one, 0)
 
 
 def place_of(where):
@@ -328,8 +348,8 @@
             src.at[pl.ds(32, 32), :], outer.at[pl.ds(d * 32, 32), pl.ds(column, half)], sems.at[1]
         ).start()
 
-    start_pieces(a, place_of(where), True, lambda src, d: take(src, d, 0))
-    start_pieces(b, place_of(where), False, lambda src, d: take(src, d, half))
+    start_pieces(a, place_of(where), True, lambda src, d: take(src, d, 0), True)
+    start_pieces(b, place_of(where), False, lambda src, d: take(src, d, half), True)
     pltpu.make_async_copy(weight, weight, sems.at[0]).wait()
 
     def gate(n, _):
@@ -429,6 +449,7 @@
 
     flat = hidden.reshape(tokens, part)
     sent = jnp.concatenate([flat, jnp.broadcast_to(norm_gain[None], (16, part))], axis=0)
+    sent = after(sent, first)
     near = across(sent, 1)
     far = across(sent, 2)
     both = across(far, 1)
@@ -441,13 +462,12 @@
         compiler_params=params(),
         cost_estimate=pl.CostEstimate(flops=1_000_000, bytes_accessed=1 << 10, transcendentals=0),
         name="prep",
-    )(sent, near, far, both)
-
-    pair = after(jnp.concatenate([in_z, out_proj.T], axis=0), first)
-    stacked = after(direct(pair, 0), middle_a, middle_b, near, far)
-    plane_a = after(direct(stacked[..., : width // 2], 2), first_a, first_b, normed)
-    plane_b = after(direct(stacked[..., width // 2 :], 1), first_a, first_b, normed)
-    around_a, around_b = ring_one(plane_a, 1), ring_one(plane_b, 2)
+    )(sent, *after((near, far, both), sides_a, sides_b))
+
+    pair = after(jnp.concatenate([in_z, out_proj.T], axis=0), middle_a, middle_b)
+    stacked = after(exchange_z(pair), sides_a, sides_b, normed)
+    plane_a = send_direct(stacked[..., : width // 2], 2)
+    plane_b = send_direct(stacked[..., width // 2 :], 1)
 
     wide_accepted = jnp.broadcast_to(accepted[:, None], (count, 128))
     inputs, sums, dt, new_conv = pl.pallas_call(
@@ -471,16 +491,17 @@
             pltpu.SemaphoreType.DMA((3,)),
         ],
         compiler_params=params(),
-        cost_estimate=pl.CostEstimate(flops=1_000_000, bytes_accessed=1 << 10, transcendentals=0),
+        cost_estimate=pl.CostEstimate(flops=12_000_000_000, bytes_accessed=1 << 10, transcendentals=0),
         name="front",
     )(
         where, page_table, wide_accepted, normed, *first_a, *first_b,
         conv_weight, conv_bias[None], conv_pool.transpose(1, 0, 2),
     )
 
+    plane_a, plane_b = (jnp.stack(p) for p in after((plane_a, plane_b), sums))
+    around_a, around_b = ring_one(plane_a, 1), ring_one(plane_b, 2)
     sums = sums + across(sums, 1)
-    other = after(across(sums, 2), around_a, around_b)
-    second = (*ring_two(plane_a, 1, around_a), *ring_two(plane_b, 2, around_b))
+    other = across(sums, 2)
     ys, kept = pl.pallas_call(
         scan_kernel,
         out_shape=(
@@ -506,6 +527,8 @@
         state_pool.reshape(slots * states, width),
     )
 
+    around_a, around_b = after((around_a, around_b), ys)
+    second = (*ring_two(plane_a, 1, around_a), *ring_two(plane_b, 2, around_b))
     new_state = pl.pallas_call(
         settle_kernel,
         out_shape=jax.ShapeDtypeStruct((slots * states, width), F32),

time: 263 us -> 253 us (0.962)
  the two profiles are of different devices: /device:TPU:1 before, /device:TPU:2 now
where the time goes in v4:
time: 253 us; the launch traced here: 250 us
  waiting for transfers between devices  90.4 us (36%)
  starting transfers between devices  79.6 us (31%)
  Pallas kernels  64.5 us (25%)
  local copies, waits for them, and re-layouts  9.26 us (4%)
  other arithmetic  4.94 us (2%)
    ppermute x31, starting transfers between devices, hop(): return lax.ppermute(value, 'dp', shift_pairs(axis, step))  53 us
    ppermute x31, waiting for transfers between devices, hop(): return lax.ppermute(value, 'dp', shift_pairs(axis, step))  44.5 us
    ppermute x7, waiting for transfers between devices, across(): return lax.ppermute(value, 'mp', [(m, m ^ flip) for m in range(4)])  25 us
    all_to_all x1, waiting for transfers between devices, on_device(): lax.all_to_all(packed, 'dp', split_axis=0, concat_axis=0, tiled=True)  20.8 us
    pallas_call x1, Pallas kernels, on_device(): pl.pallas_call(scan_kernel, out_shape=(jax.ShapeDtypeStruct((tokens, widt...  19.9 us
    pallas_call x1, Pallas kernels, on_device(): pl.pallas_call(gate_kernel, out_shape=(jax.ShapeDtypeStruct((2, tokens, p...  14 us
    all_to_all x1, starting transfers between devices, on_device(): lax.all_to_all(packed, 'dp', split_axis=0, concat_axis=0, tiled=True)  11.9 us
    pallas_call x1, Pallas kernels, on_device(): pl.pallas_call(front_kernel, out_shape=(jax.ShapeDtypeStruct((tokens, wid...  11.3 us
  transfers between devices with their start and end apart: 40, of which 16 were waited for; matrix products, arithmetic and copies ran while one was open for 3% of the time, Pallas kernels for 18%

profile of v4, /device:TPU:2, one launch (start us, length us, event | category | flops | bytes accessed | tf_op | source)
XLA Modules:
  0.0 249.8 jit_solution(17819639788110754707)
XLA Ops:
  2.3 6.3 %collective-permute-start = (bf16[48,1024]{1,0:T(8,128)(2,1)S(1)}, bf16[48,1024]{1,0:T(8,128)(2,1)S(1)}, u32[]{:S(2)}, u32[]{:S(2)}) collective-permute-start(bf16[48,1024]{1,0:T(8,128)(2,1)S(1)} %get-tuple-element.62), channel_id=1, source_target_pairs={{0,192},{4,196},{8,200},{12,204},{16,208},{20,212},{24,216},{28,22... | collective-permute-start | bytes 294920 | tf_op jit(solution)/shard_map/ppermute | solution.py:32
  9.7 2.8 %collective-permute-start.2 = (bf16[48,1024]{1,0:T(8,128)(2,1)S(1)}, bf16[48,1024]{1,0:T(8,128)(2,1)S(1)}, u32[]{:S(2)}, u32[]{:S(2)}) collective-permute-start(bf16[48,1024]{1,0:T(8,128)(2,1)S(1)} %get-tuple-element.62), channel_id=1, source_target_pairs={{0,64},{4,68},{8,72},{12,76},{16,80},{20,84},{24,88},{28,92},{32,9... | collective-permute-start | bytes 294920 | tf_op jit(solution)/shard_map/ppermute | solution.py:32
  12.5 4.6 %collective-permute-done = bf16[48,1024]{1,0:T(8,128)(2,1)S(1)} collective-permute-done((bf16[48,1024]{1,0:T(8,128)(2,1)S(1)}, bf16[48,1024]{1,0:T(8,128)(2,1)S(1)}, u32[]{:S(2)}, u32[]{:S(2)}) %collective-permute-start) | collective-permute-done | bytes 98336 | tf_op jit(solution)/shard_map/ppermute | solution.py:32
  17.1 3.2 %collective-permute-done.1 = bf16[48,1024]{1,0:T(8,128)(2,1)S(1)} collective-permute-done((bf16[48,1024]{1,0:T(8,128)(2,1)S(1)}, bf16[48,1024]{1,0:T(8,128)(2,1)S(1)}, u32[]{:S(2)}, u32[]{:S(2)}) %collective-permute-start.1) | collective-permute-done | bytes 98336 | tf_op jit(solution)/shard_map/ppermute | solution.py:32
  20.4 1.6 collective-permute-start.8
  22.5 2.1 collective-permute-start.7
  25.3 1.1 pad_maximum_fusion.4.h0
  27.4 1.9 collective-permute-done.7
  29.4 1.7 collective-permute-start.10
  31.1 1.7 collective-permute-start.11
  32.8 2.0 collective-permute-start.12
  36.5 11.9 %collective-permute-done.12 = bf16[4,32,640]{2,1,0:T(8,128)(2,1)S(1)} collective-permute-done((bf16[4,32,640]{2,1,0:T(8,128)(2,1)S(1)}, bf16[4,32,640]{2,1,0:T(8,128)(2,1)S(1)}, u32[]{:S(2)}, u32[]{:S(2)}) %collective-permute-start.12) | collective-permute-done | bytes 163872 | tf_op jit(solution)/shard_map/ppermute | solution.py:32
  49.9 7.1 %all-to-all-start = ((bf16[4,64,1024]{2,1,0:T(8,128)(2,1)}), bf16[4,64,1024]{2,1,0:T(8,128)(2,1)S(1)}, u32[]{:S(2)}, u32[]{:S(2)}) async-start(bf16[4,64,1024]{2,1,0:T(8,128)(2,1)} %broadcast_in_dim.40), calls=%async_computation | async-start | bytes 1048576 | tf_op jit(solution)/shard_map/all_to_all | solution.py:60
  57.0 2.2 collective-permute-start.15
  59.1 1.8 collective-permute-start.9
  61.5 1.0 slice.58
  62.5 7.2 %collective-permute-done.9.a1 = bf16[4,4,48,384]{3,2,1,0:T(8,128)(2,1)S(1)} collective-permute-done((bf16[4,4,48,384]{3,2,1,0:T(8,128)(2,1)S(1)}, bf16[4,4,48,384]{3,2,1,0:T(8,128)(2,1)S(1)}, u32[]{:S(2)}, u32[]{:S(2)}) %collective-permute-start.9) | collective-permute-done | bytes 589856 | tf_op jit(solution)/shard_map/ppermute | solution.py:32
  69.7 1.0 collective-permute-start.16
  71.5 2.7 %collective-permute-start.17 = (bf16[2,4,48,384]{3,2,1,0:T(8,128)(2,1)}, bf16[2,4,48,384]{3,2,1,0:T(8,128)(2,1)}, u32[]{:S(2)}, u32[]{:S(2)}) collective-permute-start(bf16[2,4,48,384]{3,2,1,0:T(8,128)(2,1)} %slice.59), channel_id=1, source_target_pairs={{0,48},{4,52},{8,56},{12,60},{16,0},{20,4},{24,8},{28,12},{32,16},... | collective-permute-start | bytes 884744 | tf_op jit(solution)/shard_map/ppermute | solution.py:32
  74.3 2.1 collective-permute-start.18
  76.4 1.2 collective-permute-start.19
  78.5 6.2 %prep.1.normed = bf16[4,512,512]{2,1,0:T(8,128)(2,1)} custom-call(bf16[528,512]{1,0:T(8,128)(2,1)} %copy-done.8, bf16[528,512]{1,0:T(8,128)(2,1)} %copy-done.13, bf16[528,512]{1,0:T(8,128)(2,1)} %copy-done.12, bf16[528,512]{1,0:T(8,128)(2,1)} %copy-done.14), custom_call_target="tpu_custom_call" | custom-call | flops 1000000 | bytes 1024 | tf_op jit(solution)/shard_map/prep/pallas_call | solution.py:456
  84.8 3.3 %collective-permute-start.22 = (bf16[4,64,512]{2,1,0:T(8,128)(2,1)S(1)}, bf16[4,64,512]{2,1,0:T(8,128)(2,1)S(1)}, u32[]{:S(2)}, u32[]{:S(2)}) collective-permute-start(bf16[4,64,512]{2,1,0:T(8,128)(2,1)S(1)} %get-tuple-element.39), channel_id=1, source_target_pairs={{0,12},{4,0},{8,4},{12,8},{16,28},{20,16},{24,20},{28,24},{32,44},... | collective-permute-start | bytes 786440 | tf_op jit(solution)/shard_map/ppermute | solution.py:32
  88.6 2.1 collective-permute-start.24
  90.8 2.0 collective-permute-start.25
  94.4 11.3 %front.1 = (bf16[512,1024]{1,0:T(8,128)(2,1)}, f32[160,512]{1,0:T(8,128)}, bf16[128,1024]{1,0:T(8,128)(2,1)}, f32[3,40,1024]{2,1,0:T(8,128)}) custom-call(s32[2]{0:T(128)} %pad_add_fusion.where, s32[32]{0:T(128)} %pages.5, s32[32,128]{1,0:T(8,128)} %broadcast_in_dim.36.accepted, bf16[4,512,512]{2,1,0:T(8,128)(2,1)} %prep.1.normed, ...), custom_call_target="tpu_custom_call" | custom-call | flops 12000000000 | bytes 1024 | tf_op jit(solution)/shard_map/front/pallas_call | solution.py:473
  105.9 3.1 %collective-permute-start.30 = (bf16[4,4,64,512]{3,2,1,0:T(8,128)(2,1)S(1)}, bf16[4,4,64,512]{3,2,1,0:T(8,128)(2,1)S(1)}, u32[]{:S(2)}, u32[]{:S(2)}) collective-permute-start(bf16[4,4,64,512]{3,2,1,0:T(8,128)(2,1)S(1)} %pad_maximum_fusion.1.b0), channel_id=1, source_target_pairs={{0,12},{4,0},{8,4},{12,8},{16,28},{20,16},{24,20},{28,24},{32,44},... | collective-permute-start | bytes 3145736 | tf_op jit(solution)/shard_map/ppermute | solution.py:32
  109.2 3.3 %collective-permute-start.28 = (bf16[4,4,64,512]{3,2,1,0:T(8,128)(2,1)S(1)}, bf16[4,4,64,512]{3,2,1,0:T(8,128)(2,1)S(1)}, u32[]{:S(2)}, u32[]{:S(2)}) collective-permute-start(bf16[4,4,64,512]{3,2,1,0:T(8,128)(2,1)S(1)} %pad_maximum_fusion.a0), channel_id=1, source_target_pairs={{0,48},{4,52},{8,56},{12,60},{16,0},{20,4},{24,8},{28,12},{32,16},... | collective-permute-start | bytes 3145736 | tf_op jit(solution)/shard_map/ppermute | solution.py:32
  112.5 1.6 collective-permute-done.20
  114.2 4.3 %collective-permute-start.21 = (f32[160,512]{1,0:T(8,128)S(1)}, f32[160,512]{1,0:T(8,128)S(1)}, u32[]{:S(2)}, u32[]{:S(2)}) collective-permute-start(f32[160,512]{1,0:T(8,128)S(1)} %add.7.sums_a), channel_id=1, source_target_pairs={{0,2},{1,3},{2,0},{3,1},{4,6},{5,7},{6,4},{7,5},{8,10},{9,11},{10,... | collective-permute-start | bytes 983048 | tf_op jit(solution)/shard_map/ppermute | solution.py:36
  118.6 8.0 %collective-permute-done.21.sums_b = f32[160,512]{1,0:T(8,128)S(1)} collective-permute-done((f32[160,512]{1,0:T(8,128)S(1)}, f32[160,512]{1,0:T(8,128)S(1)}, u32[]{:S(2)}, u32[]{:S(2)}) %collective-permute-start.21) | collective-permute-done | bytes 327712 | tf_op jit(solution)/shard_map/ppermute | solution.py:36
  127.3 19.9 %scan.1 = (f32[512,1024]{1,0:T(8,128)}, f32[8,512,128]{2,1,0:T(8,128)}) custom-call(s32[32]{0:T(128)} %pages.5, s32[32,128]{1,0:T(8,128)} %broadcast_in_dim.36.accepted, f32[160,512]{1,0:T(8,128)} %copy-done.9, f32[160,512]{1,0:T(8,128)} %copy-done.20, bf16[128,1024]{1,0:T(8,128)(2,1)} %get-tuple-element.35.dt, f32[1,1024]{1,0:T(1,128)} %bitcast.60, ...), custom_call_target="tpu_custom_call" | custom-call | flops 1000000 | bytes 1024 | tf_op jit(solution)/shard_map/scan/pallas_call | solution.py:505
  147.9 2.9 %collective-permute-start.33 = (bf16[2,4,64,512]{3,2,1,0:T(8,128)(2,1)S(1)}, bf16[2,4,64,512]{3,2,1,0:T(8,128)(2,1)S(1)}, u32[]{:S(2)}, u32[]{:S(2)}) collective-permute-start(bf16[2,4,64,512]{3,2,1,0:T(8,128)(2,1)S(1)} %slice.51), channel_id=1, source_target_pairs={{0,48},{4,52},{8,56},{12,60},{16,0},{20,4},{24,8},{28,12},{32,16},... | collective-permute-start | bytes 1572872 | tf_op jit(solution)/shard_map/ppermute | solution.py:32
  150.9 3.2 %collective-permute-start.34 = (bf16[2,4,64,512]{3,2,1,0:T(8,128)(2,1)S(1)}, bf16[2,4,64,512]{3,2,1,0:T(8,128)(2,1)S(1)}, u32[]{:S(2)}, u32[]{:S(2)}) collective-permute-start(bf16[2,4,64,512]{3,2,1,0:T(8,128)(2,1)S(1)} %slice.52), channel_id=1, source_target_pairs={{0,4},{4,8},{8,12},{12,0},{16,20},{20,24},{24,28},{28,16},{32,36},... | collective-permute-start | bytes 1572872 | tf_op jit(solution)/shard_map/ppermute | solution.py:32
  154.8 7.6 %collective-permute-done.32.a2 = bf16[2,4,64,512]{3,2,1,0:T(8,128)(2,1)S(1)} collective-permute-done((bf16[2,4,64,512]{3,2,1,0:T(8,128)(2,1)S(1)}, bf16[2,4,64,512]{3,2,1,0:T(8,128)(2,1)S(1)}, u32[]{:S(2)}, u32[]{:S(2)}) %collective-permute-start.32) | collective-permute-done | bytes 524320 | tf_op jit(solution)/shard_map/ppermute | solution.py:32
  162.4 3.6 %collective-permute-done.34.b2 = bf16[2,4,64,512]{3,2,1,0:T(8,128)(2,1)S(1)} collective-permute-done((bf16[2,4,64,512]{3,2,1,0:T(8,128)(2,1)S(1)}, bf16[2,4,64,512]{3,2,1,0:T(8,128)(2,1)S(1)}, u32[]{:S(2)}, u32[]{:S(2)}) %collective-permute-start.34) | collective-permute-done | bytes 524320 | tf_op jit(solution)/shard_map/ppermute | solution.py:32
  166.0 2.5 collective-permute-done.35.b3
  169.3 14.0 %gate.1 = (bf16[2,512,512]{2,1,0:T(8,128)(2,1)}, f32[2,512,512]{2,1,0:T(8,128)}) custom-call(s32[2]{0:T(128)} %pad_add_fusion.where, bf16[4,512,512]{2,1,0:T(8,128)(2,1)} %prep.1.normed, bf16[512,1024]{1,0:T(8,128)(2,1)} %get-tuple-element.33.inputs, f32[512,1024]{1,0:T(8,128)} %get-tuple-element.36.ys, f32[1,1024]{1,0:T(1,128)} %bitcast.59, ...), custom_call_target="tpu_custom_call" | custom-call | flops 1000000 | bytes 1024 | tf_op jit(solution)/shard_map/gate/pallas_call | solution.py:542
  183.4 2.9 %collective-permute-done.36.near = bf16[2,512,512]{2,1,0:T(8,128)(2,1)S(1)} collective-permute-done((bf16[2,512,512]{2,1,0:T(8,128)(2,1)}, bf16[2,512,512]{2,1,0:T(8,128)(2,1)S(1)}, u32[]{:S(2)}, u32[]{:S(2)}) %collective-permute-start.36) | collective-permute-done | bytes 1048608 | tf_op jit(solution)/shard_map/ppermute | solution.py:36
  186.2 1.8 fusion
  188.0 1.5 collective-permute-start.37
  189.5 12.5 %collective-permute-done.37.far = bf16[512,512]{1,0:T(8,128)(2,1)S(1)} collective-permute-done((bf16[512,512]{1,0:T(8,128)(2,1)S(1)}, bf16[512,512]{1,0:T(8,128)(2,1)S(1)}, u32[]{:S(2)}, u32[]{:S(2)}) %collective-permute-start.37) | collective-permute-done | bytes 524320 | tf_op jit(solution)/shard_map/ppermute | solution.py:36
  202.9 4.3 %join.1 = bf16[64,16,512]{2,1,0:T(8,128)(2,1)} custom-call(s32[32]{0:T(128)} %targets.3, f32[2,512,512]{2,1,0:T(8,128)} %get-tuple-element.51.keep, bf16[2,512,512]{2,1,0:T(8,128)(2,1)} %copy-done.7, bf16[512,512]{1,0:T(8,128)(2,1)} %copy-done.19, bf16[512,512]{1,0:T(8,128)(2,1)} %bitcast.40), custom_call_target="tpu_custom_call" | custom-call | flops 1000000 | bytes 1024 | tf_op jit(solution)/shard_map/join/pallas_call | solution.py:562
  207.1 11.9 %all-to-all-start.1 = ((bf16[64,16,512]{2,1,0:T(8,128)(2,1)}), bf16[64,16,512]{2,1,0:T(8,128)(2,1)S(1)}, u32[]{:S(2)}, u32[]{:S(2)}) async-start(bf16[64,16,512]{2,1,0:T(8,128)(2,1)} %join.1), calls=%async_computation.1 | async-start | bytes 2097152 | tf_op jit(solution)/shard_map/all_to_all | solution.py:572
  219.1 6.4 %settle.1 = f32[640,1024]{1,0:T(8,128)} custom-call(s32[32]{0:T(128)} %pages.5, f32[8,512,128]{2,1,0:T(8,128)} %get-tuple-element.53.kept, f32[640,1024]{1,0:T(8,128)} %bitcast.37), custom_call_target="tpu_custom_call" | custom-call | flops 1000000 | bytes 1024 | tf_op jit(solution)/shard_map/settle/pallas_call | solution.py:532
  225.5 20.8 %all-to-all-done.1.got = bf16[64,16,512]{2,1,0:T(8,128)(2,1)S(1)} async-done(((bf16[64,16,512]{2,1,0:T(8,128)(2,1)}), bf16[64,16,512]{2,1,0:T(8,128)(2,1)S(1)}, u32[]{:S(2)}, u32[]{:S(2)}) %all-to-all-start.1) | async-done | bytes 1048608 | tf_op jit(solution)/shard_map/all_to_all | solution.py:572
  246.4 1.0 copy-done.2
  247.4 2.4 unpack.1
  (125 shorter events, 16.9 us)
Async XLA Ops:
  1.3 34.1 %copy-start.25 = (bf16[1024,32]{0,1:T(8,128)(2,1)S(1)}, bf16[1024,32]{0,1:T(8,128)(2,1)}, u32[]{:S(2)}) copy-start(bf16[1024,32]{0,1:T(8,128)(2,1)} %param.28) | copy-start | bytes 196612
  1.4 34.1 %copy-start.26 = (bf16[32,1024]{1,0:T(8,128)(2,1)S(1)}, bf16[32,1024]{1,0:T(8,128)(2,1)}, u32[]{:S(2)}) copy-start(bf16[32,1024]{1,0:T(8,128)(2,1)} %param.20) | copy-start | bytes 196612
  2.3 14.7 %collective-permute-start = (bf16[48,1024]{1,0:T(8,128)(2,1)S(1)}, bf16[48,1024]{1,0:T(8,128)(2,1)S(1)}, u32[]{:S(2)}, u32[]{:S(2)}) collective-permute-start(bf16[48,1024]{1,0:T(8,128)(2,1)S(1)} %get-tuple-element.62), channel_id=1, source_target_pairs={{0,192},{4,196},{8,200},{12,204},{16,208},{20,212},{24,216},{28,22... | collective-permute-start | bytes 294920 | tf_op jit(solution)/shard_map/ppermute | solution.py:32
  8.7 11.6 %collective-permute-start.1 = (bf16[48,1024]{1,0:T(8,128)(2,1)S(1)}, bf16[48,1024]{1,0:T(8,128)(2,1)S(1)}, u32[]{:S(2)}, u32[]{:S(2)}) collective-permute-start(bf16[48,1024]{1,0:T(8,128)(2,1)S(1)} %get-tuple-element.62), channel_id=1, source_target_pairs={{0,128},{4,132},{8,136},{12,140},{16,144},{20,148},{24,152},{28,15... | collective-permute-start | bytes 294920 | tf_op jit(solution)/shard_map/ppermute | solution.py:32
  9.7 10.6 %collective-permute-start.2 = (bf16[48,1024]{1,0:T(8,128)(2,1)S(1)}, bf16[48,1024]{1,0:T(8,128)(2,1)S(1)}, u32[]{:S(2)}, u32[]{:S(2)}) collective-permute-start(bf16[48,1024]{1,0:T(8,128)(2,1)S(1)} %get-tuple-element.62), channel_id=1, source_target_pairs={{0,64},{4,68},{8,72},{12,76},{16,80},{20,84},{24,88},{28,92},{32,9... | collective-permute-start | bytes 294920 | tf_op jit(solution)/shard_map/ppermute | solution.py:32
  20.4 7.0 %collective-permute-start.8 = (bf16[4,48,384]{2,1,0:T(8,128)(2,1)S(1)}, bf16[4,48,384]{2,1,0:T(8,128)(2,1)S(1)}, u32[]{:S(2)}, u32[]{:S(2)}) collective-permute-start(bf16[4,48,384]{2,1,0:T(8,128)(2,1)S(1)} %get-tuple-element.60), channel_id=1, source_target_pairs={{0,4},{4,8},{8,12},{12,0},{16,20},{20,24},{24,28},{28,16},{32,36},... | collective-permute-start | bytes 442376 | tf_op jit(solution)/shard_map/ppermute | solution.py:32
  21.9 5.4 %collective-permute-start.6 = (bf16[4,48,384]{2,1,0:T(8,128)(2,1)S(1)}, bf16[4,48,384]{2,1,0:T(8,128)(2,1)S(1)}, u32[]{:S(2)}, u32[]{:S(2)}) collective-permute-start(bf16[4,48,384]{2,1,0:T(8,128)(2,1)S(1)} %get-tuple-element.60), channel_id=1, source_target_pairs={{0,12},{4,0},{8,4},{12,8},{16,28},{20,16},{24,20},{28,24},{32,44},... | collective-permute-start | bytes 442376 | tf_op jit(solution)/shard_map/ppermute | solution.py:32
  22.5 6.8 %collective-permute-start.7 = (bf16[4,48,384]{2,1,0:T(8,128)(2,1)S(1)}, bf16[4,48,384]{2,1,0:T(8,128)(2,1)S(1)}, u32[]{:S(2)}, u32[]{:S(2)}) collective-permute-start(bf16[4,48,384]{2,1,0:T(8,128)(2,1)S(1)} %get-tuple-element.60), channel_id=1, source_target_pairs={{0,8},{4,12},{8,0},{12,4},{16,24},{20,28},{24,16},{28,20},{32,40},... | collective-permute-start | bytes 442376 | tf_op jit(solution)/shard_map/ppermute | solution.py:32
  26.4 34.6 %copy-start.8 = (bf16[528,512]{1,0:T(8,128)(2,1)}, bf16[528,512]{1,0:T(8,128)(2,1)S(1)}, u32[]{:S(2)}) copy-start(bf16[528,512]{1,0:T(8,128)(2,1)S(1)} %pad_maximum_fusion.4.h0) | copy-start | bytes 1622020
  26.4 34.6 %collective-permute-start.4 = (bf16[528,512]{1,0:T(8,128)(2,1)S(1)}, bf16[528,512]{1,0:T(8,128)(2,1)S(1)}, u32[]{:S(2)}, u32[]{:S(2)}) collective-permute-start(bf16[528,512]{1,0:T(8,128)(2,1)S(1)} %pad_maximum_fusion.4.h0), channel_id=1, source_target_pairs={{0,2},{1,3},{2,0},{3,1},{4,6},{5,7},{6,4},{7,5},{8,10},{9,11},{10,... | collective-permute-start | bytes 1622024 | tf_op jit(solution)/shard_map/ppermute | solution.py:36
  29.4 33.1 %copy-start.11 = (bf16[4,4,48,384]{3,2,1,0:T(8,128)(2,1)}, bf16[4,4,48,384]{3,2,1,0:T(8,128)(2,1)S(1)}, u32[]{:S(2)}) copy-start(bf16[4,4,48,384]{3,2,1,0:T(8,128)(2,1)S(1)} %pad_maximum_fusion.3.a0) | copy-start | bytes 1769476
  29.4 31.6 %collective-permute-start.10 = (bf16[4,4,48,384]{3,2,1,0:T(8,128)(2,1)S(1)}, bf16[4,4,48,384]{3,2,1,0:T(8,128)(2,1)}, u32[]{:S(2)}, u32[]{:S(2)}) collective-permute-start(bf16[4,4,48,384]{3,2,1,0:T(8,128)(2,1)S(1)} %pad_maximum_fusion.3.a0), channel_id=1, source_target_pairs={{0,16},{4,20},{8,24},{12,28},{16,32},{20,36},{24,40},{28,44},{32,4... | collective-permute-start | bytes 1769480 | tf_op jit(solution)/shard_map/ppermute | solution.py:32
  31.1 5.4 %collective-permute-start.11 = (bf16[4,32,640]{2,1,0:T(8,128)(2,1)S(1)}, bf16[4,32,640]{2,1,0:T(8,128)(2,1)S(1)}, u32[]{:S(2)}, u32[]{:S(2)}) collective-permute-start(bf16[4,32,640]{2,1,0:T(8,128)(2,1)S(1)} %get-tuple-element.58), channel_id=1, source_target_pairs={{0,48},{4,52},{8,56},{12,60},{16,0},{20,4},{24,8},{28,12},{32,16},... | collective-permute-start | bytes 491528 | tf_op jit(solution)/shard_map/ppermute | solution.py:32
  32.8 15.5 %collective-permute-start.12 = (bf16[4,32,640]{2,1,0:T(8,128)(2,1)S(1)}, bf16[4,32,640]{2,1,0:T(8,128)(2,1)S(1)}, u32[]{:S(2)}, u32[]{:S(2)}) collective-permute-start(bf16[4,32,640]{2,1,0:T(8,128)(2,1)S(1)} %get-tuple-element.58), channel_id=1, source_target_pairs={{0,32},{4,36},{8,40},{12,44},{16,48},{20,52},{24,56},{28,60},{32,0... | collective-permute-start | bytes 491528 | tf_op jit(solution)/shard_map/ppermute | solution.py:32
  34.8 14.0 %collective-permute-start.13 = (bf16[4,32,640]{2,1,0:T(8,128)(2,1)S(1)}, bf16[4,32,640]{2,1,0:T(8,128)(2,1)S(1)}, u32[]{:S(2)}, u32[]{:S(2)}) collective-permute-start(bf16[4,32,640]{2,1,0:T(8,128)(2,1)S(1)} %get-tuple-element.58), channel_id=1, source_target_pairs={{0,16},{4,20},{8,24},{12,28},{16,32},{20,36},{24,40},{28,44},{32,4... | collective-permute-start | bytes 491528 | tf_op jit(solution)/shard_map/ppermute | solution.py:32
  48.9 27.5 %copy-start.10 = (bf16[4,4,32,640]{3,2,1,0:T(8,128)(2,1)}, bf16[4,4,32,640]{3,2,1,0:T(8,128)(2,1)S(1)}, u32[]{:S(2)}) copy-start(bf16[4,4,32,640]{3,2,1,0:T(8,128)(2,1)S(1)} %pad_maximum_fusion.2.b0) | copy-start | bytes 1966084
  49.9 34.8 %all-to-all-start = ((bf16[4,64,1024]{2,1,0:T(8,128)(2,1)}), bf16[4,64,1024]{2,1,0:T(8,128)(2,1)S(1)}, u32[]{:S(2)}, u32[]{:S(2)}) async-start(bf16[4,64,1024]{2,1,0:T(8,128)(2,1)} %broadcast_in_dim.40), calls=%async_computation | async-start | bytes 1048576 | tf_op jit(solution)/shard_map/all_to_all | solution.py:60
  57.0 14.5 %collective-permute-start.15 = (bf16[4,4,32,640]{3,2,1,0:T(8,128)(2,1)S(1)}, bf16[4,4,32,640]{3,2,1,0:T(8,128)(2,1)S(1)}, u32[]{:S(2)}, u32[]{:S(2)}) collective-permute-start(bf16[4,4,32,640]{3,2,1,0:T(8,128)(2,1)S(1)} %pad_maximum_fusion.2.b0), channel_id=1, source_target_pairs={{0,4},{4,8},{8,12},{12,0},{16,20},{20,24},{24,28},{28,16},{32,36},... | collective-permute-start | bytes 1966088 | tf_op jit(solution)/shard_map/ppermute | solution.py:32
  59.1 15.1 %collective-permute-start.14 = (bf16[4,4,32,640]{3,2,1,0:T(8,128)(2,1)S(1)}, bf16[4,4,32,640]{3,2,1,0:T(8,128)(2,1)S(1)}, u32[]{:S(2)}, u32[]{:S(2)}) collective-permute-start(bf16[4,4,32,640]{3,2,1,0:T(8,128)(2,1)S(1)} %pad_maximum_fusion.2.b0), channel_id=1, source_target_pairs={{0,12},{4,0},{8,4},{12,8},{16,28},{20,16},{24,20},{28,24},{32,44},... | collective-permute-start | bytes 1966088 | tf_op jit(solution)/shard_map/ppermute | solution.py:32
  59.1 10.6 %collective-permute-start.9 = (bf16[4,4,48,384]{3,2,1,0:T(8,128)(2,1)S(1)}, bf16[4,4,48,384]{3,2,1,0:T(8,128)(2,1)S(1)}, u32[]{:S(2)}, u32[]{:S(2)}) collective-permute-start(bf16[4,4,48,384]{3,2,1,0:T(8,128)(2,1)S(1)} %pad_maximum_fusion.3.a0), channel_id=1, source_target_pairs={{0,48},{4,52},{8,56},{12,60},{16,0},{20,4},{24,8},{28,12},{32,16},... | collective-permute-start | bytes 1769480 | tf_op jit(solution)/shard_map/ppermute | solution.py:32
  60.9 15.5 %collective-permute-start.3 = (bf16[528,512]{1,0:T(8,128)(2,1)S(1)}, bf16[528,512]{1,0:T(8,128)(2,1)S(1)}, u32[]{:S(2)}, u32[]{:S(2)}) collective-permute-start(bf16[528,512]{1,0:T(8,128)(2,1)S(1)} %pad_maximum_fusion.4.h0), channel_id=1, source_target_pairs={{0,1},{1,0},{2,3},{3,2},{4,5},{5,4},{6,7},{7,6},{8,9},{9,8},{10,11... | collective-permute-start | bytes 1622024 | tf_op jit(solution)/shard_map/ppermute | solution.py:36
  61.0 16.7 %collective-permute-start.5 = (bf16[528,512]{1,0:T(8,128)(2,1)S(1)}, bf16[528,512]{1,0:T(8,128)(2,1)S(1)}, u32[]{:S(2)}, u32[]{:S(2)}) collective-permute-start(bf16[528,512]{1,0:T(8,128)(2,1)S(1)} %collective-permute-done.4.h2), channel_id=1, source_target_pairs={{0,1},{1,0},{2,3},{3,2},{4,5},{5,4},{6,7},{7,6},{8,9},{9,8},{10,11... | collective-permute-start | bytes 1622024 | tf_op jit(solution)/shard_map/ppermute | solution.py:36
  69.7 18.9 %collective-permute-start.16 = (bf16[2,4,48,384]{3,2,1,0:T(8,128)(2,1)S(1)}, bf16[2,4,48,384]{3,2,1,0:T(8,128)(2,1)}, u32[]{:S(2)}, u32[]{:S(2)}) collective-permute-start(bf16[2,4,48,384]{3,2,1,0:T(8,128)(2,1)S(1)} %slice.58), channel_id=1, source_target_pairs={{0,16},{4,20},{8,24},{12,28},{16,32},{20,36},{24,40},{28,44},{32,4... | collective-permute-start | bytes 884744 | tf_op jit(solution)/shard_map/ppermute | solution.py:32
  71.5 17.1 %collective-permute-start.17 = (bf16[2,4,48,384]{3,2,1,0:T(8,128)(2,1)}, bf16[2,4,48,384]{3,2,1,0:T(8,128)(2,1)}, u32[]{:S(2)}, u32[]{:S(2)}) collective-permute-start(bf16[2,4,48,384]{3,2,1,0:T(8,128)(2,1)} %slice.59), channel_id=1, source_target_pairs={{0,48},{4,52},{8,56},{12,60},{16,0},{20,4},{24,8},{28,12},{32,16},... | collective-permute-start | bytes 884744 | tf_op jit(solution)/shard_map/ppermute | solution.py:32
  74.3 16.5 %collective-permute-start.18 = (bf16[2,4,32,640]{3,2,1,0:T(8,128)(2,1)S(1)}, bf16[2,4,32,640]{3,2,1,0:T(8,128)(2,1)}, u32[]{:S(2)}, u32[]{:S(2)}) collective-permute-start(bf16[2,4,32,640]{3,2,1,0:T(8,128)(2,1)S(1)} %slice.60), channel_id=1, source_target_pairs={{0,4},{4,8},{8,12},{12,0},{16,20},{20,24},{24,28},{28,16},{32,36},... | collective-permute-start | bytes 983048 | tf_op jit(solution)/shard_map/ppermute | solution.py:32
  76.4 17.3 %copy-start.27 = (s32[32]{0:T(128)S(1)}, s32[32]{0:T(128)}, u32[]{:S(2)}) copy-start(s32[32]{0:T(128)} %param.33) | copy-start | bytes 388
  76.4 16.3 %collective-permute-start.19 = (bf16[2,4,32,640]{3,2,1,0:T(8,128)(2,1)S(1)}, bf16[2,4,32,640]{3,2,1,0:T(8,128)(2,1)S(1)}, u32[]{:S(2)}, u32[]{:S(2)}) collective-permute-start(bf16[2,4,32,640]{3,2,1,0:T(8,128)(2,1)S(1)} %slice.61), channel_id=1, source_target_pairs={{0,12},{4,0},{8,4},{12,8},{16,28},{20,16},{24,20},{28,24},{32,44},... | collective-permute-start | bytes 983048 | tf_op jit(solution)/shard_map/ppermute | solution.py:32
  84.8 8.5 %collective-permute-start.22 = (bf16[4,64,512]{2,1,0:T(8,128)(2,1)S(1)}, bf16[4,64,512]{2,1,0:T(8,128)(2,1)S(1)}, u32[]{:S(2)}, u32[]{:S(2)}) collective-permute-start(bf16[4,64,512]{2,1,0:T(8,128)(2,1)S(1)} %get-tuple-element.39), channel_id=1, source_target_pairs={{0,12},{4,0},{8,4},{12,8},{16,28},{20,16},{24,20},{28,24},{32,44},... | collective-permute-start | bytes 786440 | tf_op jit(solution)/shard_map/ppermute | solution.py:32
  88.6 17.1 %collective-permute-start.23 = (bf16[4,64,512]{2,1,0:T(8,128)(2,1)S(1)}, bf16[4,64,512]{2,1,0:T(8,128)(2,1)S(1)}, u32[]{:S(2)}, u32[]{:S(2)}) collective-permute-start(bf16[4,64,512]{2,1,0:T(8,128)(2,1)S(1)} %get-tuple-element.39), channel_id=1, source_target_pairs={{0,8},{4,12},{8,0},{12,4},{16,24},{20,28},{24,16},{28,20},{32,40},... | collective-permute-start | bytes 786440 | tf_op jit(solution)/shard_map/ppermute | solution.py:32
  88.6 17.1 %collective-permute-start.24 = (bf16[4,64,512]{2,1,0:T(8,128)(2,1)S(1)}, bf16[4,64,512]{2,1,0:T(8,128)(2,1)S(1)}, u32[]{:S(2)}, u32[]{:S(2)}) collective-permute-start(bf16[4,64,512]{2,1,0:T(8,128)(2,1)S(1)} %get-tuple-element.39), channel_id=1, source_target_pairs={{0,4},{4,8},{8,12},{12,0},{16,20},{20,24},{24,28},{28,16},{32,36},... | collective-permute-start | bytes 786440 | tf_op jit(solution)/shard_map/ppermute | solution.py:32
  90.8 15.0 %collective-permute-start.25 = (bf16[4,64,512]{2,1,0:T(8,128)(2,1)S(1)}, bf16[4,64,512]{2,1,0:T(8,128)(2,1)S(1)}, u32[]{:S(2)}, u32[]{:S(2)}) collective-permute-start(bf16[4,64,512]{2,1,0:T(8,128)(2,1)S(1)} %get-tuple-element.43), channel_id=1, source_target_pairs={{0,48},{4,52},{8,56},{12,60},{16,0},{20,4},{24,8},{28,12},{32,16},... | collective-permute-start | bytes 786440 | tf_op jit(solution)/shard_map/ppermute | solution.py:32
  92.7 13.0 %collective-permute-start.26 = (bf16[4,64,512]{2,1,0:T(8,128)(2,1)S(1)}, bf16[4,64,512]{2,1,0:T(8,128)(2,1)S(1)}, u32[]{:S(2)}, u32[]{:S(2)}) collective-permute-start(bf16[4,64,512]{2,1,0:T(8,128)(2,1)S(1)} %get-tuple-element.43), channel_id=1, source_target_pairs={{0,32},{4,36},{8,40},{12,44},{16,48},{20,52},{24,56},{28,60},{32,0... | collective-permute-start | bytes 786440 | tf_op jit(solution)/shard_map/ppermute | solution.py:32
  93.2 12.5 %collective-permute-start.27 = (bf16[4,64,512]{2,1,0:T(8,128)(2,1)S(1)}, bf16[4,64,512]{2,1,0:T(8,128)(2,1)S(1)}, u32[]{:S(2)}, u32[]{:S(2)}) collective-permute-start(bf16[4,64,512]{2,1,0:T(8,128)(2,1)S(1)} %get-tuple-element.43), channel_id=1, source_target_pairs={{0,16},{4,20},{8,24},{12,28},{16,32},{20,36},{24,40},{28,44},{32,4... | collective-permute-start | bytes 786440 | tf_op jit(solution)/shard_map/ppermute | solution.py:32
  105.9 41.3 %copy-start = (bf16[4,4,64,512]{3,2,1,0:T(8,128)(2,1)}, bf16[4,4,64,512]{3,2,1,0:T(8,128)(2,1)S(1)}, u32[]{:S(2)}) copy-start(bf16[4,4,64,512]{3,2,1,0:T(8,128)(2,1)S(1)} %pad_maximum_fusion.1.b0) | copy-start | bytes 3145732
  105.9 41.3 %collective-permute-start.30 = (bf16[4,4,64,512]{3,2,1,0:T(8,128)(2,1)S(1)}, bf16[4,4,64,512]{3,2,1,0:T(8,128)(2,1)S(1)}, u32[]{:S(2)}, u32[]{:S(2)}) collective-permute-start(bf16[4,4,64,512]{3,2,1,0:T(8,128)(2,1)S(1)} %pad_maximum_fusion.1.b0), channel_id=1, source_target_pairs={{0,12},{4,0},{8,4},{12,8},{16,28},{20,16},{24,20},{28,24},{32,44},... | collective-permute-start | bytes 3145736 | tf_op jit(solution)/shard_map/ppermute | solution.py:32
  109.1 38.2 %collective-permute-start.31 = (bf16[4,4,64,512]{3,2,1,0:T(8,128)(2,1)S(1)}, bf16[4,4,64,512]{3,2,1,0:T(8,128)(2,1)S(1)}, u32[]{:S(2)}, u32[]{:S(2)}) collective-permute-start(bf16[4,4,64,512]{3,2,1,0:T(8,128)(2,1)S(1)} %pad_maximum_fusion.1.b0), channel_id=1, source_target_pairs={{0,4},{4,8},{8,12},{12,0},{16,20},{20,24},{24,28},{28,16},{32,36},... | collective-permute-start | bytes 3145736 | tf_op jit(solution)/shard_map/ppermute | solution.py:32
  109.2 38.0 %copy-start.1 = (bf16[4,4,64,512]{3,2,1,0:T(8,128)(2,1)}, bf16[4,4,64,512]{3,2,1,0:T(8,128)(2,1)S(1)}, u32[]{:S(2)}) copy-start(bf16[4,4,64,512]{3,2,1,0:T(8,128)(2,1)S(1)} %pad_maximum_fusion.a0) | copy-start | bytes 3145732
  109.2 38.1 %collective-permute-start.28 = (bf16[4,4,64,512]{3,2,1,0:T(8,128)(2,1)S(1)}, bf16[4,4,64,512]{3,2,1,0:T(8,128)(2,1)S(1)}, u32[]{:S(2)}, u32[]{:S(2)}) collective-permute-start(bf16[4,4,64,512]{3,2,1,0:T(8,128)(2,1)S(1)} %pad_maximum_fusion.a0), channel_id=1, source_target_pairs={{0,48},{4,52},{8,56},{12,60},{16,0},{20,4},{24,8},{28,12},{32,16},... | collective-permute-start | bytes 3145736 | tf_op jit(solution)/shard_map/ppermute | solution.py:32
  112.5 34.8 %collective-permute-start.29 = (bf16[4,4,64,512]{3,2,1,0:T(8,128)(2,1)S(1)}, bf16[4,4,64,512]{3,2,1,0:T(8,128)(2,1)S(1)}, u32[]{:S(2)}, u32[]{:S(2)}) collective-permute-start(bf16[4,4,64,512]{3,2,1,0:T(8,128)(2,1)S(1)} %pad_maximum_fusion.a0), channel_id=1, source_target_pairs={{0,16},{4,20},{8,24},{12,28},{16,32},{20,36},{24,40},{28,44},{32,4... | collective-permute-start | bytes 3145736 | tf_op jit(solution)/shard_map/ppermute | solution.py:32
  112.5 1.6 collective-permute-start.20
  114.2 12.4 %collective-permute-start.21 = (f32[160,512]{1,0:T(8,128)S(1)}, f32[160,512]{1,0:T(8,128)S(1)}, u32[]{:S(2)}, u32[]{:S(2)}) collective-permute-start(f32[160,512]{1,0:T(8,128)S(1)} %add.7.sums_a), channel_id=1, source_target_pairs={{0,2},{1,3},{2,0},{3,1},{4,6},{5,7},{6,4},{7,5},{8,10},{9,11},{10,... | collective-permute-start | bytes 983048 | tf_op jit(solution)/shard_map/ppermute | solution.py:36
  147.4 15.0 %collective-permute-start.32 = (bf16[2,4,64,512]{3,2,1,0:T(8,128)(2,1)S(1)}, bf16[2,4,64,512]{3,2,1,0:T(8,128)(2,1)S(1)}, u32[]{:S(2)}, u32[]{:S(2)}) collective-permute-start(bf16[2,4,64,512]{3,2,1,0:T(8,128)(2,1)S(1)} %slice.50), channel_id=1, source_target_pairs={{0,16},{4,20},{8,24},{12,28},{16,32},{20,36},{24,40},{28,44},{32,4... | collective-permute-start | bytes 1572872 | tf_op jit(solution)/shard_map/ppermute | solution.py:32
  147.9 14.5 %collective-permute-start.33 = (bf16[2,4,64,512]{3,2,1,0:T(8,128)(2,1)S(1)}, bf16[2,4,64,512]{3,2,1,0:T(8,128)(2,1)S(1)}, u32[]{:S(2)}, u32[]{:S(2)}) collective-permute-start(bf16[2,4,64,512]{3,2,1,0:T(8,128)(2,1)S(1)} %slice.51), channel_id=1, source_target_pairs={{0,48},{4,52},{8,56},{12,60},{16,0},{20,4},{24,8},{28,12},{32,16},... | collective-permute-start | bytes 1572872 | tf_op jit(solution)/shard_map/ppermute | solution.py:32
  150.9 15.2 %collective-permute-start.34 = (bf16[2,4,64,512]{3,2,1,0:T(8,128)(2,1)S(1)}, bf16[2,4,64,512]{3,2,1,0:T(8,128)(2,1)S(1)}, u32[]{:S(2)}, u32[]{:S(2)}) collective-permute-start(bf16[2,4,64,512]{3,2,1,0:T(8,128)(2,1)S(1)} %slice.52), channel_id=1, source_target_pairs={{0,4},{4,8},{8,12},{12,0},{16,20},{20,24},{24,28},{28,16},{32,36},... | collective-permute-start | bytes 1572872 | tf_op jit(solution)/shard_map/ppermute | solution.py:32
  154.1 14.4 %collective-permute-start.35 = (bf16[2,4,64,512]{3,2,1,0:T(8,128)(2,1)S(1)}, bf16[2,4,64,512]{3,2,1,0:T(8,128)(2,1)S(1)}, u32[]{:S(2)}, u32[]{:S(2)}) collective-permute-start(bf16[2,4,64,512]{3,2,1,0:T(8,128)(2,1)S(1)} %slice.53), channel_id=1, source_target_pairs={{0,12},{4,0},{8,4},{12,8},{16,28},{20,16},{24,20},{28,24},{32,44},... | collective-permute-start | bytes 1572872 | tf_op jit(solution)/shard_map/ppermute | solution.py:32
  183.3 3.0 %collective-permute-start.36 = (bf16[2,512,512]{2,1,0:T(8,128)(2,1)}, bf16[2,512,512]{2,1,0:T(8,128)(2,1)S(1)}, u32[]{:S(2)}, u32[]{:S(2)}) collective-permute-start(bf16[2,512,512]{2,1,0:T(8,128)(2,1)} %get-tuple-element.52), channel_id=1, source_target_pairs={{0,1},{1,0},{2,3},{3,2},{4,5},{5,4},{6,7},{7,6},{8,9},{9,8},{10,11... | collective-permute-start | bytes 3145736 | tf_op jit(solution)/shard_map/ppermute | solution.py:36
  188.0 14.1 %collective-permute-start.37 = (bf16[512,512]{1,0:T(8,128)(2,1)S(1)}, bf16[512,512]{1,0:T(8,128)(2,1)S(1)}, u32[]{:S(2)}, u32[]{:S(2)}) collective-permute-start(bf16[512,512]{1,0:T(8,128)(2,1)S(1)} %fusion), channel_id=1, source_target_pairs={{0,2},{1,3},{2,0},{3,1},{4,6},{5,7},{6,4},{7,5},{8,10},{9,11},{10,... | collective-permute-start | bytes 1572872 | tf_op jit(solution)/shard_map/ppermute | solution.py:36
  207.1 39.2 %all-to-all-start.1 = ((bf16[64,16,512]{2,1,0:T(8,128)(2,1)}), bf16[64,16,512]{2,1,0:T(8,128)(2,1)S(1)}, u32[]{:S(2)}, u32[]{:S(2)}) async-start(bf16[64,16,512]{2,1,0:T(8,128)(2,1)} %join.1), calls=%async_computation.1 | async-start | bytes 2097152 | tf_op jit(solution)/shard_map/all_to_all | solution.py:572
  (21 other events, 118.5 us)

commit v5 on v4

--- a/solution.py
+++ b/solution.py
@@ -64,13 +64,13 @@
     return jnp.stack(send_direct(block, axis))
 
 
-def start_pieces(pieces, place, middle_first, body, ordered=False):
+def start_pieces(pieces, place, middle_first, body):
     z, y, x = place
     own, above, low, high, below = pieces
 
     def one(n, _):
         i, k = n >> 2, n & 3
-        dz = k if ordered else (z + k) & 3
+        dz = (z + k) & 3
 
         def piece(f, ref, at):
             if middle_first:
@@ -242,7 +242,7 @@
         return 0
 
     lax.fori_loop(0, count, fetch, 0)
-    summed = sums_a[...] + sums_b[...]
+    summed = sums_a[...] + sums_b[...].astype(F32)
     low[...] = summed[:rank].T.astype(BF)
     rest = summed[rank:]
     high = rest.astype(BF).astype(F32)
@@ -332,33 +332,22 @@
 
 
 def gate_kernel(
-    where, normed, inputs, ys, skip, a0, a1, a2, a3, a4, b0, b1, b2, b3, b4,
-    send_out, keep_out, weight, outer, gated, sems,
+    where, normed, inputs, ys, skip, second, send_out, keep_out, weight, outer, gated, sems
 ):
     m = where[1]
     tokens, width = gated.shape
-    half = width // 2
-    a, b = (a0, a1, a2, a3, a4), (b0, b1, b2, b3, b4)
-
-    def take(src, d, column):
-        pltpu.make_async_copy(
-            src.at[pl.ds(0, 32), :], weight.at[pl.ds(d * 32, 32), pl.ds(column, half)], sems.at[0]
-        ).start()
-        pltpu.make_async_copy(
-            src.at[pl.ds(32, 32), :], outer.at[pl.ds(d * 32, 32), pl.ds(column, half)], sems.at[1]
-        ).start()
-
-    start_pieces(a, place_of(where), True, lambda src, d: take(src, d, 0), True)
-    start_pieces(b, place_of(where), False, lambda src, d: take(src, d, half), True)
+    for z in range(SIDE):
+        pltpu.make_async_copy(second.at[:, z, pl.ds(0, 32), :], weight.at[z], sems.at[0]).start()
+    for z in range(SIDE):
+        pltpu.make_async_copy(second.at[:, z, pl.ds(32, 32), :], outer.at[z], sems.at[1]).start()
     pltpu.make_async_copy(weight, weight, sems.at[0]).wait()
 
     def gate(n, _):
         at = pl.ds(pl.multiple_of(n * 256, 256), 256)
         total = jnp.zeros((tokens, 256), F32)
         for k in range(4):
-            total = total + jnp.dot(
-                normed[k], weight[pl.ds((m ^ k) * 512, 512), at], preferred_element_type=F32
-            )
+            block = weight[m ^ k, :, :, at].reshape(512, 256)
+            total = total + jnp.dot(normed[k], block, preferred_element_type=F32)
         gates = total.astype(BF).astype(F32)
         mixed = ys[:, at] + skip[:, at] * inputs[:, at].astype(F32)
         gated[:, at] = (mixed * sigmoid_times(gates)).astype(BF)
@@ -371,7 +360,7 @@
         column = pl.ds(pl.multiple_of((part & 1) * 256, 256), 256)
         for core in range(2):
             block = m ^ ((part & 2) + core)
-            rows = outer[pl.ds(pl.multiple_of(block * 512 + (part & 1) * 256, 256), 256), :]
+            rows = outer[block, pl.ds((part & 1) * 8, 8), :, :].reshape(256, width)
             value = lax.dot_general(
                 gated[...], rows, (((1,), (1,)), ((), ())), preferred_element_type=F32
             )
@@ -443,13 +432,14 @@
     first = direct(jnp.concatenate([in_x, extra], axis=0), 0)
     middle_a = direct(first[:, :, :CUT], 2)
     middle_b = direct(first[:, :32, CUT:], 1)
+    middle_a, middle_b = lax.optimization_barrier((middle_a, middle_b))
     sides_a, sides_b = ring_one(middle_a, 1), ring_one(middle_b, 2)
     first_a = ring_two(middle_a, 1, sides_a)
     first_b = ring_two(middle_b, 2, sides_b)
 
     flat = hidden.reshape(tokens, part)
     sent = jnp.concatenate([flat, jnp.broadcast_to(norm_gain[None], (16, part))], axis=0)
-    sent = after(sent, first)
+    sent = after(sent, middle_a, middle_b)
     near = across(sent, 1)
     far = across(sent, 2)
     both = across(far, 1)
@@ -464,10 +454,11 @@
         name="prep",
     )(sent, *after((near, far, both), sides_a, sides_b))
 
-    pair = after(jnp.concatenate([in_z, out_proj.T], axis=0), middle_a, middle_b)
-    stacked = after(exchange_z(pair), sides_a, sides_b, normed)
-    plane_a = send_direct(stacked[..., : width // 2], 2)
-    plane_b = send_direct(stacked[..., width // 2 :], 1)
+    pair = after(jnp.concatenate([in_z, out_proj.T], axis=0), first)
+    second = lax.all_gather(
+        exchange_z(pair), "dp", axis=0,
+        axis_index_groups=[[z * 16 + i for i in range(16)] for z in range(SIDE)],
+    )
 
     wide_accepted = jnp.broadcast_to(accepted[:, None], (count, 128))
     inputs, sums, dt, new_conv = pl.pallas_call(
@@ -498,10 +489,8 @@
         conv_weight, conv_bias[None], conv_pool.transpose(1, 0, 2),
     )
 
-    plane_a, plane_b = (jnp.stack(p) for p in after((plane_a, plane_b), sums))
-    around_a, around_b = ring_one(plane_a, 1), ring_one(plane_b, 2)
     sums = sums + across(sums, 1)
-    other = across(sums, 2)
+    other = across(sums.astype(BF), 2)
     ys, kept = pl.pallas_call(
         scan_kernel,
         out_shape=(
@@ -527,8 +516,6 @@
         state_pool.reshape(slots * states, width),
     )
 
-    around_a, around_b = after((around_a, around_b), ys)
-    second = (*ring_two(plane_a, 1, around_a), *ring_two(plane_b, 2, around_b))
     new_state = pl.pallas_call(
         settle_kernel,
         out_shape=jax.ShapeDtypeStruct((slots * states, width), F32),
@@ -545,18 +532,18 @@
             jax.ShapeDtypeStruct((2, tokens, part), BF),
             jax.ShapeDtypeStruct((2, tokens, part), F32),
         ),
-        in_specs=[SMEM] + [VMEM] * 4 + [ANY] * 10,
+        in_specs=[SMEM] + [VMEM] * 4 + [ANY],
         out_specs=(VMEM,) * 2,
         scratch_shapes=[
-            pltpu.VMEM((2048, width), BF),
-            pltpu.VMEM((2048, width), BF),
+            pltpu.VMEM((SIDE, 16, 32, width), BF),
+            pltpu.VMEM((SIDE, 16, 32, width), BF),
             pltpu.VMEM((tokens, width), BF),
             pltpu.SemaphoreType.DMA((2,)),
         ],
         compiler_params=params(),
         cost_estimate=pl.CostEstimate(flops=1_000_000, bytes_accessed=1 << 10, transcendentals=0),
         name="gate",
-    )(where, normed, inputs, ys, skip[None], *second)
+    )(where, normed, inputs, ys, skip[None], second)
     got = across(send, 1)
     remote = across((keep[1] + got[1].astype(F32)).astype(BF), 2)
     packed = pl.pallas_call(

time: 253 us -> 237 us (0.937)
  starting transfers between devices: 79.6 us -> 45.7 us
  blocking collectives: 0 us -> 21 us
  between operations: 1.14 us -> 14.2 us
  waiting for transfers between devices: 90.4 us -> 77.4 us
    ppermute x31 -> x17, starting transfers between devices: 53 us -> 31.3 us  [hop(): return lax.ppermute(value, 'dp', shift_pairs(axis, step))]
    all_to_all x0 -> x1, blocking collectives: none -> 21 us  [exchange_z(): lax.all_to_all(many, 'dp', 0, 0, tiled=True, axis_index_groups=groups)]
    ppermute x31 -> x17, waiting for transfers between devices: 44.5 us -> 28.6 us  [hop(): return lax.ppermute(value, 'dp', shift_pairs(axis, step))]
    all_to_all x1 -> x0, starting transfers between devices: 7.09 us -> none  [exchange_z(): lax.all_to_all(many, 'dp', 0, 0, tiled=True, axis_index_groups=groups)]
    ppermute x7, starting transfers between devices: 7.51 us -> 2.32 us  [across(): return lax.ppermute(value, 'mp', [(m, m ^ flip) for m in range(4)])]
  transfers between devices with their start and end apart: 40 -> 26, of which waited for: 16 -> 13; matrix products, arithmetic and copies ran while one was open for 3% -> 3% of each run, Pallas kernels for 18% -> 19%
where the time goes in v5:
time: 237 us; the launch traced here: 236 us
  waiting for transfers between devices  77.4 us (33%)
  Pallas kernels  63.4 us (27%)
  starting transfers between devices  45.7 us (19%)
  blocking collectives  21 us (9%)
  between operations  14.2 us (6%)
  local copies, waits for them, and re-layouts  7.99 us (3%)
  other arithmetic  6.24 us (3%)
    ppermute x17, starting transfers between devices, hop(): return lax.ppermute(value, 'dp', shift_pairs(axis, step))  31.3 us
    ppermute x17, waiting for transfers between devices, hop(): return lax.ppermute(value, 'dp', shift_pairs(axis, step))  28.6 us
    ppermute x7, waiting for transfers between devices, across(): return lax.ppermute(value, 'mp', [(m, m ^ flip) for m in range(4)])  26.2 us
    all_to_all x1, waiting for transfers between devices, on_device(): lax.all_to_all(packed, 'dp', split_axis=0, concat_axis=0, tiled=True)  22.6 us
    all_to_all x1, blocking collectives, exchange_z(): lax.all_to_all(many, 'dp', 0, 0, tiled=True, axis_index_groups=groups)  21 us
    pallas_call x1, Pallas kernels, on_device(): pl.pallas_call(scan_kernel, out_shape=(jax.ShapeDtypeStruct((tokens, widt...  19.8 us
    pallas_call x1, Pallas kernels, on_device(): pl.pallas_call(gate_kernel, out_shape=(jax.ShapeDtypeStruct((2, tokens, p...  12.7 us
    all_to_all x1, starting transfers between devices, on_device(): lax.all_to_all(packed, 'dp', split_axis=0, concat_axis=0, tiled=True)  12.1 us
  transfers between devices with their start and end apart: 26, of which 13 were waited for; matrix products, arithmetic and copies ran while one was open for 3% of the time, Pallas kernels for 19%

profile of v5, /device:TPU:2, one launch (start us, length us, event | category | flops | bytes accessed | tf_op | source)
XLA Modules:
  0.0 236.0 jit_solution(944412788414549310)
XLA Ops:
  7.2 0.7 reshape.26
  7.9 0.9 fusion.1
  8.9 7.2 %collective-permute-start.1 = (bf16[48,1024]{1,0:T(8,128)(2,1)S(1)}, bf16[48,1024]{1,0:T(8,128)(2,1)S(1)}, u32[]{:S(2)}, u32[]{:S(2)}) collective-permute-start(bf16[48,1024]{1,0:T(8,128)(2,1)S(1)} %get-tuple-element.40), channel_id=1, source_target_pairs={{0,128},{4,132},{8,136},{12,140},{16,144},{20,148},{24,152},{28,15... | collective-permute-start | bytes 294920 | tf_op jit(solution)/shard_map/ppermute | solution.py:32
  16.1 2.9 %collective-permute-start.2 = (bf16[48,1024]{1,0:T(8,128)(2,1)S(1)}, bf16[48,1024]{1,0:T(8,128)(2,1)S(1)}, u32[]{:S(2)}, u32[]{:S(2)}) collective-permute-start(bf16[48,1024]{1,0:T(8,128)(2,1)S(1)} %get-tuple-element.40), channel_id=1, source_target_pairs={{0,64},{4,68},{8,72},{12,76},{16,80},{20,84},{24,88},{28,92},{32,9... | collective-permute-start | bytes 294920 | tf_op jit(solution)/shard_map/ppermute | solution.py:32
  19.0 0.9 pad_maximum_fusion.4
  20.0 5.8 %collective-permute-done = bf16[48,1024]{1,0:T(8,128)(2,1)S(1)} collective-permute-done((bf16[48,1024]{1,0:T(8,128)(2,1)S(1)}, bf16[48,1024]{1,0:T(8,128)(2,1)S(1)}, u32[]{:S(2)}, u32[]{:S(2)}) %collective-permute-start) | collective-permute-done | bytes 98336 | tf_op jit(solution)/shard_map/ppermute | solution.py:32
  25.9 21.0 %all_to_all.10 = bf16[4,64,1024]{2,1,0:T(8,128)(2,1)} all-to-all(bf16[4,64,1024]{2,1,0:T(8,128)(2,1)S(1)} %broadcast_in_dim.40), channel_id=1, replica_groups={{0,64,128,192},{4,68,132,196},{8,72,136,200},{12,76,140,204},{16,80,144..., dimensions={0} | all-to-all | bytes 1048576 | tf_op jit(solution)/shard_map/all_to_all | solution.py:60
  46.9 2.2 collective-permute-start.4
  49.2 1.4 collective-permute-start.3
  51.2 3.3 %collective-permute-start.7 = (bf16[4,32,640]{2,1,0:T(8,128)(2,1)S(1)}, bf16[4,32,640]{2,1,0:T(8,128)(2,1)S(1)}, u32[]{:S(2)}, u32[]{:S(2)}) collective-permute-start(bf16[4,32,640]{2,1,0:T(8,128)(2,1)S(1)} %get-tuple-element.36), channel_id=1, source_target_pairs={{0,32},{4,36},{8,40},{12,44},{16,48},{20,52},{24,56},{28,60},{32,0... | collective-permute-start | bytes 491528 | tf_op jit(solution)/shard_map/ppermute | solution.py:32
  54.5 1.1 collective-permute-start.6
  55.6 1.0 collective-permute-start.8
  56.7 1.4 collective-permute-done.7
  58.1 3.7 %collective-permute-done.6 = bf16[4,32,640]{2,1,0:T(8,128)(2,1)S(1)} collective-permute-done((bf16[4,32,640]{2,1,0:T(8,128)(2,1)S(1)}, bf16[4,32,640]{2,1,0:T(8,128)(2,1)S(1)}, u32[]{:S(2)}, u32[]{:S(2)}) %collective-permute-start.6) | collective-permute-done | bytes 163872 | tf_op jit(solution)/shard_map/ppermute | solution.py:32
  61.8 2.6 %collective-permute-done.8 = bf16[4,32,640]{2,1,0:T(8,128)(2,1)S(1)} collective-permute-done((bf16[4,32,640]{2,1,0:T(8,128)(2,1)S(1)}, bf16[4,32,640]{2,1,0:T(8,128)(2,1)S(1)}, u32[]{:S(2)}, u32[]{:S(2)}) %collective-permute-start.8) | collective-permute-done | bytes 163872 | tf_op jit(solution)/shard_map/ppermute | solution.py:32
  64.6 0.8 collective-permute-start.10
  65.4 2.8 %collective-permute-start.14 = (bf16[4,4,32,640]{3,2,1,0:T(8,128)(2,1)S(1)}, bf16[4,4,32,640]{3,2,1,0:T(8,128)(2,1)S(1)}, u32[]{:S(2)}, u32[]{:S(2)}) collective-permute-start(bf16[4,4,32,640]{3,2,1,0:T(8,128)(2,1)S(1)} %pad_maximum_fusion.b0), channel_id=1, source_target_pairs={{0,12},{4,0},{8,4},{12,8},{16,28},{20,16},{24,20},{28,24},{32,44},... | collective-permute-start | bytes 1966088 | tf_op jit(solution)/shard_map/ppermute | solution.py:32
  68.2 3.2 %collective-permute-start.12 = (bf16[4,4,48,384]{3,2,1,0:T(8,128)(2,1)S(1)}, bf16[4,4,48,384]{3,2,1,0:T(8,128)(2,1)S(1)}, u32[]{:S(2)}, u32[]{:S(2)}) collective-permute-start(bf16[4,4,48,384]{3,2,1,0:T(8,128)(2,1)S(1)} %pad_maximum_fusion.1.a0), channel_id=1, source_target_pairs={{0,48},{4,52},{8,56},{12,60},{16,0},{20,4},{24,8},{28,12},{32,16},... | collective-permute-start | bytes 1769480 | tf_op jit(solution)/shard_map/ppermute | solution.py:32
  71.4 2.6 %collective-permute-done.10.h2 = bf16[528,512]{1,0:T(8,128)(2,1)S(1)} collective-permute-done((bf16[528,512]{1,0:T(8,128)(2,1)S(1)}, bf16[528,512]{1,0:T(8,128)(2,1)S(1)}, u32[]{:S(2)}, u32[]{:S(2)}) %collective-permute-start.10) | collective-permute-done | bytes 540704 | tf_op jit(solution)/shard_map/ppermute | solution.py:36
  74.0 9.0 %collective-permute-done.15.b4 = bf16[4,4,32,640]{3,2,1,0:T(8,128)(2,1)S(1)} collective-permute-done((bf16[4,4,32,640]{3,2,1,0:T(8,128)(2,1)S(1)}, bf16[4,4,32,640]{3,2,1,0:T(8,128)(2,1)S(1)}, u32[]{:S(2)}, u32[]{:S(2)}) %collective-permute-start.15) | collective-permute-done | bytes 655392 | tf_op jit(solution)/shard_map/ppermute | solution.py:32
  83.0 0.8 slice.36
  83.8 1.4 collective-permute-start.18
  85.2 0.8 slice.37
  86.0 0.9 collective-permute-start.19
  86.9 0.7 slice.34
  87.7 0.8 slice.35
  88.5 3.2 %collective-permute-start.17 = (bf16[2,4,48,384]{3,2,1,0:T(8,128)(2,1)}, bf16[2,4,48,384]{3,2,1,0:T(8,128)(2,1)S(1)}, u32[]{:S(2)}, u32[]{:S(2)}) collective-permute-start(bf16[2,4,48,384]{3,2,1,0:T(8,128)(2,1)} %slice.35), channel_id=1, source_target_pairs={{0,48},{4,52},{8,56},{12,60},{16,0},{20,4},{24,8},{28,12},{32,16},... | collective-permute-start | bytes 884744 | tf_op jit(solution)/shard_map/ppermute | solution.py:32
  92.3 0.8 copy-done.8
  93.1 6.2 %prep.1.normed = bf16[4,512,512]{2,1,0:T(8,128)(2,1)} custom-call(bf16[528,512]{1,0:T(8,128)(2,1)} %copy-done.2, bf16[528,512]{1,0:T(8,128)(2,1)} %copy-done.7, bf16[528,512]{1,0:T(8,128)(2,1)} %copy-done.6, bf16[528,512]{1,0:T(8,128)(2,1)} %copy-done.8), custom_call_target="tpu_custom_call" | custom-call | flops 1000000 | bytes 1024 | tf_op jit(solution)/shard_map/prep/pallas_call | solution.py:446
  99.3 5.8 %collective-permute-done.16.a2 = bf16[2,4,48,384]{3,2,1,0:T(8,128)(2,1)} collective-permute-done((bf16[2,4,48,384]{3,2,1,0:T(8,128)(2,1)}, bf16[2,4,48,384]{3,2,1,0:T(8,128)(2,1)}, u32[]{:S(2)}, u32[]{:S(2)}) %collective-permute-start.16) | collective-permute-done | bytes 294944 | tf_op jit(solution)/shard_map/ppermute | solution.py:32
  105.4 0.7 broadcast_in_dim.36.accepted
  106.1 11.6 %front.1 = (bf16[512,1024]{1,0:T(8,128)(2,1)}, f32[160,512]{1,0:T(8,128)}, bf16[128,1024]{1,0:T(8,128)(2,1)}, f32[3,40,1024]{2,1,0:T(8,128)}) custom-call(s32[2]{0:T(128)} %pad_add_fusion.where, s32[32]{0:T(128)} %pages.5, s32[32,128]{1,0:T(8,128)} %broadcast_in_dim.36.accepted, bf16[4,512,512]{2,1,0:T(8,128)(2,1)} %prep.1.normed, ...), custom_call_target="tpu_custom_call" | custom-call | flops 12000000000 | bytes 1024 | tf_op jit(solution)/shard_map/front/pallas_call | solution.py:464
  117.8 1.8 collective-permute-done.20
  119.6 1.8 fusion.2
  122.0 5.6 %collective-permute-done.21.sums_b = bf16[160,512]{1,0:T(8,128)(2,1)S(1)} collective-permute-done((bf16[160,512]{1,0:T(8,128)(2,1)S(1)}, bf16[160,512]{1,0:T(8,128)(2,1)S(1)}, u32[]{:S(2)}, u32[]{:S(2)}) %collective-permute-start.21) | collective-permute-done | bytes 163872 | tf_op jit(solution)/shard_map/ppermute | solution.py:36
  128.3 19.8 %scan.1 = (f32[512,1024]{1,0:T(8,128)}, f32[8,512,128]{2,1,0:T(8,128)}) custom-call(s32[32]{0:T(128)} %pages.5, s32[32,128]{1,0:T(8,128)} %broadcast_in_dim.36.accepted, f32[160,512]{1,0:T(8,128)} %get-tuple-element.34.sums_a, bf16[160,512]{1,0:T(8,128)(2,1)} %copy-done.10, bf16[128,1024]{1,0:T(8,128)(2,1)} %get-tuple-element.26.dt, f32[1,1024]{1,0:T(1,128)} %bitcast.46, ...), custom_call_target="tpu_custom_call" | custom-call | flops 1000000 | bytes 1024 | tf_op jit(solution)/shard_map/scan/pallas_call | solution.py:494
  148.1 12.7 %gate.1 = (bf16[2,512,512]{2,1,0:T(8,128)(2,1)}, f32[2,512,512]{2,1,0:T(8,128)}) custom-call(s32[2]{0:T(128)} %pad_add_fusion.where, bf16[4,512,512]{2,1,0:T(8,128)(2,1)} %prep.1.normed, bf16[512,1024]{1,0:T(8,128)(2,1)} %get-tuple-element.24.inputs, f32[512,1024]{1,0:T(8,128)} %get-tuple-element.27.ys, f32[1,1024]{1,0:T(1,128)} %bitcast.45, ...), custom_call_target="tpu_custom_call" | custom-call | flops 1000000 | bytes 1024 | tf_op jit(solution)/shard_map/gate/pallas_call | solution.py:529
  160.9 2.9 %collective-permute-done.22.near = bf16[2,512,512]{2,1,0:T(8,128)(2,1)S(1)} collective-permute-done((bf16[2,512,512]{2,1,0:T(8,128)(2,1)}, bf16[2,512,512]{2,1,0:T(8,128)(2,1)S(1)}, u32[]{:S(2)}, u32[]{:S(2)}) %collective-permute-start.22) | collective-permute-done | bytes 1048608 | tf_op jit(solution)/shard_map/ppermute | solution.py:36
  163.8 1.8 fusion
  165.5 0.7 collective-permute-start.23
  166.2 13.3 %collective-permute-done.23.far = bf16[512,512]{1,0:T(8,128)(2,1)S(1)} collective-permute-done((bf16[512,512]{1,0:T(8,128)(2,1)S(1)}, bf16[512,512]{1,0:T(8,128)(2,1)S(1)}, u32[]{:S(2)}, u32[]{:S(2)}) %collective-permute-start.23) | collective-permute-done | bytes 524320 | tf_op jit(solution)/shard_map/ppermute | solution.py:36
  179.6 0.8 copy-done.9
  180.4 4.2 %join.1 = bf16[64,16,512]{2,1,0:T(8,128)(2,1)} custom-call(s32[32]{0:T(128)} %targets.3, f32[2,512,512]{2,1,0:T(8,128)} %get-tuple-element.29.keep, bf16[2,512,512]{2,1,0:T(8,128)(2,1)} %copy-done.1, bf16[512,512]{1,0:T(8,128)(2,1)} %copy-done.9, bf16[512,512]{1,0:T(8,128)(2,1)} %bitcast.33), custom_call_target="tpu_custom_call" | custom-call | flops 1000000 | bytes 1024 | tf_op jit(solution)/shard_map/join/pallas_call | solution.py:549
  184.6 12.1 %all-to-all-start.1 = ((bf16[64,16,512]{2,1,0:T(8,128)(2,1)}), bf16[64,16,512]{2,1,0:T(8,128)(2,1)S(1)}, u32[]{:S(2)}, u32[]{:S(2)}) async-start(bf16[64,16,512]{2,1,0:T(8,128)(2,1)} %join.1), calls=%async_computation.1 | async-start | bytes 2097152 | tf_op jit(solution)/shard_map/all_to_all | solution.py:559
  196.7 6.4 %settle.1 = f32[640,1024]{1,0:T(8,128)} custom-call(s32[32]{0:T(128)} %pages.5, f32[8,512,128]{2,1,0:T(8,128)} %get-tuple-element.31.kept, f32[640,1024]{1,0:T(8,128)} %bitcast.30), custom_call_target="tpu_custom_call" | custom-call | flops 1000000 | bytes 1024 | tf_op jit(solution)/shard_map/settle/pallas_call | solution.py:519
  203.1 22.6 %all-to-all-done.1.got = bf16[64,16,512]{2,1,0:T(8,128)(2,1)S(1)} async-done(((bf16[64,16,512]{2,1,0:T(8,128)(2,1)}), bf16[64,16,512]{2,1,0:T(8,128)(2,1)S(1)}, u32[]{:S(2)}, u32[]{:S(2)}) %all-to-all-start.1) | async-done | bytes 1048608 | tf_op jit(solution)/shard_map/all_to_all | solution.py:559
  225.7 1.0 copy-done
  226.7 2.4 %unpack.1 = bf16[32,16,512]{2,1,0:T(8,128)(2,1)} custom-call(s32[2]{0:T(128)} %pad_add_fusion.where, s32[32]{0:T(128)} %targets.3, bf16[64,16,512]{2,1,0:T(8,128)(2,1)} %copy-done), custom_call_target="tpu_custom_call" | custom-call | tf_op jit(solution)/shard_map/unpack/pallas_call | solution.py:560
  (70 shorter events, 3.5 us)
Async XLA Ops:
  7.2 140.9 %all-gather.3.cloned.1.call-start = ((), (), s32[]{:S(2)}) async-start(), calls=%async_computation.2 | async-start | bytes 8912896 | tf_op jit(solution)/shard_map/all_gather | solution.py:458
  8.9 11.1 %collective-permute-start.1 = (bf16[48,1024]{1,0:T(8,128)(2,1)S(1)}, bf16[48,1024]{1,0:T(8,128)(2,1)S(1)}, u32[]{:S(2)}, u32[]{:S(2)}) collective-permute-start(bf16[48,1024]{1,0:T(8,128)(2,1)S(1)} %get-tuple-element.40), channel_id=1, source_target_pairs={{0,128},{4,132},{8,136},{12,140},{16,144},{20,148},{24,152},{28,15... | collective-permute-start | bytes 294920 | tf_op jit(solution)/shard_map/ppermute | solution.py:32
  16.1 9.7 %collective-permute-start = (bf16[48,1024]{1,0:T(8,128)(2,1)S(1)}, bf16[48,1024]{1,0:T(8,128)(2,1)S(1)}, u32[]{:S(2)}, u32[]{:S(2)}) collective-permute-start(bf16[48,1024]{1,0:T(8,128)(2,1)S(1)} %get-tuple-element.40), channel_id=1, source_target_pairs={{0,192},{4,196},{8,200},{12,204},{16,208},{20,212},{24,216},{28,22... | collective-permute-start | bytes 294920 | tf_op jit(solution)/shard_map/ppermute | solution.py:32
  16.1 9.7 %collective-permute-start.2 = (bf16[48,1024]{1,0:T(8,128)(2,1)S(1)}, bf16[48,1024]{1,0:T(8,128)(2,1)S(1)}, u32[]{:S(2)}, u32[]{:S(2)}) collective-permute-start(bf16[48,1024]{1,0:T(8,128)(2,1)S(1)} %get-tuple-element.40), channel_id=1, source_target_pairs={{0,64},{4,68},{8,72},{12,76},{16,80},{20,84},{24,88},{28,92},{32,9... | collective-permute-start | bytes 294920 | tf_op jit(solution)/shard_map/ppermute | solution.py:32
  19.0 37.5 %copy-start.15 = (bf16[512]{0:T(512)(128)(2,1)S(1)}, bf16[512]{0:T(512)(128)(2,1)}, u32[]{:S(2)}) copy-start(bf16[512]{0:T(512)(128)(2,1)} %param.18) | copy-start | bytes 3076
  19.0 37.5 %copy-start.3 = (bf16[32,16,512]{2,1,0:T(8,128)(2,1)S(1)}, bf16[32,16,512]{2,1,0:T(8,128)(2,1)}, u32[]{:S(2)}) copy-start(bf16[32,16,512]{2,1,0:T(8,128)(2,1)} %param.17) | copy-start | bytes 1572868
  46.9 8.6 %collective-permute-start.4 = (bf16[4,48,384]{2,1,0:T(8,128)(2,1)S(1)}, bf16[4,48,384]{2,1,0:T(8,128)(2,1)S(1)}, u32[]{:S(2)}, u32[]{:S(2)}) collective-permute-start(bf16[4,48,384]{2,1,0:T(8,128)(2,1)S(1)} %get-tuple-element.38), channel_id=1, source_target_pairs={{0,8},{4,12},{8,0},{12,4},{16,24},{20,28},{24,16},{28,20},{32,40},... | collective-permute-start | bytes 442376 | tf_op jit(solution)/shard_map/ppermute | solution.py:32
  49.2 7.4 %collective-permute-start.3 = (bf16[4,48,384]{2,1,0:T(8,128)(2,1)S(1)}, bf16[4,48,384]{2,1,0:T(8,128)(2,1)S(1)}, u32[]{:S(2)}, u32[]{:S(2)}) collective-permute-start(bf16[4,48,384]{2,1,0:T(8,128)(2,1)S(1)} %get-tuple-element.38), channel_id=1, source_target_pairs={{0,12},{4,0},{8,4},{12,8},{16,28},{20,16},{24,20},{28,24},{32,44},... | collective-permute-start | bytes 442376 | tf_op jit(solution)/shard_map/ppermute | solution.py:32
  50.6 6.0 %collective-permute-start.5 = (bf16[4,48,384]{2,1,0:T(8,128)(2,1)S(1)}, bf16[4,48,384]{2,1,0:T(8,128)(2,1)S(1)}, u32[]{:S(2)}, u32[]{:S(2)}) collective-permute-start(bf16[4,48,384]{2,1,0:T(8,128)(2,1)S(1)} %get-tuple-element.38), channel_id=1, source_target_pairs={{0,4},{4,8},{8,12},{12,0},{16,20},{20,24},{24,28},{28,16},{32,36},... | collective-permute-start | bytes 442376 | tf_op jit(solution)/shard_map/ppermute | solution.py:32
  51.2 6.9 %collective-permute-start.7 = (bf16[4,32,640]{2,1,0:T(8,128)(2,1)S(1)}, bf16[4,32,640]{2,1,0:T(8,128)(2,1)S(1)}, u32[]{:S(2)}, u32[]{:S(2)}) collective-permute-start(bf16[4,32,640]{2,1,0:T(8,128)(2,1)S(1)} %get-tuple-element.36), channel_id=1, source_target_pairs={{0,32},{4,36},{8,40},{12,44},{16,48},{20,52},{24,56},{28,60},{32,0... | collective-permute-start | bytes 491528 | tf_op jit(solution)/shard_map/ppermute | solution.py:32
  54.5 7.3 %collective-permute-start.6 = (bf16[4,32,640]{2,1,0:T(8,128)(2,1)S(1)}, bf16[4,32,640]{2,1,0:T(8,128)(2,1)S(1)}, u32[]{:S(2)}, u32[]{:S(2)}) collective-permute-start(bf16[4,32,640]{2,1,0:T(8,128)(2,1)S(1)} %get-tuple-element.36), channel_id=1, source_target_pairs={{0,48},{4,52},{8,56},{12,60},{16,0},{20,4},{24,8},{28,12},{32,16},... | collective-permute-start | bytes 491528 | tf_op jit(solution)/shard_map/ppermute | solution.py:32
  55.6 8.9 %collective-permute-start.8 = (bf16[4,32,640]{2,1,0:T(8,128)(2,1)S(1)}, bf16[4,32,640]{2,1,0:T(8,128)(2,1)S(1)}, u32[]{:S(2)}, u32[]{:S(2)}) collective-permute-start(bf16[4,32,640]{2,1,0:T(8,128)(2,1)S(1)} %get-tuple-element.36), channel_id=1, source_target_pairs={{0,16},{4,20},{8,24},{12,28},{16,32},{20,36},{24,40},{28,44},{32,4... | collective-permute-start | bytes 491528 | tf_op jit(solution)/shard_map/ppermute | solution.py:32
  56.6 31.0 %copy-start.2 = (bf16[528,512]{1,0:T(8,128)(2,1)}, bf16[528,512]{1,0:T(8,128)(2,1)S(1)}, u32[]{:S(2)}) copy-start(bf16[528,512]{1,0:T(8,128)(2,1)S(1)} %pad_maximum_fusion.2.h0) | copy-start | bytes 1622020
  56.7 42.6 %copy-start.5 = (bf16[4,4,48,384]{3,2,1,0:T(8,128)(2,1)}, bf16[4,4,48,384]{3,2,1,0:T(8,128)(2,1)S(1)}, u32[]{:S(2)}) copy-start(bf16[4,4,48,384]{3,2,1,0:T(8,128)(2,1)S(1)} %pad_maximum_fusion.1.a0) | copy-start | bytes 1769476
  64.5 34.8 %copy-start.4 = (bf16[4,4,32,640]{3,2,1,0:T(8,128)(2,1)}, bf16[4,4,32,640]{3,2,1,0:T(8,128)(2,1)S(1)}, u32[]{:S(2)}) copy-start(bf16[4,4,32,640]{3,2,1,0:T(8,128)(2,1)S(1)} %pad_maximum_fusion.b0) | copy-start | bytes 1966084
  64.6 9.4 %collective-permute-start.10 = (bf16[528,512]{1,0:T(8,128)(2,1)S(1)}, bf16[528,512]{1,0:T(8,128)(2,1)S(1)}, u32[]{:S(2)}, u32[]{:S(2)}) collective-permute-start(bf16[528,512]{1,0:T(8,128)(2,1)S(1)} %pad_maximum_fusion.2.h0), channel_id=1, source_target_pairs={{0,2},{1,3},{2,0},{3,1},{4,6},{5,7},{6,4},{7,5},{8,10},{9,11},{10,... | collective-permute-start | bytes 1622024 | tf_op jit(solution)/shard_map/ppermute | solution.py:36
  65.4 17.7 %collective-permute-start.15 = (bf16[4,4,32,640]{3,2,1,0:T(8,128)(2,1)S(1)}, bf16[4,4,32,640]{3,2,1,0:T(8,128)(2,1)S(1)}, u32[]{:S(2)}, u32[]{:S(2)}) collective-permute-start(bf16[4,4,32,640]{3,2,1,0:T(8,128)(2,1)S(1)} %pad_maximum_fusion.b0), channel_id=1, source_target_pairs={{0,4},{4,8},{8,12},{12,0},{16,20},{20,24},{24,28},{28,16},{32,36},... | collective-permute-start | bytes 1966088 | tf_op jit(solution)/shard_map/ppermute | solution.py:32
  65.4 18.5 %collective-permute-start.14 = (bf16[4,4,32,640]{3,2,1,0:T(8,128)(2,1)S(1)}, bf16[4,4,32,640]{3,2,1,0:T(8,128)(2,1)S(1)}, u32[]{:S(2)}, u32[]{:S(2)}) collective-permute-start(bf16[4,4,32,640]{3,2,1,0:T(8,128)(2,1)S(1)} %pad_maximum_fusion.b0), channel_id=1, source_target_pairs={{0,12},{4,0},{8,4},{12,8},{16,28},{20,16},{24,20},{28,24},{32,44},... | collective-permute-start | bytes 1966088 | tf_op jit(solution)/shard_map/ppermute | solution.py:32
  68.2 17.8 %collective-permute-start.13 = (bf16[4,4,48,384]{3,2,1,0:T(8,128)(2,1)S(1)}, bf16[4,4,48,384]{3,2,1,0:T(8,128)(2,1)S(1)}, u32[]{:S(2)}, u32[]{:S(2)}) collective-permute-start(bf16[4,4,48,384]{3,2,1,0:T(8,128)(2,1)S(1)} %pad_maximum_fusion.1.a0), channel_id=1, source_target_pairs={{0,16},{4,20},{8,24},{12,28},{16,32},{20,36},{24,40},{28,44},{32,4... | collective-permute-start | bytes 1769480 | tf_op jit(solution)/shard_map/ppermute | solution.py:32
  68.2 19.4 %collective-permute-start.12 = (bf16[4,4,48,384]{3,2,1,0:T(8,128)(2,1)S(1)}, bf16[4,4,48,384]{3,2,1,0:T(8,128)(2,1)S(1)}, u32[]{:S(2)}, u32[]{:S(2)}) collective-permute-start(bf16[4,4,48,384]{3,2,1,0:T(8,128)(2,1)S(1)} %pad_maximum_fusion.1.a0), channel_id=1, source_target_pairs={{0,48},{4,52},{8,56},{12,60},{16,0},{20,4},{24,8},{28,12},{32,16},... | collective-permute-start | bytes 1769480 | tf_op jit(solution)/shard_map/ppermute | solution.py:32
  74.0 18.3 %copy-start.6 = (bf16[528,512]{1,0:T(8,128)(2,1)}, bf16[528,512]{1,0:T(8,128)(2,1)S(1)}, u32[]{:S(2)}) copy-start(bf16[528,512]{1,0:T(8,128)(2,1)S(1)} %collective-permute-done.10.h2) | copy-start | bytes 1622020
  74.0 14.5 %collective-permute-start.9 = (bf16[528,512]{1,0:T(8,128)(2,1)S(1)}, bf16[528,512]{1,0:T(8,128)(2,1)S(1)}, u32[]{:S(2)}, u32[]{:S(2)}) collective-permute-start(bf16[528,512]{1,0:T(8,128)(2,1)S(1)} %pad_maximum_fusion.2.h0), channel_id=1, source_target_pairs={{0,1},{1,0},{2,3},{3,2},{4,5},{5,4},{6,7},{7,6},{8,9},{9,8},{10,11... | collective-permute-start | bytes 1622024 | tf_op jit(solution)/shard_map/ppermute | solution.py:36
  83.0 5.5 %copy-start.11 = (bf16[4,4,32,640]{3,2,1,0:T(8,128)(2,1)}, bf16[4,4,32,640]{3,2,1,0:T(8,128)(2,1)S(1)}, u32[]{:S(2)}) copy-start(bf16[4,4,32,640]{3,2,1,0:T(8,128)(2,1)S(1)} %collective-permute-done.15.b4) | copy-start | bytes 1966084
  83.0 9.3 %collective-permute-start.11 = (bf16[528,512]{1,0:T(8,128)(2,1)S(1)}, bf16[528,512]{1,0:T(8,128)(2,1)S(1)}, u32[]{:S(2)}, u32[]{:S(2)}) collective-permute-start(bf16[528,512]{1,0:T(8,128)(2,1)S(1)} %collective-permute-done.10.h2), channel_id=1, source_target_pairs={{0,1},{1,0},{2,3},{3,2},{4,5},{5,4},{6,7},{7,6},{8,9},{9,8},{10,11... | collective-permute-start | bytes 1622024 | tf_op jit(solution)/shard_map/ppermute | solution.py:36
  83.8 7.9 %copy-start.12 = (bf16[4,4,32,640]{3,2,1,0:T(8,128)(2,1)}, bf16[4,4,32,640]{3,2,1,0:T(8,128)(2,1)S(1)}, u32[]{:S(2)}) copy-start(bf16[4,4,32,640]{3,2,1,0:T(8,128)(2,1)S(1)} %collective-permute-done.14.b1) | copy-start | bytes 1966084
  83.8 21.5 %collective-permute-start.18 = (bf16[2,4,32,640]{3,2,1,0:T(8,128)(2,1)}, bf16[2,4,32,640]{3,2,1,0:T(8,128)(2,1)}, u32[]{:S(2)}, u32[]{:S(2)}) collective-permute-start(bf16[2,4,32,640]{3,2,1,0:T(8,128)(2,1)} %slice.36), channel_id=1, source_target_pairs={{0,4},{4,8},{8,12},{12,0},{16,20},{20,24},{24,28},{28,16},{32,36},... | collective-permute-start | bytes 983048 | tf_op jit(solution)/shard_map/ppermute | solution.py:32
  86.0 5.8 %copy-start.13 = (bf16[4,4,48,384]{3,2,1,0:T(8,128)(2,1)}, bf16[4,4,48,384]{3,2,1,0:T(8,128)(2,1)S(1)}, u32[]{:S(2)}) copy-start(bf16[4,4,48,384]{3,2,1,0:T(8,128)(2,1)S(1)} %collective-permute-done.13.a4) | copy-start | bytes 1769476
  86.0 19.4 %collective-permute-start.19 = (bf16[2,4,32,640]{3,2,1,0:T(8,128)(2,1)}, bf16[2,4,32,640]{3,2,1,0:T(8,128)(2,1)}, u32[]{:S(2)}, u32[]{:S(2)}) collective-permute-start(bf16[2,4,32,640]{3,2,1,0:T(8,128)(2,1)} %slice.37), channel_id=1, source_target_pairs={{0,12},{4,0},{8,4},{12,8},{16,28},{20,16},{24,20},{28,24},{32,44},... | collective-permute-start | bytes 983048 | tf_op jit(solution)/shard_map/ppermute | solution.py:32
  87.6 4.1 %copy-start.14 = (bf16[4,4,48,384]{3,2,1,0:T(8,128)(2,1)}, bf16[4,4,48,384]{3,2,1,0:T(8,128)(2,1)S(1)}, u32[]{:S(2)}) copy-start(bf16[4,4,48,384]{3,2,1,0:T(8,128)(2,1)S(1)} %collective-permute-done.12.a1) | copy-start | bytes 1769476
  87.6 17.5 %collective-permute-start.16 = (bf16[2,4,48,384]{3,2,1,0:T(8,128)(2,1)}, bf16[2,4,48,384]{3,2,1,0:T(8,128)(2,1)}, u32[]{:S(2)}, u32[]{:S(2)}) collective-permute-start(bf16[2,4,48,384]{3,2,1,0:T(8,128)(2,1)} %slice.34), channel_id=1, source_target_pairs={{0,16},{4,20},{8,24},{12,28},{16,32},{20,36},{24,40},{28,44},{32,4... | collective-permute-start | bytes 884744 | tf_op jit(solution)/shard_map/ppermute | solution.py:32
  88.5 3.8 %copy-start.7 = (bf16[528,512]{1,0:T(8,128)(2,1)}, bf16[528,512]{1,0:T(8,128)(2,1)S(1)}, u32[]{:S(2)}) copy-start(bf16[528,512]{1,0:T(8,128)(2,1)S(1)} %collective-permute-done.9.h1) | copy-start | bytes 1622020
  88.5 16.8 %collective-permute-start.17 = (bf16[2,4,48,384]{3,2,1,0:T(8,128)(2,1)}, bf16[2,4,48,384]{3,2,1,0:T(8,128)(2,1)S(1)}, u32[]{:S(2)}, u32[]{:S(2)}) collective-permute-start(bf16[2,4,48,384]{3,2,1,0:T(8,128)(2,1)} %slice.35), channel_id=1, source_target_pairs={{0,48},{4,52},{8,56},{12,60},{16,0},{20,4},{24,8},{28,12},{32,16},... | collective-permute-start | bytes 884744 | tf_op jit(solution)/shard_map/ppermute | solution.py:32
  92.3 13.1 %copy-start.16 = (s32[32]{0:T(128)S(1)}, s32[32]{0:T(128)}, u32[]{:S(2)}) copy-start(s32[32]{0:T(128)} %param.33) | copy-start | bytes 388
  92.3 0.8 copy-start.8
  105.4 0.7 copy-start.17
  117.7 1.9 collective-permute-start.20
  121.4 6.2 %collective-permute-start.21 = (bf16[160,512]{1,0:T(8,128)(2,1)S(1)}, bf16[160,512]{1,0:T(8,128)(2,1)S(1)}, u32[]{:S(2)}, u32[]{:S(2)}) collective-permute-start(bf16[160,512]{1,0:T(8,128)(2,1)S(1)} %get-tuple-element.33), channel_id=1, source_target_pairs={{0,2},{1,3},{2,0},{3,1},{4,6},{5,7},{6,4},{7,5},{8,10},{9,11},{10,... | collective-permute-start | bytes 491528 | tf_op jit(solution)/shard_map/ppermute | solution.py:36
  127.6 0.7 copy-start.10
  160.8 3.0 %collective-permute-start.22 = (bf16[2,512,512]{2,1,0:T(8,128)(2,1)}, bf16[2,512,512]{2,1,0:T(8,128)(2,1)S(1)}, u32[]{:S(2)}, u32[]{:S(2)}) collective-permute-start(bf16[2,512,512]{2,1,0:T(8,128)(2,1)} %get-tuple-element.30), channel_id=1, source_target_pairs={{0,1},{1,0},{2,3},{3,2},{4,5},{5,4},{6,7},{7,6},{8,9},{9,8},{10,11... | collective-permute-start | bytes 3145736 | tf_op jit(solution)/shard_map/ppermute | solution.py:36
  163.8 15.8 %copy-start.1 = (bf16[2,512,512]{2,1,0:T(8,128)(2,1)}, bf16[2,512,512]{2,1,0:T(8,128)(2,1)S(1)}, u32[]{:S(2)}) copy-start(bf16[2,512,512]{2,1,0:T(8,128)(2,1)S(1)} %collective-permute-done.22.near) | copy-start | bytes 3145732
  165.5 14.1 %collective-permute-start.23 = (bf16[512,512]{1,0:T(8,128)(2,1)S(1)}, bf16[512,512]{1,0:T(8,128)(2,1)S(1)}, u32[]{:S(2)}, u32[]{:S(2)}) collective-permute-start(bf16[512,512]{1,0:T(8,128)(2,1)S(1)} %fusion), channel_id=1, source_target_pairs={{0,2},{1,3},{2,0},{3,1},{4,6},{5,7},{6,4},{7,5},{8,10},{9,11},{10,... | collective-permute-start | bytes 1572872 | tf_op jit(solution)/shard_map/ppermute | solution.py:36
  179.6 0.8 copy-start.9
  184.6 41.1 %all-to-all-start.1 = ((bf16[64,16,512]{2,1,0:T(8,128)(2,1)}), bf16[64,16,512]{2,1,0:T(8,128)(2,1)S(1)}, u32[]{:S(2)}, u32[]{:S(2)}) async-start(bf16[64,16,512]{2,1,0:T(8,128)(2,1)} %join.1), calls=%async_computation.1 | async-start | bytes 2097152 | tf_op jit(solution)/shard_map/all_to_all | solution.py:559
  225.7 1.0 copy-start
Sparse Core Ops, SparseCore 0:
  47.0 83.3 all-gather.2

commit v6 on v5

--- a/solution.py
+++ b/solution.py
@@ -52,12 +52,6 @@
 
 def send_direct(block, axis):
     return block, hop(block, axis, -1), hop(block, axis, 2), hop(block, axis, 1)
-
-
-def exchange_z(block):
-    groups = [[z * SIDE * SIDE + i for z in range(SIDE)] for i in range(SIDE * SIDE)]
-    many = jnp.broadcast_to(block[None], (SIDE, *block.shape))
-    return lax.all_to_all(many, "dp", 0, 0, tiled=True, axis_index_groups=groups)
 
 
 def direct(block, axis):
@@ -337,9 +331,9 @@
     m = where[1]
     tokens, width = gated.shape
     for z in range(SIDE):
-        pltpu.make_async_copy(second.at[:, z, pl.ds(0, 32), :], weight.at[z], sems.at[0]).start()
+        pltpu.make_async_copy(second.at[z, :, pl.ds(0, 32), :], weight.at[z], sems.at[0]).start()
     for z in range(SIDE):
-        pltpu.make_async_copy(second.at[:, z, pl.ds(32, 32), :], outer.at[z], sems.at[1]).start()
+        pltpu.make_async_copy(second.at[z, :, pl.ds(32, 32), :], outer.at[z], sems.at[1]).start()
     pltpu.make_async_copy(weight, weight, sems.at[0]).wait()
 
     def gate(n, _):
@@ -454,11 +448,8 @@
         name="prep",
     )(sent, *after((near, far, both), sides_a, sides_b))
 
-    pair = after(jnp.concatenate([in_z, out_proj.T], axis=0), first)
-    second = lax.all_gather(
-        exchange_z(pair), "dp", axis=0,
-        axis_index_groups=[[z * 16 + i for i in range(16)] for z in range(SIDE)],
-    )
+    pair = jnp.concatenate([in_z, out_proj.T], axis=0)
+    second = lax.all_gather(pair, "dp", axis=0).reshape(SIDE, 16, 64, width)
 
     wide_accepted = jnp.broadcast_to(accepted[:, None], (count, 128))
     inputs, sums, dt, new_conv = pl.pallas_call(

time: 237 us -> 238 us (level)
  blocking collectives: 21 us -> 0 us
  waiting for transfers between devices: 77.4 us -> 93.6 us
    ppermute x7, waiting for transfers between devices: 26.2 us -> 56.7 us  [across(): return lax.ppermute(value, 'mp', [(m, m ^ flip) for m in range(4)])]
    all_to_all x1 -> x0, blocking collectives: 21 us -> none  [exchange_z(): lax.all_to_all(many, 'dp', 0, 0, tiled=True, axis_index_groups=groups)]
    ppermute x17, waiting for transfers between devices: 28.6 us -> 15.7 us  [hop(): return lax.ppermute(value, 'dp', shift_pairs(axis, step))]
    all_to_all x1, starting transfers between devices: 12.1 us -> 14.6 us  [on_device(): lax.all_to_all(packed, 'dp', split_axis=0, concat_axis=0, tiled=True)]
  transfers between devices with their start and end apart: 26 -> 26, of which waited for: 13 -> 13; matrix products, arithmetic and copies ran while one was open for 3% -> 4% of each run, Pallas kernels for 19% -> 19%
where the time goes in v6:
time: 238 us; the launch traced here: 235 us
  waiting for transfers between devices  93.6 us (39%)
  Pallas kernels  63.3 us (27%)
  starting transfers between devices  47.1 us (20%)
  between operations  14.2 us (6%)
  local copies, waits for them, and re-layouts  8.56 us (4%)
  other arithmetic  7.97 us (3%)
    ppermute x7, waiting for transfers between devices, across(): return lax.ppermute(value, 'mp', [(m, m ^ flip) for m in range(4)])  56.7 us
    ppermute x17, starting transfers between devices, hop(): return lax.ppermute(value, 'dp', shift_pairs(axis, step))  30.1 us
    all_to_all x1, waiting for transfers between devices, on_device(): lax.all_to_all(packed, 'dp', split_axis=0, concat_axis=0, tiled=True)  21.2 us
    pallas_call x1, Pallas kernels, on_device(): pl.pallas_call(scan_kernel, out_shape=(jax.ShapeDtypeStruct((tokens, widt...  19.8 us
    ppermute x17, waiting for transfers between devices, hop(): return lax.ppermute(value, 'dp', shift_pairs(axis, step))  15.7 us
    all_to_all x1, starting transfers between devices, on_device(): lax.all_to_all(packed, 'dp', split_axis=0, concat_axis=0, tiled=True)  14.6 us
    pallas_call x1, Pallas kernels, on_device(): pl.pallas_call(gate_kernel, out_shape=(jax.ShapeDtypeStruct((2, tokens, p...  12.7 us
    pallas_call x1, Pallas kernels, on_device(): pl.pallas_call(front_kernel, out_shape=(jax.ShapeDtypeStruct((tokens, wid...  11.5 us
  transfers between devices with their start and end apart: 26, of which 13 were waited for; matrix products, arithmetic and copies ran while one was open for 4% of the time, Pallas kernels for 19%

profile of v6, /device:TPU:2, one launch (start us, length us, event | category | flops | bytes accessed | tf_op | source)
XLA Modules:
  0.0 234.8 jit_solution(13108381617587208394)
XLA Ops:
  7.2 1.5 pad_maximum_fusion.7
  8.8 0.7 reshape.28
  9.5 0.9 fusion.1
  10.4 7.2 %collective-permute-start.1 = (bf16[48,1024]{1,0:T(8,128)(2,1)S(1)}, bf16[48,1024]{1,0:T(8,128)(2,1)S(1)}, u32[]{:S(2)}, u32[]{:S(2)}) collective-permute-start(bf16[48,1024]{1,0:T(8,128)(2,1)S(1)} %get-tuple-element.34), channel_id=1, source_target_pairs={{0,128},{4,132},{8,136},{12,140},{16,144},{20,148},{24,152},{28,15... | collective-permute-start | bytes 294920 | tf_op jit(solution)/shard_map/ppermute | solution.py:32
  17.6 2.9 %collective-permute-start.2 = (bf16[48,1024]{1,0:T(8,128)(2,1)S(1)}, bf16[48,1024]{1,0:T(8,128)(2,1)S(1)}, u32[]{:S(2)}, u32[]{:S(2)}) collective-permute-start(bf16[48,1024]{1,0:T(8,128)(2,1)S(1)} %get-tuple-element.34), channel_id=1, source_target_pairs={{0,64},{4,68},{8,72},{12,76},{16,80},{20,84},{24,88},{28,92},{32,9... | collective-permute-start | bytes 294920 | tf_op jit(solution)/shard_map/ppermute | solution.py:32
  20.6 0.7 broadcast_in_dim.27
  21.2 1.1 pad_maximum_fusion.2.h0
  22.3 5.0 %collective-permute-done = bf16[48,1024]{1,0:T(8,128)(2,1)S(1)} collective-permute-done((bf16[48,1024]{1,0:T(8,128)(2,1)S(1)}, bf16[48,1024]{1,0:T(8,128)(2,1)S(1)}, u32[]{:S(2)}, u32[]{:S(2)}) %collective-permute-start) | collective-permute-done | bytes 98336 | tf_op jit(solution)/shard_map/ppermute | solution.py:32
  27.3 2.2 collective-permute-start.4
  29.5 1.4 collective-permute-start.3
  31.6 3.1 %collective-permute-start.6 = (bf16[4,32,640]{2,1,0:T(8,128)(2,1)S(1)}, bf16[4,32,640]{2,1,0:T(8,128)(2,1)S(1)}, u32[]{:S(2)}, u32[]{:S(2)}) collective-permute-start(bf16[4,32,640]{2,1,0:T(8,128)(2,1)S(1)} %pad_maximum_fusion.3), channel_id=1, source_target_pairs={{0,48},{4,52},{8,56},{12,60},{16,0},{20,4},{24,8},{28,12},{32,16},... | collective-permute-start | bytes 491528 | tf_op jit(solution)/shard_map/ppermute | solution.py:32
  35.8 1.6 collective-permute-start.8
  37.4 1.0 collective-permute-done.3
  38.5 3.1 %collective-permute-done.6 = bf16[4,32,640]{2,1,0:T(8,128)(2,1)S(1)} collective-permute-done((bf16[4,32,640]{2,1,0:T(8,128)(2,1)S(1)}, bf16[4,32,640]{2,1,0:T(8,128)(2,1)S(1)}, u32[]{:S(2)}, u32[]{:S(2)}) %collective-permute-start.6) | collective-permute-done | bytes 163872 | tf_op jit(solution)/shard_map/ppermute | solution.py:32
  41.6 2.0 collective-permute-done.7
  43.6 1.7 collective-permute-done.8
  46.1 1.6 collective-permute-start.14
  47.7 3.2 %collective-permute-start.12 = (bf16[4,4,48,384]{3,2,1,0:T(8,128)(2,1)S(1)}, bf16[4,4,48,384]{3,2,1,0:T(8,128)(2,1)S(1)}, u32[]{:S(2)}, u32[]{:S(2)}) collective-permute-start(bf16[4,4,48,384]{3,2,1,0:T(8,128)(2,1)S(1)} %pad_maximum_fusion.1.a0), channel_id=1, source_target_pairs={{0,48},{4,52},{8,56},{12,60},{16,0},{20,4},{24,8},{28,12},{32,16},... | collective-permute-start | bytes 1769480 | tf_op jit(solution)/shard_map/ppermute | solution.py:32
  50.9 17.0 %collective-permute-done.10.h2 = bf16[528,512]{1,0:T(8,128)(2,1)S(1)} collective-permute-done((bf16[528,512]{1,0:T(8,128)(2,1)S(1)}, bf16[528,512]{1,0:T(8,128)(2,1)S(1)}, u32[]{:S(2)}, u32[]{:S(2)}) %collective-permute-start.10) | collective-permute-done | bytes 540704 | tf_op jit(solution)/shard_map/ppermute | solution.py:36
  68.5 0.8 slice.34
  69.2 0.8 slice.35
  70.0 2.0 collective-permute-start.19
  72.0 0.7 slice.32
  72.8 0.8 slice.33
  73.6 3.2 %collective-permute-start.17 = (bf16[2,4,48,384]{3,2,1,0:T(8,128)(2,1)}, bf16[2,4,48,384]{3,2,1,0:T(8,128)(2,1)S(1)}, u32[]{:S(2)}, u32[]{:S(2)}) collective-permute-start(bf16[2,4,48,384]{3,2,1,0:T(8,128)(2,1)} %slice.33), channel_id=1, source_target_pairs={{0,48},{4,52},{8,56},{12,60},{16,0},{20,4},{24,8},{28,12},{32,16},... | collective-permute-start | bytes 884744 | tf_op jit(solution)/shard_map/ppermute | solution.py:32
  76.8 0.6 pad_add_fusion.where
  77.5 0.8 copy-done.7
  78.3 6.2 %prep.1.normed = bf16[4,512,512]{2,1,0:T(8,128)(2,1)} custom-call(bf16[528,512]{1,0:T(8,128)(2,1)} %copy-done.2, bf16[528,512]{1,0:T(8,128)(2,1)} %copy-done.6, bf16[528,512]{1,0:T(8,128)(2,1)} %copy-done.5, bf16[528,512]{1,0:T(8,128)(2,1)} %copy-done.7), custom_call_target="tpu_custom_call" | custom-call | flops 1000000 | bytes 1024 | tf_op jit(solution)/shard_map/prep/pallas_call | solution.py:440
  84.5 2.5 %collective-permute-done.17.a3 = bf16[2,4,48,384]{3,2,1,0:T(8,128)(2,1)S(1)} collective-permute-done((bf16[2,4,48,384]{3,2,1,0:T(8,128)(2,1)}, bf16[2,4,48,384]{3,2,1,0:T(8,128)(2,1)S(1)}, u32[]{:S(2)}, u32[]{:S(2)}) %collective-permute-start.17) | collective-permute-done | bytes 294944 | tf_op jit(solution)/shard_map/ppermute | solution.py:32
  87.0 0.7 broadcast_in_dim.30.accepted
  87.7 11.5 %front.1 = (bf16[512,1024]{1,0:T(8,128)(2,1)}, f32[160,512]{1,0:T(8,128)}, bf16[128,1024]{1,0:T(8,128)(2,1)}, f32[3,40,1024]{2,1,0:T(8,128)}) custom-call(s32[2]{0:T(128)} %pad_add_fusion.where, s32[32]{0:T(128)} %pages.5, s32[32,128]{1,0:T(8,128)} %broadcast_in_dim.30.accepted, bf16[4,512,512]{2,1,0:T(8,128)(2,1)} %prep.1.normed, ...), custom_call_target="tpu_custom_call" | custom-call | flops 12000000000 | bytes 1024 | tf_op jit(solution)/shard_map/front/pallas_call | solution.py:455
  99.3 1.8 collective-permute-done.20
  101.1 1.8 fusion.2
  102.9 22.3 %collective-permute-done.21.sums_b = bf16[160,512]{1,0:T(8,128)(2,1)S(1)} collective-permute-done((bf16[160,512]{1,0:T(8,128)(2,1)S(1)}, bf16[160,512]{1,0:T(8,128)(2,1)S(1)}, u32[]{:S(2)}, u32[]{:S(2)}) %collective-permute-start.21) | collective-permute-done | bytes 163872 | tf_op jit(solution)/shard_map/ppermute | solution.py:36
  125.2 0.7 copy-done.9
  125.9 19.8 %scan.1 = (f32[512,1024]{1,0:T(8,128)}, f32[8,512,128]{2,1,0:T(8,128)}) custom-call(s32[32]{0:T(128)} %pages.5, s32[32,128]{1,0:T(8,128)} %broadcast_in_dim.30.accepted, f32[160,512]{1,0:T(8,128)} %get-tuple-element.32.sums_a, bf16[160,512]{1,0:T(8,128)(2,1)} %copy-done.9, bf16[128,1024]{1,0:T(8,128)(2,1)} %get-tuple-element.25.dt, f32[1,1024]{1,0:T(1,128)} %bitcast.55, ...), custom_call_target="tpu_custom_call" | custom-call | flops 1000000 | bytes 1024 | tf_op jit(solution)/shard_map/scan/pallas_call | solution.py:485
  145.7 12.7 %gate.1 = (bf16[2,512,512]{2,1,0:T(8,128)(2,1)}, f32[2,512,512]{2,1,0:T(8,128)}) custom-call(s32[2]{0:T(128)} %pad_add_fusion.where, bf16[4,512,512]{2,1,0:T(8,128)(2,1)} %prep.1.normed, bf16[512,1024]{1,0:T(8,128)(2,1)} %get-tuple-element.23.inputs, f32[512,1024]{1,0:T(8,128)} %get-tuple-element.26.ys, f32[1,1024]{1,0:T(1,128)} %bitcast.54, ...), custom_call_target="tpu_custom_call" | custom-call | flops 1000000 | bytes 1024 | tf_op jit(solution)/shard_map/gate/pallas_call | solution.py:520
  158.5 2.9 %collective-permute-done.22.near = bf16[2,512,512]{2,1,0:T(8,128)(2,1)S(1)} collective-permute-done((bf16[2,512,512]{2,1,0:T(8,128)(2,1)}, bf16[2,512,512]{2,1,0:T(8,128)(2,1)S(1)}, u32[]{:S(2)}, u32[]{:S(2)}) %collective-permute-start.22) | collective-permute-done | bytes 1048608 | tf_op jit(solution)/shard_map/ppermute | solution.py:36
  161.4 1.8 fusion
  163.2 1.5 collective-permute-start.23
  164.6 12.6 %collective-permute-done.23.far = bf16[512,512]{1,0:T(8,128)(2,1)S(1)} collective-permute-done((bf16[512,512]{1,0:T(8,128)(2,1)S(1)}, bf16[512,512]{1,0:T(8,128)(2,1)S(1)}, u32[]{:S(2)}, u32[]{:S(2)}) %collective-permute-start.23) | collective-permute-done | bytes 524320 | tf_op jit(solution)/shard_map/ppermute | solution.py:36
  177.2 0.8 copy-done.8
  178.0 4.3 %join.1 = bf16[64,16,512]{2,1,0:T(8,128)(2,1)} custom-call(s32[32]{0:T(128)} %targets.3, f32[2,512,512]{2,1,0:T(8,128)} %get-tuple-element.27.keep, bf16[2,512,512]{2,1,0:T(8,128)(2,1)} %copy-done.1, bf16[512,512]{1,0:T(8,128)(2,1)} %copy-done.8, bf16[512,512]{1,0:T(8,128)(2,1)} %bitcast.34), custom_call_target="tpu_custom_call" | custom-call | flops 1000000 | bytes 1024 | tf_op jit(solution)/shard_map/join/pallas_call | solution.py:540
  182.3 14.6 %all-to-all-start = ((bf16[64,16,512]{2,1,0:T(8,128)(2,1)}), bf16[64,16,512]{2,1,0:T(8,128)(2,1)S(1)}, u32[]{:S(2)}, u32[]{:S(2)}) async-start(bf16[64,16,512]{2,1,0:T(8,128)(2,1)} %join.1), calls=%async_computation | async-start | bytes 2097152 | tf_op jit(solution)/shard_map/all_to_all | solution.py:550
  196.9 6.4 %settle.1 = f32[640,1024]{1,0:T(8,128)} custom-call(s32[32]{0:T(128)} %pages.5, f32[8,512,128]{2,1,0:T(8,128)} %get-tuple-element.29.kept, f32[640,1024]{1,0:T(8,128)} %bitcast.30), custom_call_target="tpu_custom_call" | custom-call | flops 1000000 | bytes 1024 | tf_op jit(solution)/shard_map/settle/pallas_call | solution.py:510
  203.3 21.2 %all-to-all-done.got = bf16[64,16,512]{2,1,0:T(8,128)(2,1)S(1)} async-done(((bf16[64,16,512]{2,1,0:T(8,128)(2,1)}), bf16[64,16,512]{2,1,0:T(8,128)(2,1)S(1)}, u32[]{:S(2)}, u32[]{:S(2)}) %all-to-all-start) | async-done | bytes 1048608 | tf_op jit(solution)/shard_map/all_to_all | solution.py:550
  224.5 1.0 copy-done
  225.5 2.4 %unpack.1 = bf16[32,16,512]{2,1,0:T(8,128)(2,1)} custom-call(s32[2]{0:T(128)} %pad_add_fusion.where, s32[32]{0:T(128)} %targets.3, bf16[64,16,512]{2,1,0:T(8,128)(2,1)} %copy-done), custom_call_target="tpu_custom_call" | custom-call | tf_op jit(solution)/shard_map/unpack/pallas_call | solution.py:551
  (65 shorter events, 3.4 us)
Async XLA Ops:
  7.2 138.5 %all-gather.3.cloned.1.call-start = ((), (), s32[]{:S(2)}) async-start(), calls=%async_computation.1 | async-start | bytes 8519680 | tf_op jit(solution)/shard_map/all_gather | solution.py:452
  10.4 11.9 %collective-permute-start.1 = (bf16[48,1024]{1,0:T(8,128)(2,1)S(1)}, bf16[48,1024]{1,0:T(8,128)(2,1)S(1)}, u32[]{:S(2)}, u32[]{:S(2)}) collective-permute-start(bf16[48,1024]{1,0:T(8,128)(2,1)S(1)} %get-tuple-element.34), channel_id=1, source_target_pairs={{0,128},{4,132},{8,136},{12,140},{16,144},{20,148},{24,152},{28,15... | collective-permute-start | bytes 294920 | tf_op jit(solution)/shard_map/ppermute | solution.py:32
  17.6 9.7 %collective-permute-start = (bf16[48,1024]{1,0:T(8,128)(2,1)S(1)}, bf16[48,1024]{1,0:T(8,128)(2,1)S(1)}, u32[]{:S(2)}, u32[]{:S(2)}) collective-permute-start(bf16[48,1024]{1,0:T(8,128)(2,1)S(1)} %get-tuple-element.34), channel_id=1, source_target_pairs={{0,192},{4,196},{8,200},{12,204},{16,208},{20,212},{24,216},{28,22... | collective-permute-start | bytes 294920 | tf_op jit(solution)/shard_map/ppermute | solution.py:32
  17.6 9.7 %collective-permute-start.2 = (bf16[48,1024]{1,0:T(8,128)(2,1)S(1)}, bf16[48,1024]{1,0:T(8,128)(2,1)S(1)}, u32[]{:S(2)}, u32[]{:S(2)}) collective-permute-start(bf16[48,1024]{1,0:T(8,128)(2,1)S(1)} %get-tuple-element.34), channel_id=1, source_target_pairs={{0,64},{4,68},{8,72},{12,76},{16,80},{20,84},{24,88},{28,92},{32,9... | collective-permute-start | bytes 294920 | tf_op jit(solution)/shard_map/ppermute | solution.py:32
  22.3 45.6 %copy-start.2 = (bf16[528,512]{1,0:T(8,128)(2,1)}, bf16[528,512]{1,0:T(8,128)(2,1)S(1)}, u32[]{:S(2)}) copy-start(bf16[528,512]{1,0:T(8,128)(2,1)S(1)} %pad_maximum_fusion.2.h0) | copy-start | bytes 1622020
  27.3 8.4 %collective-permute-start.4 = (bf16[4,48,384]{2,1,0:T(8,128)(2,1)S(1)}, bf16[4,48,384]{2,1,0:T(8,128)(2,1)S(1)}, u32[]{:S(2)}, u32[]{:S(2)}) collective-permute-start(bf16[4,48,384]{2,1,0:T(8,128)(2,1)S(1)} %pad_maximum_fusion.6), channel_id=1, source_target_pairs={{0,8},{4,12},{8,0},{12,4},{16,24},{20,28},{24,16},{28,20},{32,40},... | collective-permute-start | bytes 442376 | tf_op jit(solution)/shard_map/ppermute | solution.py:32
  29.5 8.8 %collective-permute-start.3 = (bf16[4,48,384]{2,1,0:T(8,128)(2,1)S(1)}, bf16[4,48,384]{2,1,0:T(8,128)(2,1)S(1)}, u32[]{:S(2)}, u32[]{:S(2)}) collective-permute-start(bf16[4,48,384]{2,1,0:T(8,128)(2,1)S(1)} %pad_maximum_fusion.6), channel_id=1, source_target_pairs={{0,12},{4,0},{8,4},{12,8},{16,28},{20,16},{24,20},{28,24},{32,44},... | collective-permute-start | bytes 442376 | tf_op jit(solution)/shard_map/ppermute | solution.py:32
  31.0 7.4 %collective-permute-start.5 = (bf16[4,48,384]{2,1,0:T(8,128)(2,1)S(1)}, bf16[4,48,384]{2,1,0:T(8,128)(2,1)S(1)}, u32[]{:S(2)}, u32[]{:S(2)}) collective-permute-start(bf16[4,48,384]{2,1,0:T(8,128)(2,1)S(1)} %pad_maximum_fusion.6), channel_id=1, source_target_pairs={{0,4},{4,8},{8,12},{12,0},{16,20},{20,24},{24,28},{28,16},{32,36},... | collective-permute-start | bytes 442376 | tf_op jit(solution)/shard_map/ppermute | solution.py:32
  31.6 10.0 %collective-permute-start.6 = (bf16[4,32,640]{2,1,0:T(8,128)(2,1)S(1)}, bf16[4,32,640]{2,1,0:T(8,128)(2,1)S(1)}, u32[]{:S(2)}, u32[]{:S(2)}) collective-permute-start(bf16[4,32,640]{2,1,0:T(8,128)(2,1)S(1)} %pad_maximum_fusion.3), channel_id=1, source_target_pairs={{0,48},{4,52},{8,56},{12,60},{16,0},{20,4},{24,8},{28,12},{32,16},... | collective-permute-start | bytes 491528 | tf_op jit(solution)/shard_map/ppermute | solution.py:32
  34.7 8.9 %collective-permute-start.7 = (bf16[4,32,640]{2,1,0:T(8,128)(2,1)S(1)}, bf16[4,32,640]{2,1,0:T(8,128)(2,1)S(1)}, u32[]{:S(2)}, u32[]{:S(2)}) collective-permute-start(bf16[4,32,640]{2,1,0:T(8,128)(2,1)S(1)} %pad_maximum_fusion.3), channel_id=1, source_target_pairs={{0,32},{4,36},{8,40},{12,44},{16,48},{20,52},{24,56},{28,60},{32,0... | collective-permute-start | bytes 491528 | tf_op jit(solution)/shard_map/ppermute | solution.py:32
  35.8 9.6 %collective-permute-start.8 = (bf16[4,32,640]{2,1,0:T(8,128)(2,1)S(1)}, bf16[4,32,640]{2,1,0:T(8,128)(2,1)S(1)}, u32[]{:S(2)}, u32[]{:S(2)}) collective-permute-start(bf16[4,32,640]{2,1,0:T(8,128)(2,1)S(1)} %pad_maximum_fusion.3), channel_id=1, source_target_pairs={{0,16},{4,20},{8,24},{12,28},{16,32},{20,36},{24,40},{28,44},{32,4... | collective-permute-start | bytes 491528 | tf_op jit(solution)/shard_map/ppermute | solution.py:32
  38.5 46.0 %copy-start.4 = (bf16[4,4,48,384]{3,2,1,0:T(8,128)(2,1)}, bf16[4,4,48,384]{3,2,1,0:T(8,128)(2,1)S(1)}, u32[]{:S(2)}) copy-start(bf16[4,4,48,384]{3,2,1,0:T(8,128)(2,1)S(1)} %pad_maximum_fusion.1.a0) | copy-start | bytes 1769476
  45.4 39.1 %copy-start.3 = (bf16[4,4,32,640]{3,2,1,0:T(8,128)(2,1)}, bf16[4,4,32,640]{3,2,1,0:T(8,128)(2,1)S(1)}, u32[]{:S(2)}) copy-start(bf16[4,4,32,640]{3,2,1,0:T(8,128)(2,1)S(1)} %pad_maximum_fusion.b0) | copy-start | bytes 1966084
  45.4 22.5 %collective-permute-start.10 = (bf16[528,512]{1,0:T(8,128)(2,1)S(1)}, bf16[528,512]{1,0:T(8,128)(2,1)S(1)}, u32[]{:S(2)}, u32[]{:S(2)}) collective-permute-start(bf16[528,512]{1,0:T(8,128)(2,1)S(1)} %pad_maximum_fusion.2.h0), channel_id=1, source_target_pairs={{0,2},{1,3},{2,0},{3,1},{4,6},{5,7},{6,4},{7,5},{8,10},{9,11},{10,... | collective-permute-start | bytes 1622024 | tf_op jit(solution)/shard_map/ppermute | solution.py:36
  45.6 22.3 %collective-permute-start.15 = (bf16[4,4,32,640]{3,2,1,0:T(8,128)(2,1)S(1)}, bf16[4,4,32,640]{3,2,1,0:T(8,128)(2,1)S(1)}, u32[]{:S(2)}, u32[]{:S(2)}) collective-permute-start(bf16[4,4,32,640]{3,2,1,0:T(8,128)(2,1)S(1)} %pad_maximum_fusion.b0), channel_id=1, source_target_pairs={{0,4},{4,8},{8,12},{12,0},{16,20},{20,24},{24,28},{28,16},{32,36},... | collective-permute-start | bytes 1966088 | tf_op jit(solution)/shard_map/ppermute | solution.py:32
  46.1 23.2 %collective-permute-start.14 = (bf16[4,4,32,640]{3,2,1,0:T(8,128)(2,1)S(1)}, bf16[4,4,32,640]{3,2,1,0:T(8,128)(2,1)S(1)}, u32[]{:S(2)}, u32[]{:S(2)}) collective-permute-start(bf16[4,4,32,640]{3,2,1,0:T(8,128)(2,1)S(1)} %pad_maximum_fusion.b0), channel_id=1, source_target_pairs={{0,12},{4,0},{8,4},{12,8},{16,28},{20,16},{24,20},{28,24},{32,44},... | collective-permute-start | bytes 1966088 | tf_op jit(solution)/shard_map/ppermute | solution.py:32
  47.7 22.4 %collective-permute-start.13 = (bf16[4,4,48,384]{3,2,1,0:T(8,128)(2,1)S(1)}, bf16[4,4,48,384]{3,2,1,0:T(8,128)(2,1)S(1)}, u32[]{:S(2)}, u32[]{:S(2)}) collective-permute-start(bf16[4,4,48,384]{3,2,1,0:T(8,128)(2,1)S(1)} %pad_maximum_fusion.1.a0), channel_id=1, source_target_pairs={{0,16},{4,20},{8,24},{12,28},{16,32},{20,36},{24,40},{28,44},{32,4... | collective-permute-start | bytes 1769480 | tf_op jit(solution)/shard_map/ppermute | solution.py:32
  47.7 25.1 %collective-permute-start.12 = (bf16[4,4,48,384]{3,2,1,0:T(8,128)(2,1)S(1)}, bf16[4,4,48,384]{3,2,1,0:T(8,128)(2,1)S(1)}, u32[]{:S(2)}, u32[]{:S(2)}) collective-permute-start(bf16[4,4,48,384]{3,2,1,0:T(8,128)(2,1)S(1)} %pad_maximum_fusion.1.a0), channel_id=1, source_target_pairs={{0,48},{4,52},{8,56},{12,60},{16,0},{20,4},{24,8},{28,12},{32,16},... | collective-permute-start | bytes 1769480 | tf_op jit(solution)/shard_map/ppermute | solution.py:32
  67.9 9.5 %copy-start.5 = (bf16[528,512]{1,0:T(8,128)(2,1)}, bf16[528,512]{1,0:T(8,128)(2,1)S(1)}, u32[]{:S(2)}) copy-start(bf16[528,512]{1,0:T(8,128)(2,1)S(1)} %collective-permute-done.10.h2) | copy-start | bytes 1622020
  67.9 5.6 %collective-permute-start.9 = (bf16[528,512]{1,0:T(8,128)(2,1)S(1)}, bf16[528,512]{1,0:T(8,128)(2,1)S(1)}, u32[]{:S(2)}, u32[]{:S(2)}) collective-permute-start(bf16[528,512]{1,0:T(8,128)(2,1)S(1)} %pad_maximum_fusion.2.h0), channel_id=1, source_target_pairs={{0,1},{1,0},{2,3},{3,2},{4,5},{5,4},{6,7},{7,6},{8,9},{9,8},{10,11... | collective-permute-start | bytes 1622024 | tf_op jit(solution)/shard_map/ppermute | solution.py:36
  68.0 5.6 %copy-start.10 = (bf16[4,4,32,640]{3,2,1,0:T(8,128)(2,1)}, bf16[4,4,32,640]{3,2,1,0:T(8,128)(2,1)S(1)}, u32[]{:S(2)}) copy-start(bf16[4,4,32,640]{3,2,1,0:T(8,128)(2,1)S(1)} %collective-permute-done.15.b4) | copy-start | bytes 1966084
  68.0 9.5 %collective-permute-start.11 = (bf16[528,512]{1,0:T(8,128)(2,1)S(1)}, bf16[528,512]{1,0:T(8,128)(2,1)S(1)}, u32[]{:S(2)}, u32[]{:S(2)}) collective-permute-start(bf16[528,512]{1,0:T(8,128)(2,1)S(1)} %collective-permute-done.10.h2), channel_id=1, source_target_pairs={{0,1},{1,0},{2,3},{3,2},{4,5},{5,4},{6,7},{7,6},{8,9},{9,8},{10,11... | collective-permute-start | bytes 1622024 | tf_op jit(solution)/shard_map/ppermute | solution.py:36
  69.2 7.6 %copy-start.11 = (bf16[4,4,32,640]{3,2,1,0:T(8,128)(2,1)}, bf16[4,4,32,640]{3,2,1,0:T(8,128)(2,1)S(1)}, u32[]{:S(2)}) copy-start(bf16[4,4,32,640]{3,2,1,0:T(8,128)(2,1)S(1)} %collective-permute-done.14.b1) | copy-start | bytes 1966084
  69.2 17.8 %collective-permute-start.18 = (bf16[2,4,32,640]{3,2,1,0:T(8,128)(2,1)}, bf16[2,4,32,640]{3,2,1,0:T(8,128)(2,1)}, u32[]{:S(2)}, u32[]{:S(2)}) collective-permute-start(bf16[2,4,32,640]{3,2,1,0:T(8,128)(2,1)} %slice.34), channel_id=1, source_target_pairs={{0,4},{4,8},{8,12},{12,0},{16,20},{20,24},{24,28},{28,16},{32,36},... | collective-permute-start | bytes 983048 | tf_op jit(solution)/shard_map/ppermute | solution.py:32
  70.0 6.8 %copy-start.12 = (bf16[4,4,48,384]{3,2,1,0:T(8,128)(2,1)}, bf16[4,4,48,384]{3,2,1,0:T(8,128)(2,1)S(1)}, u32[]{:S(2)}) copy-start(bf16[4,4,48,384]{3,2,1,0:T(8,128)(2,1)S(1)} %collective-permute-done.13.a4) | copy-start | bytes 1769476
  70.0 16.9 %collective-permute-start.19 = (bf16[2,4,32,640]{3,2,1,0:T(8,128)(2,1)}, bf16[2,4,32,640]{3,2,1,0:T(8,128)(2,1)}, u32[]{:S(2)}, u32[]{:S(2)}) collective-permute-start(bf16[2,4,32,640]{3,2,1,0:T(8,128)(2,1)} %slice.35), channel_id=1, source_target_pairs={{0,12},{4,0},{8,4},{12,8},{16,28},{20,16},{24,20},{28,24},{32,44},... | collective-permute-start | bytes 983048 | tf_op jit(solution)/shard_map/ppermute | solution.py:32
  72.7 4.1 %copy-start.13 = (bf16[4,4,48,384]{3,2,1,0:T(8,128)(2,1)}, bf16[4,4,48,384]{3,2,1,0:T(8,128)(2,1)S(1)}, u32[]{:S(2)}) copy-start(bf16[4,4,48,384]{3,2,1,0:T(8,128)(2,1)S(1)} %collective-permute-done.12.a1) | copy-start | bytes 1769476
  72.7 11.8 %collective-permute-start.16 = (bf16[2,4,48,384]{3,2,1,0:T(8,128)(2,1)}, bf16[2,4,48,384]{3,2,1,0:T(8,128)(2,1)}, u32[]{:S(2)}, u32[]{:S(2)}) collective-permute-start(bf16[2,4,48,384]{3,2,1,0:T(8,128)(2,1)} %slice.32), channel_id=1, source_target_pairs={{0,16},{4,20},{8,24},{12,28},{16,32},{20,36},{24,40},{28,44},{32,4... | collective-permute-start | bytes 884744 | tf_op jit(solution)/shard_map/ppermute | solution.py:32
  73.6 3.9 %copy-start.6 = (bf16[528,512]{1,0:T(8,128)(2,1)}, bf16[528,512]{1,0:T(8,128)(2,1)S(1)}, u32[]{:S(2)}) copy-start(bf16[528,512]{1,0:T(8,128)(2,1)S(1)} %collective-permute-done.9.h1) | copy-start | bytes 1622020
  73.6 13.4 %collective-permute-start.17 = (bf16[2,4,48,384]{3,2,1,0:T(8,128)(2,1)}, bf16[2,4,48,384]{3,2,1,0:T(8,128)(2,1)S(1)}, u32[]{:S(2)}, u32[]{:S(2)}) collective-permute-start(bf16[2,4,48,384]{3,2,1,0:T(8,128)(2,1)} %slice.33), channel_id=1, source_target_pairs={{0,48},{4,52},{8,56},{12,60},{16,0},{20,4},{24,8},{28,12},{32,16},... | collective-permute-start | bytes 884744 | tf_op jit(solution)/shard_map/ppermute | solution.py:32
  77.5 9.5 %copy-start.14 = (s32[32]{0:T(128)S(1)}, s32[32]{0:T(128)}, u32[]{:S(2)}) copy-start(s32[32]{0:T(128)} %param.33) | copy-start | bytes 388
  77.5 0.8 copy-start.7
  87.0 0.8 copy-start.15
  99.2 1.9 collective-permute-start.20
  102.9 22.3 %collective-permute-start.21 = (bf16[160,512]{1,0:T(8,128)(2,1)S(1)}, bf16[160,512]{1,0:T(8,128)(2,1)S(1)}, u32[]{:S(2)}, u32[]{:S(2)}) collective-permute-start(bf16[160,512]{1,0:T(8,128)(2,1)S(1)} %get-tuple-element.31), channel_id=1, source_target_pairs={{0,2},{1,3},{2,0},{3,1},{4,6},{5,7},{6,4},{7,5},{8,10},{9,11},{10,... | collective-permute-start | bytes 491528 | tf_op jit(solution)/shard_map/ppermute | solution.py:36
  125.2 0.7 copy-start.9
  158.4 3.0 %collective-permute-start.22 = (bf16[2,512,512]{2,1,0:T(8,128)(2,1)}, bf16[2,512,512]{2,1,0:T(8,128)(2,1)S(1)}, u32[]{:S(2)}, u32[]{:S(2)}) collective-permute-start(bf16[2,512,512]{2,1,0:T(8,128)(2,1)} %get-tuple-element.28), channel_id=1, source_target_pairs={{0,1},{1,0},{2,3},{3,2},{4,5},{5,4},{6,7},{7,6},{8,9},{9,8},{10,11... | collective-permute-start | bytes 3145736 | tf_op jit(solution)/shard_map/ppermute | solution.py:36
  161.4 15.8 %copy-start.1 = (bf16[2,512,512]{2,1,0:T(8,128)(2,1)}, bf16[2,512,512]{2,1,0:T(8,128)(2,1)S(1)}, u32[]{:S(2)}) copy-start(bf16[2,512,512]{2,1,0:T(8,128)(2,1)S(1)} %collective-permute-done.22.near) | copy-start | bytes 3145732
  163.2 14.1 %collective-permute-start.23 = (bf16[512,512]{1,0:T(8,128)(2,1)S(1)}, bf16[512,512]{1,0:T(8,128)(2,1)S(1)}, u32[]{:S(2)}, u32[]{:S(2)}) collective-permute-start(bf16[512,512]{1,0:T(8,128)(2,1)S(1)} %fusion), channel_id=1, source_target_pairs={{0,2},{1,3},{2,0},{3,1},{4,6},{5,7},{6,4},{7,5},{8,10},{9,11},{10,... | collective-permute-start | bytes 1572872 | tf_op jit(solution)/shard_map/ppermute | solution.py:36
  177.2 0.8 copy-start.8
  182.3 42.2 %all-to-all-start = ((bf16[64,16,512]{2,1,0:T(8,128)(2,1)}), bf16[64,16,512]{2,1,0:T(8,128)(2,1)S(1)}, u32[]{:S(2)}, u32[]{:S(2)}) async-start(bf16[64,16,512]{2,1,0:T(8,128)(2,1)} %join.1), calls=%async_computation | async-start | bytes 2097152 | tf_op jit(solution)/shard_map/all_to_all | solution.py:550
  224.5 1.0 copy-start
Sparse Core Ops, SparseCore 0:
  11.3 123.1 all-gather.2

commit v7 on v5

--- a/solution.py
+++ b/solution.py
@@ -52,12 +52,6 @@
 
 def send_direct(block, axis):
     return block, hop(block, axis, -1), hop(block, axis, 2), hop(block, axis, 1)
-
-
-def exchange_z(block):
-    groups = [[z * SIDE * SIDE + i for z in range(SIDE)] for i in range(SIDE * SIDE)]
-    many = jnp.broadcast_to(block[None], (SIDE, *block.shape))
-    return lax.all_to_all(many, "dp", 0, 0, tiled=True, axis_index_groups=groups)
 
 
 def direct(block, axis):
@@ -337,9 +331,11 @@
     m = where[1]
     tokens, width = gated.shape
     for z in range(SIDE):
-        pltpu.make_async_copy(second.at[:, z, pl.ds(0, 32), :], weight.at[z], sems.at[0]).start()
+        at = (z + SIDE - (where[0] >> 4)) & 3
+        pltpu.make_async_copy(second.at[:, at, pl.ds(0, 32), :], weight.at[z], sems.at[0]).start()
     for z in range(SIDE):
-        pltpu.make_async_copy(second.at[:, z, pl.ds(32, 32), :], outer.at[z], sems.at[1]).start()
+        at = (z + SIDE - (where[0] >> 4)) & 3
+        pltpu.make_async_copy(second.at[:, at, pl.ds(32, 32), :], outer.at[z], sems.at[1]).start()
     pltpu.make_async_copy(weight, weight, sems.at[0]).wait()
 
     def gate(n, _):
@@ -456,7 +452,7 @@
 
     pair = after(jnp.concatenate([in_z, out_proj.T], axis=0), first)
     second = lax.all_gather(
-        exchange_z(pair), "dp", axis=0,
+        jnp.stack(after(send_direct(pair, 0), middle_a, middle_b)), "dp", axis=0,
         axis_index_groups=[[z * 16 + i for i in range(16)] for z in range(SIDE)],
     )
 

time: 237 us -> 223 us (0.941)
  blocking collectives: 21 us -> 0 us
  starting transfers between devices: 45.7 us -> 59 us
  waiting for transfers between devices: 77.4 us -> 71.5 us
    all_to_all x1 -> x0, blocking collectives: 21 us -> none  [exchange_z(): lax.all_to_all(many, 'dp', 0, 0, tiled=True, axis_index_groups=groups)]
    ppermute x17 -> x20, starting transfers between devices: 31.3 us -> 40.6 us  [hop(): return lax.ppermute(value, 'dp', shift_pairs(axis, step))]
    ppermute x17 -> x20, waiting for transfers between devices: 28.6 us -> 23.2 us  [hop(): return lax.ppermute(value, 'dp', shift_pairs(axis, step))]
    ppermute x7, starting transfers between devices: 2.32 us -> 6.05 us  [across(): return lax.ppermute(value, 'mp', [(m, m ^ flip) for m in range(4)])]
  transfers between devices with their start and end apart: 26 -> 29, of which waited for: 13 -> 16; matrix products, arithmetic and copies ran while one was open for 3% -> 2% of each run, Pallas kernels for 19% -> 20%
where the time goes in v7:
time: 223 us; the launch traced here: 220 us
  waiting for transfers between devices  71.5 us (32%)
  Pallas kernels  63.1 us (28%)
  starting transfers between devices  59 us (26%)
  between operations  14.3 us (6%)
  other arithmetic  6.26 us (3%)
  local copies, waits for them, and re-layouts  5.68 us (3%)
    ppermute x20, starting transfers between devices, hop(): return lax.ppermute(value, 'dp', shift_pairs(axis, step))  40.6 us
    ppermute x7, waiting for transfers between devices, across(): return lax.ppermute(value, 'mp', [(m, m ^ flip) for m in range(4)])  26.2 us
    ppermute x20, waiting for transfers between devices, hop(): return lax.ppermute(value, 'dp', shift_pairs(axis, step))  23.2 us
    all_to_all x1, waiting for transfers between devices, on_device(): lax.all_to_all(packed, 'dp', split_axis=0, concat_axis=0, tiled=True)  20.9 us
    pallas_call x1, Pallas kernels, on_device(): pl.pallas_call(scan_kernel, out_shape=(jax.ShapeDtypeStruct((tokens, widt...  19.8 us
    pallas_call x1, Pallas kernels, on_device(): pl.pallas_call(gate_kernel, out_shape=(jax.ShapeDtypeStruct((2, tokens, p...  12.7 us
    all_to_all x1, starting transfers between devices, on_device(): lax.all_to_all(packed, 'dp', split_axis=0, concat_axis=0, tiled=True)  12.3 us
    pallas_call x1, Pallas kernels, on_device(): pl.pallas_call(front_kernel, out_shape=(jax.ShapeDtypeStruct((tokens, wid...  11.3 us
  transfers between devices with their start and end apart: 29, of which 16 were waited for; matrix products, arithmetic and copies ran while one was open for 2% of the time, Pallas kernels for 20%

profile of v7, /device:TPU:2, one launch (start us, length us, event | category | flops | bytes accessed | tf_op | source)
XLA Modules:
  0.0 219.9 jit_solution(11483650731937297014)
XLA Ops:
  7.9 0.9 fusion.1
  8.9 7.2 %collective-permute-start.1 = (bf16[48,1024]{1,0:T(8,128)(2,1)S(1)}, bf16[48,1024]{1,0:T(8,128)(2,1)S(1)}, u32[]{:S(2)}, u32[]{:S(2)}) collective-permute-start(bf16[48,1024]{1,0:T(8,128)(2,1)S(1)} %get-tuple-element.48), channel_id=1, source_target_pairs={{0,128},{4,132},{8,136},{12,140},{16,144},{20,148},{24,152},{28,15... | collective-permute-start | bytes 294920 | tf_op jit(solution)/shard_map/ppermute | solution.py:32
  16.1 2.9 %collective-permute-start.2 = (bf16[48,1024]{1,0:T(8,128)(2,1)S(1)}, bf16[48,1024]{1,0:T(8,128)(2,1)S(1)}, u32[]{:S(2)}, u32[]{:S(2)}) collective-permute-start(bf16[48,1024]{1,0:T(8,128)(2,1)S(1)} %get-tuple-element.48), channel_id=1, source_target_pairs={{0,64},{4,68},{8,72},{12,76},{16,80},{20,84},{24,88},{28,92},{32,9... | collective-permute-start | bytes 294920 | tf_op jit(solution)/shard_map/ppermute | solution.py:32
  19.0 6.7 %collective-permute-done = bf16[48,1024]{1,0:T(8,128)(2,1)S(1)} collective-permute-done((bf16[48,1024]{1,0:T(8,128)(2,1)S(1)}, bf16[48,1024]{1,0:T(8,128)(2,1)S(1)}, u32[]{:S(2)}, u32[]{:S(2)}) %collective-permute-start) | collective-permute-done | bytes 98336 | tf_op jit(solution)/shard_map/ppermute | solution.py:32
  25.9 2.2 %collective-permute-start.4 = (bf16[4,48,384]{2,1,0:T(8,128)(2,1)S(1)}, bf16[4,48,384]{2,1,0:T(8,128)(2,1)S(1)}, u32[]{:S(2)}, u32[]{:S(2)}) collective-permute-start(bf16[4,48,384]{2,1,0:T(8,128)(2,1)S(1)} %get-tuple-element.46), channel_id=1, source_target_pairs={{0,8},{4,12},{8,0},{12,4},{16,24},{20,28},{24,16},{28,20},{32,40},... | collective-permute-start | bytes 442376 | tf_op jit(solution)/shard_map/ppermute | solution.py:32
  28.1 3.3 %collective-permute-start.7 = (bf16[4,32,640]{2,1,0:T(8,128)(2,1)S(1)}, bf16[4,32,640]{2,1,0:T(8,128)(2,1)S(1)}, u32[]{:S(2)}, u32[]{:S(2)}) collective-permute-start(bf16[4,32,640]{2,1,0:T(8,128)(2,1)S(1)} %get-tuple-element.44), channel_id=1, source_target_pairs={{0,32},{4,36},{8,40},{12,44},{16,48},{20,52},{24,56},{28,60},{32,0... | collective-permute-start | bytes 491528 | tf_op jit(solution)/shard_map/ppermute | solution.py:32
  31.4 1.4 collective-permute-start.3
  33.4 1.1 collective-permute-start.6
  34.5 1.3 collective-permute-start.8
  36.5 1.4 collective-permute-start.24
  38.0 4.0 %collective-permute-start.23 = (bf16[64,1024]{1,0:T(8,128)(2,1)S(1)}, bf16[64,1024]{1,0:T(8,128)(2,1)S(1)}, u32[]{:S(2)}, u32[]{:S(2)}) collective-permute-start(bf16[64,1024]{1,0:T(8,128)(2,1)S(1)} %pad_maximum_fusion.5), channel_id=1, source_target_pairs={{0,128},{4,132},{8,136},{12,140},{16,144},{20,148},{24,152},{28,15... | collective-permute-start | bytes 393224 | tf_op jit(solution)/shard_map/ppermute | solution.py:32
  42.0 1.2 collective-permute-start.22
  43.4 4.8 %collective-permute-done.24 = bf16[64,1024]{1,0:T(8,128)(2,1)S(1)} collective-permute-done((bf16[64,1024]{1,0:T(8,128)(2,1)S(1)}, bf16[64,1024]{1,0:T(8,128)(2,1)S(1)}, u32[]{:S(2)}, u32[]{:S(2)}) %collective-permute-start.24) | collective-permute-done | bytes 131104 | tf_op jit(solution)/shard_map/ppermute | solution.py:32
  48.2 2.6 %collective-permute-done.23 = bf16[64,1024]{1,0:T(8,128)(2,1)S(1)} collective-permute-done((bf16[64,1024]{1,0:T(8,128)(2,1)S(1)}, bf16[64,1024]{1,0:T(8,128)(2,1)S(1)}, u32[]{:S(2)}, u32[]{:S(2)}) %collective-permute-start.23) | collective-permute-done | bytes 131104 | tf_op jit(solution)/shard_map/ppermute | solution.py:32
  51.5 0.9 pad_maximum_fusion.3
  52.4 2.4 %collective-permute-start.10 = (bf16[528,512]{1,0:T(8,128)(2,1)S(1)}, bf16[528,512]{1,0:T(8,128)(2,1)S(1)}, u32[]{:S(2)}, u32[]{:S(2)}) collective-permute-start(bf16[528,512]{1,0:T(8,128)(2,1)S(1)} %pad_maximum_fusion.2.h0), channel_id=1, source_target_pairs={{0,2},{1,3},{2,0},{3,1},{4,6},{5,7},{6,4},{7,5},{8,10},{9,11},{10,... | collective-permute-start | bytes 1622024 | tf_op jit(solution)/shard_map/ppermute | solution.py:36
  55.4 1.5 collective-permute-start.14
  56.9 1.3 collective-permute-start.13
  58.1 2.0 collective-permute-start.12
  60.1 4.7 %collective-permute-done.10.h2 = bf16[528,512]{1,0:T(8,128)(2,1)S(1)} collective-permute-done((bf16[528,512]{1,0:T(8,128)(2,1)S(1)}, bf16[528,512]{1,0:T(8,128)(2,1)S(1)}, u32[]{:S(2)}, u32[]{:S(2)}) %collective-permute-start.10) | collective-permute-done | bytes 540704 | tf_op jit(solution)/shard_map/ppermute | solution.py:36
  64.8 6.0 %collective-permute-done.15.b4 = bf16[4,4,32,640]{3,2,1,0:T(8,128)(2,1)S(1)} collective-permute-done((bf16[4,4,32,640]{3,2,1,0:T(8,128)(2,1)S(1)}, bf16[4,4,32,640]{3,2,1,0:T(8,128)(2,1)S(1)}, u32[]{:S(2)}, u32[]{:S(2)}) %collective-permute-start.15) | collective-permute-done | bytes 655392 | tf_op jit(solution)/shard_map/ppermute | solution.py:32
  71.4 2.9 %collective-permute-start.18 = (bf16[2,4,32,640]{3,2,1,0:T(8,128)(2,1)S(1)}, bf16[2,4,32,640]{3,2,1,0:T(8,128)(2,1)}, u32[]{:S(2)}, u32[]{:S(2)}) collective-permute-start(bf16[2,4,32,640]{3,2,1,0:T(8,128)(2,1)S(1)} %slice.36), channel_id=1, source_target_pairs={{0,4},{4,8},{8,12},{12,0},{16,20},{20,24},{24,28},{28,16},{32,36},... | collective-permute-start | bytes 983048 | tf_op jit(solution)/shard_map/ppermute | solution.py:32
  74.3 0.8 slice.37
  75.7 1.9 collective-permute-start.19
  77.6 0.7 slice.34
  78.3 2.5 %collective-permute-start.16 = (bf16[2,4,48,384]{3,2,1,0:T(8,128)(2,1)}, bf16[2,4,48,384]{3,2,1,0:T(8,128)(2,1)S(1)}, u32[]{:S(2)}, u32[]{:S(2)}) collective-permute-start(bf16[2,4,48,384]{3,2,1,0:T(8,128)(2,1)} %slice.34), channel_id=1, source_target_pairs={{0,16},{4,20},{8,24},{12,28},{16,32},{20,36},{24,40},{28,44},{32,4... | collective-permute-start | bytes 884744 | tf_op jit(solution)/shard_map/ppermute | solution.py:32
  80.9 1.5 collective-permute-start.17
  83.1 6.2 %prep.1.normed = bf16[4,512,512]{2,1,0:T(8,128)(2,1)} custom-call(bf16[528,512]{1,0:T(8,128)(2,1)} %copy-done.2, bf16[528,512]{1,0:T(8,128)(2,1)} %copy-done.7, bf16[528,512]{1,0:T(8,128)(2,1)} %copy-done.6, bf16[528,512]{1,0:T(8,128)(2,1)} %collective-permute-done.11.h3), custom_call_target="tpu_custom_call" | custom-call | flops 1000000 | bytes 1024 | tf_op jit(solution)/shard_map/prep/pallas_call | solution.py:442
  89.6 0.8 broadcast_in_dim.30.accepted
  90.4 11.3 %front.1 = (bf16[512,1024]{1,0:T(8,128)(2,1)}, f32[160,512]{1,0:T(8,128)}, bf16[128,1024]{1,0:T(8,128)(2,1)}, f32[3,40,1024]{2,1,0:T(8,128)}) custom-call(s32[2]{0:T(128)} %pad_add_fusion.where, s32[32]{0:T(128)} %pages.5, s32[32,128]{1,0:T(8,128)} %broadcast_in_dim.30.accepted, bf16[4,512,512]{2,1,0:T(8,128)(2,1)} %prep.1.normed, ...), custom_call_target="tpu_custom_call" | custom-call | flops 12000000000 | bytes 1024 | tf_op jit(solution)/shard_map/front/pallas_call | solution.py:460
  101.9 1.8 collective-permute-done.20
  103.7 1.8 fusion.2
  105.4 1.8 collective-permute-start.21
  107.2 4.5 %collective-permute-done.21.sums_b = bf16[160,512]{1,0:T(8,128)(2,1)S(1)} collective-permute-done((bf16[160,512]{1,0:T(8,128)(2,1)S(1)}, bf16[160,512]{1,0:T(8,128)(2,1)S(1)}, u32[]{:S(2)}, u32[]{:S(2)}) %collective-permute-start.21) | collective-permute-done | bytes 163872 | tf_op jit(solution)/shard_map/ppermute | solution.py:36
  112.4 19.8 %scan.1 = (f32[512,1024]{1,0:T(8,128)}, f32[8,512,128]{2,1,0:T(8,128)}) custom-call(s32[32]{0:T(128)} %pages.5, s32[32,128]{1,0:T(8,128)} %broadcast_in_dim.30.accepted, f32[160,512]{1,0:T(8,128)} %get-tuple-element.42.sums_a, bf16[160,512]{1,0:T(8,128)(2,1)} %copy-done.9, bf16[128,1024]{1,0:T(8,128)(2,1)} %get-tuple-element.30.dt, f32[1,1024]{1,0:T(1,128)} %bitcast.54, ...), custom_call_target="tpu_custom_call" | custom-call | flops 1000000 | bytes 1024 | tf_op jit(solution)/shard_map/scan/pallas_call | solution.py:490
  132.2 1.2 all-gather.3.cloned.1.call-done
  133.4 12.7 %gate.1 = (bf16[2,512,512]{2,1,0:T(8,128)(2,1)}, f32[2,512,512]{2,1,0:T(8,128)}) custom-call(s32[2]{0:T(128)} %pad_add_fusion.where, bf16[4,512,512]{2,1,0:T(8,128)(2,1)} %prep.1.normed, bf16[512,1024]{1,0:T(8,128)(2,1)} %get-tuple-element.28.inputs, f32[512,1024]{1,0:T(8,128)} %get-tuple-element.31.ys, f32[1,1024]{1,0:T(1,128)} %bitcast.53, ...), custom_call_target="tpu_custom_call" | custom-call | flops 1000000 | bytes 1024 | tf_op jit(solution)/shard_map/gate/pallas_call | solution.py:525
  146.2 2.9 %collective-permute-done.25.near = bf16[2,512,512]{2,1,0:T(8,128)(2,1)S(1)} collective-permute-done((bf16[2,512,512]{2,1,0:T(8,128)(2,1)}, bf16[2,512,512]{2,1,0:T(8,128)(2,1)S(1)}, u32[]{:S(2)}, u32[]{:S(2)}) %collective-permute-start.25) | collective-permute-done | bytes 1048608 | tf_op jit(solution)/shard_map/ppermute | solution.py:36
  149.0 1.8 fusion
  150.8 1.6 collective-permute-start.26
  152.5 12.4 %collective-permute-done.26.far = bf16[512,512]{1,0:T(8,128)(2,1)S(1)} collective-permute-done((bf16[512,512]{1,0:T(8,128)(2,1)S(1)}, bf16[512,512]{1,0:T(8,128)(2,1)S(1)}, u32[]{:S(2)}, u32[]{:S(2)}) %collective-permute-start.26) | collective-permute-done | bytes 524320 | tf_op jit(solution)/shard_map/ppermute | solution.py:36
  164.9 0.8 copy-done.8
  165.7 4.2 %join.1 = bf16[64,16,512]{2,1,0:T(8,128)(2,1)} custom-call(s32[32]{0:T(128)} %targets.3, f32[2,512,512]{2,1,0:T(8,128)} %get-tuple-element.37.keep, bf16[2,512,512]{2,1,0:T(8,128)(2,1)} %copy-done.1, bf16[512,512]{1,0:T(8,128)(2,1)} %copy-done.8, bf16[512,512]{1,0:T(8,128)(2,1)} %bitcast.37), custom_call_target="tpu_custom_call" | custom-call | flops 1000000 | bytes 1024 | tf_op jit(solution)/shard_map/join/pallas_call | solution.py:545
  169.9 12.3 %all-to-all-start = ((bf16[64,16,512]{2,1,0:T(8,128)(2,1)}), bf16[64,16,512]{2,1,0:T(8,128)(2,1)S(1)}, u32[]{:S(2)}, u32[]{:S(2)}) async-start(bf16[64,16,512]{2,1,0:T(8,128)(2,1)} %join.1), calls=%async_computation | async-start | bytes 2097152 | tf_op jit(solution)/shard_map/all_to_all | solution.py:555
  182.2 6.4 %settle.1 = f32[640,1024]{1,0:T(8,128)} custom-call(s32[32]{0:T(128)} %pages.5, f32[8,512,128]{2,1,0:T(8,128)} %get-tuple-element.39.kept, f32[640,1024]{1,0:T(8,128)} %bitcast.34), custom_call_target="tpu_custom_call" | custom-call | flops 1000000 | bytes 1024 | tf_op jit(solution)/shard_map/settle/pallas_call | solution.py:515
  188.7 20.9 %all-to-all-done.got = bf16[64,16,512]{2,1,0:T(8,128)(2,1)S(1)} async-done(((bf16[64,16,512]{2,1,0:T(8,128)(2,1)}), bf16[64,16,512]{2,1,0:T(8,128)(2,1)S(1)}, u32[]{:S(2)}, u32[]{:S(2)}) %all-to-all-start) | async-done | bytes 1048608 | tf_op jit(solution)/shard_map/all_to_all | solution.py:555
  209.6 1.0 copy-done
  210.7 2.4 %unpack.1 = bf16[32,16,512]{2,1,0:T(8,128)(2,1)} custom-call(s32[2]{0:T(128)} %pad_add_fusion.where, s32[32]{0:T(128)} %targets.3, bf16[64,16,512]{2,1,0:T(8,128)(2,1)} %copy-done), custom_call_target="tpu_custom_call" | custom-call | tf_op jit(solution)/shard_map/unpack/pallas_call | solution.py:556
  (79 shorter events, 7.0 us)
Async XLA Ops:
  7.2 28.6 %copy-start.14 = (bf16[1024,32]{0,1:T(8,128)(2,1)S(1)}, bf16[1024,32]{0,1:T(8,128)(2,1)}, u32[]{:S(2)}) copy-start(bf16[1024,32]{0,1:T(8,128)(2,1)} %param.28) | copy-start | bytes 196612
  7.2 28.6 %copy-start.15 = (bf16[32,1024]{1,0:T(8,128)(2,1)S(1)}, bf16[32,1024]{1,0:T(8,128)(2,1)}, u32[]{:S(2)}) copy-start(bf16[32,1024]{1,0:T(8,128)(2,1)} %param.20) | copy-start | bytes 196612
  7.2 126.2 %all-gather.3.cloned.1.call-start = ((), (), s32[]{:S(2)}) async-start(), calls=%async_computation.1 | async-start | bytes 8912896 | tf_op jit(solution)/shard_map/all_gather | solution.py:454
  8.9 10.1 %collective-permute-start.1 = (bf16[48,1024]{1,0:T(8,128)(2,1)S(1)}, bf16[48,1024]{1,0:T(8,128)(2,1)S(1)}, u32[]{:S(2)}, u32[]{:S(2)}) collective-permute-start(bf16[48,1024]{1,0:T(8,128)(2,1)S(1)} %get-tuple-element.48), channel_id=1, source_target_pairs={{0,128},{4,132},{8,136},{12,140},{16,144},{20,148},{24,152},{28,15... | collective-permute-start | bytes 294920 | tf_op jit(solution)/shard_map/ppermute | solution.py:32
  16.1 9.7 %collective-permute-start = (bf16[48,1024]{1,0:T(8,128)(2,1)S(1)}, bf16[48,1024]{1,0:T(8,128)(2,1)S(1)}, u32[]{:S(2)}, u32[]{:S(2)}) collective-permute-start(bf16[48,1024]{1,0:T(8,128)(2,1)S(1)} %get-tuple-element.48), channel_id=1, source_target_pairs={{0,192},{4,196},{8,200},{12,204},{16,208},{20,212},{24,216},{28,22... | collective-permute-start | bytes 294920 | tf_op jit(solution)/shard_map/ppermute | solution.py:32
  16.1 9.7 %collective-permute-start.2 = (bf16[48,1024]{1,0:T(8,128)(2,1)S(1)}, bf16[48,1024]{1,0:T(8,128)(2,1)S(1)}, u32[]{:S(2)}, u32[]{:S(2)}) collective-permute-start(bf16[48,1024]{1,0:T(8,128)(2,1)S(1)} %get-tuple-element.48), channel_id=1, source_target_pairs={{0,64},{4,68},{8,72},{12,76},{16,80},{20,84},{24,88},{28,92},{32,9... | collective-permute-start | bytes 294920 | tf_op jit(solution)/shard_map/ppermute | solution.py:32
  25.9 8.6 %collective-permute-start.4 = (bf16[4,48,384]{2,1,0:T(8,128)(2,1)S(1)}, bf16[4,48,384]{2,1,0:T(8,128)(2,1)S(1)}, u32[]{:S(2)}, u32[]{:S(2)}) collective-permute-start(bf16[4,48,384]{2,1,0:T(8,128)(2,1)S(1)} %get-tuple-element.46), channel_id=1, source_target_pairs={{0,8},{4,12},{8,0},{12,4},{16,24},{20,28},{24,16},{28,20},{32,40},... | collective-permute-start | bytes 442376 | tf_op jit(solution)/shard_map/ppermute | solution.py:32
  28.1 13.9 %collective-permute-start.7 = (bf16[4,32,640]{2,1,0:T(8,128)(2,1)S(1)}, bf16[4,32,640]{2,1,0:T(8,128)(2,1)S(1)}, u32[]{:S(2)}, u32[]{:S(2)}) collective-permute-start(bf16[4,32,640]{2,1,0:T(8,128)(2,1)S(1)} %get-tuple-element.44), channel_id=1, source_target_pairs={{0,32},{4,36},{8,40},{12,44},{16,48},{20,52},{24,56},{28,60},{32,0... | collective-permute-start | bytes 491528 | tf_op jit(solution)/shard_map/ppermute | solution.py:32
  31.4 5.2 %collective-permute-start.3 = (bf16[4,48,384]{2,1,0:T(8,128)(2,1)S(1)}, bf16[4,48,384]{2,1,0:T(8,128)(2,1)S(1)}, u32[]{:S(2)}, u32[]{:S(2)}) collective-permute-start(bf16[4,48,384]{2,1,0:T(8,128)(2,1)S(1)} %get-tuple-element.46), channel_id=1, source_target_pairs={{0,12},{4,0},{8,4},{12,8},{16,28},{20,16},{24,20},{28,24},{32,44},... | collective-permute-start | bytes 442376 | tf_op jit(solution)/shard_map/ppermute | solution.py:32
  32.8 5.1 %collective-permute-start.5 = (bf16[4,48,384]{2,1,0:T(8,128)(2,1)S(1)}, bf16[4,48,384]{2,1,0:T(8,128)(2,1)S(1)}, u32[]{:S(2)}, u32[]{:S(2)}) collective-permute-start(bf16[4,48,384]{2,1,0:T(8,128)(2,1)S(1)} %get-tuple-element.46), channel_id=1, source_target_pairs={{0,4},{4,8},{8,12},{12,0},{16,20},{20,24},{24,28},{28,16},{32,36},... | collective-permute-start | bytes 442376 | tf_op jit(solution)/shard_map/ppermute | solution.py:32
  33.4 9.8 %collective-permute-start.6 = (bf16[4,32,640]{2,1,0:T(8,128)(2,1)S(1)}, bf16[4,32,640]{2,1,0:T(8,128)(2,1)S(1)}, u32[]{:S(2)}, u32[]{:S(2)}) collective-permute-start(bf16[4,32,640]{2,1,0:T(8,128)(2,1)S(1)} %get-tuple-element.44), channel_id=1, source_target_pairs={{0,48},{4,52},{8,56},{12,60},{16,0},{20,4},{24,8},{28,12},{32,16},... | collective-permute-start | bytes 491528 | tf_op jit(solution)/shard_map/ppermute | solution.py:32
  34.5 8.8 %collective-permute-start.8 = (bf16[4,32,640]{2,1,0:T(8,128)(2,1)S(1)}, bf16[4,32,640]{2,1,0:T(8,128)(2,1)S(1)}, u32[]{:S(2)}, u32[]{:S(2)}) collective-permute-start(bf16[4,32,640]{2,1,0:T(8,128)(2,1)S(1)} %get-tuple-element.44), channel_id=1, source_target_pairs={{0,16},{4,20},{8,24},{12,28},{16,32},{20,36},{24,40},{28,44},{32,4... | collective-permute-start | bytes 491528 | tf_op jit(solution)/shard_map/ppermute | solution.py:32
  35.8 16.6 %copy-start.16 = (bf16[512]{0:T(512)(128)(2,1)S(1)}, bf16[512]{0:T(512)(128)(2,1)}, u32[]{:S(2)}) copy-start(bf16[512]{0:T(512)(128)(2,1)} %param.18) | copy-start | bytes 3076
  35.8 16.6 %copy-start.3 = (bf16[32,16,512]{2,1,0:T(8,128)(2,1)S(1)}, bf16[32,16,512]{2,1,0:T(8,128)(2,1)}, u32[]{:S(2)}) copy-start(bf16[32,16,512]{2,1,0:T(8,128)(2,1)} %param.17) | copy-start | bytes 1572868
  36.5 11.7 %collective-permute-start.24 = (bf16[64,1024]{1,0:T(8,128)(2,1)S(1)}, bf16[64,1024]{1,0:T(8,128)(2,1)S(1)}, u32[]{:S(2)}, u32[]{:S(2)}) collective-permute-start(bf16[64,1024]{1,0:T(8,128)(2,1)S(1)} %pad_maximum_fusion.5), channel_id=1, source_target_pairs={{0,64},{4,68},{8,72},{12,76},{16,80},{20,84},{24,88},{28,92},{32,9... | collective-permute-start | bytes 393224 | tf_op jit(solution)/shard_map/ppermute | solution.py:32
  38.0 12.8 %collective-permute-start.23 = (bf16[64,1024]{1,0:T(8,128)(2,1)S(1)}, bf16[64,1024]{1,0:T(8,128)(2,1)S(1)}, u32[]{:S(2)}, u32[]{:S(2)}) collective-permute-start(bf16[64,1024]{1,0:T(8,128)(2,1)S(1)} %pad_maximum_fusion.5), channel_id=1, source_target_pairs={{0,128},{4,132},{8,136},{12,140},{16,144},{20,148},{24,152},{28,15... | collective-permute-start | bytes 393224 | tf_op jit(solution)/shard_map/ppermute | solution.py:32
  42.0 9.5 %collective-permute-start.22 = (bf16[64,1024]{1,0:T(8,128)(2,1)S(1)}, bf16[64,1024]{1,0:T(8,128)(2,1)S(1)}, u32[]{:S(2)}, u32[]{:S(2)}) collective-permute-start(bf16[64,1024]{1,0:T(8,128)(2,1)S(1)} %pad_maximum_fusion.5), channel_id=1, source_target_pairs={{0,192},{4,196},{8,200},{12,204},{16,208},{20,212},{24,216},{28,22... | collective-permute-start | bytes 393224 | tf_op jit(solution)/shard_map/ppermute | solution.py:32
  43.2 27.5 %copy-start.5 = (bf16[4,4,48,384]{3,2,1,0:T(8,128)(2,1)}, bf16[4,4,48,384]{3,2,1,0:T(8,128)(2,1)S(1)}, u32[]{:S(2)}) copy-start(bf16[4,4,48,384]{3,2,1,0:T(8,128)(2,1)S(1)} %pad_maximum_fusion.1.a0) | copy-start | bytes 1769476
  43.4 35.0 %copy-start.4 = (bf16[4,4,32,640]{3,2,1,0:T(8,128)(2,1)}, bf16[4,4,32,640]{3,2,1,0:T(8,128)(2,1)S(1)}, u32[]{:S(2)}) copy-start(bf16[4,4,32,640]{3,2,1,0:T(8,128)(2,1)S(1)} %pad_maximum_fusion.b0) | copy-start | bytes 1966084
  52.4 30.7 %copy-start.2 = (bf16[528,512]{1,0:T(8,128)(2,1)}, bf16[528,512]{1,0:T(8,128)(2,1)S(1)}, u32[]{:S(2)}) copy-start(bf16[528,512]{1,0:T(8,128)(2,1)S(1)} %pad_maximum_fusion.2.h0) | copy-start | bytes 1622020
  52.4 12.3 %collective-permute-start.10 = (bf16[528,512]{1,0:T(8,128)(2,1)S(1)}, bf16[528,512]{1,0:T(8,128)(2,1)S(1)}, u32[]{:S(2)}, u32[]{:S(2)}) collective-permute-start(bf16[528,512]{1,0:T(8,128)(2,1)S(1)} %pad_maximum_fusion.2.h0), channel_id=1, source_target_pairs={{0,2},{1,3},{2,0},{3,1},{4,6},{5,7},{6,4},{7,5},{8,10},{9,11},{10,... | collective-permute-start | bytes 1622024 | tf_op jit(solution)/shard_map/ppermute | solution.py:36
  54.8 15.9 %collective-permute-start.15 = (bf16[4,4,32,640]{3,2,1,0:T(8,128)(2,1)S(1)}, bf16[4,4,32,640]{3,2,1,0:T(8,128)(2,1)S(1)}, u32[]{:S(2)}, u32[]{:S(2)}) collective-permute-start(bf16[4,4,32,640]{3,2,1,0:T(8,128)(2,1)S(1)} %pad_maximum_fusion.b0), channel_id=1, source_target_pairs={{0,4},{4,8},{8,12},{12,0},{16,20},{20,24},{24,28},{28,16},{32,36},... | collective-permute-start | bytes 1966088 | tf_op jit(solution)/shard_map/ppermute | solution.py:32
  55.4 16.0 %collective-permute-start.14 = (bf16[4,4,32,640]{3,2,1,0:T(8,128)(2,1)S(1)}, bf16[4,4,32,640]{3,2,1,0:T(8,128)(2,1)S(1)}, u32[]{:S(2)}, u32[]{:S(2)}) collective-permute-start(bf16[4,4,32,640]{3,2,1,0:T(8,128)(2,1)S(1)} %pad_maximum_fusion.b0), channel_id=1, source_target_pairs={{0,12},{4,0},{8,4},{12,8},{16,28},{20,16},{24,20},{28,24},{32,44},... | collective-permute-start | bytes 1966088 | tf_op jit(solution)/shard_map/ppermute | solution.py:32
  56.9 18.8 %collective-permute-start.13 = (bf16[4,4,48,384]{3,2,1,0:T(8,128)(2,1)S(1)}, bf16[4,4,48,384]{3,2,1,0:T(8,128)(2,1)S(1)}, u32[]{:S(2)}, u32[]{:S(2)}) collective-permute-start(bf16[4,4,48,384]{3,2,1,0:T(8,128)(2,1)S(1)} %pad_maximum_fusion.1.a0), channel_id=1, source_target_pairs={{0,16},{4,20},{8,24},{12,28},{16,32},{20,36},{24,40},{28,44},{32,4... | collective-permute-start | bytes 1769480 | tf_op jit(solution)/shard_map/ppermute | solution.py:32
  58.1 20.2 %collective-permute-start.12 = (bf16[4,4,48,384]{3,2,1,0:T(8,128)(2,1)S(1)}, bf16[4,4,48,384]{3,2,1,0:T(8,128)(2,1)S(1)}, u32[]{:S(2)}, u32[]{:S(2)}) collective-permute-start(bf16[4,4,48,384]{3,2,1,0:T(8,128)(2,1)S(1)} %pad_maximum_fusion.1.a0), channel_id=1, source_target_pairs={{0,48},{4,52},{8,56},{12,60},{16,0},{20,4},{24,8},{28,12},{32,16},... | collective-permute-start | bytes 1769480 | tf_op jit(solution)/shard_map/ppermute | solution.py:32
  64.8 18.3 %copy-start.6 = (bf16[528,512]{1,0:T(8,128)(2,1)}, bf16[528,512]{1,0:T(8,128)(2,1)S(1)}, u32[]{:S(2)}) copy-start(bf16[528,512]{1,0:T(8,128)(2,1)S(1)} %collective-permute-done.10.h2) | copy-start | bytes 1622020
  64.8 16.1 %collective-permute-start.9 = (bf16[528,512]{1,0:T(8,128)(2,1)S(1)}, bf16[528,512]{1,0:T(8,128)(2,1)S(1)}, u32[]{:S(2)}, u32[]{:S(2)}) collective-permute-start(bf16[528,512]{1,0:T(8,128)(2,1)S(1)} %pad_maximum_fusion.2.h0), channel_id=1, source_target_pairs={{0,1},{1,0},{2,3},{3,2},{4,5},{5,4},{6,7},{7,6},{8,9},{9,8},{10,11... | collective-permute-start | bytes 1622024 | tf_op jit(solution)/shard_map/ppermute | solution.py:36
  70.7 11.7 %copy-start.10 = (bf16[4,4,32,640]{3,2,1,0:T(8,128)(2,1)}, bf16[4,4,32,640]{3,2,1,0:T(8,128)(2,1)S(1)}, u32[]{:S(2)}) copy-start(bf16[4,4,32,640]{3,2,1,0:T(8,128)(2,1)S(1)} %collective-permute-done.15.b4) | copy-start | bytes 1966084
  70.7 12.3 %collective-permute-start.11 = (bf16[528,512]{1,0:T(8,128)(2,1)S(1)}, bf16[528,512]{1,0:T(8,128)(2,1)}, u32[]{:S(2)}, u32[]{:S(2)}) collective-permute-start(bf16[528,512]{1,0:T(8,128)(2,1)S(1)} %collective-permute-done.10.h2), channel_id=1, source_target_pairs={{0,1},{1,0},{2,3},{3,2},{4,5},{5,4},{6,7},{7,6},{8,9},{9,8},{10,11... | collective-permute-start | bytes 1622024 | tf_op jit(solution)/shard_map/ppermute | solution.py:36
  71.4 11.0 %copy-start.11 = (bf16[4,4,32,640]{3,2,1,0:T(8,128)(2,1)}, bf16[4,4,32,640]{3,2,1,0:T(8,128)(2,1)S(1)}, u32[]{:S(2)}) copy-start(bf16[4,4,32,640]{3,2,1,0:T(8,128)(2,1)S(1)} %collective-permute-done.14.b1) | copy-start | bytes 1966084
  71.4 18.2 %collective-permute-start.18 = (bf16[2,4,32,640]{3,2,1,0:T(8,128)(2,1)S(1)}, bf16[2,4,32,640]{3,2,1,0:T(8,128)(2,1)}, u32[]{:S(2)}, u32[]{:S(2)}) collective-permute-start(bf16[2,4,32,640]{3,2,1,0:T(8,128)(2,1)S(1)} %slice.36), channel_id=1, source_target_pairs={{0,4},{4,8},{8,12},{12,0},{16,20},{20,24},{24,28},{28,16},{32,36},... | collective-permute-start | bytes 983048 | tf_op jit(solution)/shard_map/ppermute | solution.py:32
  75.7 6.7 %copy-start.12 = (bf16[4,4,48,384]{3,2,1,0:T(8,128)(2,1)}, bf16[4,4,48,384]{3,2,1,0:T(8,128)(2,1)S(1)}, u32[]{:S(2)}) copy-start(bf16[4,4,48,384]{3,2,1,0:T(8,128)(2,1)S(1)} %collective-permute-done.13.a4) | copy-start | bytes 1769476
  75.7 13.9 %collective-permute-start.19 = (bf16[2,4,32,640]{3,2,1,0:T(8,128)(2,1)}, bf16[2,4,32,640]{3,2,1,0:T(8,128)(2,1)}, u32[]{:S(2)}, u32[]{:S(2)}) collective-permute-start(bf16[2,4,32,640]{3,2,1,0:T(8,128)(2,1)} %slice.37), channel_id=1, source_target_pairs={{0,12},{4,0},{8,4},{12,8},{16,28},{20,16},{24,20},{28,24},{32,44},... | collective-permute-start | bytes 983048 | tf_op jit(solution)/shard_map/ppermute | solution.py:32
  78.3 4.1 %copy-start.13 = (bf16[4,4,48,384]{3,2,1,0:T(8,128)(2,1)}, bf16[4,4,48,384]{3,2,1,0:T(8,128)(2,1)S(1)}, u32[]{:S(2)}) copy-start(bf16[4,4,48,384]{3,2,1,0:T(8,128)(2,1)S(1)} %collective-permute-done.12.a1) | copy-start | bytes 1769476
  78.3 11.3 %collective-permute-start.16 = (bf16[2,4,48,384]{3,2,1,0:T(8,128)(2,1)}, bf16[2,4,48,384]{3,2,1,0:T(8,128)(2,1)S(1)}, u32[]{:S(2)}, u32[]{:S(2)}) collective-permute-start(bf16[2,4,48,384]{3,2,1,0:T(8,128)(2,1)} %slice.34), channel_id=1, source_target_pairs={{0,16},{4,20},{8,24},{12,28},{16,32},{20,36},{24,40},{28,44},{32,4... | collective-permute-start | bytes 884744 | tf_op jit(solution)/shard_map/ppermute | solution.py:32
  80.9 2.2 %copy-start.7 = (bf16[528,512]{1,0:T(8,128)(2,1)}, bf16[528,512]{1,0:T(8,128)(2,1)S(1)}, u32[]{:S(2)}) copy-start(bf16[528,512]{1,0:T(8,128)(2,1)S(1)} %collective-permute-done.9.h1) | copy-start | bytes 1622020
  80.9 8.7 %collective-permute-start.17 = (bf16[2,4,48,384]{3,2,1,0:T(8,128)(2,1)S(1)}, bf16[2,4,48,384]{3,2,1,0:T(8,128)(2,1)S(1)}, u32[]{:S(2)}, u32[]{:S(2)}) collective-permute-start(bf16[2,4,48,384]{3,2,1,0:T(8,128)(2,1)S(1)} %slice.35), channel_id=1, source_target_pairs={{0,48},{4,52},{8,56},{12,60},{16,0},{20,4},{24,8},{28,12},{32,16},... | collective-permute-start | bytes 884744 | tf_op jit(solution)/shard_map/ppermute | solution.py:32
  83.1 6.5 %copy-start.17 = (s32[32]{0:T(128)S(1)}, s32[32]{0:T(128)}, u32[]{:S(2)}) copy-start(s32[32]{0:T(128)} %param.33) | copy-start | bytes 388
  89.6 0.8 copy-start.18
  89.6 0.8 copy-start.19
  101.8 1.9 collective-permute-start.20
  105.4 6.3 %collective-permute-start.21 = (bf16[160,512]{1,0:T(8,128)(2,1)S(1)}, bf16[160,512]{1,0:T(8,128)(2,1)S(1)}, u32[]{:S(2)}, u32[]{:S(2)}) collective-permute-start(bf16[160,512]{1,0:T(8,128)(2,1)S(1)} %get-tuple-element.41), channel_id=1, source_target_pairs={{0,2},{1,3},{2,0},{3,1},{4,6},{5,7},{6,4},{7,5},{8,10},{9,11},{10,... | collective-permute-start | bytes 491528 | tf_op jit(solution)/shard_map/ppermute | solution.py:36
  146.1 3.0 %collective-permute-start.25 = (bf16[2,512,512]{2,1,0:T(8,128)(2,1)}, bf16[2,512,512]{2,1,0:T(8,128)(2,1)S(1)}, u32[]{:S(2)}, u32[]{:S(2)}) collective-permute-start(bf16[2,512,512]{2,1,0:T(8,128)(2,1)} %get-tuple-element.38), channel_id=1, source_target_pairs={{0,1},{1,0},{2,3},{3,2},{4,5},{5,4},{6,7},{7,6},{8,9},{9,8},{10,11... | collective-permute-start | bytes 3145736 | tf_op jit(solution)/shard_map/ppermute | solution.py:36
  149.0 15.8 %copy-start.1 = (bf16[2,512,512]{2,1,0:T(8,128)(2,1)}, bf16[2,512,512]{2,1,0:T(8,128)(2,1)S(1)}, u32[]{:S(2)}) copy-start(bf16[2,512,512]{2,1,0:T(8,128)(2,1)S(1)} %collective-permute-done.25.near) | copy-start | bytes 3145732
  150.8 14.1 %collective-permute-start.26 = (bf16[512,512]{1,0:T(8,128)(2,1)S(1)}, bf16[512,512]{1,0:T(8,128)(2,1)S(1)}, u32[]{:S(2)}, u32[]{:S(2)}) collective-permute-start(bf16[512,512]{1,0:T(8,128)(2,1)S(1)} %fusion), channel_id=1, source_target_pairs={{0,2},{1,3},{2,0},{3,1},{4,6},{5,7},{6,4},{7,5},{8,10},{9,11},{10,... | collective-permute-start | bytes 1572872 | tf_op jit(solution)/shard_map/ppermute | solution.py:36
  164.9 0.8 copy-start.8
  169.9 39.7 %all-to-all-start = ((bf16[64,16,512]{2,1,0:T(8,128)(2,1)}), bf16[64,16,512]{2,1,0:T(8,128)(2,1)S(1)}, u32[]{:S(2)}, u32[]{:S(2)}) async-start(bf16[64,16,512]{2,1,0:T(8,128)(2,1)} %join.1), calls=%async_computation | async-start | bytes 2097152 | tf_op jit(solution)/shard_map/all_to_all | solution.py:555
  209.6 1.0 copy-start
  (1 other events, 0.7 us)
Sparse Core Ops, SparseCore 0:
  52.5 80.8 all-gather.2

commit v8 on v7

--- a/solution.py
+++ b/solution.py
@@ -105,7 +105,7 @@
     return ((i % count) * drafts + i // count == j).astype(BF)
 
 
-def prep_kernel(h0, h1, h2, h3, normed_out, plain):
+def prep_kernel(h0, h1, h2, h3, normed_out, base_out, plain):
     tokens = normed_out.shape[1]
     count = 32
     blocks = (h0, h1, h2, h3)
@@ -123,6 +123,7 @@
 
     lax.fori_loop(0, tokens // step, norm, 0)
     order = order_matrix(tokens, tokens, tokens // count, count)
+    base_out[...] = jnp.dot(order, h0[:tokens, :], preferred_element_type=F32).astype(BF)
     for k in range(4):
         normed_out[k] = jnp.dot(order, plain[k], preferred_element_type=F32).astype(BF)
 
@@ -269,32 +270,37 @@
                 wide[:, q + p] = spread[:, p * 128 : (p + 1) * 128].reshape(drafts, 8, 128)
         last = accepted[eight, :] - 1
 
-        def columns(cb, _):
-            at = pl.ds(pl.multiple_of(cb * 128, 128), 128)
+        def columns(cp, _):
+            ats = [pl.ds(pl.multiple_of(cp * 256 + h * 128, 128), 128) for h in range(2)]
             first = tuple(
-                start[cb, pl.ds(rb * 8 * states + s, 8, stride=states), :] for s in range(states)
+                start[cp * 2 + h, pl.ds(rb * 8 * states + s, 8, stride=states), :]
+                for h in range(2)
+                for s in range(states)
             )
 
             def advance(t, state):
                 rows = pl.ds(pl.multiple_of(t * count + rb * 8, 8), 8)
-                d = delta[rows, at]
-                drive = d * inputs[rows, at].astype(F32)
+                d = [delta[rows, at] for at in ats]
+                drive = [d[h] * inputs[rows, ats[h]].astype(F32) for h in range(2)]
                 here = last == t
-                out = None
-                nexts = []
+                out = [None, None]
+                nexts = [[], []]
                 for s in range(states):
-                    new = jnp.exp2(d * decay[s, :, at]) * state[s] + drive * wide[t, s]
-                    term = new * wide[t, states + s]
-                    out = term if out is None else out + term
-                    pltpu.store(kept.at[cb, pl.ds(pl.multiple_of(s * count + rb * 8, 8), 8), :], new, mask=here)
-                    nexts.append(new)
-                ys_out[rows, at] = out
-                return tuple(nexts)
+                    b, c = wide[t, s], wide[t, states + s]
+                    for h in range(2):
+                        new = jnp.exp2(d[h] * decay[s, :, ats[h]]) * state[h * states + s] + drive[h] * b
+                        term = new * c
+                        out[h] = term if out[h] is None else out[h] + term
+                        pltpu.store(kept.at[cp * 2 + h, pl.ds(pl.multiple_of(s * count + rb * 8, 8), 8), :], new, mask=here)
+                        nexts[h].append(new)
+                for h in range(2):
+                    ys_out[rows, ats[h]] = out[h]
+                return (*nexts[0], *nexts[1])
 
             lax.fori_loop(0, drafts, advance, first, unroll=4)
             return 0
 
-        lax.fori_loop(0, width // 128, columns, 0)
+        lax.fori_loop(0, width // 256, columns, 0)
         return 0
 
     lax.fori_loop(0, count // 8, some, 0)
@@ -369,14 +375,13 @@
     lax.fori_loop(0, 4, out, 0)
 
 
-def join_kernel(targets, keep, near, far, hidden, out, total):
-    tokens, width = hidden.shape
+def join_kernel(targets, keep, near, far, base, out, total):
+    tokens, width = base.shape
     count = targets.shape[0]
     drafts = tokens // count
     order = order_matrix(tokens, tokens, drafts, count)
-    base = jnp.dot(order, hidden[...], preferred_element_type=F32)
     summed = keep[0] + near[0].astype(F32) + far[...].astype(F32)
-    rounded = (summed + base).astype(BF)
+    rounded = (summed + base[...].astype(F32)).astype(BF)
     back = lax.dot_general(order, rounded, (((0,), (0,)), ((), ())), preferred_element_type=F32)
     total[...] = back.astype(BF).reshape(count, drafts, width)
     out[...] = jnp.zeros(out.shape, BF)
@@ -439,11 +444,14 @@
     near = across(sent, 1)
     far = across(sent, 2)
     both = across(far, 1)
-    normed = pl.pallas_call(
+    normed, base = pl.pallas_call(
         prep_kernel,
-        out_shape=jax.ShapeDtypeStruct((4, tokens, part), BF),
+        out_shape=(
+            jax.ShapeDtypeStruct((4, tokens, part), BF),
+            jax.ShapeDtypeStruct((tokens, part), BF),
+        ),
         in_specs=[VMEM] * 4,
-        out_specs=VMEM,
+        out_specs=(VMEM,) * 2,
         scratch_shapes=[pltpu.VMEM((4, tokens, part), BF)],
         compiler_params=params(),
         cost_estimate=pl.CostEstimate(flops=1_000_000, bytes_accessed=1 << 10, transcendentals=0),
@@ -551,7 +559,7 @@
         compiler_params=params(),
         cost_estimate=pl.CostEstimate(flops=1_000_000, bytes_accessed=1 << 10, transcendentals=0),
         name="join",
-    )(permutation, keep, got, remote, flat)
+    )(permutation, keep, got, remote, base)
     arrived = lax.all_to_all(packed, "dp", split_axis=0, concat_axis=0, tiled=True)
     verified = pl.pallas_call(
         unpack_kernel,

time: 223 us -> 224 us (level)
  waiting for transfers between devices: 71.5 us -> 69.2 us
  transfers between devices with their start and end apart: 29 -> 29, of which waited for: 16 -> 13; matrix products, arithmetic and copies ran while one was open for 2% -> 3% of each run, Pallas kernels for 20% -> 20%
where the time goes in v8:
time: 224 us; the launch traced here: 221 us
  waiting for transfers between devices  69.2 us (31%)
  Pallas kernels  63.3 us (28%)
  starting transfers between devices  60.3 us (27%)
  between operations  14.3 us (6%)
  local copies, waits for them, and re-layouts  7.29 us (3%)
  other arithmetic  6.29 us (3%)
    ppermute x20, starting transfers between devices, hop(): return lax.ppermute(value, 'dp', shift_pairs(axis, step))  40.9 us
    ppermute x7, waiting for transfers between devices, across(): return lax.ppermute(value, 'mp', [(m, m ^ flip) for m in range(4)])  26 us
    ppermute x20, waiting for transfers between devices, hop(): return lax.ppermute(value, 'dp', shift_pairs(axis, step))  22.2 us
    all_to_all x1, waiting for transfers between devices, on_device(): lax.all_to_all(packed, 'dp', split_axis=0, concat_axis=0, tiled=True)  20.9 us
    pallas_call x1, Pallas kernels, on_device(): pl.pallas_call(scan_kernel, out_shape=(jax.ShapeDtypeStruct((tokens, widt...  19.4 us
    pallas_call x1, Pallas kernels, on_device(): pl.pallas_call(gate_kernel, out_shape=(jax.ShapeDtypeStruct((2, tokens, p...  12.7 us
    all_to_all x1, starting transfers between devices, on_device(): lax.all_to_all(packed, 'dp', split_axis=0, concat_axis=0, tiled=True)  12.6 us
    pallas_call x1, Pallas kernels, on_device(): pl.pallas_call(front_kernel, out_shape=(jax.ShapeDtypeStruct((tokens, wid...  11.8 us
  transfers between devices with their start and end apart: 29, of which 13 were waited for; matrix products, arithmetic and copies ran while one was open for 3% of the time, Pallas kernels for 20%

profile of v8, /device:TPU:2, one launch (start us, length us, event | category | flops | bytes accessed | tf_op | source)
XLA Modules:
  0.0 220.6 jit_solution(9819122106143403000)
XLA Ops:
  7.9 0.9 fusion.1
  8.9 7.2 %collective-permute-start.1 = (bf16[48,1024]{1,0:T(8,128)(2,1)S(1)}, bf16[48,1024]{1,0:T(8,128)(2,1)S(1)}, u32[]{:S(2)}, u32[]{:S(2)}) collective-permute-start(bf16[48,1024]{1,0:T(8,128)(2,1)S(1)} %get-tuple-element.52), channel_id=1, source_target_pairs={{0,128},{4,132},{8,136},{12,140},{16,144},{20,148},{24,152},{28,15... | collective-permute-start | bytes 294920 | tf_op jit(solution)/shard_map/ppermute | solution.py:32
  16.1 2.9 %collective-permute-start.2 = (bf16[48,1024]{1,0:T(8,128)(2,1)S(1)}, bf16[48,1024]{1,0:T(8,128)(2,1)S(1)}, u32[]{:S(2)}, u32[]{:S(2)}) collective-permute-start(bf16[48,1024]{1,0:T(8,128)(2,1)S(1)} %get-tuple-element.52), channel_id=1, source_target_pairs={{0,64},{4,68},{8,72},{12,76},{16,80},{20,84},{24,88},{28,92},{32,9... | collective-permute-start | bytes 294920 | tf_op jit(solution)/shard_map/ppermute | solution.py:32
  19.0 6.7 %collective-permute-done = bf16[48,1024]{1,0:T(8,128)(2,1)S(1)} collective-permute-done((bf16[48,1024]{1,0:T(8,128)(2,1)S(1)}, bf16[48,1024]{1,0:T(8,128)(2,1)S(1)}, u32[]{:S(2)}, u32[]{:S(2)}) %collective-permute-start) | collective-permute-done | bytes 98336 | tf_op jit(solution)/shard_map/ppermute | solution.py:32
  25.9 2.2 %collective-permute-start.4 = (bf16[4,48,384]{2,1,0:T(8,128)(2,1)S(1)}, bf16[4,48,384]{2,1,0:T(8,128)(2,1)S(1)}, u32[]{:S(2)}, u32[]{:S(2)}) collective-permute-start(bf16[4,48,384]{2,1,0:T(8,128)(2,1)S(1)} %get-tuple-element.50), channel_id=1, source_target_pairs={{0,8},{4,12},{8,0},{12,4},{16,24},{20,28},{24,16},{28,20},{32,40},... | collective-permute-start | bytes 442376 | tf_op jit(solution)/shard_map/ppermute | solution.py:32
  28.1 3.3 %collective-permute-start.7 = (bf16[4,32,640]{2,1,0:T(8,128)(2,1)S(1)}, bf16[4,32,640]{2,1,0:T(8,128)(2,1)S(1)}, u32[]{:S(2)}, u32[]{:S(2)}) collective-permute-start(bf16[4,32,640]{2,1,0:T(8,128)(2,1)S(1)} %get-tuple-element.48), channel_id=1, source_target_pairs={{0,32},{4,36},{8,40},{12,44},{16,48},{20,52},{24,56},{28,60},{32,0... | collective-permute-start | bytes 491528 | tf_op jit(solution)/shard_map/ppermute | solution.py:32
  31.4 1.4 collective-permute-start.3
  33.4 1.1 collective-permute-start.6
  34.5 1.3 collective-permute-start.8
  36.5 1.4 collective-permute-start.24
  38.0 4.0 %collective-permute-start.23 = (bf16[64,1024]{1,0:T(8,128)(2,1)S(1)}, bf16[64,1024]{1,0:T(8,128)(2,1)S(1)}, u32[]{:S(2)}, u32[]{:S(2)}) collective-permute-start(bf16[64,1024]{1,0:T(8,128)(2,1)S(1)} %pad_maximum_fusion.5), channel_id=1, source_target_pairs={{0,128},{4,132},{8,136},{12,140},{16,144},{20,148},{24,152},{28,15... | collective-permute-start | bytes 393224 | tf_op jit(solution)/shard_map/ppermute | solution.py:32
  42.0 1.2 collective-permute-start.22
  43.4 4.8 %collective-permute-done.24 = bf16[64,1024]{1,0:T(8,128)(2,1)S(1)} collective-permute-done((bf16[64,1024]{1,0:T(8,128)(2,1)S(1)}, bf16[64,1024]{1,0:T(8,128)(2,1)S(1)}, u32[]{:S(2)}, u32[]{:S(2)}) %collective-permute-start.24) | collective-permute-done | bytes 131104 | tf_op jit(solution)/shard_map/ppermute | solution.py:32
  48.2 2.6 %collective-permute-done.23 = bf16[64,1024]{1,0:T(8,128)(2,1)S(1)} collective-permute-done((bf16[64,1024]{1,0:T(8,128)(2,1)S(1)}, bf16[64,1024]{1,0:T(8,128)(2,1)S(1)}, u32[]{:S(2)}, u32[]{:S(2)}) %collective-permute-start.23) | collective-permute-done | bytes 131104 | tf_op jit(solution)/shard_map/ppermute | solution.py:32
  51.5 0.9 pad_maximum_fusion.3
  52.4 2.4 %collective-permute-start.10 = (bf16[528,512]{1,0:T(8,128)(2,1)S(1)}, bf16[528,512]{1,0:T(8,128)(2,1)S(1)}, u32[]{:S(2)}, u32[]{:S(2)}) collective-permute-start(bf16[528,512]{1,0:T(8,128)(2,1)S(1)} %pad_maximum_fusion.2.h0), channel_id=1, source_target_pairs={{0,2},{1,3},{2,0},{3,1},{4,6},{5,7},{6,4},{7,5},{8,10},{9,11},{10,... | collective-permute-start | bytes 1622024 | tf_op jit(solution)/shard_map/ppermute | solution.py:36
  55.4 1.5 collective-permute-start.14
  56.9 1.3 collective-permute-start.13
  58.2 2.0 collective-permute-start.12
  60.1 4.6 %collective-permute-done.10.h2 = bf16[528,512]{1,0:T(8,128)(2,1)S(1)} collective-permute-done((bf16[528,512]{1,0:T(8,128)(2,1)S(1)}, bf16[528,512]{1,0:T(8,128)(2,1)S(1)}, u32[]{:S(2)}, u32[]{:S(2)}) %collective-permute-start.10) | collective-permute-done | bytes 540704 | tf_op jit(solution)/shard_map/ppermute | solution.py:36
  64.8 6.0 %collective-permute-done.15.b4 = bf16[4,4,32,640]{3,2,1,0:T(8,128)(2,1)S(1)} collective-permute-done((bf16[4,4,32,640]{3,2,1,0:T(8,128)(2,1)S(1)}, bf16[4,4,32,640]{3,2,1,0:T(8,128)(2,1)S(1)}, u32[]{:S(2)}, u32[]{:S(2)}) %collective-permute-start.15) | collective-permute-done | bytes 655392 | tf_op jit(solution)/shard_map/ppermute | solution.py:32
  70.7 0.8 slice.36
  71.6 2.8 %collective-permute-start.18 = (bf16[2,4,32,640]{3,2,1,0:T(8,128)(2,1)}, bf16[2,4,32,640]{3,2,1,0:T(8,128)(2,1)}, u32[]{:S(2)}, u32[]{:S(2)}) collective-permute-start(bf16[2,4,32,640]{3,2,1,0:T(8,128)(2,1)} %slice.36), channel_id=1, source_target_pairs={{0,4},{4,8},{8,12},{12,0},{16,20},{20,24},{24,28},{28,16},{32,36},... | collective-permute-start | bytes 983048 | tf_op jit(solution)/shard_map/ppermute | solution.py:32
  74.3 0.8 slice.37
  75.7 1.9 collective-permute-start.19
  78.4 2.5 %collective-permute-start.16 = (bf16[2,4,48,384]{3,2,1,0:T(8,128)(2,1)}, bf16[2,4,48,384]{3,2,1,0:T(8,128)(2,1)S(1)}, u32[]{:S(2)}, u32[]{:S(2)}) collective-permute-start(bf16[2,4,48,384]{3,2,1,0:T(8,128)(2,1)} %slice.34), channel_id=1, source_target_pairs={{0,16},{4,20},{8,24},{12,28},{16,32},{20,36},{24,40},{28,44},{32,4... | collective-permute-start | bytes 884744 | tf_op jit(solution)/shard_map/ppermute | solution.py:32
  80.9 1.9 collective-permute-start.17
  83.6 0.8 copy-done.7
  84.4 6.5 %prep.1 = (bf16[4,512,512]{2,1,0:T(8,128)(2,1)}, bf16[512,512]{1,0:T(8,128)(2,1)}) custom-call(bf16[528,512]{1,0:T(8,128)(2,1)} %copy-done.2, bf16[528,512]{1,0:T(8,128)(2,1)} %copy-done.6, bf16[528,512]{1,0:T(8,128)(2,1)} %copy-done.5, bf16[528,512]{1,0:T(8,128)(2,1)} %copy-done.7), custom_call_target="tpu_custom_call" | custom-call | flops 1000000 | bytes 1024 | tf_op jit(solution)/shard_map/prep/pallas_call | solution.py:447
  90.9 0.8 broadcast_in_dim.30.accepted
  91.7 11.8 %front.1 = (bf16[512,1024]{1,0:T(8,128)(2,1)}, f32[160,512]{1,0:T(8,128)}, bf16[128,1024]{1,0:T(8,128)(2,1)}, f32[3,40,1024]{2,1,0:T(8,128)}) custom-call(s32[2]{0:T(128)} %pad_add_fusion.where, s32[32]{0:T(128)} %pages.5, s32[32,128]{1,0:T(8,128)} %broadcast_in_dim.30.accepted, bf16[4,512,512]{2,1,0:T(8,128)(2,1)} %get-tuple-element.30.normed, ...), custom_call_target="tpu_custom_call" | custom-call | flops 12000000000 | bytes 1024 | tf_op jit(solution)/shard_map/front/pallas_call | solution.py:468
  103.6 1.8 collective-permute-done.20
  105.4 1.8 fusion.2
  107.1 2.3 %collective-permute-start.21 = (bf16[160,512]{1,0:T(8,128)(2,1)S(1)}, bf16[160,512]{1,0:T(8,128)(2,1)S(1)}, u32[]{:S(2)}, u32[]{:S(2)}) collective-permute-start(bf16[160,512]{1,0:T(8,128)(2,1)S(1)} %get-tuple-element.45), channel_id=1, source_target_pairs={{0,2},{1,3},{2,0},{3,1},{4,6},{5,7},{6,4},{7,5},{8,10},{9,11},{10,... | collective-permute-start | bytes 491528 | tf_op jit(solution)/shard_map/ppermute | solution.py:36
  109.4 4.5 %collective-permute-done.21.sums_b = bf16[160,512]{1,0:T(8,128)(2,1)S(1)} collective-permute-done((bf16[160,512]{1,0:T(8,128)(2,1)S(1)}, bf16[160,512]{1,0:T(8,128)(2,1)S(1)}, u32[]{:S(2)}, u32[]{:S(2)}) %collective-permute-start.21) | collective-permute-done | bytes 163872 | tf_op jit(solution)/shard_map/ppermute | solution.py:36
  114.6 19.4 %scan.1 = (f32[512,1024]{1,0:T(8,128)}, f32[8,512,128]{2,1,0:T(8,128)}) custom-call(s32[32]{0:T(128)} %pages.5, s32[32,128]{1,0:T(8,128)} %broadcast_in_dim.30.accepted, f32[160,512]{1,0:T(8,128)} %get-tuple-element.46.sums_a, bf16[160,512]{1,0:T(8,128)(2,1)} %copy-done.10, bf16[128,1024]{1,0:T(8,128)(2,1)} %get-tuple-element.33.dt, f32[1,1024]{1,0:T(1,128)} %bitcast.53, ...), custom_call_target="tpu_custom_call" | custom-call | flops 1000000 | bytes 1024 | tf_op jit(solution)/shard_map/scan/pallas_call | solution.py:498
  134.0 12.7 %gate.1 = (bf16[2,512,512]{2,1,0:T(8,128)(2,1)}, f32[2,512,512]{2,1,0:T(8,128)}) custom-call(s32[2]{0:T(128)} %pad_add_fusion.where, bf16[4,512,512]{2,1,0:T(8,128)(2,1)} %get-tuple-element.30.normed, bf16[512,1024]{1,0:T(8,128)(2,1)} %get-tuple-element.31.inputs, f32[512,1024]{1,0:T(8,128)} %get-tuple-element.34.ys, f32[1,1024]{1,0:T(1,128)} %bitcast.52, ...), custom_call_target="tpu_custom_call" | custom-call | flops 1000000 | bytes 1024 | tf_op jit(solution)/shard_map/gate/pallas_call | solution.py:533
  146.8 2.9 %collective-permute-done.25.near = bf16[2,512,512]{2,1,0:T(8,128)(2,1)S(1)} collective-permute-done((bf16[2,512,512]{2,1,0:T(8,128)(2,1)}, bf16[2,512,512]{2,1,0:T(8,128)(2,1)S(1)}, u32[]{:S(2)}, u32[]{:S(2)}) %collective-permute-start.25) | collective-permute-done | bytes 1048608 | tf_op jit(solution)/shard_map/ppermute | solution.py:36
  149.7 1.8 fusion
  151.4 1.8 collective-permute-start.26
  153.3 12.2 %collective-permute-done.26.far = bf16[512,512]{1,0:T(8,128)(2,1)S(1)} collective-permute-done((bf16[512,512]{1,0:T(8,128)(2,1)S(1)}, bf16[512,512]{1,0:T(8,128)(2,1)S(1)}, u32[]{:S(2)}, u32[]{:S(2)}) %collective-permute-start.26) | collective-permute-done | bytes 524320 | tf_op jit(solution)/shard_map/ppermute | solution.py:36
  165.5 0.8 copy-done.9
  166.3 4.0 %join.1 = bf16[64,16,512]{2,1,0:T(8,128)(2,1)} custom-call(s32[32]{0:T(128)} %targets.3, f32[2,512,512]{2,1,0:T(8,128)} %get-tuple-element.40.keep, bf16[2,512,512]{2,1,0:T(8,128)(2,1)} %copy-done.1, bf16[512,512]{1,0:T(8,128)(2,1)} %copy-done.9, bf16[512,512]{1,0:T(8,128)(2,1)} %get-tuple-element.42.base), custom_call_target="tpu_custom_call" | custom-call | flops 1000000 | bytes 1024 | tf_op jit(solution)/shard_map/join/pallas_call | solution.py:553
  170.3 12.6 %all-to-all-start = ((bf16[64,16,512]{2,1,0:T(8,128)(2,1)}), bf16[64,16,512]{2,1,0:T(8,128)(2,1)S(1)}, u32[]{:S(2)}, u32[]{:S(2)}) async-start(bf16[64,16,512]{2,1,0:T(8,128)(2,1)} %join.1), calls=%async_computation | async-start | bytes 2097152 | tf_op jit(solution)/shard_map/all_to_all | solution.py:563
  183.0 6.4 %settle.1 = f32[640,1024]{1,0:T(8,128)} custom-call(s32[32]{0:T(128)} %pages.5, f32[8,512,128]{2,1,0:T(8,128)} %get-tuple-element.43.kept, f32[640,1024]{1,0:T(8,128)} %bitcast.34), custom_call_target="tpu_custom_call" | custom-call | flops 1000000 | bytes 1024 | tf_op jit(solution)/shard_map/settle/pallas_call | solution.py:523
  189.4 20.9 %all-to-all-done.got = bf16[64,16,512]{2,1,0:T(8,128)(2,1)S(1)} async-done(((bf16[64,16,512]{2,1,0:T(8,128)(2,1)}), bf16[64,16,512]{2,1,0:T(8,128)(2,1)S(1)}, u32[]{:S(2)}, u32[]{:S(2)}) %all-to-all-start) | async-done | bytes 1048608 | tf_op jit(solution)/shard_map/all_to_all | solution.py:563
  210.3 1.0 copy-done
  211.4 2.4 %unpack.1 = bf16[32,16,512]{2,1,0:T(8,128)(2,1)} custom-call(s32[2]{0:T(128)} %pad_add_fusion.where, s32[32]{0:T(128)} %targets.3, bf16[64,16,512]{2,1,0:T(8,128)(2,1)} %copy-done), custom_call_target="tpu_custom_call" | custom-call | tf_op jit(solution)/shard_map/unpack/pallas_call | solution.py:564
  (81 shorter events, 6.8 us)
Async XLA Ops:
  7.2 28.6 %copy-start.15 = (bf16[1024,32]{0,1:T(8,128)(2,1)S(1)}, bf16[1024,32]{0,1:T(8,128)(2,1)}, u32[]{:S(2)}) copy-start(bf16[1024,32]{0,1:T(8,128)(2,1)} %param.28) | copy-start | bytes 196612
  7.2 28.6 %copy-start.16 = (bf16[32,1024]{1,0:T(8,128)(2,1)S(1)}, bf16[32,1024]{1,0:T(8,128)(2,1)}, u32[]{:S(2)}) copy-start(bf16[32,1024]{1,0:T(8,128)(2,1)} %param.20) | copy-start | bytes 196612
  7.2 126.8 %all-gather.3.cloned.1.call-start = ((), (), s32[]{:S(2)}) async-start(), calls=%async_computation.1 | async-start | bytes 8912896 | tf_op jit(solution)/shard_map/all_gather | solution.py:462
  8.9 10.1 %collective-permute-start.1 = (bf16[48,1024]{1,0:T(8,128)(2,1)S(1)}, bf16[48,1024]{1,0:T(8,128)(2,1)S(1)}, u32[]{:S(2)}, u32[]{:S(2)}) collective-permute-start(bf16[48,1024]{1,0:T(8,128)(2,1)S(1)} %get-tuple-element.52), channel_id=1, source_target_pairs={{0,128},{4,132},{8,136},{12,140},{16,144},{20,148},{24,152},{28,15... | collective-permute-start | bytes 294920 | tf_op jit(solution)/shard_map/ppermute | solution.py:32
  16.1 9.7 %collective-permute-start = (bf16[48,1024]{1,0:T(8,128)(2,1)S(1)}, bf16[48,1024]{1,0:T(8,128)(2,1)S(1)}, u32[]{:S(2)}, u32[]{:S(2)}) collective-permute-start(bf16[48,1024]{1,0:T(8,128)(2,1)S(1)} %get-tuple-element.52), channel_id=1, source_target_pairs={{0,192},{4,196},{8,200},{12,204},{16,208},{20,212},{24,216},{28,22... | collective-permute-start | bytes 294920 | tf_op jit(solution)/shard_map/ppermute | solution.py:32
  16.1 9.7 %collective-permute-start.2 = (bf16[48,1024]{1,0:T(8,128)(2,1)S(1)}, bf16[48,1024]{1,0:T(8,128)(2,1)S(1)}, u32[]{:S(2)}, u32[]{:S(2)}) collective-permute-start(bf16[48,1024]{1,0:T(8,128)(2,1)S(1)} %get-tuple-element.52), channel_id=1, source_target_pairs={{0,64},{4,68},{8,72},{12,76},{16,80},{20,84},{24,88},{28,92},{32,9... | collective-permute-start | bytes 294920 | tf_op jit(solution)/shard_map/ppermute | solution.py:32
  25.9 8.6 %collective-permute-start.4 = (bf16[4,48,384]{2,1,0:T(8,128)(2,1)S(1)}, bf16[4,48,384]{2,1,0:T(8,128)(2,1)S(1)}, u32[]{:S(2)}, u32[]{:S(2)}) collective-permute-start(bf16[4,48,384]{2,1,0:T(8,128)(2,1)S(1)} %get-tuple-element.50), channel_id=1, source_target_pairs={{0,8},{4,12},{8,0},{12,4},{16,24},{20,28},{24,16},{28,20},{32,40},... | collective-permute-start | bytes 442376 | tf_op jit(solution)/shard_map/ppermute | solution.py:32
  28.1 13.9 %collective-permute-start.7 = (bf16[4,32,640]{2,1,0:T(8,128)(2,1)S(1)}, bf16[4,32,640]{2,1,0:T(8,128)(2,1)S(1)}, u32[]{:S(2)}, u32[]{:S(2)}) collective-permute-start(bf16[4,32,640]{2,1,0:T(8,128)(2,1)S(1)} %get-tuple-element.48), channel_id=1, source_target_pairs={{0,32},{4,36},{8,40},{12,44},{16,48},{20,52},{24,56},{28,60},{32,0... | collective-permute-start | bytes 491528 | tf_op jit(solution)/shard_map/ppermute | solution.py:32
  31.4 5.2 %collective-permute-start.3 = (bf16[4,48,384]{2,1,0:T(8,128)(2,1)S(1)}, bf16[4,48,384]{2,1,0:T(8,128)(2,1)S(1)}, u32[]{:S(2)}, u32[]{:S(2)}) collective-permute-start(bf16[4,48,384]{2,1,0:T(8,128)(2,1)S(1)} %get-tuple-element.50), channel_id=1, source_target_pairs={{0,12},{4,0},{8,4},{12,8},{16,28},{20,16},{24,20},{28,24},{32,44},... | collective-permute-start | bytes 442376 | tf_op jit(solution)/shard_map/ppermute | solution.py:32
  32.8 5.1 %collective-permute-start.5 = (bf16[4,48,384]{2,1,0:T(8,128)(2,1)S(1)}, bf16[4,48,384]{2,1,0:T(8,128)(2,1)S(1)}, u32[]{:S(2)}, u32[]{:S(2)}) collective-permute-start(bf16[4,48,384]{2,1,0:T(8,128)(2,1)S(1)} %get-tuple-element.50), channel_id=1, source_target_pairs={{0,4},{4,8},{8,12},{12,0},{16,20},{20,24},{24,28},{28,16},{32,36},... | collective-permute-start | bytes 442376 | tf_op jit(solution)/shard_map/ppermute | solution.py:32
  33.4 9.8 %collective-permute-start.6 = (bf16[4,32,640]{2,1,0:T(8,128)(2,1)S(1)}, bf16[4,32,640]{2,1,0:T(8,128)(2,1)S(1)}, u32[]{:S(2)}, u32[]{:S(2)}) collective-permute-start(bf16[4,32,640]{2,1,0:T(8,128)(2,1)S(1)} %get-tuple-element.48), channel_id=1, source_target_pairs={{0,48},{4,52},{8,56},{12,60},{16,0},{20,4},{24,8},{28,12},{32,16},... | collective-permute-start | bytes 491528 | tf_op jit(solution)/shard_map/ppermute | solution.py:32
  34.5 8.8 %collective-permute-start.8 = (bf16[4,32,640]{2,1,0:T(8,128)(2,1)S(1)}, bf16[4,32,640]{2,1,0:T(8,128)(2,1)S(1)}, u32[]{:S(2)}, u32[]{:S(2)}) collective-permute-start(bf16[4,32,640]{2,1,0:T(8,128)(2,1)S(1)} %get-tuple-element.48), channel_id=1, source_target_pairs={{0,16},{4,20},{8,24},{12,28},{16,32},{20,36},{24,40},{28,44},{32,4... | collective-permute-start | bytes 491528 | tf_op jit(solution)/shard_map/ppermute | solution.py:32
  35.8 16.6 %copy-start.17 = (bf16[512]{0:T(512)(128)(2,1)S(1)}, bf16[512]{0:T(512)(128)(2,1)}, u32[]{:S(2)}) copy-start(bf16[512]{0:T(512)(128)(2,1)} %param.18) | copy-start | bytes 3076
  35.8 16.6 %copy-start.8 = (bf16[32,16,512]{2,1,0:T(8,128)(2,1)S(1)}, bf16[32,16,512]{2,1,0:T(8,128)(2,1)}, u32[]{:S(2)}) copy-start(bf16[32,16,512]{2,1,0:T(8,128)(2,1)} %param.17) | copy-start | bytes 1572868
  36.5 11.7 %collective-permute-start.24 = (bf16[64,1024]{1,0:T(8,128)(2,1)S(1)}, bf16[64,1024]{1,0:T(8,128)(2,1)S(1)}, u32[]{:S(2)}, u32[]{:S(2)}) collective-permute-start(bf16[64,1024]{1,0:T(8,128)(2,1)S(1)} %pad_maximum_fusion.5), channel_id=1, source_target_pairs={{0,64},{4,68},{8,72},{12,76},{16,80},{20,84},{24,88},{28,92},{32,9... | collective-permute-start | bytes 393224 | tf_op jit(solution)/shard_map/ppermute | solution.py:32
  38.0 12.8 %collective-permute-start.23 = (bf16[64,1024]{1,0:T(8,128)(2,1)S(1)}, bf16[64,1024]{1,0:T(8,128)(2,1)S(1)}, u32[]{:S(2)}, u32[]{:S(2)}) collective-permute-start(bf16[64,1024]{1,0:T(8,128)(2,1)S(1)} %pad_maximum_fusion.5), channel_id=1, source_target_pairs={{0,128},{4,132},{8,136},{12,140},{16,144},{20,148},{24,152},{28,15... | collective-permute-start | bytes 393224 | tf_op jit(solution)/shard_map/ppermute | solution.py:32
  42.0 9.5 %collective-permute-start.22 = (bf16[64,1024]{1,0:T(8,128)(2,1)S(1)}, bf16[64,1024]{1,0:T(8,128)(2,1)S(1)}, u32[]{:S(2)}, u32[]{:S(2)}) collective-permute-start(bf16[64,1024]{1,0:T(8,128)(2,1)S(1)} %pad_maximum_fusion.5), channel_id=1, source_target_pairs={{0,192},{4,196},{8,200},{12,204},{16,208},{20,212},{24,216},{28,22... | collective-permute-start | bytes 393224 | tf_op jit(solution)/shard_map/ppermute | solution.py:32
  43.2 28.3 %copy-start.4 = (bf16[4,4,48,384]{3,2,1,0:T(8,128)(2,1)}, bf16[4,4,48,384]{3,2,1,0:T(8,128)(2,1)S(1)}, u32[]{:S(2)}) copy-start(bf16[4,4,48,384]{3,2,1,0:T(8,128)(2,1)S(1)} %pad_maximum_fusion.1.a0) | copy-start | bytes 1769476
  43.4 35.0 %copy-start.3 = (bf16[4,4,32,640]{3,2,1,0:T(8,128)(2,1)}, bf16[4,4,32,640]{3,2,1,0:T(8,128)(2,1)S(1)}, u32[]{:S(2)}) copy-start(bf16[4,4,32,640]{3,2,1,0:T(8,128)(2,1)S(1)} %pad_maximum_fusion.b0) | copy-start | bytes 1966084
  52.4 31.1 %copy-start.2 = (bf16[528,512]{1,0:T(8,128)(2,1)}, bf16[528,512]{1,0:T(8,128)(2,1)S(1)}, u32[]{:S(2)}) copy-start(bf16[528,512]{1,0:T(8,128)(2,1)S(1)} %pad_maximum_fusion.2.h0) | copy-start | bytes 1622020
  52.4 12.3 %collective-permute-start.10 = (bf16[528,512]{1,0:T(8,128)(2,1)S(1)}, bf16[528,512]{1,0:T(8,128)(2,1)S(1)}, u32[]{:S(2)}, u32[]{:S(2)}) collective-permute-start(bf16[528,512]{1,0:T(8,128)(2,1)S(1)} %pad_maximum_fusion.2.h0), channel_id=1, source_target_pairs={{0,2},{1,3},{2,0},{3,1},{4,6},{5,7},{6,4},{7,5},{8,10},{9,11},{10,... | collective-permute-start | bytes 1622024 | tf_op jit(solution)/shard_map/ppermute | solution.py:36
  54.8 15.9 %collective-permute-start.15 = (bf16[4,4,32,640]{3,2,1,0:T(8,128)(2,1)S(1)}, bf16[4,4,32,640]{3,2,1,0:T(8,128)(2,1)S(1)}, u32[]{:S(2)}, u32[]{:S(2)}) collective-permute-start(bf16[4,4,32,640]{3,2,1,0:T(8,128)(2,1)S(1)} %pad_maximum_fusion.b0), channel_id=1, source_target_pairs={{0,4},{4,8},{8,12},{12,0},{16,20},{20,24},{24,28},{28,16},{32,36},... | collective-permute-start | bytes 1966088 | tf_op jit(solution)/shard_map/ppermute | solution.py:32
  55.4 16.1 %collective-permute-start.14 = (bf16[4,4,32,640]{3,2,1,0:T(8,128)(2,1)S(1)}, bf16[4,4,32,640]{3,2,1,0:T(8,128)(2,1)S(1)}, u32[]{:S(2)}, u32[]{:S(2)}) collective-permute-start(bf16[4,4,32,640]{3,2,1,0:T(8,128)(2,1)S(1)} %pad_maximum_fusion.b0), channel_id=1, source_target_pairs={{0,12},{4,0},{8,4},{12,8},{16,28},{20,16},{24,20},{28,24},{32,44},... | collective-permute-start | bytes 1966088 | tf_op jit(solution)/shard_map/ppermute | solution.py:32
  56.9 18.8 %collective-permute-start.13 = (bf16[4,4,48,384]{3,2,1,0:T(8,128)(2,1)S(1)}, bf16[4,4,48,384]{3,2,1,0:T(8,128)(2,1)S(1)}, u32[]{:S(2)}, u32[]{:S(2)}) collective-permute-start(bf16[4,4,48,384]{3,2,1,0:T(8,128)(2,1)S(1)} %pad_maximum_fusion.1.a0), channel_id=1, source_target_pairs={{0,16},{4,20},{8,24},{12,28},{16,32},{20,36},{24,40},{28,44},{32,4... | collective-permute-start | bytes 1769480 | tf_op jit(solution)/shard_map/ppermute | solution.py:32
  58.2 20.2 %collective-permute-start.12 = (bf16[4,4,48,384]{3,2,1,0:T(8,128)(2,1)S(1)}, bf16[4,4,48,384]{3,2,1,0:T(8,128)(2,1)S(1)}, u32[]{:S(2)}, u32[]{:S(2)}) collective-permute-start(bf16[4,4,48,384]{3,2,1,0:T(8,128)(2,1)S(1)} %pad_maximum_fusion.1.a0), channel_id=1, source_target_pairs={{0,48},{4,52},{8,56},{12,60},{16,0},{20,4},{24,8},{28,12},{32,16},... | collective-permute-start | bytes 1769480 | tf_op jit(solution)/shard_map/ppermute | solution.py:32
  64.8 18.8 %copy-start.5 = (bf16[528,512]{1,0:T(8,128)(2,1)}, bf16[528,512]{1,0:T(8,128)(2,1)S(1)}, u32[]{:S(2)}) copy-start(bf16[528,512]{1,0:T(8,128)(2,1)S(1)} %collective-permute-done.10.h2) | copy-start | bytes 1622020
  64.8 16.2 %collective-permute-start.9 = (bf16[528,512]{1,0:T(8,128)(2,1)S(1)}, bf16[528,512]{1,0:T(8,128)(2,1)S(1)}, u32[]{:S(2)}, u32[]{:S(2)}) collective-permute-start(bf16[528,512]{1,0:T(8,128)(2,1)S(1)} %pad_maximum_fusion.2.h0), channel_id=1, source_target_pairs={{0,1},{1,0},{2,3},{3,2},{4,5},{5,4},{6,7},{7,6},{8,9},{9,8},{10,11... | collective-permute-start | bytes 1622024 | tf_op jit(solution)/shard_map/ppermute | solution.py:36
  70.7 12.1 %copy-start.11 = (bf16[4,4,32,640]{3,2,1,0:T(8,128)(2,1)}, bf16[4,4,32,640]{3,2,1,0:T(8,128)(2,1)S(1)}, u32[]{:S(2)}) copy-start(bf16[4,4,32,640]{3,2,1,0:T(8,128)(2,1)S(1)} %collective-permute-done.15.b4) | copy-start | bytes 1966084
  70.7 12.8 %collective-permute-start.11 = (bf16[528,512]{1,0:T(8,128)(2,1)S(1)}, bf16[528,512]{1,0:T(8,128)(2,1)S(1)}, u32[]{:S(2)}, u32[]{:S(2)}) collective-permute-start(bf16[528,512]{1,0:T(8,128)(2,1)S(1)} %collective-permute-done.10.h2), channel_id=1, source_target_pairs={{0,1},{1,0},{2,3},{3,2},{4,5},{5,4},{6,7},{7,6},{8,9},{9,8},{10,11... | collective-permute-start | bytes 1622024 | tf_op jit(solution)/shard_map/ppermute | solution.py:36
  71.6 19.3 %copy-start.18 = (s32[32]{0:T(128)S(1)}, s32[32]{0:T(128)}, u32[]{:S(2)}) copy-start(s32[32]{0:T(128)} %param.33) | copy-start | bytes 388
  71.6 11.3 %copy-start.12 = (bf16[4,4,32,640]{3,2,1,0:T(8,128)(2,1)}, bf16[4,4,32,640]{3,2,1,0:T(8,128)(2,1)S(1)}, u32[]{:S(2)}) copy-start(bf16[4,4,32,640]{3,2,1,0:T(8,128)(2,1)S(1)} %collective-permute-done.14.b1) | copy-start | bytes 1966084
  71.6 19.3 %collective-permute-start.18 = (bf16[2,4,32,640]{3,2,1,0:T(8,128)(2,1)}, bf16[2,4,32,640]{3,2,1,0:T(8,128)(2,1)}, u32[]{:S(2)}, u32[]{:S(2)}) collective-permute-start(bf16[2,4,32,640]{3,2,1,0:T(8,128)(2,1)} %slice.36), channel_id=1, source_target_pairs={{0,4},{4,8},{8,12},{12,0},{16,20},{20,24},{24,28},{28,16},{32,36},... | collective-permute-start | bytes 983048 | tf_op jit(solution)/shard_map/ppermute | solution.py:32
  75.7 7.2 %copy-start.13 = (bf16[4,4,48,384]{3,2,1,0:T(8,128)(2,1)}, bf16[4,4,48,384]{3,2,1,0:T(8,128)(2,1)S(1)}, u32[]{:S(2)}) copy-start(bf16[4,4,48,384]{3,2,1,0:T(8,128)(2,1)S(1)} %collective-permute-done.13.a4) | copy-start | bytes 1769476
  75.7 15.2 %collective-permute-start.19 = (bf16[2,4,32,640]{3,2,1,0:T(8,128)(2,1)}, bf16[2,4,32,640]{3,2,1,0:T(8,128)(2,1)}, u32[]{:S(2)}, u32[]{:S(2)}) collective-permute-start(bf16[2,4,32,640]{3,2,1,0:T(8,128)(2,1)} %slice.37), channel_id=1, source_target_pairs={{0,12},{4,0},{8,4},{12,8},{16,28},{20,16},{24,20},{28,24},{32,44},... | collective-permute-start | bytes 983048 | tf_op jit(solution)/shard_map/ppermute | solution.py:32
  78.4 4.5 %copy-start.14 = (bf16[4,4,48,384]{3,2,1,0:T(8,128)(2,1)}, bf16[4,4,48,384]{3,2,1,0:T(8,128)(2,1)S(1)}, u32[]{:S(2)}) copy-start(bf16[4,4,48,384]{3,2,1,0:T(8,128)(2,1)S(1)} %collective-permute-done.12.a1) | copy-start | bytes 1769476
  78.4 12.5 %collective-permute-start.16 = (bf16[2,4,48,384]{3,2,1,0:T(8,128)(2,1)}, bf16[2,4,48,384]{3,2,1,0:T(8,128)(2,1)S(1)}, u32[]{:S(2)}, u32[]{:S(2)}) collective-permute-start(bf16[2,4,48,384]{3,2,1,0:T(8,128)(2,1)} %slice.34), channel_id=1, source_target_pairs={{0,16},{4,20},{8,24},{12,28},{16,32},{20,36},{24,40},{28,44},{32,4... | collective-permute-start | bytes 884744 | tf_op jit(solution)/shard_map/ppermute | solution.py:32
  80.9 2.6 %copy-start.6 = (bf16[528,512]{1,0:T(8,128)(2,1)}, bf16[528,512]{1,0:T(8,128)(2,1)S(1)}, u32[]{:S(2)}) copy-start(bf16[528,512]{1,0:T(8,128)(2,1)S(1)} %collective-permute-done.9.h1) | copy-start | bytes 1622020
  80.9 9.9 %collective-permute-start.17 = (bf16[2,4,48,384]{3,2,1,0:T(8,128)(2,1)S(1)}, bf16[2,4,48,384]{3,2,1,0:T(8,128)(2,1)S(1)}, u32[]{:S(2)}, u32[]{:S(2)}) collective-permute-start(bf16[2,4,48,384]{3,2,1,0:T(8,128)(2,1)S(1)} %slice.35), channel_id=1, source_target_pairs={{0,48},{4,52},{8,56},{12,60},{16,0},{20,4},{24,8},{28,12},{32,16},... | collective-permute-start | bytes 884744 | tf_op jit(solution)/shard_map/ppermute | solution.py:32
  90.8 0.8 copy-start.19
  90.9 0.8 copy-start.20
  103.5 1.9 collective-permute-start.20
  107.1 6.7 %collective-permute-start.21 = (bf16[160,512]{1,0:T(8,128)(2,1)S(1)}, bf16[160,512]{1,0:T(8,128)(2,1)S(1)}, u32[]{:S(2)}, u32[]{:S(2)}) collective-permute-start(bf16[160,512]{1,0:T(8,128)(2,1)S(1)} %get-tuple-element.45), channel_id=1, source_target_pairs={{0,2},{1,3},{2,0},{3,1},{4,6},{5,7},{6,4},{7,5},{8,10},{9,11},{10,... | collective-permute-start | bytes 491528 | tf_op jit(solution)/shard_map/ppermute | solution.py:36
  146.7 3.0 %collective-permute-start.25 = (bf16[2,512,512]{2,1,0:T(8,128)(2,1)}, bf16[2,512,512]{2,1,0:T(8,128)(2,1)S(1)}, u32[]{:S(2)}, u32[]{:S(2)}) collective-permute-start(bf16[2,512,512]{2,1,0:T(8,128)(2,1)} %get-tuple-element.41), channel_id=1, source_target_pairs={{0,1},{1,0},{2,3},{3,2},{4,5},{5,4},{6,7},{7,6},{8,9},{9,8},{10,11... | collective-permute-start | bytes 3145736 | tf_op jit(solution)/shard_map/ppermute | solution.py:36
  149.7 15.8 %copy-start.1 = (bf16[2,512,512]{2,1,0:T(8,128)(2,1)}, bf16[2,512,512]{2,1,0:T(8,128)(2,1)S(1)}, u32[]{:S(2)}) copy-start(bf16[2,512,512]{2,1,0:T(8,128)(2,1)S(1)} %collective-permute-done.25.near) | copy-start | bytes 3145732
  151.4 14.1 %collective-permute-start.26 = (bf16[512,512]{1,0:T(8,128)(2,1)S(1)}, bf16[512,512]{1,0:T(8,128)(2,1)S(1)}, u32[]{:S(2)}, u32[]{:S(2)}) collective-permute-start(bf16[512,512]{1,0:T(8,128)(2,1)S(1)} %fusion), channel_id=1, source_target_pairs={{0,2},{1,3},{2,0},{3,1},{4,6},{5,7},{6,4},{7,5},{8,10},{9,11},{10,... | collective-permute-start | bytes 1572872 | tf_op jit(solution)/shard_map/ppermute | solution.py:36
  165.5 0.8 copy-start.9
  170.3 40.0 %all-to-all-start = ((bf16[64,16,512]{2,1,0:T(8,128)(2,1)}), bf16[64,16,512]{2,1,0:T(8,128)(2,1)S(1)}, u32[]{:S(2)}, u32[]{:S(2)}) async-start(bf16[64,16,512]{2,1,0:T(8,128)(2,1)} %join.1), calls=%async_computation | async-start | bytes 2097152 | tf_op jit(solution)/shard_map/all_to_all | solution.py:563
  210.3 1.0 copy-start
  (2 other events, 1.5 us)
Sparse Core Ops, SparseCore 0:
  52.5 80.2 all-gather.2
